TPU v7x, 32 devices: a whole 2x2x4 slice. The times are simulated.
32 devices in a mesh: dp: 4 (over z), vocab: 8 (over y, x, core).
Axes of the slice: x: 2, y: 2, z: 4, core: 2. Of those that a mesh axis runs over, the one named last changes fastest.
Arguments:
- token_ids: int32 [32, 512], P(('dp', 'vocab')), may hold values from 0 to 15359, as said below
- lengths: int32 [32], P(('dp', 'vocab')), may hold values from 120 to 512
- mask_pos: int32 [32, 120], P(('dp', 'vocab')), may hold values from 0 to 511, as said below
- mask_count: int32 [32], P(('dp', 'vocab')), may hold values from 5 to 120
- owner_order: int32 [58624], replicated, may hold values from 0 to 58623, as said below
- step_count: int32 [1], replicated, may hold values from 1 to 20
- teacher_flat: bfloat16 [58624, 128], P(('dp', 'vocab')), may hold values from -4 to 4
- mentor_lexicon_weights: bfloat16 [15360, 768], P('vocab'), may hold values from -2 to 2
- student_flat: float32 [58624, 128], P(('dp', 'vocab')), may hold values from -4 to 4
- flat_first: float32 [58624, 128], P(('dp', 'vocab')), may hold values from -3.8146973e-06 to 3.8146973e-06
- flat_second: float32 [58624, 128], P(('dp', 'vocab')), may hold values from 1.0585976e-13 to 4.2343903e-13
- student_embed: float32 [15360, 768], P('vocab', 'dp'), may hold values from -2 to 2
- embed_first: float32 [15360, 768], P('vocab', 'dp'), may hold values from -3.8146973e-06 to 3.8146973e-06
- embed_second: float32 [15360, 768], P('vocab', 'dp'), may hold values from 1.0585976e-13 to 4.2343903e-13
Outputs:
- loss: float32 [], replicated
- grad_norm: float32 [], replicated
- new_flat: float32 [58624, 128], P(('dp', 'vocab'))
- new_flat_first: float32 [58624, 128], P(('dp', 'vocab'))
- new_flat_second: float32 [58624, 128], P(('dp', 'vocab'))
- new_embed: float32 [15360, 768], P('vocab', 'dp')
- new_embed_first: float32 [15360, 768], P('vocab', 'dp')
- new_embed_second: float32 [15360, 768], P('vocab', 'dp')
Inputs may be any that keep to these rules, and one draw needn't show every extreme that they name: `token_ids`: ids of the vocabulary. `owner_order`: each stored tile holds a different tile of the vector. `mask_pos`: positions distinct within a row and less than that sequence's length.
All inputs are finite; a program needn't handle non-finite values.
Results may differ from a plain program's by a relative error of at most 0.002.
The roundings to bfloat16 on the way count: a program that leaves them out, or rounds other values in their place, can miss the bound.
Values may be sent and summed in bfloat16 or wider, within the bound.
No kernel may reach another device: no remote copies, remote signals or barrier semaphores. Data moves between devices by JAX's collectives and lax.ppermute only.
A program may use at most 256 MiB of HBM per device.

v0:
```python
import jax
import jax.numpy as jnp
from jax import lax
from jax.sharding import PartitionSpec as P

D = 768
HEADS = 12
HEAD_DIM = 64
FF = 3072
LEN = 512
CAP = 120
TILE = 128


smoothing_heat_scale = 2.0
mixing_coefficient = 5.0
cosine_weight = 20.0
clip_norm = 0.01
beta_first = 0.9
beta_second = 0.98
adam_eps = 1e-08
weight_decay = 0.01
learn_rate = 0.1
norm_eps = 1e-12
cosine_eps = 1e-06


def combined_all(value, axis, combine):
    everything = jax.tree.map(lambda part: lax.all_gather(part, axis), value)
    first = jax.tree.map(lambda part: part[0], everything)

    def step(k, so_far):
        return combine(so_far, jax.tree.map(lambda part: part[k], everything))

    return lax.fori_loop(1, lax.axis_size(axis), step, first)


def array_multiply(left_side, right_side):
    return jnp.dot(left_side, right_side, preferred_element_type=jnp.float32)


def matmul_left(left_side, right_side):
    return lax.dot_general(
        left_side, right_side, (((0,), (0,)), ((), ())), preferred_element_type=jnp.float32
    )


def trailing_array_multiply(left_side, right_side):
    return lax.dot_general(
        left_side, right_side, (((1,), (1,)), ((), ())), preferred_element_type=jnp.float32
    )


def unpack(vector):
    layout = [
        ("qkv", (D, 3 * D)),
        ("out", (D, D)),
        ("up", (D, FF)),
        ("down", (FF, D)),
        ("place", (LEN, D)),
        ("small", (10, D)),
        ("upbias", (FF,)),
    ]
    pieces = {}
    offset = 0
    for piece_name, piece_dims in layout:
        entries = 1
        for extent in piece_dims:
            entries = entries * extent
        pieces[piece_name] = vector[offset : offset + entries].reshape(piece_dims)
        offset = offset + entries
    return pieces


def norm_forward(values, gain_row, shift_row):
    center = values - jnp.mean(values, axis=-1, keepdims=True)
    inverse = lax.rsqrt(jnp.mean(center * center, axis=-1, keepdims=True) + norm_eps)
    normed = center * inverse
    return (normed * gain_row + shift_row, normed, inverse)


def norm_backward(grad_out, normed, inverse, gain_row):
    scaled = grad_out * gain_row
    grad_in = inverse * (
        scaled
        - jnp.mean(scaled, axis=-1, keepdims=True)
        - normed * jnp.mean(scaled * normed, axis=-1, keepdims=True)
    )
    return (grad_in, jnp.sum(grad_out * normed, axis=0), jnp.sum(grad_out, axis=0))


def gelu_slope(values):
    return (
        0.5 * (1.0 + lax.erf(values * 0.7071067811865476))
        + values * jnp.exp(-0.5 * values * values) * 0.3989422804014327
    )


def key_scores(projected, lengths):
    seqs_count = lengths.shape[0]
    split_heads = projected.reshape(seqs_count, LEN, 3, HEADS, HEAD_DIM)
    scores = jnp.einsum(
        "sqhd,skhd->shqk",
        split_heads[:, :, 0],
        split_heads[:, :, 1],
        preferred_element_type=jnp.float32,
    ) * HEAD_DIM ** (-0.5)
    live_keys = jnp.arange(LEN)[None, :] < lengths[:, None]
    return (jnp.where(live_keys[:, None, None, :], scores, -1000000000.0), split_heads)


def layer_forward(pieces, looked, lengths):
    small_rows = pieces["small"].astype(jnp.float32)
    seqs_count = lengths.shape[0]
    rows_here = seqs_count * LEN
    summed = (
        looked.reshape(seqs_count, LEN, D) + pieces["place"].astype(jnp.float32)[None]
    ).reshape(rows_here, D)
    first_norm, normed_zero, inverse_zero = norm_forward(summed, small_rows[4], small_rows[5])
    inputs = first_norm.astype(jnp.bfloat16)
    qkv_bias = jnp.concatenate([small_rows[0], jnp.zeros((D,), jnp.float32), small_rows[1]])
    projected = (array_multiply(inputs, pieces["qkv"]) + qkv_bias).astype(jnp.bfloat16)
    scores, split_heads = key_scores(projected, lengths)
    peak = jnp.max(scores, axis=-1, keepdims=True)
    exps = jnp.exp(scores - peak)
    totals = jnp.sum(exps, axis=-1, keepdims=True)
    probabilities = (exps / totals).astype(jnp.bfloat16)
    logsum = peak + jnp.log(totals)
    context = jnp.einsum(
        "shqk,skhd->sqhd", probabilities, split_heads[:, :, 2], preferred_element_type=jnp.float32
    )
    context = context.reshape(rows_here, D).astype(jnp.bfloat16)
    attended = array_multiply(context, pieces["out"]) + small_rows[2]
    middle, normed_one, inverse_one = norm_forward(
        first_norm + attended, small_rows[6], small_rows[7]
    )
    middle_low = middle.astype(jnp.bfloat16)
    hidden = array_multiply(middle_low, pieces["up"]) + pieces["upbias"].astype(jnp.float32)
    activated = jax.nn.gelu(hidden, approximate=False).astype(jnp.bfloat16)
    output = array_multiply(activated, pieces["down"]) + small_rows[3]
    final_lines, normed_two, inverse_two = norm_forward(
        middle + output, small_rows[8], small_rows[9]
    )
    saved = {
        "inputs": inputs,
        "projected": projected,
        "logsum": logsum,
        "context": context,
        "middle_low": middle_low,
        "hidden": hidden,
        "activated": activated,
        "normed_zero": normed_zero,
        "inverse_zero": inverse_zero,
        "normed_one": normed_one,
        "inverse_one": inverse_one,
        "normed_two": normed_two,
        "inverse_two": inverse_two,
    }
    return (final_lines, saved)


def layer_backward(pieces, saved, grad_final, lengths):
    small_rows = pieces["small"].astype(jnp.float32)
    seqs_count = lengths.shape[0]
    rows_here = seqs_count * LEN
    grad_sum_two, grad_gain_two, grad_shift_two = norm_backward(
        grad_final, saved["normed_two"], saved["inverse_two"], small_rows[8]
    )
    grad_out = grad_sum_two.astype(jnp.bfloat16)
    grad_down = matmul_left(saved["activated"], grad_out)
    grad_act = trailing_array_multiply(grad_out, pieces["down"])
    grad_hidden = (grad_act * gelu_slope(saved["hidden"])).astype(jnp.bfloat16)
    grad_up = matmul_left(saved["middle_low"], grad_hidden)
    grad_middle = grad_sum_two + trailing_array_multiply(grad_hidden, pieces["up"])
    grad_sum_one, grad_gain_one, grad_shift_one = norm_backward(
        grad_middle, saved["normed_one"], saved["inverse_one"], small_rows[6]
    )
    grad_att = grad_sum_one.astype(jnp.bfloat16)
    grad_outw = matmul_left(saved["context"], grad_att)
    grad_context = (
        trailing_array_multiply(grad_att, pieces["out"])
        .astype(jnp.bfloat16)
        .reshape(seqs_count, LEN, HEADS, HEAD_DIM)
    )
    scores, split_heads = key_scores(saved["projected"], lengths)
    probabilities = jnp.exp(scores - saved["logsum"])
    grad_probs = jnp.einsum(
        "sqhd,skhd->shqk", grad_context, split_heads[:, :, 2], preferred_element_type=jnp.float32
    )
    grad_values = jnp.einsum(
        "shqk,sqhd->skhd",
        probabilities.astype(jnp.bfloat16),
        grad_context,
        preferred_element_type=jnp.float32,
    )
    grad_scores = probabilities * (
        grad_probs - jnp.sum(grad_probs * probabilities, axis=-1, keepdims=True)
    )
    grad_scores = grad_scores.astype(jnp.bfloat16)
    grad_queries = jnp.einsum(
        "shqk,skhd->sqhd", grad_scores, split_heads[:, :, 1], preferred_element_type=jnp.float32
    ) * HEAD_DIM ** (-0.5)
    grad_keys = jnp.einsum(
        "shqk,sqhd->skhd", grad_scores, split_heads[:, :, 0], preferred_element_type=jnp.float32
    ) * HEAD_DIM ** (-0.5)
    grad_proj = (
        jnp.stack([grad_queries, grad_keys, grad_values], axis=2)
        .reshape(rows_here, 3 * D)
        .astype(jnp.bfloat16)
    )
    grad_qkv = matmul_left(saved["inputs"], grad_proj)
    grad_bias_all = jnp.sum(grad_proj.astype(jnp.float32), axis=0)
    grad_first = grad_sum_one + trailing_array_multiply(grad_proj, pieces["qkv"])
    grad_embedded, grad_gain_zero, grad_shift_zero = norm_backward(
        grad_first, saved["normed_zero"], saved["inverse_zero"], small_rows[4]
    )
    grad_place = jnp.sum(grad_embedded.reshape(seqs_count, LEN, D), axis=0)
    grad_small = jnp.stack(
        [
            grad_bias_all[:D],
            grad_bias_all[2 * D :],
            jnp.sum(grad_att.astype(jnp.float32), axis=0),
            jnp.sum(grad_out.astype(jnp.float32), axis=0),
            grad_gain_zero,
            grad_shift_zero,
            grad_gain_one,
            grad_shift_one,
            grad_gain_two,
            grad_shift_two,
        ]
    )
    grad_upbias = jnp.sum(grad_hidden.astype(jnp.float32), axis=0)
    flat_local = jnp.concatenate(
        [
            grad_qkv.reshape(-1),
            grad_outw.reshape(-1),
            grad_up.reshape(-1),
            grad_down.reshape(-1),
            grad_place.reshape(-1),
            grad_small.reshape(-1),
            grad_upbias,
        ]
    )
    return (flat_local, grad_embedded)


def combine_stats(earlier, later):
    peak_s = jnp.maximum(earlier[0], later[0])
    peak_t = jnp.maximum(earlier[2], later[2])
    factor_early = jnp.exp(earlier[0] - peak_s)
    factor_late = jnp.exp(later[0] - peak_s)
    teacher_early = jnp.exp(earlier[2] - peak_t)
    teacher_late = jnp.exp(later[2] - peak_t)
    return (
        peak_s,
        earlier[1] * factor_early + later[1] * factor_late,
        peak_t,
        earlier[3] * teacher_early + later[3] * teacher_late,
        earlier[4] * teacher_early + later[4] * teacher_late,
    )


def adam_step(weight, first_moment, second, gradient, step_float):
    new_first = beta_first * first_moment + (1.0 - beta_first) * gradient
    new_second = beta_second * second + (1.0 - beta_second) * gradient * gradient
    fix_first = 1.0 - jnp.power(beta_first, step_float)
    fix_second = 1.0 - jnp.power(beta_second, step_float)
    update = new_first / fix_first / (jnp.sqrt(new_second / fix_second) + adam_eps)
    return (weight - learn_rate * (update + weight_decay * weight), new_first, new_second)


def on_device(
    token_ids,
    lengths,
    mask_pos,
    mask_count,
    owner_order,
    step_count,
    teacher_flat,
    mentor_lexicon_weights,
    student_flat,
    flat_first,
    flat_second,
    student_embed,
    embed_first,
    embed_second,
):
    student_tiles, teacher_tiles = (
        lax.all_gather(student_flat.astype(jnp.bfloat16), ("dp", "vocab"), axis=0, tiled=True),
        lax.all_gather(teacher_flat, ("dp", "vocab"), axis=0, tiled=True),
    )
    logical = jnp.zeros_like(student_tiles).at[owner_order].set(student_tiles)
    student = unpack(logical.reshape(-1))
    teacher = unpack(teacher_tiles.reshape(-1))
    table_low = lax.all_gather(student_embed.astype(jnp.bfloat16), "dp", axis=1, tiled=True)
    token_total, masked_total = lax.psum(
        (jnp.sum(lengths).astype(jnp.float32), jnp.sum(mask_count).astype(jnp.float32)),
        ("dp", "vocab"),
    )
    seqs_here = token_ids.shape[0]
    rows_here = seqs_here * LEN
    group_ids = lax.all_gather(token_ids.reshape(rows_here), "vocab", axis=0, tiled=True)
    vocab_rows = table_low.shape[0]
    local_ids = group_ids - lax.axis_index("vocab") * vocab_rows
    inside = (local_ids >= 0) & (local_ids < vocab_rows)
    clipped = jnp.clip(local_ids, 0, vocab_rows - 1)
    rows_student = jnp.where(inside[:, None], table_low[clipped].astype(jnp.float32), 0.0)
    rows_teacher = jnp.where(
        inside[:, None], mentor_lexicon_weights[clipped].astype(jnp.float32), 0.0
    )
    looked_s, looked_t = (
        lax.psum_scatter(
            rows_student.astype(jnp.bfloat16), "vocab", scatter_dimension=0, tiled=True
        ).astype(jnp.float32),
        lax.psum_scatter(
            rows_teacher.astype(jnp.bfloat16), "vocab", scatter_dimension=0, tiled=True
        ).astype(jnp.float32),
    )
    final_t = layer_forward(teacher, looked_t, lengths)[0]
    final_s, saved = layer_forward(student, looked_s, lengths)
    offsets = (mask_pos + jnp.arange(seqs_here)[:, None] * LEN).reshape(-1)
    slot_live = (jnp.arange(CAP)[None, :] < mask_count[:, None]).reshape(-1)
    picked_s = final_s[offsets].astype(jnp.bfloat16)
    picked_t = final_t[offsets].astype(jnp.bfloat16)
    learner_picked, mentor_picked, all_live = (
        lax.all_gather(picked_s, "vocab", axis=0, tiled=True),
        lax.all_gather(picked_t, "vocab", axis=0, tiled=True),
        lax.all_gather(slot_live.astype(jnp.bfloat16), "vocab", axis=0, tiled=True),
    )
    learner_energy = trailing_array_multiply(learner_picked, table_low) / smoothing_heat_scale
    teacher_logit = (
        trailing_array_multiply(mentor_picked, mentor_lexicon_weights) / smoothing_heat_scale
    )
    peak_s = jnp.max(learner_energy, axis=1)
    peak_t = jnp.max(teacher_logit, axis=1)
    teacher_exps = jnp.exp(teacher_logit - peak_t[:, None])
    local_stats = (
        peak_s,
        jnp.sum(jnp.exp(learner_energy - peak_s[:, None]), axis=1),
        peak_t,
        jnp.sum(teacher_exps, axis=1),
        jnp.sum(teacher_exps * (teacher_logit - learner_energy), axis=1),
    )
    merged_stats = combined_all(local_stats, "vocab", combine_stats)
    logsum_s = merged_stats[0] + jnp.log(merged_stats[1])
    logsum_t = merged_stats[2] + jnp.log(merged_stats[3])
    live_weighting = all_live.astype(jnp.float32)
    diverge = merged_stats[4] / merged_stats[3] - logsum_t + logsum_s
    block_rows = seqs_here * CAP
    divergence_part = jnp.sum(
        lax.dynamic_slice_in_dim(
            diverge * live_weighting, lax.axis_index("vocab") * block_rows, block_rows
        )
    )
    student_probs = jnp.exp(learner_energy - logsum_s[:, None])
    teacher_probs = jnp.exp(teacher_logit - logsum_t[:, None])
    grad_logit = (
        mixing_coefficient
        * smoothing_heat_scale
        / masked_total
        * live_weighting[:, None]
        * (student_probs - teacher_probs)
    ).astype(jnp.bfloat16)
    grad_rows = lax.psum_scatter(
        array_multiply(grad_logit, table_low), "vocab", scatter_dimension=0, tiled=True
    )
    grad_table = matmul_left(grad_logit, learner_picked)
    products = jnp.sum(final_s * final_t, axis=1)
    inverse_s = lax.rsqrt(jnp.sum(final_s * final_s, axis=1) + cosine_eps)
    inverse_t = lax.rsqrt(jnp.sum(final_t * final_t, axis=1) + cosine_eps)
    live_rows = (jnp.arange(LEN)[None, :] < lengths[:, None]).reshape(-1)
    cosine = products * inverse_s * inverse_t
    cosine_term = jnp.sum(jnp.where(live_rows, 1.0 - cosine, 0.0))
    weighting = jnp.where(live_rows, -cosine_weight / token_total, 0.0) * inverse_s * inverse_t
    grad_final = weighting[:, None] * (
        final_t - (products * inverse_s * inverse_s)[:, None] * final_s
    )
    grad_final = grad_final.at[offsets].add(grad_rows)
    flat_local, grad_embedded = layer_backward(student, saved, grad_final, lengths)
    all_grads = lax.all_gather(grad_embedded.astype(jnp.bfloat16), "vocab", axis=0, tiled=True)
    target_rows = jnp.where(inside, local_ids, vocab_rows)
    grad_table = grad_table + jnp.zeros_like(grad_table).at[target_rows].add(
        all_grads.astype(jnp.float32), mode="drop"
    )
    tiles_all = owner_order.shape[0]
    padded = jnp.concatenate(
        [flat_local, jnp.zeros((tiles_all * TILE - flat_local.shape[0],), jnp.float32)]
    ).reshape(tiles_all, TILE)
    grad_tiles = padded[owner_order]
    flat_grad = lax.psum_scatter(grad_tiles, ("dp", "vocab"), scatter_dimension=0, tiled=True)
    width_share = student_embed.shape[1]
    summed_table = lax.psum(grad_table, "dp")
    table_grad = lax.dynamic_slice_in_dim(
        summed_table, lax.axis_index("dp") * width_share, width_share, 1
    )
    loss_term = (
        mixing_coefficient * smoothing_heat_scale**2 * divergence_part / masked_total
        + cosine_weight * cosine_term / token_total
    )
    squares, loss_value = lax.psum(
        (jnp.sum(flat_grad * flat_grad) + jnp.sum(table_grad * table_grad), loss_term),
        ("dp", "vocab"),
    )
    grad_norm = jnp.sqrt(squares)
    factor = clip_norm / jnp.maximum(grad_norm, clip_norm)
    step_float = step_count[0].astype(jnp.float32)
    new_flat, new_flat_first, new_flat_second = adam_step(
        student_flat, flat_first, flat_second, flat_grad * factor, step_float
    )
    new_embed, new_embed_first, new_embed_second = adam_step(
        student_embed, embed_first, embed_second, table_grad * factor, step_float
    )
    return (
        loss_value,
        grad_norm,
        new_flat,
        new_flat_first,
        new_flat_second,
        new_embed,
        new_embed_first,
        new_embed_second,
    )


def solution(mesh):
    return jax.shard_map(
        on_device,
        mesh=mesh,
        in_specs=(
            P(("dp", "vocab"), None),
            P(("dp", "vocab")),
            P(("dp", "vocab"), None),
            P(("dp", "vocab")),
            P(),
            P(),
            P(("dp", "vocab"), None),
            P("vocab", None),
            P(("dp", "vocab"), None),
            P(("dp", "vocab"), None),
            P(("dp", "vocab"), None),
            P("vocab", "dp"),
            P("vocab", "dp"),
            P("vocab", "dp"),
        ),
        out_specs=(
            P(),
            P(),
            P(("dp", "vocab"), None),
            P(("dp", "vocab"), None),
            P(("dp", "vocab"), None),
            P("vocab", "dp"),
            P("vocab", "dp"),
            P("vocab", "dp"),
        ),
        check_vma=False,
    )
```

profile of v0, /device:TPU:0, one launch (start us, length us, event | category | flops | bytes accessed | tf_op | source)
XLA Modules:
  0.0 1603.8 jit_solution(4864075580942943663)
XLA Ops:
  12.6 10.4 all-gather
  23.6 17.8 %gather_fusion.2 = bf16[4096,768]{1,0:T(8,128)(2,1)} fusion(bf16[1920,768]{1,0:T(8,128)(2,1)S(1)} %copy-done, s32[4096]{0:T(1024)S(1)} %get-tuple-element.408), kind=kCustom, calls=%fused_computation.2 | custom fusion | bytes 12599296 | tf_op jit(solution)/shard_map/gather | solution.py:309
  41.4 31.8 %all-gather.13.cloned.1.call-done = bf16[1920,768]{0,1:T(8,128)(2,1)} async-done(((bf16[1920,192]{0,1:T(8,128)(2,1)}), bf16[1920,768]{0,1:T(8,128)(2,1)}) %all-gather.13.cloned.1.call-update) | async-done | bytes 2949136 | tf_op jit(solution)/shard_map/all_gather | solution.py:295
  77.7 21.3 %gather_fusion = bf16[4096,768]{1,0:T(8,128)(2,1)} fusion(bf16[1920,768]{1,0:T(8,128)(2,1)} %copy.96, s32[4096]{0:T(1024)S(1)} %get-tuple-element.408), kind=kCustom, calls=%fused_computation | custom fusion | bytes 12599296 | tf_op jit(solution)/shard_map/gather | solution.py:307
  99.0 11.4 select_convert_fusion.1
  111.9 70.3 %all-gather.15.cloned.1.call-done = bf16[58624,128]{1,0:T(8,128)(2,1)} async-done(((bf16[1832,128]{1,0:T(8,128)(2,1)}), bf16[58624,128]{1,0:T(8,128)(2,1)}) %all-gather.15.cloned.1.call-update) | async-done | bytes 15007760 | tf_op jit(solution)/shard_map/all_gather | solution.py:289
  182.2 217.3 %scatter_custom_fusion = bf16[58624,128]{1,0:T(8,128)(2,1)} fusion(s32[58624]{0:T(1024)S(1)} %compare_select_fusion, bf16[58624,128]{1,0:T(8,128)(2,1)} %all-gather.15.cloned.1.call-done, bf16[]{:T(256)} %constant.75.clone.1), kind=kCustom, calls=%fused_computation.38 | custom fusion | bytes 15008256 | tf_op jit(solution)/shard_map/scatter | solution.py:292
  400.2 8.4 fusion.131
  418.1 8.4 fusion.132
  426.4 9.2 reshape.674
  435.7 8.2 reshape.673
  447.4 7.6 reshape.667
  464.6 5.6 fusion.44
  480.2 8.2 reshape.664
  488.4 7.6 reshape.658
  499.0 10.8 fusion.134
  509.9 6.2 fusion.50
  519.5 23.2 %fusion.136 = (f32[512]{0:T(512)S(1)}, f32[512,768]{1,0:T(8,128)}) fusion(f32[768]{0:T(1024)S(1)} %get-tuple-element.398, bf16[3072,768]{1,0:T(8,128)(2,1)} %reshape.674, bf16[768,3072]{1,0:T(8,128)(2,1)} %reshape.673, f32[3072]{0:T(1024)S(1)} %fusion.80, f32[512,768]{1,0:T(8,128)} %copy-done.29, f32[768]{0:T(1024)S(1)} %get-tuple-element.399, ...), kind=kOutput, calls=%fused_computation.312 | convolution fusion | flops 4940365312 | bytes 12610560 | tf_op jit(solution)/shard_map/dot_general | solution.py:39
  575.3 9.2 reshape.665
  584.5 20.6 %fusion.11 = (bf16[512,3072]{1,0:T(8,128)(2,1)S(1)}, f32[512,3072]{1,0:T(8,128)}) fusion(f32[3072]{0:T(1024)S(1)} %fusion.81, bf16[768,3072]{1,0:T(8,128)(2,1)} %reshape.664, f32[512,768]{1,0:T(8,128)} %copy-done.12, f32[768]{0:T(1024)S(1)} %get-tuple-element.388, f32[768]{0:T(1024)S(1)} %get-tuple-element.389, f32[512]{0:T(512)S(1)} %add_rsqrt_fusion.6, ...), kind=kOutput, calls=%fused_computation.47 | convolution fusion | flops 2521694208 | bytes 15751168 | tf_op jit(solution)/shard_map/dot_general | solution.py:39
  618.2 38.9 %all-reduce.8 = (f32[]{:T(128)}, f32[]{:T(128)}) all-reduce(f32[]{:T(128)S(6)} %convert_element_type.264, f32[]{:T(128)S(6)} %convert_element_type.265), channel_id=1, replica_groups=mesh['dp'=4,'vocab'=8] {'dp','vocab'}, use_global_device_ids=true, to_apply=%region_27.28 | all-reduce | flops 2 | bytes 16 | tf_op jit(solution)/shard_map/psum | solution.py:296
  659.6 8.4 multiply_reduce_fusion.3
  668.2 6.9 multiply_reduce_fusion.2
  675.4 7.4 multiply_reduce_fusion.1
  684.7 12.9 all-reduce.5
  697.6 40.6 %all-reduce.15.cloned.1.call-done = (f32[7680]{0:T(1024)}, f32[7680]{0:T(1024)}, f32[7680]{0:T(1024)}, f32[7680]{0:T(1024)}, f32[7680]{0:T(1024)}) async-done(((f32[7680]{0:T(1024)}, f32[7680]{0:T(1024)}, f32[7680]{0:T(1024)}, f32[7680]{0:T(1024)}, f32[7680]{0:T(1024)}), (f32[7680]{0:T(1024)}, f32[7680]{0:T(1024)}, f32[7680]{0:T(1024)}, f32[7680]{0:T(1024)}, f32[7680]{0:T(1024)})) %all-reduce.15.cloned.1.call-update) | async-done | bytes 153616
  747.5 6.9 multiply_convert_fusion.1
  764.9 7.2 fusion.143
  772.1 35.1 %reduce-scatter.12.cloned.1.call-done = f32[120,768]{1,0:T(8,128)} async-done(((f32[960,768]{1,0:T(8,128)}), f32[120,768]{1,0:T(8,128)}) %reduce-scatter.12.cloned.1.call-update) | async-done | bytes 368656 | tf_op jit(solution)/shard_map/reduce_scatter | solution.py:364
  813.9 7.8 convert_reduce_fusion
  828.6 7.0 fusion.46
  835.6 9.0 multiply_reduce_fusion
  844.6 7.0 multiply_convert_fusion
  858.5 5.5 convolution_bitcast_fusion
  864.0 5.2 fusion.86
  870.6 5.2 fusion.124
  879.5 7.9 reshape.676
  896.0 9.4 copy.111
  905.4 10.7 reshape.679
  922.9 9.4 constant_dynamic-update-slice_fusion.4
  937.7 27.4 %all-gather.23.cloned.1.call-done = bf16[4096,768]{1,0:T(8,128)(2,1)} async-done(((bf16[512,768]{1,0:T(8,128)(2,1)}), bf16[4096,768]{1,0:T(8,128)(2,1)}) %all-gather.23.cloned.1.call-update) | async-done | bytes 6291472 | tf_op jit(solution)/shard_map/all_gather | solution.py:380
  965.1 33.3 %scatter_custom_fusion.2 = f32[1920,768]{1,0:T(8,128)} fusion(f32[1920,768]{1,0:T(8,128)} %fusion.143, s32[4096]{0:T(1024)} %get-tuple-element.407, bf16[4096,768]{1,0:T(8,128)(2,1)} %all-gather.23.cloned.1.call-done), kind=kCustom, calls=%fused_computation.19 | custom fusion | flops 6291456 | bytes 12189696 | tf_op jit(solution)/shard_map/scatter-add | solution.py:382
  998.4 6.4 copy.105
  1010.8 117.5 %gather_fusion.4 = f32[58624,128]{1,0:T(8,128)} fusion(f32[58624,128]{1,0:T(8,128)} %bitcast.193, s32[59392]{0:T(1024)S(1)} %pad_clamp_fusion), kind=kCustom, calls=%fused_computation.4 | custom fusion | bytes 60265472 | tf_op jit(solution)/shard_map/gather | solution.py:389
  1132.9 82.2 %all-reduce.13.cloned.1.call-done = f32[1920,768]{0,1:T(8,128)} async-done(((f32[1920,768]{0,1:T(8,128)}), f32[1920,768]{0,1:T(8,128)}) %all-reduce.13.cloned.1.call-update) | async-done | bytes 5898256 | tf_op jit(solution)/shard_map/psum | solution.py:392
  1217.5 318.2 %reduce-scatter.14.cloned.1.call-done = f32[1832,128]{1,0:T(8,128)} async-done(((f32[58624,128]{1,0:T(8,128)}), f32[1832,128]{1,0:T(8,128)}) %reduce-scatter.14.cloned.1.call-update) | async-done | bytes 938000
  1539.0 46.3 %all-reduce.7 = (f32[]{:T(128)}, f32[]{:T(128)}) all-reduce(f32[]{:T(128)S(6)} %add.466, f32[]{:T(128)S(6)} %add.474), channel_id=1, replica_groups=mesh['dp'=4,'vocab'=8] {'dp','vocab'}, use_global_device_ids=true, to_apply=%region_33.34 | all-reduce | flops 2 | bytes 16 | tf_op jit(solution)/shard_map/psum | solution.py:400
  1590.2 5.5 multiply_subtract_fusion
  (361 shorter events, 180.1 us)
Async XLA Ops:
  7.2 16.4 %copy-start = (bf16[1920,768]{1,0:T(8,128)(2,1)S(1)}, bf16[1920,768]{1,0:T(8,128)(2,1)}, u32[]{:S(2)}) copy-start(bf16[1920,768]{1,0:T(8,128)(2,1)} %param.23) | copy-start | bytes 8847364
  7.2 5.4 copy-start.56
  7.2 66.0 %all-gather.13.cloned.1.call-start = ((), (), s32[]{:S(2)}) async-start(), calls=%async_computation.4 | async-start | bytes 3686400 | tf_op jit(solution)/shard_map/all_gather | solution.py:295
  9.7 172.5 %all-gather.15.cloned.1.call-start = ((), (), s32[]{:S(2)}) async-start(), calls=%async_computation.6 | async-start | bytes 15476736 | tf_op jit(solution)/shard_map/all_gather | solution.py:289
  11.8 404.9 %all-gather.19.cloned.1.call-start = ((), (), s32[]{:S(2)}) async-start(), calls=%async_computation.9 | async-start | bytes 15476736 | tf_op jit(solution)/shard_map/all_gather | solution.py:290
  12.5 448.0 %reduce-scatter.10.cloned.1.call-start = ((), (), s32[]{:S(2)}) async-start(), calls=%async_computation.8 | async-start | bytes 7077888 | tf_op jit(solution)/shard_map/reduce_scatter | solution.py:315
  110.4 433.1 %reduce-scatter.8.cloned.1.call-start = ((), (), s32[]{:S(2)}) async-start(), calls=%async_computation.5 | async-start | bytes 7077888 | tf_op jit(solution)/shard_map/reduce_scatter | solution.py:312
  111.8 287.7 %copy-start.32 = (s32[58624]{0:T(1024)}, s32[58624]{0:T(1024)S(1)}, u32[]{:S(2)}) copy-start(s32[58624]{0:T(1024)S(1)} %compare_select_fusion) | copy-start | bytes 703492
  111.8 547.7 %all-gather.17.cloned.1.call-start = ((), (), s32[]{:S(2)}) async-start(), calls=%async_computation.7 | async-start | bytes 1658880 | tf_op jit(solution)/shard_map/all_gather | solution.py:326
  455.5 115.2 %copy-start.44 = (f32[768]{0:T(1024)}, f32[768]{0:T(1024)S(1)}, u32[]{:S(2)}) copy-start(f32[768]{0:T(1024)S(1)} %get-tuple-element.394) | copy-start | bytes 9220
  455.6 115.2 %copy-start.51 = (f32[768]{0:T(1024)}, f32[768]{0:T(1024)S(1)}, u32[]{:S(2)}) copy-start(f32[768]{0:T(1024)S(1)} %get-tuple-element.393) | copy-start | bytes 9220
  509.9 6.2 copy-start.8
  509.9 6.2 copy-start.27
  509.9 6.2 copy-start.31
  545.4 25.3 %copy-start.42 = (f32[512]{0:T(512)}, f32[512]{0:T(512)S(1)}, u32[]{:S(2)}) copy-start(f32[512]{0:T(512)S(1)} %broadcast_multiply_fusion.11) | copy-start | bytes 6148
  545.7 25.0 %copy-start.49 = (f32[512]{0:T(512)}, f32[512]{0:T(512)S(1)}, u32[]{:S(2)}) copy-start(f32[512]{0:T(512)S(1)} %add_rsqrt_fusion.7) | copy-start | bytes 6148
  558.4 4.6 copy-start.2
  584.5 20.6 %copy-start.13 = (f32[512,768]{1,0:T(8,128)S(1)}, f32[512,768]{1,0:T(8,128)}, u32[]{:S(2)}) copy-start(f32[512,768]{1,0:T(8,128)} %copy-done.12) | copy-start | bytes 4718596
  584.5 20.6 %copy-start.19 = (bf16[3072,768]{1,0:T(8,128)(2,1)S(1)}, bf16[3072,768]{1,0:T(8,128)(2,1)}, u32[]{:S(2)}) copy-start(bf16[3072,768]{1,0:T(8,128)(2,1)} %reshape.665) | copy-start | bytes 14155780
  584.5 20.6 %copy-start.53 = (f32[768]{0:T(1024)S(1)}, f32[768]{0:T(1024)}, u32[]{:S(2)}) copy-start(f32[768]{0:T(1024)} %get-tuple-element.385) | copy-start | bytes 9220
  608.6 48.5 %copy-start.58 = (u32[32]{0:T(128)S(1)}, u32[32]{0:T(128)}, u32[]{:S(2)}) copy-start(u32[32]{0:T(128)} %constant.216) | copy-start | bytes 388
  614.2 54.0 %all-gather.21.cloned.1.call-start = ((), (), s32[]{:S(2)}) async-start(), calls=%async_computation.10 | async-start | bytes 1658880 | tf_op jit(solution)/shard_map/all_gather | solution.py:327
  617.5 120.8 %all-reduce.15.cloned.1.call-start = ((), (), s32[]{:S(2)}) async-start(), calls=%async_computation.15 | async-start | bytes 327680
  668.2 6.9 copy-start.39
  675.4 7.4 copy-start.40
  684.4 122.9 %reduce-scatter.12.cloned.1.call-start = ((), (), s32[]{:S(2)}) async-start(), calls=%async_computation.11 | async-start | bytes 3317760 | tf_op jit(solution)/shard_map/reduce_scatter | solution.py:364
  747.5 8.7 copy-start.28
  756.2 5.5 copy-start.33
  761.1 204.0 %all-gather.23.cloned.1.call-start = ((), (), s32[]{:S(2)}) async-start(), calls=%async_computation.12 | async-start | bytes 7077888 | tf_op jit(solution)/shard_map/all_gather | solution.py:380
  764.9 42.3 %copy-start.55 = (s32[120]{0:T(128)S(1)}, s32[120]{0:T(128)}, u32[]{:S(2)}) copy-start(s32[120]{0:T(128)} %copy-done.54) | copy-start | bytes 1444
  809.6 12.0 slice-start.6
  813.8 7.8 copy-start.10
  813.8 7.8 copy-start.14
  813.9 7.8 slice-start.7
  828.5 7.0 copy-start.4
  828.5 7.0 copy-start.9
  828.5 16.1 %slice-start = ((s8[12582912]{0:T(1024)(128)(4,1)}), s8[4194304]{0:T(1024)(128)(4,1)S(1)}, s32[]{:S(2)}) async-start(s8[12582912]{0:T(1024)(128)(4,1)} %bitcast.194), calls=%async_computation.16 | async-start | bytes 8388608
  828.5 16.1 %slice-start.1 = ((s8[12582912]{0:T(1024)(128)(4,1)}), s8[4194304]{0:T(1024)(128)(4,1)S(1)}, s32[]{:S(2)}) async-start(s8[12582912]{0:T(1024)(128)(4,1)} %bitcast.194), calls=%async_computation.17 | async-start | bytes 8388608
  835.6 9.0 slice-start.2
  858.5 5.6 copy-start.11
  858.5 5.6 copy-start.25
  870.6 5.2 copy-start.23
  919.4 295.7 %all-reduce.13.cloned.1.call-start = ((), (), s32[]{:S(2)}) async-start(), calls=%async_computation.13 | async-start | bytes 11796480 | tf_op jit(solution)/shard_map/psum | solution.py:392
  919.5 12.9 slice-start.3
  922.9 9.4 slice-start.4
  922.9 9.4 slice-start.5
  1004.8 530.8 %reduce-scatter.14.cloned.1.call-start = ((), (), s32[]{:S(2)}) async-start(), calls=%async_computation.14 | async-start | bytes 30953472
  1586.0 9.7 copy-start.1
  (33 other events, 68.4 us)
Sparse Core Ops, SparseCore 0:
  10.2 62.9 all-gather.12
  76.6 105.5 all-gather.14
  185.1 105.0 all-gather.18
  293.5 59.8 reduce-scatter.9
  357.0 61.7 reduce-scatter.7
  614.4 24.0 all-gather.16
  640.9 25.3 all-gather.20
  684.5 53.6 all-reduce.14
  761.2 45.9 reduce-scatter.11
  919.6 45.4 all-gather.22
  1005.0 210.1 all-reduce.12
  1217.3 318.3 reduce-scatter.13
where the time goes:
time: 1610 us; the launch traced here: 1600 us
  waiting for transfers between devices  606 us (38%)
  local copies, waits for them, and re-layouts  576 us (36%)
  matrix products  165 us (10%)
  other arithmetic  121 us (8%)
  blocking collectives  108 us (7%)
  between operations  25.7 us (2%)
    unnamed x14, waiting for transfers between devices  360 us
    scatter x1, local copies, waits for them, and re-layouts, on_device(): logical = jnp.zeros_like(student_tiles).at[owner_order].set(student_tiles)  217 us
    gather x1, local copies, waits for them, and re-layouts, on_device(): grad_tiles = padded[owner_order]  117 us
    psum x1, waiting for transfers between devices, on_device(): summed_table = lax.psum(grad_table, 'dp')  82.2 us
    all_gather x1, waiting for transfers between devices, on_device(): lax.all_gather(student_flat.astype(jnp.bfloat16), ('dp', 'vocab'), axis=0...  70.3 us
    dot_general x8, matrix products, array_multiply(): return jnp.dot(left_side, right_side, preferred_element_type=jnp.float32)  64.9 us
    reshape x8, local copies, waits for them, and re-layouts, unpack(): pieces[piece_name] = vector[offset:offset + entries].reshape(piece_dims)  56.8 us
    unnamed x159, local copies, waits for them, and re-layouts  49.7 us
  transfers between devices with their start and end apart: 12, of which 7 were waited for; matrix products, arithmetic and copies ran while one was open for 37% of the time, Pallas kernels for 0%

commit v1 on v0

--- a/solution.py
+++ b/solution.py
@@ -1,6 +1,10 @@
+import functools
+
 import jax
 import jax.numpy as jnp
 from jax import lax
+from jax.experimental import pallas as pl
+from jax.experimental.pallas import tpu as pltpu
 from jax.sharding import PartitionSpec as P
 
 D = 768
@@ -9,8 +13,19 @@
 FF = 3072
 LEN = 512
 CAP = 120
+SLOTS = 128
 TILE = 128
 
+QKV = (0, D, 18)
+OUT = (13824, D, 6)
+UP = (18432, D, 24)
+DOWN = (36864, FF, 6)
+PLACE = (55296, LEN, 6)
+MATRICES = (QKV, OUT, UP, DOWN, PLACE)
+TAIL = 58368
+TAIL_TILES = 88
+
+VMEM_LIMIT = 60 * 1024 * 1024
 
 smoothing_heat_scale = 2.0
 mixing_coefficient = 5.0
@@ -24,15 +39,243 @@
 norm_eps = 1e-12
 cosine_eps = 1e-06
 
-
-def combined_all(value, axis, combine):
-    everything = jax.tree.map(lambda part: lax.all_gather(part, axis), value)
-    first = jax.tree.map(lambda part: part[0], everything)
-
-    def step(k, so_far):
-        return combine(so_far, jax.tree.map(lambda part: part[k], everything))
-
-    return lax.fori_loop(1, lax.axis_size(axis), step, first)
+CORE, ACROSS, DEEP = 1, 2, 4
+
+
+def swap(value, bit):
+    return lax.ppermute(value, "vocab", [(i, i ^ bit) for i in range(8)])
+
+
+def shift(value, steps):
+    size = lax.axis_size("dp")
+    return lax.ppermute(value, "dp", [(i, (i + steps) % size) for i in range(size)])
+
+
+def gather_near(value):
+    value = value[None]
+    for bit in (ACROSS, DEEP, CORE):
+        value = jnp.concatenate([value, swap(value, bit)])
+    return value
+
+
+def scatter_near(value_far, value_near):
+    half = value_near.shape[2] // 2
+    value = value_near + swap(value_far, CORE)
+    upper, lower = value[:, :, :half], value[:, :, half:]
+    upper = upper[:, 0] + swap(upper[:, 1], ACROSS)
+    lower = lower[0] + swap(lower[1], DEEP)
+    upper = upper[0] + swap(upper[1], DEEP)
+    lower = lower[0] + swap(lower[1], ACROSS)
+    return jnp.concatenate([upper, lower])
+
+
+def sum_everywhere(value):
+    for bit in (CORE, ACROSS, DEEP):
+        value = value + swap(value, bit)
+    for step in (1, 2):
+        value = value + lax.ppermute(value, "dp", [(i, i ^ step) for i in range(4)])
+    return value
+
+
+def relative_order(table, per_device):
+    here = lax.axis_index("vocab")
+    table = table.reshape(4, 2, 2, 2, per_device)
+    for axis, bit in ((1, DEEP), (2, ACROSS), (3, CORE)):
+        table = jnp.where((here & bit) != 0, jnp.flip(table, axis), table)
+    return table
+
+
+def rolled(table, downward):
+    z = lax.axis_index("dp")
+    order = (z - jnp.arange(4)) % 4 if downward else (z + jnp.arange(4)) % 4
+    return jnp.stack([lax.dynamic_index_in_dim(table, order[k], keepdims=False) for k in range(4)])
+
+
+def rows_of_tiles(tiles):
+    rows = tiles
+    for first, height, across in MATRICES:
+        inside = (tiles >= first) & (tiles < first + height * across)
+        at = tiles - first
+        rows = jnp.where(inside, first + (at % across) * height + at // across, rows)
+    return rows
+
+
+def unpack_kernel(source, target, stage, *, across):
+    stage[...] = source[...].astype(jnp.float32)
+
+    def step(g, carry):
+        for column in range(across):
+            lines = stage[pl.ds(g * 16 * across + column, 16, stride=across), :]
+            target[pl.ds(pl.multiple_of(g * 16, 16), 16), column * TILE : (column + 1) * TILE] = lines.astype(
+                jnp.bfloat16
+            )
+        return carry
+
+    lax.fori_loop(0, target.shape[0] // 16, step, 0)
+
+
+def unpack_matrix(tiles, piece):
+    first, height, across = piece
+    lines = 64 if across > 6 else 128
+    block = lines * across
+    return pl.pallas_call(
+        functools.partial(unpack_kernel, across=across),
+        grid=(height // lines,),
+        in_specs=[pl.BlockSpec((block, TILE), lambda i: (first // block + i, 0))],
+        out_specs=pl.BlockSpec((lines, across * TILE), lambda i: (i, 0)),
+        out_shape=jax.ShapeDtypeStruct((height, across * TILE), jnp.bfloat16),
+        scratch_shapes=[pltpu.VMEM((block, TILE), jnp.float32)],
+        name="unpack_matrix",
+    )(tiles)
+
+
+def place_kernel(rows, *refs, places, count, per):
+    arrivals = refs[: len(places)]
+    targets = refs[len(places) : len(places) + 5]
+    tail = refs[len(places) + 5]
+    landed, stage, full, packed, in_sems, out_sems, tail_sem = refs[len(places) + 6 :]
+    copies = []
+    for n, (arrival, place) in enumerate(zip(arrivals, places)):
+        target = landed if place is None else landed.at[place[0], pl.ds(place[1], place[2])]
+        copies.append(pltpu.make_async_copy(arrival, target, in_sems.at[n]))
+    for copy in copies:
+        copy.start()
+    for copy in copies:
+        copy.wait()
+
+    def lines(block, start, size):
+        stage[pl.ds(0, size), :] = landed[block, pl.ds(start, size), :].astype(jnp.float32)
+        base = block * per + start
+        for u in range(size):
+            full[pl.ds(rows[base + u], 1), :] = stage[pl.ds(u, 1), :]
+
+    whole, rest = divmod(per, 128)
+
+    def one_block(block, carry):
+        def one_step(i, inner):
+            lines(block, pl.multiple_of(i * 128, 128), 128)
+            return inner
+
+        lax.fori_loop(0, whole, one_step, 0)
+        if rest:
+            lines(block, whole * 128, rest)
+        return carry
+
+    lax.fori_loop(0, count, one_block, 0)
+    tail_copy = pltpu.make_async_copy(full.at[pl.ds(TAIL, TAIL_TILES)], tail, tail_sem)
+    tail_copy.start()
+    for target, (first, height, across) in zip(targets, MATRICES):
+        size = min(height, D)
+        parts = height // size
+
+        def out_copy(n, slot, target=target, size=size, parts=parts):
+            column, part = n // parts, n % parts
+            return pltpu.make_async_copy(
+                packed.at[slot, pl.ds(0, size)],
+                target.at[
+                    pl.ds(pl.multiple_of(part * size, 256), size),
+                    pl.ds(pl.multiple_of(column * TILE, TILE), TILE),
+                ],
+                out_sems.at[slot],
+            )
+
+        def one_column(n, carry, first=first, size=size, out_copy=out_copy):
+            slot = n % 2
+
+            @pl.when(n >= 2)
+            def _():
+                out_copy(n - 2, slot).wait()
+
+            packed[slot, pl.ds(0, size), :] = full[pl.ds(pl.multiple_of(first + n * size, 128), size), :].astype(
+                jnp.bfloat16
+            )
+            out_copy(n, slot).start()
+            return carry
+
+        total = across * parts
+        lax.fori_loop(0, total, one_column, 0)
+        for n in (total - 2, total - 1):
+            out_copy(n, n % 2).wait()
+    tail_copy.wait()
+
+
+def place_tiles(rows, arrivals, places, count, per):
+    shapes = [jax.ShapeDtypeStruct((h, a * TILE), jnp.bfloat16) for _, h, a in MATRICES]
+    return pl.pallas_call(
+        functools.partial(place_kernel, places=places, count=count, per=per),
+        in_specs=[pl.BlockSpec(memory_space=pltpu.SMEM)] + [pl.BlockSpec(memory_space=pl.ANY)] * len(arrivals),
+        out_specs=[pl.BlockSpec(memory_space=pl.ANY)] * 6,
+        out_shape=shapes + [jax.ShapeDtypeStruct((TAIL_TILES, TILE), jnp.float32)],
+        scratch_shapes=[
+            pltpu.VMEM((count, per, TILE), jnp.bfloat16),
+            pltpu.VMEM((128, TILE), jnp.float32),
+            pltpu.VMEM((count * per, TILE), jnp.float32),
+            pltpu.VMEM((2, D, TILE), jnp.bfloat16),
+            pltpu.SemaphoreType.DMA((len(arrivals),)),
+            pltpu.SemaphoreType.DMA((2,)),
+            pltpu.SemaphoreType.DMA,
+        ],
+        compiler_params=pltpu.CompilerParams(vmem_limit_bytes=VMEM_LIMIT),
+        cost_estimate=pl.CostEstimate(flops=0, bytes_accessed=180_000_000, transcendentals=0),
+        name="place_tiles",
+    )(rows, *arrivals)
+
+
+def step_size(rows):
+    return max(n for n in range(8, 193, 8) if rows % n == 0)
+
+
+def collect_kernel(rows, *refs, outs, blocks, per, begin):
+    sources, targets = refs[:6], refs[6 : 6 + outs]
+    full, sems = refs[6 + outs :]
+    block = pl.program_id(0)
+
+    @pl.when(block == 0)
+    def _():
+        copies = []
+        for source, (first, height, across) in zip(sources, MATRICES):
+            for column in range(across):
+                copies.append(
+                    pltpu.make_async_copy(
+                        source.at[:, pl.ds(column * TILE, TILE)],
+                        full.at[pl.ds(first + column * height, height)],
+                        sems.at[len(copies)],
+                    )
+                )
+        copies.append(pltpu.make_async_copy(sources[5], full.at[pl.ds(TAIL, TAIL_TILES)], sems.at[len(copies)]))
+        for copy in copies:
+            copy.start()
+        unused = full.shape[0] - TAIL - TAIL_TILES
+        full[pl.ds(TAIL + TAIL_TILES, unused), :] = jnp.zeros((unused, TILE), jnp.float32)
+        for copy in copies:
+            copy.wait()
+
+    size = step_size(targets[0].shape[1])
+    for n, target in enumerate(targets):
+        base = (n * blocks + block) * per + begin
+
+        def one_step(i, carry, target=target, base=base):
+            start = pl.multiple_of(i * size, 8)
+            for u in range(size):
+                target[0, pl.ds(start + u, 1), :] = full[pl.ds(rows[base + start + u], 1), :]
+            return carry
+
+        lax.fori_loop(0, target.shape[1] // size, one_step, 0)
+
+
+def collect_tiles(rows, sources, tiles_all, per, outs, begin, lines):
+    blocks = tiles_all // per // outs
+    return pl.pallas_call(
+        functools.partial(collect_kernel, outs=outs, blocks=blocks, per=per, begin=begin),
+        grid=(blocks,),
+        in_specs=[pl.BlockSpec(memory_space=pltpu.SMEM)] + [pl.BlockSpec(memory_space=pl.ANY)] * 6,
+        out_specs=[pl.BlockSpec((1, lines, TILE), lambda i: (i, 0, 0))] * outs,
+        out_shape=[jax.ShapeDtypeStruct((blocks, lines, TILE), jnp.float32)] * outs,
+        scratch_shapes=[pltpu.VMEM((tiles_all, TILE), jnp.float32), pltpu.SemaphoreType.DMA((61,))],
+        compiler_params=pltpu.CompilerParams(vmem_limit_bytes=VMEM_LIMIT),
+        cost_estimate=pl.CostEstimate(flops=0, bytes_accessed=80_000_000, transcendentals=0),
+        name="collect_tiles",
+    )(rows, *sources)
 
 
 def array_multiply(left_side, right_side):
@@ -51,25 +294,17 @@
     )
 
 
-def unpack(vector):
-    layout = [
-        ("qkv", (D, 3 * D)),
-        ("out", (D, D)),
-        ("up", (D, FF)),
-        ("down", (FF, D)),
-        ("place", (LEN, D)),
-        ("small", (10, D)),
-        ("upbias", (FF,)),
-    ]
-    pieces = {}
-    offset = 0
-    for piece_name, piece_dims in layout:
-        entries = 1
-        for extent in piece_dims:
-            entries = entries * extent
-        pieces[piece_name] = vector[offset : offset + entries].reshape(piece_dims)
-        offset = offset + entries
-    return pieces
+def pieces_of(matrices, tail):
+    qkv, out, up, down, place = matrices
+    return {
+        "qkv": qkv,
+        "out": out,
+        "up": up,
+        "down": down,
+        "place": place,
+        "small": tail[:60].reshape(10, D),
+        "upbias": tail[60:84].reshape(FF),
+    }
 
 
 def norm_forward(values, gain_row, shift_row):
@@ -230,18 +465,10 @@
         ]
     )
     grad_upbias = jnp.sum(grad_hidden.astype(jnp.float32), axis=0)
-    flat_local = jnp.concatenate(
-        [
-            grad_qkv.reshape(-1),
-            grad_outw.reshape(-1),
-            grad_up.reshape(-1),
-            grad_down.reshape(-1),
-            grad_place.reshape(-1),
-            grad_small.reshape(-1),
-            grad_upbias,
-        ]
-    )
-    return (flat_local, grad_embedded)
+    tail = jnp.concatenate(
+        [grad_small.reshape(60, TILE), grad_upbias.reshape(24, TILE), jnp.zeros((4, TILE), jnp.float32)]
+    )
+    return ((grad_qkv, grad_outw, grad_up, grad_down, grad_place, tail), grad_embedded)
 
 
 def combine_stats(earlier, later):
@@ -251,12 +478,14 @@
     factor_late = jnp.exp(later[0] - peak_s)
     teacher_early = jnp.exp(earlier[2] - peak_t)
     teacher_late = jnp.exp(later[2] - peak_t)
-    return (
-        peak_s,
-        earlier[1] * factor_early + later[1] * factor_late,
-        peak_t,
-        earlier[3] * teacher_early + later[3] * teacher_late,
-        earlier[4] * teacher_early + later[4] * teacher_late,
+    return jnp.stack(
+        [
+            peak_s,
+            earlier[1] * factor_early + later[1] * factor_late,
+            peak_t,
+            earlier[3] * teacher_early + later[3] * teacher_late,
+            earlier[4] * teacher_early + later[4] * teacher_late,
+        ]
     )
 
 
@@ -269,7 +498,44 @@
     return (weight - learn_rate * (update + weight_decay * weight), new_first, new_second)
 
 
+def gather_student(tiles):
+    per = tiles.shape[0]
+    half = per // 16 * 8
+    arrivals, places = [], []
+
+    def keep(value, plane, near, start):
+        for core in (0, 1):
+            arrivals.append(swap(value, CORE) if core else value)
+            places.append((plane * 8 + near * 2 + core, start, value.shape[0]))
+
+    for plane in range(4):
+        across, deep = swap(tiles, ACROSS), swap(tiles, DEEP)
+        keep(tiles, plane, 0, 0)
+        keep(across, plane, 1, 0)
+        keep(deep, plane, 2, 0)
+        keep(swap(across[:half], DEEP), plane, 3, 0)
+        keep(swap(deep[half:], ACROSS), plane, 3, half)
+        if plane < 3:
+            tiles = shift(tiles, 1)
+    return arrivals, places
+
+
+def reduce_chunk(mine, other):
+    lines = mine.shape[1]
+    value = (mine + swap(other, CORE)).reshape(4, 2, 2, lines, TILE)
+    first, second = value[2:], value[:2]
+    first = first[:, :, 0] + swap(first[:, :, 1], ACROSS)
+    second = second[:, 0] + swap(second[:, 1], DEEP)
+    first = first[:, 0] + swap(first[:, 1], DEEP)
+    second = second[:, 0] + swap(second[:, 1], ACROSS)
+    moving = shift(first[1], 1)
+    moving = shift(first[0] + moving, 1)
+    moving = shift(second[1] + moving, 1)
+    return second[0] + moving
+
+
 def on_device(
+    near,
     token_ids,
     lengths,
     mask_pos,
@@ -285,73 +551,107 @@
     embed_first,
     embed_second,
 ):
-    student_tiles, teacher_tiles = (
-        lax.all_gather(student_flat.astype(jnp.bfloat16), ("dp", "vocab"), axis=0, tiled=True),
-        lax.all_gather(teacher_flat, ("dp", "vocab"), axis=0, tiled=True),
-    )
-    logical = jnp.zeros_like(student_tiles).at[owner_order].set(student_tiles)
-    student = unpack(logical.reshape(-1))
-    teacher = unpack(teacher_tiles.reshape(-1))
-    table_low = lax.all_gather(student_embed.astype(jnp.bfloat16), "dp", axis=1, tiled=True)
-    token_total, masked_total = lax.psum(
-        (jnp.sum(lengths).astype(jnp.float32), jnp.sum(mask_count).astype(jnp.float32)),
-        ("dp", "vocab"),
-    )
-    seqs_here = token_ids.shape[0]
-    rows_here = seqs_here * LEN
-    group_ids = lax.all_gather(token_ids.reshape(rows_here), "vocab", axis=0, tiled=True)
-    vocab_rows = table_low.shape[0]
-    local_ids = group_ids - lax.axis_index("vocab") * vocab_rows
-    inside = (local_ids >= 0) & (local_ids < vocab_rows)
-    clipped = jnp.clip(local_ids, 0, vocab_rows - 1)
-    rows_student = jnp.where(inside[:, None], table_low[clipped].astype(jnp.float32), 0.0)
-    rows_teacher = jnp.where(
-        inside[:, None], mentor_lexicon_weights[clipped].astype(jnp.float32), 0.0
-    )
-    looked_s, looked_t = (
-        lax.psum_scatter(
-            rows_student.astype(jnp.bfloat16), "vocab", scatter_dimension=0, tiled=True
-        ).astype(jnp.float32),
-        lax.psum_scatter(
-            rows_teacher.astype(jnp.bfloat16), "vocab", scatter_dimension=0, tiled=True
-        ).astype(jnp.float32),
-    )
+    per = student_flat.shape[0]
+    tiles_all = owner_order.shape[0]
+    vocab_rows, width_share = student_embed.shape
+    planes = lax.axis_size("dp")
+    group = lax.axis_size("vocab")
+    here = lax.axis_index("vocab")
+
+    facts = jnp.concatenate([token_ids.reshape(LEN), lengths, mask_count, jnp.zeros((TILE - 2,), jnp.int32)])
+    target_rows = rows_of_tiles(owner_order)
+    student_low = student_flat.astype(jnp.bfloat16)
+    table_low = lax.all_gather(student_embed.T.astype(jnp.bfloat16), "dp", axis=0, tiled=True)
+    teacher_tiles = lax.all_gather(teacher_flat, ("dp", "vocab"), axis=0, tiled=True)
+    if near:
+        plane_facts = gather_near(facts)
+        by_plane = [facts, shift(facts, 1), shift(facts, 2), shift(facts, 3)]
+        other_facts = gather_near(jnp.stack(by_plane[1:]))
+        all_facts = jnp.concatenate([plane_facts[:, None], other_facts], axis=1)
+        arrivals, places = gather_student(student_low)
+        relative = relative_order(target_rows, per)
+        downward = rolled(relative, True).reshape(-1)
+        upward = rolled(relative.transpose(3, 0, 1, 2, 4).swapaxes(0, 1), False).swapaxes(0, 1).reshape(-1)
+        matrices = place_tiles(downward, arrivals, tuple(places), planes * group, per)
+    else:
+        by_plane = lax.all_gather(facts, "dp", axis=0)
+        all_facts = lax.all_gather(by_plane, "vocab", axis=0)
+        plane_facts = lax.dynamic_index_in_dim(all_facts, lax.axis_index("dp"), 1, keepdims=False)
+        student_tiles = lax.all_gather(student_low, ("dp", "vocab"), axis=0, tiled=True)
+        matrices = place_tiles(
+            target_rows, [student_tiles.reshape(planes * group, per, TILE)], (None,), planes * group, per
+        )
+    student = pieces_of(matrices[:5], matrices[5])
+    teacher = pieces_of(
+        [unpack_matrix(teacher_tiles, piece) for piece in MATRICES],
+        teacher_tiles[TAIL : TAIL + TAIL_TILES].astype(jnp.float32),
+    )
+    token_total = jnp.sum(all_facts[:, :, LEN]).astype(jnp.float32)
+    masked_total = jnp.sum(all_facts[:, :, LEN + 1]).astype(jnp.float32)
+
+    words = jnp.arange(vocab_rows, dtype=jnp.int32)
+
+    def chosen(ids):
+        return (ids.reshape(-1, 1) - here * vocab_rows == words[None]).astype(jnp.bfloat16)
+
+    def looked_up(multiply):
+        if near:
+            far = multiply(chosen(plane_facts[4:, :LEN])).astype(jnp.bfloat16)
+            close = multiply(chosen(plane_facts[:4, :LEN])).astype(jnp.bfloat16)
+            total = scatter_near(far.reshape(2, 2, LEN, D), close.reshape(2, 2, LEN, D))
+        else:
+            rows = multiply(chosen(plane_facts[:, :LEN])).astype(jnp.bfloat16)
+            total = lax.psum_scatter(rows, "vocab", scatter_dimension=0, tiled=True)
+        return total.astype(jnp.float32)
+
+    looked_t = looked_up(lambda pick: array_multiply(pick, mentor_lexicon_weights))
+    looked_s = looked_up(lambda pick: trailing_array_multiply(pick, table_low))
+    final_s, saved = layer_forward(student, looked_s, lengths)
     final_t = layer_forward(teacher, looked_t, lengths)[0]
-    final_s, saved = layer_forward(student, looked_s, lengths)
-    offsets = (mask_pos + jnp.arange(seqs_here)[:, None] * LEN).reshape(-1)
-    slot_live = (jnp.arange(CAP)[None, :] < mask_count[:, None]).reshape(-1)
+
+    offsets = jnp.concatenate([mask_pos.reshape(CAP), jnp.zeros((SLOTS - CAP,), jnp.int32)])
     picked_s = final_s[offsets].astype(jnp.bfloat16)
     picked_t = final_t[offsets].astype(jnp.bfloat16)
-    learner_picked, mentor_picked, all_live = (
-        lax.all_gather(picked_s, "vocab", axis=0, tiled=True),
-        lax.all_gather(picked_t, "vocab", axis=0, tiled=True),
-        lax.all_gather(slot_live.astype(jnp.bfloat16), "vocab", axis=0, tiled=True),
-    )
-    learner_energy = trailing_array_multiply(learner_picked, table_low) / smoothing_heat_scale
+    if near:
+        learner_picked = gather_near(picked_s).reshape(-1, D)
+        mentor_picked = gather_near(picked_t).reshape(-1, D)
+    else:
+        learner_picked = lax.all_gather(picked_s, "vocab", axis=0, tiled=True)
+        mentor_picked = lax.all_gather(picked_t, "vocab", axis=0, tiled=True)
+    live_weighting = (
+        (jnp.arange(SLOTS)[None] < plane_facts[:, LEN + 1, None]).astype(jnp.float32).reshape(-1)
+    )
+    learner_energy = array_multiply(learner_picked, table_low) / smoothing_heat_scale
     teacher_logit = (
         trailing_array_multiply(mentor_picked, mentor_lexicon_weights) / smoothing_heat_scale
     )
     peak_s = jnp.max(learner_energy, axis=1)
     peak_t = jnp.max(teacher_logit, axis=1)
     teacher_exps = jnp.exp(teacher_logit - peak_t[:, None])
-    local_stats = (
-        peak_s,
-        jnp.sum(jnp.exp(learner_energy - peak_s[:, None]), axis=1),
-        peak_t,
-        jnp.sum(teacher_exps, axis=1),
-        jnp.sum(teacher_exps * (teacher_logit - learner_energy), axis=1),
-    )
-    merged_stats = combined_all(local_stats, "vocab", combine_stats)
-    logsum_s = merged_stats[0] + jnp.log(merged_stats[1])
-    logsum_t = merged_stats[2] + jnp.log(merged_stats[3])
-    live_weighting = all_live.astype(jnp.float32)
-    diverge = merged_stats[4] / merged_stats[3] - logsum_t + logsum_s
-    block_rows = seqs_here * CAP
-    divergence_part = jnp.sum(
-        lax.dynamic_slice_in_dim(
-            diverge * live_weighting, lax.axis_index("vocab") * block_rows, block_rows
-        )
-    )
+    stats = jnp.stack(
+        [
+            peak_s,
+            jnp.sum(jnp.exp(learner_energy - peak_s[:, None]), axis=1),
+            peak_t,
+            jnp.sum(teacher_exps, axis=1),
+            jnp.sum(teacher_exps * (teacher_logit - learner_energy), axis=1),
+        ]
+    )
+    if near:
+        stats = stats.reshape(5, 2, 2, 2, SLOTS)
+        for axis, bit in ((1, CORE), (2, DEEP), (3, ACROSS)):
+            stats = combine_stats(stats, jnp.flip(swap(stats, bit), axis))
+        stats = stats.reshape(5, -1)
+    else:
+        everything = lax.all_gather(stats, "vocab", axis=0)
+        stats = everything[0]
+        for k in range(1, group):
+            stats = combine_stats(stats, everything[k])
+    logsum_s = stats[0] + jnp.log(stats[1])
+    logsum_t = stats[2] + jnp.log(stats[3])
+    diverge = stats[4] / stats[3] - logsum_t + logsum_s
+    mine = 0 if near else here * SLOTS
+    divergence_part = jnp.sum(lax.dynamic_slice_in_dim(diverge * live_weighting, mine, SLOTS))
     student_probs = jnp.exp(learner_energy - logsum_s[:, None])
     teacher_probs = jnp.exp(teacher_logit - logsum_t[:, None])
     grad_logit = (
@@ -361,10 +661,18 @@
         * live_weighting[:, None]
         * (student_probs - teacher_probs)
     ).astype(jnp.bfloat16)
-    grad_rows = lax.psum_scatter(
-        array_multiply(grad_logit, table_low), "vocab", scatter_dimension=0, tiled=True
-    )
-    grad_table = matmul_left(grad_logit, learner_picked)
+    if near:
+        half = grad_logit.shape[0] // 2
+        far = trailing_array_multiply(grad_logit[half:], table_low).reshape(2, 2, SLOTS, D)
+        close = trailing_array_multiply(grad_logit[:half], table_low).reshape(2, 2, SLOTS, D)
+        grad_rows = scatter_near(far, close)
+    else:
+        grad_rows = lax.psum_scatter(
+            trailing_array_multiply(grad_logit, table_low), "vocab", scatter_dimension=0, tiled=True
+        )
+    head_part = lax.psum_scatter(
+        matmul_left(learner_picked, grad_logit), "dp", scatter_dimension=0, tiled=True
+    )
     products = jnp.sum(final_s * final_t, axis=1)
     inverse_s = lax.rsqrt(jnp.sum(final_s * final_s, axis=1) + cosine_eps)
     inverse_t = lax.rsqrt(jnp.sum(final_t * final_t, axis=1) + cosine_eps)
@@ -376,31 +684,45 @@
         final_t - (products * inverse_s * inverse_s)[:, None] * final_s
     )
     grad_final = grad_final.at[offsets].add(grad_rows)
-    flat_local, grad_embedded = layer_backward(student, saved, grad_final, lengths)
-    all_grads = lax.all_gather(grad_embedded.astype(jnp.bfloat16), "vocab", axis=0, tiled=True)
-    target_rows = jnp.where(inside, local_ids, vocab_rows)
-    grad_table = grad_table + jnp.zeros_like(grad_table).at[target_rows].add(
-        all_grads.astype(jnp.float32), mode="drop"
-    )
-    tiles_all = owner_order.shape[0]
-    padded = jnp.concatenate(
-        [flat_local, jnp.zeros((tiles_all * TILE - flat_local.shape[0],), jnp.float32)]
-    ).reshape(tiles_all, TILE)
-    grad_tiles = padded[owner_order]
-    flat_grad = lax.psum_scatter(grad_tiles, ("dp", "vocab"), scatter_dimension=0, tiled=True)
-    width_share = student_embed.shape[1]
-    summed_table = lax.psum(grad_table, "dp")
-    table_grad = lax.dynamic_slice_in_dim(
-        summed_table, lax.axis_index("dp") * width_share, width_share, 1
-    )
+    layer_grads, grad_embedded = layer_backward(student, saved, grad_final, lengths)
+
+    shares = grad_embedded.astype(jnp.bfloat16).reshape(LEN, planes, width_share).transpose(1, 0, 2)
+    if near:
+        z = lax.axis_index("dp")
+        own = [lax.dynamic_index_in_dim(shares, (z + k) % 4, keepdims=False) for k in range(4)]
+        shares = jnp.stack([own[0]] + [shift(own[k], k) for k in (1, 2, 3)])
+        ids = all_facts[:, :, :LEN].reshape(2, 2, 2, planes, LEN)
+        for axis, bit in ((0, CORE), (1, DEEP), (2, ACROSS)):
+            ids = jnp.where((here & bit) != 0, jnp.flip(ids, axis), ids)
+        ids = ids.transpose(1, 2, 0, 3, 4)
+    else:
+        shares = lax.all_to_all(shares, "dp", 0, 0)
+        ids = all_facts[:, :, :LEN]
+    token_grads = lax.all_gather(shares.reshape(-1, width_share), "vocab", axis=0, tiled=True)
+    token_part = matmul_left(token_grads, chosen(ids))
+    table_grad = (head_part + token_part).T
+
+    if near:
+        split = per // 16 * 8
+        parts = []
+        for begin, end in ((0, split), (split, per)):
+            own_tiles, other_tiles = collect_tiles(upward, layer_grads, tiles_all, per, 2, begin, end - begin)
+            parts.append(reduce_chunk(own_tiles, other_tiles))
+        flat_grad = jnp.concatenate(parts)
+    else:
+        (grad_tiles,) = collect_tiles(target_rows, layer_grads, tiles_all, per, 1, 0, per)
+        flat_grad = lax.psum_scatter(
+            grad_tiles.reshape(tiles_all, TILE), ("dp", "vocab"), scatter_dimension=0, tiled=True
+        )
     loss_term = (
         mixing_coefficient * smoothing_heat_scale**2 * divergence_part / masked_total
         + cosine_weight * cosine_term / token_total
     )
-    squares, loss_value = lax.psum(
-        (jnp.sum(flat_grad * flat_grad) + jnp.sum(table_grad * table_grad), loss_term),
-        ("dp", "vocab"),
-    )
+    squares = jnp.sum(flat_grad * flat_grad) + jnp.sum(table_grad * table_grad)
+    if near:
+        squares, loss_value = sum_everywhere(jnp.stack([squares, loss_term]))
+    else:
+        squares, loss_value = lax.psum((squares, loss_term), ("dp", "vocab"))
     grad_norm = jnp.sqrt(squares)
     factor = clip_norm / jnp.maximum(grad_norm, clip_norm)
     step_float = step_count[0].astype(jnp.float32)
@@ -423,8 +745,9 @@
 
 
 def solution(mesh):
+    near = mesh.shape["dp"] == 4 and mesh.shape["vocab"] == 8
     return jax.shard_map(
-        on_device,
+        functools.partial(on_device, near),
         mesh=mesh,
         in_specs=(
             P(("dp", "vocab"), None),

time: 1610 us -> 1040 us (0.65)
  local copies, waits for them, and re-layouts: 576 us -> 79.8 us
  waiting for transfers between devices: 606 us -> 272 us
  Pallas kernels: 0 us -> 212 us
  blocking collectives: 108 us -> 0 us
  starting transfers between devices: 0.49 us -> 84.7 us
  matrix products: 165 us -> 231 us
    unnamed x14 -> x4, waiting for transfers between devices: 360 us -> 0.75 us
    ppermute x0 -> x96, waiting for transfers between devices: none -> 271 us  [the longest x79 182 us: swap(): return lax.ppermute(value, 'vocab', [(i, i ^ bit) for i in range(8)])]
    scatter x1 -> x0, local copies, waits for them, and re-layouts: 217 us -> none  [on_device(): logical = jnp.zeros_like(student_tiles).at[owner_order].set(student_tiles)]
    pallas_call x0 -> x8, Pallas kernels: none -> 212 us  [the longest x1 88.7 us: place_tiles(): pl.pallas_call(functools.partial(place_kernel, places=places, count=count...]
    gather x3 -> x0, local copies, waits for them, and re-layouts: 157 us -> none  [the longest x1 117 us: on_device(): grad_tiles = padded[owner_order]]
    all_gather x5 -> x2, waiting for transfers between devices: 130 us -> 0.02 us  [the longest x1 0.02 us: on_device(): lax.all_gather(shares.reshape(-1, width_share), 'vocab', axis=0, tiled=True)]
    psum x2 -> x0, blocking collectives: 85.2 us -> none  [the longest x1 46.3 us: on_device(): lax.psum((jnp.sum(flat_grad * flat_grad) + jnp.sum(table_grad * table_gra...]
    ppermute x0 -> x96, starting transfers between devices: none -> 84.6 us  [the longest x79 65.6 us: swap(): return lax.ppermute(value, 'vocab', [(i, i ^ bit) for i in range(8)])]
  transfers between devices with their start and end apart: 12 -> 100, of which waited for: 7 -> 42; matrix products, arithmetic and copies ran while one was open for 37% -> 20% of each run, Pallas kernels for 0% -> 17%
where the time goes in v1:
time: 1040 us; the launch traced here: 1030 us
  waiting for transfers between devices  272 us (26%)
  matrix products  231 us (22%)
  Pallas kernels  212 us (20%)
  other arithmetic  108 us (10%)
  starting transfers between devices  84.7 us (8%)
  local copies, waits for them, and re-layouts  79.8 us (8%)
  between operations  39.7 us (4%)
    ppermute x79, waiting for transfers between devices, swap(): return lax.ppermute(value, 'vocab', [(i, i ^ bit) for i in range(8)])  182 us
    pallas_call x1, Pallas kernels, place_tiles(): pl.pallas_call(functools.partial(place_kernel, places=places, count=count...  88.7 us
    pallas_call x2, Pallas kernels, collect_tiles(): pl.pallas_call(functools.partial(collect_kernel, outs=outs, blocks=blocks...  81.6 us
    ppermute x15, waiting for transfers between devices, shift(): lax.ppermute(value, 'dp', [(i, (i + steps) % size) for i in range(size)])  81.3 us
    dot_general x10, matrix products, array_multiply(): return jnp.dot(left_side, right_side, preferred_element_type=jnp.float32)  81 us
    ppermute x79, starting transfers between devices, swap(): return lax.ppermute(value, 'vocab', [(i, i ^ bit) for i in range(8)])  65.6 us
    dot_general x6, matrix products, matmul_left(): lax.dot_general(left_side, right_side, (((0,), (0,)), ((), ())), preferre...  59.8 us
    dot_general x9, matrix products, trailing_array_multiply(): lax.dot_general(left_side, right_side, (((1,), (1,)), ((), ())), preferre...  45.3 us
  transfers between devices with their start and end apart: 100, of which 42 were waited for; matrix products, arithmetic and copies ran while one was open for 20% of the time, Pallas kernels for 17%

profile of v1, /device:TPU:0, one launch (start us, length us, event | category | flops | bytes accessed | tf_op | source)
XLA Modules:
  0.0 1026.9 jit_solution(2806138658189029325)
XLA Ops:
  16.3 9.4 collective-permute-done
  35.0 8.4 fusion.54
  48.7 6.8 collective-permute-done.17.refs_10_
  61.2 8.6 collective-permute-start.27
  73.2 5.2 rev.32
  80.0 13.3 %collective-permute-done.27.refs_20_ = bf16[1832,128]{1,0:T(8,128)(2,1)} collective-permute-done((bf16[1832,128]{1,0:T(8,128)(2,1)}, bf16[1832,128]{1,0:T(8,128)(2,1)}, u32[]{:S(2)}, u32[]{:S(2)}) %collective-permute-start.27) | collective-permute-done | bytes 469024 | tf_op jit(solution)/shard_map/ppermute | solution.py:51
  98.4 15.3 %collective-permute-done.37.refs_30_ = bf16[1832,128]{1,0:T(8,128)(2,1)} collective-permute-done((bf16[1832,128]{1,0:T(8,128)(2,1)}, bf16[1832,128]{1,0:T(8,128)(2,1)}, u32[]{:S(2)}, u32[]{:S(2)}) %collective-permute-start.37) | collective-permute-done | bytes 469024 | tf_op jit(solution)/shard_map/ppermute | solution.py:51
  134.5 7.6 fusion.52
  163.2 7.5 collective-permute-done.43.refs_36_
  170.6 10.3 %fusion.53 = bf16[2048,768]{1,0:T(8,128)(2,1)} fusion(bf16[768,1920]{1,0:T(8,128)(2,1)} %all-gather.4.cloned.1.call-done, s32[2048]{0:T(1024)S(1)} %bitcast.494), kind=kOutput, calls=%fused_computation.97 | convolution fusion | flops 6045302784 | bytes 6103040 | tf_op jit(solution)/shard_map/dot_general | solution.py:292
  192.2 88.7 %place_tiles.1 = (bf16[768,2304]{1,0:T(8,128)(2,1)}, bf16[768,768]{1,0:T(8,128)(2,1)}, bf16[768,3072]{1,0:T(8,128)(2,1)}, bf16[3072,768]{1,0:T(8,128)(2,1)}, bf1...) custom-call(s32[58624]{0:T(1024)} %reshape.737.rows, bf16[1832,128]{1,0:T(8,128)(2,1)} %copy-done.43, ...), custom_call_target="tpu_custom_call" | custom-call | bytes 180000000 | tf_op jit(solution)/shard_map/place_tiles/pallas_call | solution.py:204
  285.1 7.9 fusion.51
  301.5 22.3 %collective-permute-done.57 = bf16[256,768]{1,0:T(8,128)(2,1)S(1)} collective-permute-done((bf16[256,768]{1,0:T(8,128)(2,1)S(1)}, bf16[256,768]{1,0:T(8,128)(2,1)S(1)}, u32[]{:S(2)}, u32[]{:S(2)}) %collective-permute-start.57) | collective-permute-done | bytes 393248 | tf_op jit(solution)/shard_map/ppermute | solution.py:46
  326.5 8.7 collective-permute-done.7
  344.8 5.6 fusion.49
  354.8 8.5 unpack_matrix.6
  363.4 6.1 fusion.50
  373.9 10.9 %fusion.250 = (f32[12,512]{1,0:T(8,128)S(1)}, f32[12,512,512]{1,2,0:T(8,128)}) fusion(pred[512]{0:T(512)(128)(4,1)S(1)} %iota_compare_fusion.17, bf16[1,512,3,12,64]{1,4,3,2,0:T(8,128)(2,1)} %bitcast.449), kind=kOutput, calls=%fused_computation.547 | convolution fusion | flops 415236608 | bytes 14180864 | tf_op jit(solution)/shard_map/sub | solution.py:360
  384.8 6.9 fusion.73
  400.9 14.9 %unpack_matrix.9 = bf16[3072,768]{1,0:T(8,128)(2,1)} custom-call(bf16[58624,128]{1,0:T(8,128)(2,1)} %all-gather.6.cloned.1.call-done.source), custom_call_target="tpu_custom_call" | custom-call | tf_op jit(solution)/shard_map/unpack_matrix/pallas_call | solution.py:121
  415.9 9.8 unpack_matrix.8
  425.7 23.2 %fusion.252 = (f32[512]{0:T(512)S(1)}, f32[512,768]{1,0:T(8,128)}) fusion(f32[768]{0:T(1024)S(1)} %get-tuple-element.119, bf16[3072,768]{1,0:T(8,128)(2,1)} %unpack_matrix.9, bf16[768,3072]{1,0:T(8,128)(2,1)} %unpack_matrix.8, f32[3072]{0:T(1024)S(1)} %slice_bitcast_fusion.63, f32[512,768]{1,0:T(8,128)} %copy-done.48, f32[768]{0:T(1024)S(1)} %get-tuple-element.120, ...), kind=kOutput, calls=%fused_computation.549 | convolution fusion | flops 4940365312 | bytes 12610560 | tf_op jit(solution)/shard_map/dot_general | solution.py:282
  464.8 19.6 %fusion.17 = (bf16[512,3072]{1,0:T(8,128)(2,1)S(1)}, f32[512,3072]{1,0:T(8,128)}) fusion(f32[3072]{0:T(1024)S(1)} %copy-done.110, bf16[768,3072]{1,0:T(8,128)(2,1)} %get-tuple-element.22, f32[512,768]{1,0:T(8,128)S(1)} %get-tuple-element.173, f32[768]{0:T(1024)S(1)} %copy-done.122, f32[768]{0:T(1024)S(1)} %copy-done.97, f32[512]{0:T(512)S(1)} %add_rsqrt_fusion.6, ...), kind=kOutput, calls=%fused_computation.41 | convolution fusion | flops 2521694208 | bytes 15751168 | tf_op jit(solution)/shard_map/dot_general | solution.py:282
  536.7 4.7 multiply_reduce_fusion.1
  551.7 7.2 multiply_convert_fusion.1
  575.1 6.5 collective-permute-done.68
  597.7 8.8 convert_reduce_fusion
  614.4 7.0 fusion.64
  621.4 9.0 multiply_reduce_fusion
  630.5 7.0 multiply_convert_fusion
  654.1 4.7 collective-permute-done.90
  658.9 10.5 %collective-permute-done.89 = bf16[512,192]{0,1:T(8,128)(2,1)S(1)} collective-permute-done((bf16[512,192]{0,1:T(8,128)(2,1)S(1)}, bf16[512,192]{0,1:T(8,128)(2,1)S(1)}, u32[]{:S(2)}, u32[]{:S(2)}) %collective-permute-start.89) | collective-permute-done | bytes 196640 | tf_op jit(solution)/shard_map/ppermute | solution.py:51
  679.0 5.2 fusion.160.refs_0_
  684.3 5.3 fusion.189.refs_3_
  689.6 5.5 fusion.226.refs_2_
  695.1 40.9 %collect_tiles.2 = (f32[16,912,128]{2,1,0:T(8,128)}, f32[16,912,128]{2,1,0:T(8,128)}) custom-call(s32[58624]{0:T(1024)} %reshape.733.rows, f32[768,2304]{1,0:T(8,128)} %fusion.160.refs_0_, f32[768,768]{1,0:T(8,128)} %fusion.186.refs_1_, f32[768,3072]{1,0:T(8,128)} %fusion.226.refs_2_, f32[3072,768]{1,0:T(8,128)} %fusion.189.refs_3_, ...), custom_call_target="tpu_custom_call" | custom-call | bytes 80000000 | tf_op jit(solution)/shard_map/collect_tiles/pallas_call | solution.py:268
  736.1 40.6 %collect_tiles.3 = (f32[16,920,128]{2,1,0:T(8,128)}, f32[16,920,128]{2,1,0:T(8,128)}) custom-call(s32[58624]{0:T(1024)} %reshape.733.rows, f32[768,2304]{1,0:T(8,128)} %fusion.160.refs_0_, f32[768,768]{1,0:T(8,128)} %fusion.186.refs_1_, f32[768,3072]{1,0:T(8,128)} %fusion.226.refs_2_, f32[3072,768]{1,0:T(8,128)} %fusion.189.refs_3_, ...), custom_call_target="tpu_custom_call" | custom-call | bytes 80000000 | tf_op jit(solution)/shard_map/collect_tiles/pallas_call | solution.py:268
  777.2 7.9 fusion.258
  786.0 6.6 add.733
  801.4 6.2 add.741
  819.8 20.1 %collective-permute-done.75 = f32[2,2,912,128]{3,2,0,1:T(8,128)} collective-permute-done((f32[2,2,912,128]{3,2,0,1:T(8,128)}, f32[2,2,912,128]{3,2,0,1:T(8,128)}, u32[]{:S(2)}, u32[]{:S(2)}) %collective-permute-start.75) | collective-permute-done | bytes 1867808 | tf_op jit(solution)/shard_map/ppermute | solution.py:46
  846.9 33.4 %collective-permute-done.83 = f32[2,2,920,128]{3,2,0,1:T(8,128)} collective-permute-done((f32[2,2,920,128]{3,2,0,1:T(8,128)}, f32[2,2,920,128]{3,2,0,1:T(8,128)}, u32[]{:S(2)}, u32[]{:S(2)}) %collective-permute-start.83) | collective-permute-done | bytes 1884192 | tf_op jit(solution)/shard_map/ppermute | solution.py:46
  885.5 18.4 %collective-permute-done.76 = f32[2,912,128]{2,1,0:T(8,128)S(1)} collective-permute-done((f32[2,912,128]{2,1,0:T(8,128)S(1)}, f32[2,912,128]{2,1,0:T(8,128)S(1)}, u32[]{:S(2)}, u32[]{:S(2)}) %collective-permute-start.76) | collective-permute-done | bytes 933920 | tf_op jit(solution)/shard_map/ppermute | solution.py:46
  904.3 18.8 %collective-permute-done.84 = f32[2,920,128]{2,1,0:T(8,128)S(1)} collective-permute-done((f32[2,920,128]{2,1,0:T(8,128)S(1)}, f32[2,920,128]{2,1,0:T(8,128)S(1)}, u32[]{:S(2)}, u32[]{:S(2)}) %collective-permute-start.84) | collective-permute-done | bytes 942112 | tf_op jit(solution)/shard_map/ppermute | solution.py:46
  926.9 11.9 %collective-permute-done.85 = f32[920,128]{1,0:T(8,128)S(1)} collective-permute-done((f32[920,128]{1,0:T(8,128)S(1)}, f32[920,128]{1,0:T(8,128)S(1)}, u32[]{:S(2)}, u32[]{:S(2)}) %collective-permute-start.85) | collective-permute-done | bytes 471072 | tf_op jit(solution)/shard_map/ppermute | solution.py:51
  938.9 9.9 collective-permute-done.78
  949.0 32.4 %fusion.1 = f32[192,1920]{1,0:T(8,128)} fusion(bf16[16384,192]{0,1:T(8,128)(2,1)} %all-gather.8.cloned.1.call-done, s32[16384]{0:T(1024)S(1)} %bitcast.478), kind=kOutput, calls=%fused_computation.5 | convolution fusion | flops 12111052800 | bytes 7831552 | tf_op jit(solution)/shard_map/dot_general | solution.py:286
  987.3 4.9 collective-permute-done.87
  (730 shorter events, 328.0 us)
Async XLA Ops:
  7.2 163.5 %all-gather.4.cloned.1.call-start = ((), (), s32[]{:S(2)}) async-start(), calls=%async_computation.1 | async-start | bytes 3686400 | tf_op jit(solution)/shard_map/all_gather | solution.py:564
  9.7 326.8 %all-gather.6.cloned.1.call-start = ((), (), s32[]{:S(2)}) async-start(), calls=%async_computation.2 | async-start | bytes 15476736 | tf_op jit(solution)/shard_map/all_gather | solution.py:565
  10.5 938.5 %all-gather.8.cloned.1.call-start = ((), (), s32[]{:S(2)}) async-start(), calls=%async_computation.4 | async-start | bytes 7077888 | tf_op jit(solution)/shard_map/all_gather | solution.py:701
  11.8 21.7 %collective-permute-start.9 = (bf16[1832,128]{1,0:T(8,128)(2,1)S(1)}, bf16[1832,128]{1,0:T(8,128)(2,1)}, u32[]{:S(2)}, u32[]{:S(2)}) collective-permute-start(bf16[1832,128]{1,0:T(8,128)(2,1)S(1)} %convert_element_type.208.refs_0_), channel_id=1, source_target_pairs={{0,2},{1,3},{2,0},{3,1},{4,6},{5,7},{6,4},{7,5},{8,10},{9,11},{10,... | collective-permute-start | bytes 1406984 | tf_op jit(solution)/shard_map/ppermute | solution.py:46
  30.0 25.5 %collective-permute-start.17 = (bf16[1832,128]{1,0:T(8,128)(2,1)S(1)}, bf16[1832,128]{1,0:T(8,128)(2,1)}, u32[]{:S(2)}, u32[]{:S(2)}) collective-permute-start(bf16[1832,128]{1,0:T(8,128)(2,1)S(1)} %convert_element_type.208.refs_0_), channel_id=1, source_target_pairs={{0,8},{8,16},{16,24},{24,0},{1,9},{9,17},{17,25},{25,1},{2,10},{10... | collective-permute-start | bytes 1406984 | tf_op jit(solution)/shard_map/ppermute | solution.py:51
  33.4 27.8 %collective-permute-start.8 = (bf16[1832,128]{1,0:T(8,128)(2,1)S(1)}, bf16[1832,128]{1,0:T(8,128)(2,1)}, u32[]{:S(2)}, u32[]{:S(2)}) collective-permute-start(bf16[1832,128]{1,0:T(8,128)(2,1)S(1)} %convert_element_type.208.refs_0_), channel_id=1, source_target_pairs={{0,1},{1,0},{2,3},{3,2},{4,5},{5,4},{6,7},{7,6},{8,9},{9,8},{10,11... | collective-permute-start | bytes 1406984 | tf_op jit(solution)/shard_map/ppermute | solution.py:46
  34.5 22.8 %collective-permute-start.13 = (bf16[912,128]{1,0:T(8,128)(2,1)S(1)}, bf16[912,128]{1,0:T(8,128)(2,1)}, u32[]{:S(2)}, u32[]{:S(2)}) collective-permute-start(bf16[912,128]{1,0:T(8,128)(2,1)S(1)} %slice.679), channel_id=1, source_target_pairs={{0,4},{1,5},{2,6},{3,7},{4,0},{5,1},{6,2},{7,3},{8,12},{9,13},{10,... | collective-permute-start | bytes 700424 | tf_op jit(solution)/shard_map/ppermute | solution.py:46
  43.5 90.6 %collective-permute-start.53 = (bf16[2,2,512,768]{3,2,1,0:T(8,128)(2,1)}, bf16[2,2,512,768]{3,2,1,0:T(8,128)(2,1)}, u32[]{:S(2)}, u32[]{:S(2)}) collective-permute-start(bf16[2,2,512,768]{3,2,1,0:T(8,128)(2,1)} %bitcast.47), channel_id=1, source_target_pairs={{0,1},{1,0},{2,3},{3,2},{4,5},{5,4},{6,7},{7,6},{8,9},{9,8},{10,11... | collective-permute-start | bytes 9437192 | tf_op jit(solution)/shard_map/ppermute | solution.py:46
  47.3 22.6 %collective-permute-start.15 = (bf16[920,128]{1,0:T(8,128)(2,1)}, bf16[920,128]{1,0:T(8,128)(2,1)}, u32[]{:S(2)}, u32[]{:S(2)}) collective-permute-start(bf16[920,128]{1,0:T(8,128)(2,1)} %slice.680), channel_id=1, source_target_pairs={{0,2},{1,3},{2,0},{3,1},{4,6},{5,7},{6,4},{7,5},{8,10},{9,11},{10,... | collective-permute-start | bytes 706568 | tf_op jit(solution)/shard_map/ppermute | solution.py:46
  61.2 32.1 %collective-permute-start.27 = (bf16[1832,128]{1,0:T(8,128)(2,1)}, bf16[1832,128]{1,0:T(8,128)(2,1)}, u32[]{:S(2)}, u32[]{:S(2)}) collective-permute-start(bf16[1832,128]{1,0:T(8,128)(2,1)} %collective-permute-done.17.refs_10_), channel_id=1, source_target_pairs={{0,8},{8,16},{16,24},{24,0},{1,9},{9,17},{17,25},{25,1},{2,10},{10... | collective-permute-start | bytes 1406984 | tf_op jit(solution)/shard_map/ppermute | solution.py:51
  69.9 23.5 %collective-permute-start.21 = (bf16[1832,128]{1,0:T(8,128)(2,1)}, bf16[1832,128]{1,0:T(8,128)(2,1)}, u32[]{:S(2)}, u32[]{:S(2)}) collective-permute-start(bf16[1832,128]{1,0:T(8,128)(2,1)} %collective-permute-done.17.refs_10_), channel_id=1, source_target_pairs={{0,4},{1,5},{2,6},{3,7},{4,0},{5,1},{6,2},{7,3},{8,12},{9,13},{10,... | collective-permute-start | bytes 1406984 | tf_op jit(solution)/shard_map/ppermute | solution.py:46
  71.4 22.4 %collective-permute-start.18 = (bf16[1832,128]{1,0:T(8,128)(2,1)}, bf16[1832,128]{1,0:T(8,128)(2,1)}, u32[]{:S(2)}, u32[]{:S(2)}) collective-permute-start(bf16[1832,128]{1,0:T(8,128)(2,1)} %collective-permute-done.17.refs_10_), channel_id=1, source_target_pairs={{0,1},{1,0},{2,3},{3,2},{4,5},{5,4},{6,7},{7,6},{8,9},{9,8},{10,11... | collective-permute-start | bytes 1406984 | tf_op jit(solution)/shard_map/ppermute | solution.py:46
  71.4 23.9 %collective-permute-start.12 = (bf16[1832,128]{1,0:T(8,128)(2,1)}, bf16[1832,128]{1,0:T(8,128)(2,1)}, u32[]{:S(2)}, u32[]{:S(2)}) collective-permute-start(bf16[1832,128]{1,0:T(8,128)(2,1)} %collective-permute-done.11.refs_4_), channel_id=1, source_target_pairs={{0,1},{1,0},{2,3},{3,2},{4,5},{5,4},{6,7},{7,6},{8,9},{9,8},{10,11... | collective-permute-start | bytes 1406984 | tf_op jit(solution)/shard_map/ppermute | solution.py:46
  93.8 19.9 %collective-permute-start.23 = (bf16[912,128]{1,0:T(8,128)(2,1)}, bf16[912,128]{1,0:T(8,128)(2,1)}, u32[]{:S(2)}, u32[]{:S(2)}) collective-permute-start(bf16[912,128]{1,0:T(8,128)(2,1)} %slice.681), channel_id=1, source_target_pairs={{0,4},{1,5},{2,6},{3,7},{4,0},{5,1},{6,2},{7,3},{8,12},{9,13},{10,... | collective-permute-start | bytes 700424 | tf_op jit(solution)/shard_map/ppermute | solution.py:46
  95.3 18.4 %collective-permute-start.37 = (bf16[1832,128]{1,0:T(8,128)(2,1)}, bf16[1832,128]{1,0:T(8,128)(2,1)}, u32[]{:S(2)}, u32[]{:S(2)}) collective-permute-start(bf16[1832,128]{1,0:T(8,128)(2,1)} %collective-permute-done.27.refs_20_), channel_id=1, source_target_pairs={{0,8},{8,16},{16,24},{24,0},{1,9},{9,17},{17,25},{25,1},{2,10},{10... | collective-permute-start | bytes 1406984 | tf_op jit(solution)/shard_map/ppermute | solution.py:51
  96.1 36.7 %collective-permute-start.31 = (bf16[1832,128]{1,0:T(8,128)(2,1)}, bf16[1832,128]{1,0:T(8,128)(2,1)}, u32[]{:S(2)}, u32[]{:S(2)}) collective-permute-start(bf16[1832,128]{1,0:T(8,128)(2,1)} %collective-permute-done.27.refs_20_), channel_id=1, source_target_pairs={{0,4},{1,5},{2,6},{3,7},{4,0},{5,1},{6,2},{7,3},{8,12},{9,13},{10,... | collective-permute-start | bytes 1406984 | tf_op jit(solution)/shard_map/ppermute | solution.py:46
  97.0 36.5 %collective-permute-start.29 = (bf16[1832,128]{1,0:T(8,128)(2,1)}, bf16[1832,128]{1,0:T(8,128)(2,1)}, u32[]{:S(2)}, u32[]{:S(2)}) collective-permute-start(bf16[1832,128]{1,0:T(8,128)(2,1)} %collective-permute-done.27.refs_20_), channel_id=1, source_target_pairs={{0,2},{1,3},{2,0},{3,1},{4,6},{5,7},{6,4},{7,5},{8,10},{9,11},{10,... | collective-permute-start | bytes 1406984 | tf_op jit(solution)/shard_map/ppermute | solution.py:46
  113.7 19.7 %collective-permute-start.41 = (bf16[1832,128]{1,0:T(8,128)(2,1)}, bf16[1832,128]{1,0:T(8,128)(2,1)}, u32[]{:S(2)}, u32[]{:S(2)}) collective-permute-start(bf16[1832,128]{1,0:T(8,128)(2,1)} %collective-permute-done.37.refs_30_), channel_id=1, source_target_pairs={{0,4},{1,5},{2,6},{3,7},{4,0},{5,1},{6,2},{7,3},{8,12},{9,13},{10,... | collective-permute-start | bytes 1406984 | tf_op jit(solution)/shard_map/ppermute | solution.py:46
  113.7 20.2 %collective-permute-start.39 = (bf16[1832,128]{1,0:T(8,128)(2,1)}, bf16[1832,128]{1,0:T(8,128)(2,1)}, u32[]{:S(2)}, u32[]{:S(2)}) collective-permute-start(bf16[1832,128]{1,0:T(8,128)(2,1)} %collective-permute-done.37.refs_30_), channel_id=1, source_target_pairs={{0,2},{1,3},{2,0},{3,1},{4,6},{5,7},{6,4},{7,5},{8,10},{9,11},{10,... | collective-permute-start | bytes 1406984 | tf_op jit(solution)/shard_map/ppermute | solution.py:46
  133.4 18.3 %collective-permute-start.22 = (bf16[1832,128]{1,0:T(8,128)(2,1)}, bf16[1832,128]{1,0:T(8,128)(2,1)S(1)}, u32[]{:S(2)}, u32[]{:S(2)}) collective-permute-start(bf16[1832,128]{1,0:T(8,128)(2,1)} %collective-permute-done.21.refs_14_), channel_id=1, source_target_pairs={{0,1},{1,0},{2,3},{3,2},{4,5},{5,4},{6,7},{7,6},{8,9},{9,8},{10,11... | collective-permute-start | bytes 1406984 | tf_op jit(solution)/shard_map/ppermute | solution.py:46
  134.0 19.1 %collective-permute-start.20 = (bf16[1832,128]{1,0:T(8,128)(2,1)}, bf16[1832,128]{1,0:T(8,128)(2,1)S(1)}, u32[]{:S(2)}, u32[]{:S(2)}) collective-permute-start(bf16[1832,128]{1,0:T(8,128)(2,1)} %collective-permute-done.19.refs_12_), channel_id=1, source_target_pairs={{0,1},{1,0},{2,3},{3,2},{4,5},{5,4},{6,7},{7,6},{8,9},{9,8},{10,11... | collective-permute-start | bytes 1406984 | tf_op jit(solution)/shard_map/ppermute | solution.py:46
  161.0 20.0 %collective-permute-start.30 = (bf16[1832,128]{1,0:T(8,128)(2,1)}, bf16[1832,128]{1,0:T(8,128)(2,1)S(1)}, u32[]{:S(2)}, u32[]{:S(2)}) collective-permute-start(bf16[1832,128]{1,0:T(8,128)(2,1)} %collective-permute-done.29.refs_22_), channel_id=1, source_target_pairs={{0,1},{1,0},{2,3},{3,2},{4,5},{5,4},{6,7},{7,6},{8,9},{9,8},{10,11... | collective-permute-start | bytes 1406984 | tf_op jit(solution)/shard_map/ppermute | solution.py:46
  161.0 20.5 %collective-permute-start.36 = (bf16[920,128]{1,0:T(8,128)(2,1)}, bf16[920,128]{1,0:T(8,128)(2,1)}, u32[]{:S(2)}, u32[]{:S(2)}) collective-permute-start(bf16[920,128]{1,0:T(8,128)(2,1)} %collective-permute-done.35.refs_28_), channel_id=1, source_target_pairs={{0,1},{1,0},{2,3},{3,2},{4,5},{5,4},{6,7},{7,6},{8,9},{9,8},{10,11... | collective-permute-start | bytes 706568 | tf_op jit(solution)/shard_map/ppermute | solution.py:46
  161.6 21.3 %collective-permute-start.45 = (bf16[920,128]{1,0:T(8,128)(2,1)}, bf16[920,128]{1,0:T(8,128)(2,1)}, u32[]{:S(2)}, u32[]{:S(2)}) collective-permute-start(bf16[920,128]{1,0:T(8,128)(2,1)} %slice.686), channel_id=1, source_target_pairs={{0,2},{1,3},{2,0},{3,1},{4,6},{5,7},{6,4},{7,5},{8,10},{9,11},{10,... | collective-permute-start | bytes 706568 | tf_op jit(solution)/shard_map/ppermute | solution.py:46
  163.1 22.9 %collective-permute-start.42 = (bf16[1832,128]{1,0:T(8,128)(2,1)}, bf16[1832,128]{1,0:T(8,128)(2,1)}, u32[]{:S(2)}, u32[]{:S(2)}) collective-permute-start(bf16[1832,128]{1,0:T(8,128)(2,1)} %collective-permute-done.41.refs_34_), channel_id=1, source_target_pairs={{0,1},{1,0},{2,3},{3,2},{4,5},{5,4},{6,7},{7,6},{8,9},{9,8},{10,11... | collective-permute-start | bytes 1406984 | tf_op jit(solution)/shard_map/ppermute | solution.py:46
  181.5 100.8 %collective-permute-start.54 = (bf16[2,256,768]{2,1,0:T(8,128)(2,1)}, bf16[2,256,768]{2,1,0:T(8,128)(2,1)}, u32[]{:S(2)}, u32[]{:S(2)}) collective-permute-start(bf16[2,256,768]{2,1,0:T(8,128)(2,1)} %slice_bitcast_fusion.14), channel_id=1, source_target_pairs={{0,2},{1,3},{2,0},{3,1},{4,6},{5,7},{6,4},{7,5},{8,10},{9,11},{10,... | collective-permute-start | bytes 2359304 | tf_op jit(solution)/shard_map/ppermute | solution.py:46
  182.9 99.4 %collective-permute-start.56 = (bf16[2,256,768]{2,1,0:T(8,128)(2,1)}, bf16[2,256,768]{2,1,0:T(8,128)(2,1)}, u32[]{:S(2)}, u32[]{:S(2)}) collective-permute-start(bf16[2,256,768]{2,1,0:T(8,128)(2,1)} %slice_bitcast_fusion.12), channel_id=1, source_target_pairs={{0,4},{1,5},{2,6},{3,7},{4,0},{5,1},{6,2},{7,3},{8,12},{9,13},{10,... | collective-permute-start | bytes 2359304 | tf_op jit(solution)/shard_map/ppermute | solution.py:46
  185.0 107.9 %collective-permute-start.3 = (bf16[2,2,512,768]{3,2,1,0:T(8,128)(2,1)}, bf16[2,2,512,768]{3,2,1,0:T(8,128)(2,1)}, u32[]{:S(2)}, u32[]{:S(2)}) collective-permute-start(bf16[2,2,512,768]{3,2,1,0:T(8,128)(2,1)} %bitcast.12), channel_id=1, source_target_pairs={{0,1},{1,0},{2,3},{3,2},{4,5},{5,4},{6,7},{7,6},{8,9},{9,8},{10,11... | collective-permute-start | bytes 9437192 | tf_op jit(solution)/shard_map/ppermute | solution.py:46
  295.8 28.9 %collective-permute-start.4 = (bf16[2,256,768]{2,1,0:T(8,128)(2,1)S(1)}, bf16[2,256,768]{2,1,0:T(8,128)(2,1)S(1)}, u32[]{:S(2)}, u32[]{:S(2)}) collective-permute-start(bf16[2,256,768]{2,1,0:T(8,128)(2,1)S(1)} %slice_bitcast_fusion.21), channel_id=1, source_target_pairs={{0,2},{1,3},{2,0},{3,1},{4,6},{5,7},{6,4},{7,5},{8,10},{9,11},{10,... | collective-permute-start | bytes 2359304 | tf_op jit(solution)/shard_map/ppermute | solution.py:46
  296.5 28.1 %collective-permute-start.6 = (bf16[2,256,768]{2,1,0:T(8,128)(2,1)S(1)}, bf16[2,256,768]{2,1,0:T(8,128)(2,1)S(1)}, u32[]{:S(2)}, u32[]{:S(2)}) collective-permute-start(bf16[2,256,768]{2,1,0:T(8,128)(2,1)S(1)} %slice_bitcast_fusion.19), channel_id=1, source_target_pairs={{0,4},{1,5},{2,6},{3,7},{4,0},{5,1},{6,2},{7,3},{8,12},{9,13},{10,... | collective-permute-start | bytes 2359304 | tf_op jit(solution)/shard_map/ppermute | solution.py:46
  296.7 27.1 %collective-permute-start.57 = (bf16[256,768]{1,0:T(8,128)(2,1)S(1)}, bf16[256,768]{1,0:T(8,128)(2,1)S(1)}, u32[]{:S(2)}, u32[]{:S(2)}) collective-permute-start(bf16[256,768]{1,0:T(8,128)(2,1)S(1)} %slice_bitcast_fusion.51), channel_id=1, source_target_pairs={{0,2},{1,3},{2,0},{3,1},{4,6},{5,7},{6,4},{7,5},{8,10},{9,11},{10,... | collective-permute-start | bytes 1179656 | tf_op jit(solution)/shard_map/ppermute | solution.py:46
  299.4 26.3 %collective-permute-start.55 = (bf16[256,768]{1,0:T(8,128)(2,1)S(1)}, bf16[256,768]{1,0:T(8,128)(2,1)S(1)}, u32[]{:S(2)}, u32[]{:S(2)}) collective-permute-start(bf16[256,768]{1,0:T(8,128)(2,1)S(1)} %slice_bitcast_fusion.53), channel_id=1, source_target_pairs={{0,4},{1,5},{2,6},{3,7},{4,0},{5,1},{6,2},{7,3},{8,12},{9,13},{10,... | collective-permute-start | bytes 1179656 | tf_op jit(solution)/shard_map/ppermute | solution.py:46
  523.8 20.8 %collective-permute-start.51 = (s32[2,3,640]{2,1,0:T(4,128)S(1)}, s32[2,3,640]{2,1,0:T(4,128)S(1)}, u32[]{:S(2)}, u32[]{:S(2)}) collective-permute-start(s32[2,3,640]{2,1,0:T(4,128)S(1)} %pad_add_fusion.7), channel_id=1, source_target_pairs={{0,4},{1,5},{2,6},{3,7},{4,0},{5,1},{6,2},{7,3},{8,12},{9,13},{10,... | collective-permute-start | bytes 46088 | tf_op jit(solution)/shard_map/ppermute | solution.py:46
  670.6 311.6 %reduce-scatter.2.cloned.1.call-start = ((), (), s32[]{:S(2)}) async-start(), calls=%async_computation.3 | async-start | bytes 7372800 | tf_op jit(solution)/shard_map/reduce_scatter | solution.py:673
  736.1 49.9 %collective-permute-start.72 = (f32[16,912,128]{2,1,0:T(8,128)}, f32[16,912,128]{2,1,0:T(8,128)}, u32[]{:S(2)}, u32[]{:S(2)}) collective-permute-start(f32[16,912,128]{2,1,0:T(8,128)} %get-tuple-element.25), channel_id=1, source_target_pairs={{0,1},{1,0},{2,3},{3,2},{4,5},{5,4},{6,7},{7,6},{8,9},{9,8},{10,11... | collective-permute-start | bytes 22413320 | tf_op jit(solution)/shard_map/ppermute | solution.py:46
  776.8 24.6 %collective-permute-start.80 = (f32[16,920,128]{2,1,0:T(8,128)}, f32[16,920,128]{2,1,0:T(8,128)}, u32[]{:S(2)}, u32[]{:S(2)}) collective-permute-start(f32[16,920,128]{2,1,0:T(8,128)} %get-tuple-element.27), channel_id=1, source_target_pairs={{0,1},{1,0},{2,3},{3,2},{4,5},{5,4},{6,7},{7,6},{8,9},{9,8},{10,11... | collective-permute-start | bytes 22609928 | tf_op jit(solution)/shard_map/ppermute | solution.py:46
  796.0 43.9 %collective-permute-start.75 = (f32[2,2,912,128]{3,2,0,1:T(8,128)}, f32[2,2,912,128]{3,2,0,1:T(8,128)}, u32[]{:S(2)}, u32[]{:S(2)}) collective-permute-start(f32[2,2,912,128]{3,2,0,1:T(8,128)} %bitcast.418), channel_id=1, source_target_pairs={{0,2},{1,3},{2,0},{3,1},{4,6},{5,7},{6,4},{7,5},{8,10},{9,11},{10,... | collective-permute-start | bytes 5603336 | tf_op jit(solution)/shard_map/ppermute | solution.py:46
  799.8 43.9 %collective-permute-start.73 = (f32[2,2,912,128]{3,2,0,1:T(8,128)}, f32[2,2,912,128]{3,2,0,1:T(8,128)}, u32[]{:S(2)}, u32[]{:S(2)}) collective-permute-start(f32[2,2,912,128]{3,2,0,1:T(8,128)} %bitcast.419), channel_id=1, source_target_pairs={{0,4},{1,5},{2,6},{3,7},{4,0},{5,1},{6,2},{7,3},{8,12},{9,13},{10,... | collective-permute-start | bytes 5603336 | tf_op jit(solution)/shard_map/ppermute | solution.py:46
  812.9 67.5 %collective-permute-start.83 = (f32[2,2,920,128]{3,2,0,1:T(8,128)}, f32[2,2,920,128]{3,2,0,1:T(8,128)}, u32[]{:S(2)}, u32[]{:S(2)}) collective-permute-start(f32[2,2,920,128]{3,2,0,1:T(8,128)} %bitcast.416), channel_id=1, source_target_pairs={{0,2},{1,3},{2,0},{3,1},{4,6},{5,7},{6,4},{7,5},{8,10},{9,11},{10,... | collective-permute-start | bytes 5652488 | tf_op jit(solution)/shard_map/ppermute | solution.py:46
  818.9 65.1 %collective-permute-start.81 = (f32[2,2,920,128]{3,2,0,1:T(8,128)S(1)}, f32[2,2,920,128]{3,2,0,1:T(8,128)S(1)}, u32[]{:S(2)}, u32[]{:S(2)}) collective-permute-start(f32[2,2,920,128]{3,2,0,1:T(8,128)S(1)} %bitcast.451), channel_id=1, source_target_pairs={{0,4},{1,5},{2,6},{3,7},{4,0},{5,1},{6,2},{7,3},{8,12},{9,13},{10,... | collective-permute-start | bytes 5652488 | tf_op jit(solution)/shard_map/ppermute | solution.py:46
  841.9 62.0 %collective-permute-start.76 = (f32[2,912,128]{2,1,0:T(8,128)S(1)}, f32[2,912,128]{2,1,0:T(8,128)S(1)}, u32[]{:S(2)}, u32[]{:S(2)}) collective-permute-start(f32[2,912,128]{2,1,0:T(8,128)S(1)} %slice_bitcast_fusion.4), channel_id=1, source_target_pairs={{0,4},{1,5},{2,6},{3,7},{4,0},{5,1},{6,2},{7,3},{8,12},{9,13},{10,... | collective-permute-start | bytes 2801672 | tf_op jit(solution)/shard_map/ppermute | solution.py:46
  845.6 58.6 %collective-permute-start.74 = (f32[2,912,128]{2,1,0:T(8,128)S(1)}, f32[2,912,128]{2,1,0:T(8,128)S(1)}, u32[]{:S(2)}, u32[]{:S(2)}) collective-permute-start(f32[2,912,128]{2,1,0:T(8,128)S(1)} %slice_bitcast_fusion.6), channel_id=1, source_target_pairs={{0,2},{1,3},{2,0},{3,1},{4,6},{5,7},{6,4},{7,5},{8,10},{9,11},{10,... | collective-permute-start | bytes 2801672 | tf_op jit(solution)/shard_map/ppermute | solution.py:46
  882.2 40.9 %collective-permute-start.84 = (f32[2,920,128]{2,1,0:T(8,128)S(1)}, f32[2,920,128]{2,1,0:T(8,128)S(1)}, u32[]{:S(2)}, u32[]{:S(2)}) collective-permute-start(f32[2,920,128]{2,1,0:T(8,128)S(1)} %slice_bitcast_fusion), channel_id=1, source_target_pairs={{0,4},{1,5},{2,6},{3,7},{4,0},{5,1},{6,2},{7,3},{8,12},{9,13},{10,... | collective-permute-start | bytes 2826248 | tf_op jit(solution)/shard_map/ppermute | solution.py:46
  884.2 41.6 %collective-permute-start.82 = (f32[2,920,128]{2,1,0:T(8,128)S(1)}, f32[2,920,128]{2,1,0:T(8,128)S(1)}, u32[]{:S(2)}, u32[]{:S(2)}) collective-permute-start(f32[2,920,128]{2,1,0:T(8,128)S(1)} %slice_bitcast_fusion.2), channel_id=1, source_target_pairs={{0,2},{1,3},{2,0},{3,1},{4,6},{5,7},{6,4},{7,5},{8,10},{9,11},{10,... | collective-permute-start | bytes 2826248 | tf_op jit(solution)/shard_map/ppermute | solution.py:46
  904.1 19.2 %collective-permute-start.77 = (f32[912,128]{1,0:T(8,128)S(1)}, f32[912,128]{1,0:T(8,128)S(1)}, u32[]{:S(2)}, u32[]{:S(2)}) collective-permute-start(f32[912,128]{1,0:T(8,128)S(1)} %slice_bitcast_fusion.43), channel_id=1, source_target_pairs={{0,8},{8,16},{16,24},{24,0},{1,9},{9,17},{17,25},{25,1},{2,10},{10... | collective-permute-start | bytes 1400840 | tf_op jit(solution)/shard_map/ppermute | solution.py:51
  923.4 25.4 %collective-permute-start.78 = (f32[912,128]{1,0:T(8,128)S(1)}, f32[912,128]{1,0:T(8,128)S(1)}, u32[]{:S(2)}, u32[]{:S(2)}) collective-permute-start(f32[912,128]{1,0:T(8,128)S(1)} %fusion.111), channel_id=1, source_target_pairs={{0,8},{8,16},{16,24},{24,0},{1,9},{9,17},{17,25},{25,1},{2,10},{10... | collective-permute-start | bytes 1400840 | tf_op jit(solution)/shard_map/ppermute | solution.py:51
  938.9 42.5 %collective-permute-start.86 = (f32[920,128]{1,0:T(8,128)S(1)}, f32[920,128]{1,0:T(8,128)S(1)}, u32[]{:S(2)}, u32[]{:S(2)}) collective-permute-start(f32[920,128]{1,0:T(8,128)S(1)} %fusion.108), channel_id=1, source_target_pairs={{0,8},{8,16},{16,24},{24,0},{1,9},{9,17},{17,25},{25,1},{2,10},{10... | collective-permute-start | bytes 1413128 | tf_op jit(solution)/shard_map/ppermute | solution.py:51
  948.9 37.2 %collective-permute-start.79 = (f32[912,128]{1,0:T(8,128)S(1)}, f32[912,128]{1,0:T(8,128)}, u32[]{:S(2)}, u32[]{:S(2)}) collective-permute-start(f32[912,128]{1,0:T(8,128)S(1)} %fusion.112), channel_id=1, source_target_pairs={{0,8},{8,16},{16,24},{24,0},{1,9},{9,17},{17,25},{25,1},{2,10},{10... | collective-permute-start | bytes 1400840 | tf_op jit(solution)/shard_map/ppermute | solution.py:51
  (202 other events, 2340.3 us)
Sparse Core Ops, SparseCore 0:
  10.2 80.1 all-gather.3
  93.3 132.0 all-gather.5
  670.7 44.9 all-gather.7
  785.2 103.7 reduce-scatter.1

commit v2 on v1

--- a/solution.py
+++ b/solution.py
@@ -520,14 +520,18 @@
     return arrivals, places
 
 
-def reduce_chunk(mine, other):
-    lines = mine.shape[1]
-    value = (mine + swap(other, CORE)).reshape(4, 2, 2, lines, TILE)
+def sent_low(value, bit):
+    return swap(value.astype(jnp.bfloat16), bit).astype(jnp.float32)
+
+
+def reduce_chunk(value):
+    lines = value.shape[1]
+    value = value.reshape(4, 2, 2, lines, TILE)
     first, second = value[2:], value[:2]
-    first = first[:, :, 0] + swap(first[:, :, 1], ACROSS)
-    second = second[:, 0] + swap(second[:, 1], DEEP)
-    first = first[:, 0] + swap(first[:, 1], DEEP)
-    second = second[:, 0] + swap(second[:, 1], ACROSS)
+    first = first[:, :, 0] + sent_low(first[:, :, 1], ACROSS)
+    second = second[:, 0] + sent_low(second[:, 1], DEEP)
+    first = first[:, 0] + sent_low(first[:, 1], DEEP)
+    second = second[:, 0] + sent_low(second[:, 1], ACROSS)
     moving = shift(first[1], 1)
     moving = shift(first[0] + moving, 1)
     moving = shift(second[1] + moving, 1)
@@ -568,24 +572,14 @@
         by_plane = [facts, shift(facts, 1), shift(facts, 2), shift(facts, 3)]
         other_facts = gather_near(jnp.stack(by_plane[1:]))
         all_facts = jnp.concatenate([plane_facts[:, None], other_facts], axis=1)
-        arrivals, places = gather_student(student_low)
         relative = relative_order(target_rows, per)
         downward = rolled(relative, True).reshape(-1)
         upward = rolled(relative.transpose(3, 0, 1, 2, 4).swapaxes(0, 1), False).swapaxes(0, 1).reshape(-1)
-        matrices = place_tiles(downward, arrivals, tuple(places), planes * group, per)
     else:
         by_plane = lax.all_gather(facts, "dp", axis=0)
         all_facts = lax.all_gather(by_plane, "vocab", axis=0)
         plane_facts = lax.dynamic_index_in_dim(all_facts, lax.axis_index("dp"), 1, keepdims=False)
         student_tiles = lax.all_gather(student_low, ("dp", "vocab"), axis=0, tiled=True)
-        matrices = place_tiles(
-            target_rows, [student_tiles.reshape(planes * group, per, TILE)], (None,), planes * group, per
-        )
-    student = pieces_of(matrices[:5], matrices[5])
-    teacher = pieces_of(
-        [unpack_matrix(teacher_tiles, piece) for piece in MATRICES],
-        teacher_tiles[TAIL : TAIL + TAIL_TILES].astype(jnp.float32),
-    )
     token_total = jnp.sum(all_facts[:, :, LEN]).astype(jnp.float32)
     masked_total = jnp.sum(all_facts[:, :, LEN + 1]).astype(jnp.float32)
 
@@ -606,6 +600,19 @@
 
     looked_t = looked_up(lambda pick: array_multiply(pick, mentor_lexicon_weights))
     looked_s = looked_up(lambda pick: trailing_array_multiply(pick, table_low))
+    if near:
+        arrivals, places = gather_student(student_low)
+        arrivals, looked_t, looked_s = lax.optimization_barrier((arrivals, looked_t, looked_s))
+        matrices = place_tiles(downward, arrivals, tuple(places), planes * group, per)
+    else:
+        matrices = place_tiles(
+            target_rows, [student_tiles.reshape(planes * group, per, TILE)], (None,), planes * group, per
+        )
+    student = pieces_of(matrices[:5], matrices[5])
+    teacher = pieces_of(
+        [unpack_matrix(teacher_tiles, piece) for piece in MATRICES],
+        teacher_tiles[TAIL : TAIL + TAIL_TILES].astype(jnp.float32),
+    )
     final_s, saved = layer_forward(student, looked_s, lengths)
     final_t = layer_forward(teacher, looked_t, lengths)[0]
 
@@ -670,9 +677,9 @@
         grad_rows = lax.psum_scatter(
             trailing_array_multiply(grad_logit, table_low), "vocab", scatter_dimension=0, tiled=True
         )
-    head_part = lax.psum_scatter(
-        matmul_left(learner_picked, grad_logit), "dp", scatter_dimension=0, tiled=True
-    )
+    head_grad = matmul_left(learner_picked, grad_logit)
+    head_grad, grad_rows = lax.optimization_barrier((head_grad, grad_rows))
+    head_part = lax.psum_scatter(head_grad, "dp", scatter_dimension=0, tiled=True)
     products = jnp.sum(final_s * final_t, axis=1)
     inverse_s = lax.rsqrt(jnp.sum(final_s * final_s, axis=1) + cosine_eps)
     inverse_t = lax.rsqrt(jnp.sum(final_t * final_t, axis=1) + cosine_eps)
@@ -685,6 +692,7 @@
     )
     grad_final = grad_final.at[offsets].add(grad_rows)
     layer_grads, grad_embedded = layer_backward(student, saved, grad_final, lengths)
+    layer_grads, head_part = lax.optimization_barrier((layer_grads, head_part))
 
     shares = grad_embedded.astype(jnp.bfloat16).reshape(LEN, planes, width_share).transpose(1, 0, 2)
     if near:
@@ -699,21 +707,22 @@
         shares = lax.all_to_all(shares, "dp", 0, 0)
         ids = all_facts[:, :, :LEN]
     token_grads = lax.all_gather(shares.reshape(-1, width_share), "vocab", axis=0, tiled=True)
-    token_part = matmul_left(token_grads, chosen(ids))
-    table_grad = (head_part + token_part).T
-
     if near:
         split = per // 16 * 8
-        parts = []
+        sums = []
         for begin, end in ((0, split), (split, per)):
             own_tiles, other_tiles = collect_tiles(upward, layer_grads, tiles_all, per, 2, begin, end - begin)
-            parts.append(reduce_chunk(own_tiles, other_tiles))
-        flat_grad = jnp.concatenate(parts)
+            chip = own_tiles + swap(other_tiles, CORE)
+            chip, upward, token_grads = lax.optimization_barrier((chip, upward, token_grads))
+            sums.append(reduce_chunk(chip))
+        flat_grad = jnp.concatenate(sums)
     else:
         (grad_tiles,) = collect_tiles(target_rows, layer_grads, tiles_all, per, 1, 0, per)
         flat_grad = lax.psum_scatter(
             grad_tiles.reshape(tiles_all, TILE), ("dp", "vocab"), scatter_dimension=0, tiled=True
         )
+    token_part = matmul_left(token_grads, chosen(ids))
+    table_grad = (head_part + token_part).T
     loss_term = (
         mixing_coefficient * smoothing_heat_scale**2 * divergence_part / masked_total
         + cosine_weight * cosine_term / token_total

time: 1040 us -> 1060 us (1.019)
  waiting for transfers between devices: 272 us -> 305 us
    all_gather x1, waiting for transfers between devices: 0.01 us -> 32.4 us  [on_device(): lax.all_gather(student_embed.T.astype(jnp.bfloat16), 'dp', axis=0, tiled=...]
    ppermute x15, waiting for transfers between devices: 81.3 us -> 96.3 us  [shift(): lax.ppermute(value, 'dp', [(i, (i + steps) % size) for i in range(size)])]
    ppermute x79, waiting for transfers between devices: 182 us -> 170 us  [swap(): return lax.ppermute(value, 'vocab', [(i, i ^ bit) for i in range(8)])]
  transfers between devices with their start and end apart: 100 -> 100, of which waited for: 42 -> 46; matrix products, arithmetic and copies ran while one was open for 20% -> 25% of each run, Pallas kernels for 17% -> 12%
where the time goes in v2:
time: 1060 us; the launch traced here: 1050 us
  waiting for transfers between devices  305 us (29%)
  matrix products  234 us (22%)
  Pallas kernels  212 us (20%)
  other arithmetic  105 us (10%)
  starting transfers between devices  79.6 us (8%)
  local copies, waits for them, and re-layouts  76.8 us (7%)
  between operations  40 us (4%)
    ppermute x79, waiting for transfers between devices, swap(): return lax.ppermute(value, 'vocab', [(i, i ^ bit) for i in range(8)])  170 us
    ppermute x15, waiting for transfers between devices, shift(): lax.ppermute(value, 'dp', [(i, (i + steps) % size) for i in range(size)])  96.3 us
    pallas_call x1, Pallas kernels, place_tiles(): pl.pallas_call(functools.partial(place_kernel, places=places, count=count...  88.7 us
    pallas_call x2, Pallas kernels, collect_tiles(): pl.pallas_call(functools.partial(collect_kernel, outs=outs, blocks=blocks...  82.3 us
    dot_general x10, matrix products, array_multiply(): return jnp.dot(left_side, right_side, preferred_element_type=jnp.float32)  82 us
    dot_general x6, matrix products, matmul_left(): lax.dot_general(left_side, right_side, (((0,), (0,)), ((), ())), preferre...  63.5 us
    ppermute x79, starting transfers between devices, swap(): return lax.ppermute(value, 'vocab', [(i, i ^ bit) for i in range(8)])  60.9 us
    dot_general x9, matrix products, trailing_array_multiply(): lax.dot_general(left_side, right_side, (((1,), (1,)), ((), ())), preferre...  45.4 us
  transfers between devices with their start and end apart: 100, of which 46 were waited for; matrix products, arithmetic and copies ran while one was open for 25% of the time, Pallas kernels for 12%

profile of v2, /device:TPU:0, one launch (start us, length us, event | category | flops | bytes accessed | tf_op | source)
XLA Modules:
  0.0 1053.2 jit_solution(3441362242975654709)
XLA Ops:
  20.9 5.4 rev.32
  32.1 8.5 fusion.53
  40.8 32.4 %all-gather.4.cloned.1.call-done = bf16[768,1920]{1,0:T(8,128)(2,1)} async-done(((bf16[192,1920]{1,0:T(8,128)(2,1)}), bf16[768,1920]{1,0:T(8,128)(2,1)}) %all-gather.4.cloned.1.call-update) | async-done | bytes 2949136 | tf_op jit(solution)/shard_map/all_gather | solution.py:568
  73.2 10.3 fusion.54
  83.5 7.7 fusion.51
  120.9 15.8 %collective-permute-done.9.refs_10_ = bf16[1832,128]{1,0:T(8,128)(2,1)S(1)} collective-permute-done((bf16[1832,128]{1,0:T(8,128)(2,1)}, bf16[1832,128]{1,0:T(8,128)(2,1)S(1)}, u32[]{:S(2)}, u32[]{:S(2)}) %collective-permute-start.9) | collective-permute-done | bytes 469024 | tf_op jit(solution)/shard_map/ppermute | solution.py:51
  145.5 7.7 collective-permute-done.19.refs_20_
  155.4 7.4 fusion.52
  167.8 11.8 %collective-permute-done.29.refs_30_ = bf16[1832,128]{1,0:T(8,128)(2,1)S(1)} collective-permute-done((bf16[1832,128]{1,0:T(8,128)(2,1)S(1)}, bf16[1832,128]{1,0:T(8,128)(2,1)S(1)}, u32[]{:S(2)}, u32[]{:S(2)}) %collective-permute-start.29) | collective-permute-done | bytes 469024 | tf_op jit(solution)/shard_map/ppermute | solution.py:51
  186.9 9.8 collective-permute-done.21.refs_22_
  198.7 8.0 collective-permute-done.31.refs_32_
  221.2 17.4 %collective-permute-done.15.refs_16_ = bf16[912,128]{1,0:T(8,128)(2,1)S(1)} collective-permute-done((bf16[912,128]{1,0:T(8,128)(2,1)S(1)}, bf16[912,128]{1,0:T(8,128)(2,1)S(1)}, u32[]{:S(2)}, u32[]{:S(2)}) %collective-permute-start.15) | collective-permute-done | bytes 233504 | tf_op jit(solution)/shard_map/ppermute | solution.py:46
  257.6 6.5 collective-permute-done.51
  271.8 88.7 %place_tiles.1 = (bf16[768,2304]{1,0:T(8,128)(2,1)}, bf16[768,768]{1,0:T(8,128)(2,1)}, bf16[768,3072]{1,0:T(8,128)(2,1)}, bf16[3072,768]{1,0:T(8,128)(2,1)}, bf1...) custom-call(s32[58624]{0:T(1024)} %reshape.747.rows, bf16[1832,128]{1,0:T(8,128)(2,1)} %convert_element_type.259.refs_0_, ...), custom_call_target="tpu_custom_call" | custom-call | bytes 180000000 | tf_op jit(solution)/shard_map/place_tiles/pallas_call | solution.py:204
  373.6 8.7 unpack_matrix.6
  382.3 6.4 fusion.50
  393.0 10.9 %fusion.246 = (f32[12,512]{1,0:T(8,128)S(1)}, f32[12,512,512]{1,2,0:T(8,128)}) fusion(pred[512]{0:T(512)(128)(4,1)S(1)} %copy-done.143, bf16[1,512,3,12,64]{1,4,3,2,0:T(8,128)(2,1)} %bitcast.449), kind=kOutput, calls=%fused_computation.547 | convolution fusion | flops 415236608 | bytes 14180864 | tf_op jit(solution)/shard_map/sub | solution.py:360
  403.9 6.9 fusion.70
  420.2 15.0 %unpack_matrix.9 = bf16[3072,768]{1,0:T(8,128)(2,1)} custom-call(bf16[58624,128]{1,0:T(8,128)(2,1)} %all-gather.6.cloned.1.call-done.source), custom_call_target="tpu_custom_call" | custom-call | tf_op jit(solution)/shard_map/unpack_matrix/pallas_call | solution.py:121
  435.2 9.8 unpack_matrix.8
  445.0 23.2 %fusion.248 = (f32[512]{0:T(512)S(1)}, f32[512,768]{1,0:T(8,128)}) fusion(f32[768]{0:T(1024)S(1)} %get-tuple-element.223, bf16[3072,768]{1,0:T(8,128)(2,1)} %unpack_matrix.9, bf16[768,3072]{1,0:T(8,128)(2,1)} %unpack_matrix.8, f32[3072]{0:T(1024)S(1)} %slice_bitcast_fusion.59, f32[512,768]{1,0:T(8,128)} %copy-done.39, f32[768]{0:T(1024)S(1)} %get-tuple-element.224, ...), kind=kOutput, calls=%fused_computation.549 | convolution fusion | flops 4940365312 | bytes 12610560 | tf_op jit(solution)/shard_map/dot_general | solution.py:282
  469.9 6.1 fusion.49
  494.5 19.6 %fusion.17 = (bf16[512,3072]{1,0:T(8,128)(2,1)S(1)}, f32[512,3072]{1,0:T(8,128)}) fusion(f32[3072]{0:T(1024)S(1)} %copy-done.123, bf16[768,3072]{1,0:T(8,128)(2,1)} %get-tuple-element.119, f32[512,768]{1,0:T(8,128)S(1)} %get-tuple-element.277, f32[768]{0:T(1024)S(1)} %copy-done.133, f32[768]{0:T(1024)S(1)} %copy-done.114, f32[512]{0:T(512)S(1)} %add_rsqrt_fusion.6, ...), kind=kOutput, calls=%fused_computation.41 | convolution fusion | flops 2521694208 | bytes 15751168 | tf_op jit(solution)/shard_map/dot_general | solution.py:282
  524.2 6.2 collective-permute-done.58
  536.2 5.9 collective-permute-done.59
  581.6 7.2 multiply_convert_fusion.1
  629.4 8.5 convert_reduce_fusion
  637.9 7.3 multiply_reduce_fusion.5
  650.9 12.3 %multiply_reduce_fusion = (f32[12,512]{1,0:T(8,128)S(1)}, f32[12,512,512]{1,2,0:T(8,128)}) fusion(f32[12,512,512]{1,2,0:T(8,128)} %copy-done.1, f32[12,512]{1,0:T(8,128)S(1)} %log_add_fusion, bf16[512,12,64]{0,2,1:T(8,128)(2,1)} %bitcast.433, bf16[1,512,3,12,64]{1,4,3,2,0:T(8,128)(2,1)} %bitcast.422), kind=kOutput, calls=%fused_computation.14 | convolution fusion | flops 412084224 | bytes 26787840 | tf_op jit(solution)/shard_map/sqhd,skhd->shqk/dot_general | solution.py:422
  663.2 7.2 multiply_convert_fusion
  690.1 11.3 %collective-permute-done.75 = bf16[512,192]{0,1:T(8,128)(2,1)S(1)} collective-permute-done((bf16[512,192]{0,1:T(8,128)(2,1)S(1)}, bf16[512,192]{0,1:T(8,128)(2,1)S(1)}, u32[]{:S(2)}, u32[]{:S(2)}) %collective-permute-start.75) | collective-permute-done | bytes 196640 | tf_op jit(solution)/shard_map/ppermute | solution.py:51
  701.4 28.3 %collective-permute-done.74 = bf16[512,192]{0,1:T(8,128)(2,1)S(1)} collective-permute-done((bf16[512,192]{0,1:T(8,128)(2,1)S(1)}, bf16[512,192]{0,1:T(8,128)(2,1)S(1)}, u32[]{:S(2)}, u32[]{:S(2)}) %collective-permute-start.74) | collective-permute-done | bytes 196640 | tf_op jit(solution)/shard_map/ppermute | solution.py:51
  744.4 5.4 fusion.187.refs_3_
  749.8 5.5 fusion.224.refs_2_
  755.3 41.8 %collect_tiles.2 = (f32[16,912,128]{2,1,0:T(8,128)}, f32[16,912,128]{2,1,0:T(8,128)}) custom-call(s32[58624]{0:T(1024)} %reshape.741.rows, f32[768,2304]{1,0:T(8,128)} %fusion.228.refs_0_, f32[768,768]{1,0:T(8,128)} %fusion.184.refs_1_, f32[768,3072]{1,0:T(8,128)} %fusion.224.refs_2_, f32[3072,768]{1,0:T(8,128)} %fusion.187.refs_3_, ...), custom_call_target="tpu_custom_call" | custom-call | bytes 80000000 | tf_op jit(solution)/shard_map/collect_tiles/pallas_call | solution.py:268
  797.2 12.0 %collective-permute-done.72 = f32[16,912,128]{2,1,0:T(8,128)S(1)} collective-permute-done((f32[16,912,128]{2,1,0:T(8,128)}, f32[16,912,128]{2,1,0:T(8,128)S(1)}, u32[]{:S(2)}, u32[]{:S(2)}) %collective-permute-start.72) | collective-permute-done | bytes 7471136 | tf_op jit(solution)/shard_map/ppermute | solution.py:46
  809.3 7.1 add.733
  816.4 40.5 %collect_tiles.3 = (f32[16,920,128]{2,1,0:T(8,128)}, f32[16,920,128]{2,1,0:T(8,128)}) custom-call(s32[58624]{0:T(1024)} %reshape.741.rows, f32[768,2304]{1,0:T(8,128)} %fusion.228.refs_0_, f32[768,768]{1,0:T(8,128)} %fusion.184.refs_1_, f32[768,3072]{1,0:T(8,128)} %fusion.224.refs_2_, f32[3072,768]{1,0:T(8,128)} %fusion.187.refs_3_, ...), custom_call_target="tpu_custom_call" | custom-call | bytes 80000000 | tf_op jit(solution)/shard_map/collect_tiles/pallas_call | solution.py:268
  857.1 5.6 fusion.238
  865.0 20.8 %collective-permute-done.78 = bf16[2,2,912,128]{3,2,0,1:T(8,128)(2,1)S(1)} collective-permute-done((bf16[2,2,912,128]{3,2,0,1:T(8,128)(2,1)S(1)}, bf16[2,2,912,128]{3,2,0,1:T(8,128)(2,1)S(1)}, u32[]{:S(2)}, u32[]{:S(2)}) %collective-permute-start.78) | collective-permute-done | bytes 933920 | tf_op jit(solution)/shard_map/ppermute | solution.py:46
  894.7 6.4 collective-permute-done.79
  903.3 6.2 add.752
  911.6 8.1 collective-permute-done.76
  925.3 8.8 collective-permute-done.86
  943.6 11.5 %collective-permute-done.87 = bf16[2,920,128]{2,1,0:T(8,128)(2,1)S(1)} collective-permute-done((bf16[2,920,128]{2,1,0:T(8,128)(2,1)S(1)}, bf16[2,920,128]{2,1,0:T(8,128)(2,1)S(1)}, u32[]{:S(2)}, u32[]{:S(2)}) %collective-permute-start.87) | collective-permute-done | bytes 471072 | tf_op jit(solution)/shard_map/ppermute | solution.py:46
  959.5 7.7 collective-permute-done.88
  969.0 9.3 collective-permute-done.89
  979.4 38.3 %multiply_reduce_fusion.19 = (f32[]{:T(128)}, f32[192,1920]{1,0:T(8,128)}) fusion(f32[192,1920]{1,0:T(8,128)S(1)} %copy-done.148, bf16[16384,192]{0,1:T(8,128)(2,1)S(1)} %bitcast.498, s32[16384]{0:T(1024)S(1)} %bitcast.477), kind=kOutput, calls=%fused_computation.163 | convolution fusion | flops 12112158720 | bytes 9306116 | tf_op jit(solution)/shard_map/dot_general | solution.py:286
  (750 shorter events, 340.0 us)
Async XLA Ops:
  7.2 66.0 %all-gather.4.cloned.1.call-start = ((), (), s32[]{:S(2)}) async-start(), calls=%async_computation.1 | async-start | bytes 3686400 | tf_op jit(solution)/shard_map/all_gather | solution.py:568
  9.7 355.4 %all-gather.6.cloned.1.call-start = ((), (), s32[]{:S(2)}) async-start(), calls=%async_computation.2 | async-start | bytes 15476736 | tf_op jit(solution)/shard_map/all_gather | solution.py:569
  10.5 744.8 %reduce-scatter.2.cloned.1.call-start = ((), (), s32[]{:S(2)}) async-start(), calls=%async_computation.3 | async-start | bytes 7372800 | tf_op jit(solution)/shard_map/reduce_scatter | solution.py:682
  12.5 103.6 %collective-permute-start.1 = (bf16[1832,128]{1,0:T(8,128)(2,1)}, bf16[1832,128]{1,0:T(8,128)(2,1)}, u32[]{:S(2)}, u32[]{:S(2)}) collective-permute-start(bf16[1832,128]{1,0:T(8,128)(2,1)} %convert_element_type.259.refs_0_), channel_id=1, source_target_pairs={{0,2},{1,3},{2,0},{3,1},{4,6},{5,7},{6,4},{7,5},{8,10},{9,11},{10,... | collective-permute-start | bytes 1406984 | tf_op jit(solution)/shard_map/ppermute | solution.py:46
  15.5 102.4 %collective-permute-start.3 = (bf16[1832,128]{1,0:T(8,128)(2,1)}, bf16[1832,128]{1,0:T(8,128)(2,1)}, u32[]{:S(2)}, u32[]{:S(2)}) collective-permute-start(bf16[1832,128]{1,0:T(8,128)(2,1)} %convert_element_type.259.refs_0_), channel_id=1, source_target_pairs={{0,4},{1,5},{2,6},{3,7},{4,0},{5,1},{6,2},{7,3},{8,12},{9,13},{10,... | collective-permute-start | bytes 1406984 | tf_op jit(solution)/shard_map/ppermute | solution.py:46
  40.6 50.6 %collective-permute-start.42 = (bf16[2,2,512,768]{3,2,1,0:T(8,128)(2,1)}, bf16[2,2,512,768]{3,2,1,0:T(8,128)(2,1)}, u32[]{:S(2)}, u32[]{:S(2)}) collective-permute-start(bf16[2,2,512,768]{3,2,1,0:T(8,128)(2,1)} %bitcast.11), channel_id=1, source_target_pairs={{0,1},{1,0},{2,3},{3,2},{4,5},{5,4},{6,7},{7,6},{8,9},{9,8},{10,11... | collective-permute-start | bytes 9437192 | tf_op jit(solution)/shard_map/ppermute | solution.py:46
  83.5 71.8 %collective-permute-start.47 = (bf16[2,2,512,768]{3,2,1,0:T(8,128)(2,1)}, bf16[2,2,512,768]{3,2,1,0:T(8,128)(2,1)}, u32[]{:S(2)}, u32[]{:S(2)}) collective-permute-start(bf16[2,2,512,768]{3,2,1,0:T(8,128)(2,1)} %bitcast.22), channel_id=1, source_target_pairs={{0,1},{1,0},{2,3},{3,2},{4,5},{5,4},{6,7},{7,6},{8,9},{9,8},{10,11... | collective-permute-start | bytes 9437192 | tf_op jit(solution)/shard_map/ppermute | solution.py:46
  96.9 39.9 %collective-permute-start.43 = (bf16[2,256,768]{2,1,0:T(8,128)(2,1)}, bf16[2,256,768]{2,1,0:T(8,128)(2,1)}, u32[]{:S(2)}, u32[]{:S(2)}) collective-permute-start(bf16[2,256,768]{2,1,0:T(8,128)(2,1)} %slice_bitcast_fusion.17), channel_id=1, source_target_pairs={{0,2},{1,3},{2,0},{3,1},{4,6},{5,7},{6,4},{7,5},{8,10},{9,11},{10,... | collective-permute-start | bytes 2359304 | tf_op jit(solution)/shard_map/ppermute | solution.py:46
  98.4 38.5 %collective-permute-start.45 = (bf16[2,256,768]{2,1,0:T(8,128)(2,1)}, bf16[2,256,768]{2,1,0:T(8,128)(2,1)}, u32[]{:S(2)}, u32[]{:S(2)}) collective-permute-start(bf16[2,256,768]{2,1,0:T(8,128)(2,1)} %slice_bitcast_fusion.15), channel_id=1, source_target_pairs={{0,4},{1,5},{2,6},{3,7},{4,0},{5,1},{6,2},{7,3},{8,12},{9,13},{10,... | collective-permute-start | bytes 2359304 | tf_op jit(solution)/shard_map/ppermute | solution.py:46
  116.1 20.5 %collective-permute-start.9 = (bf16[1832,128]{1,0:T(8,128)(2,1)}, bf16[1832,128]{1,0:T(8,128)(2,1)S(1)}, u32[]{:S(2)}, u32[]{:S(2)}) collective-permute-start(bf16[1832,128]{1,0:T(8,128)(2,1)} %convert_element_type.259.refs_0_), channel_id=1, source_target_pairs={{0,8},{8,16},{16,24},{24,0},{1,9},{9,17},{17,25},{25,1},{2,10},{10... | collective-permute-start | bytes 1406984 | tf_op jit(solution)/shard_map/ppermute | solution.py:51
  117.9 18.8 %collective-permute-start.5 = (bf16[912,128]{1,0:T(8,128)(2,1)S(1)}, bf16[912,128]{1,0:T(8,128)(2,1)S(1)}, u32[]{:S(2)}, u32[]{:S(2)}) collective-permute-start(bf16[912,128]{1,0:T(8,128)(2,1)S(1)} %slice.677), channel_id=1, source_target_pairs={{0,4},{1,5},{2,6},{3,7},{4,0},{5,1},{6,2},{7,3},{8,12},{9,13},{10,... | collective-permute-start | bytes 700424 | tf_op jit(solution)/shard_map/ppermute | solution.py:46
  136.8 16.4 %collective-permute-start.19 = (bf16[1832,128]{1,0:T(8,128)(2,1)S(1)}, bf16[1832,128]{1,0:T(8,128)(2,1)S(1)}, u32[]{:S(2)}, u32[]{:S(2)}) collective-permute-start(bf16[1832,128]{1,0:T(8,128)(2,1)S(1)} %collective-permute-done.9.refs_10_), channel_id=1, source_target_pairs={{0,8},{8,16},{16,24},{24,0},{1,9},{9,17},{17,25},{25,1},{2,10},{10... | collective-permute-start | bytes 1406984 | tf_op jit(solution)/shard_map/ppermute | solution.py:51
  141.0 24.5 %collective-permute-start.2 = (bf16[1832,128]{1,0:T(8,128)(2,1)}, bf16[1832,128]{1,0:T(8,128)(2,1)S(1)}, u32[]{:S(2)}, u32[]{:S(2)}) collective-permute-start(bf16[1832,128]{1,0:T(8,128)(2,1)} %collective-permute-done.1.refs_2_), channel_id=1, source_target_pairs={{0,1},{1,0},{2,3},{3,2},{4,5},{5,4},{6,7},{7,6},{8,9},{9,8},{10,11... | collective-permute-start | bytes 1406984 | tf_op jit(solution)/shard_map/ppermute | solution.py:46
  145.0 20.7 %collective-permute-start.4 = (bf16[1832,128]{1,0:T(8,128)(2,1)}, bf16[1832,128]{1,0:T(8,128)(2,1)S(1)}, u32[]{:S(2)}, u32[]{:S(2)}) collective-permute-start(bf16[1832,128]{1,0:T(8,128)(2,1)} %collective-permute-done.3.refs_4_), channel_id=1, source_target_pairs={{0,1},{1,0},{2,3},{3,2},{4,5},{5,4},{6,7},{7,6},{8,9},{9,8},{10,11... | collective-permute-start | bytes 1406984 | tf_op jit(solution)/shard_map/ppermute | solution.py:46
  145.0 20.8 %collective-permute-start.10 = (bf16[1832,128]{1,0:T(8,128)(2,1)S(1)}, bf16[1832,128]{1,0:T(8,128)(2,1)S(1)}, u32[]{:S(2)}, u32[]{:S(2)}) collective-permute-start(bf16[1832,128]{1,0:T(8,128)(2,1)S(1)} %collective-permute-done.9.refs_10_), channel_id=1, source_target_pairs={{0,1},{1,0},{2,3},{3,2},{4,5},{5,4},{6,7},{7,6},{8,9},{9,8},{10,11... | collective-permute-start | bytes 1406984 | tf_op jit(solution)/shard_map/ppermute | solution.py:46
  153.2 27.7 %collective-permute-start.11 = (bf16[1832,128]{1,0:T(8,128)(2,1)S(1)}, bf16[1832,128]{1,0:T(8,128)(2,1)S(1)}, u32[]{:S(2)}, u32[]{:S(2)}) collective-permute-start(bf16[1832,128]{1,0:T(8,128)(2,1)S(1)} %collective-permute-done.9.refs_10_), channel_id=1, source_target_pairs={{0,2},{1,3},{2,0},{3,1},{4,6},{5,7},{6,4},{7,5},{8,10},{9,11},{10,... | collective-permute-start | bytes 1406984 | tf_op jit(solution)/shard_map/ppermute | solution.py:46
  155.4 24.3 %collective-permute-start.29 = (bf16[1832,128]{1,0:T(8,128)(2,1)S(1)}, bf16[1832,128]{1,0:T(8,128)(2,1)S(1)}, u32[]{:S(2)}, u32[]{:S(2)}) collective-permute-start(bf16[1832,128]{1,0:T(8,128)(2,1)S(1)} %collective-permute-done.19.refs_20_), channel_id=1, source_target_pairs={{0,8},{8,16},{16,24},{24,0},{1,9},{9,17},{17,25},{25,1},{2,10},{10... | collective-permute-start | bytes 1406984 | tf_op jit(solution)/shard_map/ppermute | solution.py:51
  165.6 21.2 %collective-permute-start.13 = (bf16[1832,128]{1,0:T(8,128)(2,1)S(1)}, bf16[1832,128]{1,0:T(8,128)(2,1)S(1)}, u32[]{:S(2)}, u32[]{:S(2)}) collective-permute-start(bf16[1832,128]{1,0:T(8,128)(2,1)S(1)} %collective-permute-done.9.refs_10_), channel_id=1, source_target_pairs={{0,4},{1,5},{2,6},{3,7},{4,0},{5,1},{6,2},{7,3},{8,12},{9,13},{10,... | collective-permute-start | bytes 1406984 | tf_op jit(solution)/shard_map/ppermute | solution.py:46
  165.7 31.0 %collective-permute-start.21 = (bf16[1832,128]{1,0:T(8,128)(2,1)S(1)}, bf16[1832,128]{1,0:T(8,128)(2,1)S(1)}, u32[]{:S(2)}, u32[]{:S(2)}) collective-permute-start(bf16[1832,128]{1,0:T(8,128)(2,1)S(1)} %collective-permute-done.19.refs_20_), channel_id=1, source_target_pairs={{0,2},{1,3},{2,0},{3,1},{4,6},{5,7},{6,4},{7,5},{8,10},{9,11},{10,... | collective-permute-start | bytes 1406984 | tf_op jit(solution)/shard_map/ppermute | solution.py:46
  165.8 31.5 %collective-permute-start.23 = (bf16[1832,128]{1,0:T(8,128)(2,1)S(1)}, bf16[1832,128]{1,0:T(8,128)(2,1)S(1)}, u32[]{:S(2)}, u32[]{:S(2)}) collective-permute-start(bf16[1832,128]{1,0:T(8,128)(2,1)S(1)} %collective-permute-done.19.refs_20_), channel_id=1, source_target_pairs={{0,4},{1,5},{2,6},{3,7},{4,0},{5,1},{6,2},{7,3},{8,12},{9,13},{10,... | collective-permute-start | bytes 1406984 | tf_op jit(solution)/shard_map/ppermute | solution.py:46
  179.7 27.1 %collective-permute-start.31 = (bf16[1832,128]{1,0:T(8,128)(2,1)S(1)}, bf16[1832,128]{1,0:T(8,128)(2,1)S(1)}, u32[]{:S(2)}, u32[]{:S(2)}) collective-permute-start(bf16[1832,128]{1,0:T(8,128)(2,1)S(1)} %collective-permute-done.29.refs_30_), channel_id=1, source_target_pairs={{0,2},{1,3},{2,0},{3,1},{4,6},{5,7},{6,4},{7,5},{8,10},{9,11},{10,... | collective-permute-start | bytes 1406984 | tf_op jit(solution)/shard_map/ppermute | solution.py:46
  180.9 27.6 %collective-permute-start.33 = (bf16[1832,128]{1,0:T(8,128)(2,1)S(1)}, bf16[1832,128]{1,0:T(8,128)(2,1)S(1)}, u32[]{:S(2)}, u32[]{:S(2)}) collective-permute-start(bf16[1832,128]{1,0:T(8,128)(2,1)S(1)} %collective-permute-done.29.refs_30_), channel_id=1, source_target_pairs={{0,4},{1,5},{2,6},{3,7},{4,0},{5,1},{6,2},{7,3},{8,12},{9,13},{10,... | collective-permute-start | bytes 1406984 | tf_op jit(solution)/shard_map/ppermute | solution.py:46
  186.8 31.5 %collective-permute-start.8 = (bf16[920,128]{1,0:T(8,128)(2,1)}, bf16[920,128]{1,0:T(8,128)(2,1)}, u32[]{:S(2)}, u32[]{:S(2)}) collective-permute-start(bf16[920,128]{1,0:T(8,128)(2,1)} %collective-permute-done.7.refs_8_), channel_id=1, source_target_pairs={{0,1},{1,0},{2,3},{3,2},{4,5},{5,4},{6,7},{7,6},{8,9},{9,8},{10,11... | collective-permute-start | bytes 706568 | tf_op jit(solution)/shard_map/ppermute | solution.py:46
  196.7 22.5 %collective-permute-start.46 = (bf16[256,768]{1,0:T(8,128)(2,1)}, bf16[256,768]{1,0:T(8,128)(2,1)}, u32[]{:S(2)}, u32[]{:S(2)}) collective-permute-start(bf16[256,768]{1,0:T(8,128)(2,1)} %slice_bitcast_fusion.51), channel_id=1, source_target_pairs={{0,2},{1,3},{2,0},{3,1},{4,6},{5,7},{6,4},{7,5},{8,10},{9,11},{10,... | collective-permute-start | bytes 1179656 | tf_op jit(solution)/shard_map/ppermute | solution.py:46
  197.3 43.0 %collective-permute-start.48 = (bf16[2,256,768]{2,1,0:T(8,128)(2,1)}, bf16[2,256,768]{2,1,0:T(8,128)(2,1)}, u32[]{:S(2)}, u32[]{:S(2)}) collective-permute-start(bf16[2,256,768]{2,1,0:T(8,128)(2,1)} %slice_bitcast_fusion.13), channel_id=1, source_target_pairs={{0,2},{1,3},{2,0},{3,1},{4,6},{5,7},{6,4},{7,5},{8,10},{9,11},{10,... | collective-permute-start | bytes 2359304 | tf_op jit(solution)/shard_map/ppermute | solution.py:46
  206.7 34.0 %collective-permute-start.50 = (bf16[2,256,768]{2,1,0:T(8,128)(2,1)}, bf16[2,256,768]{2,1,0:T(8,128)(2,1)}, u32[]{:S(2)}, u32[]{:S(2)}) collective-permute-start(bf16[2,256,768]{2,1,0:T(8,128)(2,1)} %slice_bitcast_fusion.11), channel_id=1, source_target_pairs={{0,4},{1,5},{2,6},{3,7},{4,0},{5,1},{6,2},{7,3},{8,12},{9,13},{10,... | collective-permute-start | bytes 2359304 | tf_op jit(solution)/shard_map/ppermute | solution.py:46
  209.4 29.7 %collective-permute-start.44 = (bf16[256,768]{1,0:T(8,128)(2,1)}, bf16[256,768]{1,0:T(8,128)(2,1)}, u32[]{:S(2)}, u32[]{:S(2)}) collective-permute-start(bf16[256,768]{1,0:T(8,128)(2,1)} %slice_bitcast_fusion.53), channel_id=1, source_target_pairs={{0,4},{1,5},{2,6},{3,7},{4,0},{5,1},{6,2},{7,3},{8,12},{9,13},{10,... | collective-permute-start | bytes 1179656 | tf_op jit(solution)/shard_map/ppermute | solution.py:46
  218.4 20.2 %collective-permute-start.15 = (bf16[912,128]{1,0:T(8,128)(2,1)S(1)}, bf16[912,128]{1,0:T(8,128)(2,1)S(1)}, u32[]{:S(2)}, u32[]{:S(2)}) collective-permute-start(bf16[912,128]{1,0:T(8,128)(2,1)S(1)} %slice.679), channel_id=1, source_target_pairs={{0,4},{1,5},{2,6},{3,7},{4,0},{5,1},{6,2},{7,3},{8,12},{9,13},{10,... | collective-permute-start | bytes 700424 | tf_op jit(solution)/shard_map/ppermute | solution.py:46
  219.2 19.4 %collective-permute-start.17 = (bf16[920,128]{1,0:T(8,128)(2,1)S(1)}, bf16[920,128]{1,0:T(8,128)(2,1)S(1)}, u32[]{:S(2)}, u32[]{:S(2)}) collective-permute-start(bf16[920,128]{1,0:T(8,128)(2,1)S(1)} %slice.680), channel_id=1, source_target_pairs={{0,2},{1,3},{2,0},{3,1},{4,6},{5,7},{6,4},{7,5},{8,10},{9,11},{10,... | collective-permute-start | bytes 706568 | tf_op jit(solution)/shard_map/ppermute | solution.py:46
  252.5 16.2 %collective-permute-start.49 = (bf16[256,768]{1,0:T(8,128)(2,1)S(1)}, bf16[256,768]{1,0:T(8,128)(2,1)S(1)}, u32[]{:S(2)}, u32[]{:S(2)}) collective-permute-start(bf16[256,768]{1,0:T(8,128)(2,1)S(1)} %slice_bitcast_fusion.49), channel_id=1, source_target_pairs={{0,4},{1,5},{2,6},{3,7},{4,0},{5,1},{6,2},{7,3},{8,12},{9,13},{10,... | collective-permute-start | bytes 1179656 | tf_op jit(solution)/shard_map/ppermute | solution.py:46
  543.2 14.9 %collective-permute-start.60 = (bf16[4,128,768]{2,1,0:T(8,128)(2,1)S(1)}, bf16[4,128,768]{2,1,0:T(8,128)(2,1)S(1)}, u32[]{:S(2)}, u32[]{:S(2)}) collective-permute-start(bf16[4,128,768]{2,1,0:T(8,128)(2,1)S(1)} %pad_maximum_fusion.3), channel_id=1, source_target_pairs={{0,1},{1,0},{2,3},{3,2},{4,5},{5,4},{6,7},{7,6},{8,9},{9,8},{10,11... | collective-permute-start | bytes 2359304 | tf_op jit(solution)/shard_map/ppermute | solution.py:46
  543.4 14.6 %collective-permute-start.62 = (bf16[2,128,768]{2,1,0:T(8,128)(2,1)S(1)}, bf16[2,128,768]{2,1,0:T(8,128)(2,1)S(1)}, u32[]{:S(2)}, u32[]{:S(2)}) collective-permute-start(bf16[2,128,768]{2,1,0:T(8,128)(2,1)S(1)} %pad_maximum_fusion.6), channel_id=1, source_target_pairs={{0,4},{1,5},{2,6},{3,7},{4,0},{5,1},{6,2},{7,3},{8,12},{9,13},{10,... | collective-permute-start | bytes 1179656 | tf_op jit(solution)/shard_map/ppermute | solution.py:46
  557.6 17.0 %collective-permute-start.56 = (s32[2,3,640]{2,1,0:T(4,128)S(1)}, s32[2,3,640]{2,1,0:T(4,128)S(1)}, u32[]{:S(2)}, u32[]{:S(2)}) collective-permute-start(s32[2,3,640]{2,1,0:T(4,128)S(1)} %pad_add_fusion.7), channel_id=1, source_target_pairs={{0,4},{1,5},{2,6},{3,7},{4,0},{5,1},{6,2},{7,3},{8,12},{9,13},{10,... | collective-permute-start | bytes 46088 | tf_op jit(solution)/shard_map/ppermute | solution.py:46
  616.9 199.5 %all-gather.8.cloned.1.call-start = ((), (), s32[]{:S(2)}) async-start(), calls=%async_computation.4 | async-start | bytes 7077888 | tf_op jit(solution)/shard_map/all_gather | solution.py:709
  687.1 14.3 %collective-permute-start.75 = (bf16[512,192]{0,1:T(8,128)(2,1)S(1)}, bf16[512,192]{0,1:T(8,128)(2,1)S(1)}, u32[]{:S(2)}, u32[]{:S(2)}) collective-permute-start(bf16[512,192]{0,1:T(8,128)(2,1)S(1)} %get-tuple-element.199), channel_id=1, source_target_pairs={{0,24},{8,0},{16,8},{24,16},{1,25},{9,1},{17,9},{25,17},{2,26},{10... | collective-permute-start | bytes 589832 | tf_op jit(solution)/shard_map/ppermute | solution.py:51
  687.4 42.3 %collective-permute-start.74 = (bf16[512,192]{0,1:T(8,128)(2,1)S(1)}, bf16[512,192]{0,1:T(8,128)(2,1)S(1)}, u32[]{:S(2)}, u32[]{:S(2)}) collective-permute-start(bf16[512,192]{0,1:T(8,128)(2,1)S(1)} %get-tuple-element.200), channel_id=1, source_target_pairs={{0,16},{8,24},{16,0},{24,8},{1,17},{9,25},{17,1},{25,9},{2,18},{10... | collective-permute-start | bytes 589832 | tf_op jit(solution)/shard_map/ppermute | solution.py:51
  688.2 41.6 %collective-permute-start.73 = (bf16[512,192]{0,1:T(8,128)(2,1)S(1)}, bf16[512,192]{0,1:T(8,128)(2,1)S(1)}, u32[]{:S(2)}, u32[]{:S(2)}) collective-permute-start(bf16[512,192]{0,1:T(8,128)(2,1)S(1)} %get-tuple-element.201), channel_id=1, source_target_pairs={{0,8},{8,16},{16,24},{24,0},{1,9},{9,17},{17,25},{25,1},{2,10},{10... | collective-permute-start | bytes 589832 | tf_op jit(solution)/shard_map/ppermute | solution.py:51
  856.9 46.5 %collective-permute-start.83 = (f32[16,920,128]{2,1,0:T(8,128)}, f32[16,920,128]{2,1,0:T(8,128)}, u32[]{:S(2)}, u32[]{:S(2)}) collective-permute-start(f32[16,920,128]{2,1,0:T(8,128)} %get-tuple-element.135), channel_id=1, source_target_pairs={{0,1},{1,0},{2,3},{3,2},{4,5},{5,4},{6,7},{7,6},{8,9},{9,8},{10,11... | collective-permute-start | bytes 22609928 | tf_op jit(solution)/shard_map/ppermute | solution.py:46
  862.8 23.0 %collective-permute-start.78 = (bf16[2,2,912,128]{3,2,0,1:T(8,128)(2,1)S(1)}, bf16[2,2,912,128]{3,2,0,1:T(8,128)(2,1)S(1)}, u32[]{:S(2)}, u32[]{:S(2)}) collective-permute-start(bf16[2,2,912,128]{3,2,0,1:T(8,128)(2,1)S(1)} %fusion.86), channel_id=1, source_target_pairs={{0,2},{1,3},{2,0},{3,1},{4,6},{5,7},{6,4},{7,5},{8,10},{9,11},{10,... | collective-permute-start | bytes 2801672 | tf_op jit(solution)/shard_map/ppermute | solution.py:46
  894.3 25.4 %collective-permute-start.76 = (bf16[2,2,912,128]{3,2,0,1:T(8,128)(2,1)}, bf16[2,2,912,128]{3,2,0,1:T(8,128)(2,1)}, u32[]{:S(2)}, u32[]{:S(2)}) collective-permute-start(bf16[2,2,912,128]{3,2,0,1:T(8,128)(2,1)} %fusion.85), channel_id=1, source_target_pairs={{0,4},{1,5},{2,6},{3,7},{4,0},{5,1},{6,2},{7,3},{8,12},{9,13},{10,... | collective-permute-start | bytes 2801672 | tf_op jit(solution)/shard_map/ppermute | solution.py:46
  903.3 19.2 %collective-permute-start.80 = (f32[912,128]{1,0:T(8,128)}, f32[912,128]{1,0:T(8,128)}, u32[]{:S(2)}, u32[]{:S(2)}) collective-permute-start(f32[912,128]{1,0:T(8,128)} %slice_bitcast_fusion.39), channel_id=1, source_target_pairs={{0,8},{8,16},{16,24},{24,0},{1,9},{9,17},{17,25},{25,1},{2,10},{10... | collective-permute-start | bytes 1400840 | tf_op jit(solution)/shard_map/ppermute | solution.py:51
  910.2 23.9 %collective-permute-start.86 = (bf16[2,2,920,128]{3,2,0,1:T(8,128)(2,1)S(1)}, bf16[2,2,920,128]{3,2,0,1:T(8,128)(2,1)S(1)}, u32[]{:S(2)}, u32[]{:S(2)}) collective-permute-start(bf16[2,2,920,128]{3,2,0,1:T(8,128)(2,1)S(1)} %fusion.81), channel_id=1, source_target_pairs={{0,2},{1,3},{2,0},{3,1},{4,6},{5,7},{6,4},{7,5},{8,10},{9,11},{10,... | collective-permute-start | bytes 2826248 | tf_op jit(solution)/shard_map/ppermute | solution.py:46
  921.1 19.1 %collective-permute-start.77 = (bf16[2,912,128]{2,1,0:T(8,128)(2,1)S(1)}, bf16[2,912,128]{2,1,0:T(8,128)(2,1)S(1)}, u32[]{:S(2)}, u32[]{:S(2)}) collective-permute-start(bf16[2,912,128]{2,1,0:T(8,128)(2,1)S(1)} %fusion.113), channel_id=1, source_target_pairs={{0,2},{1,3},{2,0},{3,1},{4,6},{5,7},{6,4},{7,5},{8,10},{9,11},{10,... | collective-permute-start | bytes 1400840 | tf_op jit(solution)/shard_map/ppermute | solution.py:46
  923.6 16.8 %collective-permute-start.81 = (f32[912,128]{1,0:T(8,128)S(1)}, f32[912,128]{1,0:T(8,128)S(1)}, u32[]{:S(2)}, u32[]{:S(2)}) collective-permute-start(f32[912,128]{1,0:T(8,128)S(1)} %fusion.115), channel_id=1, source_target_pairs={{0,8},{8,16},{16,24},{24,0},{1,9},{9,17},{17,25},{25,1},{2,10},{10... | collective-permute-start | bytes 1400840 | tf_op jit(solution)/shard_map/ppermute | solution.py:51
  923.8 34.1 %collective-permute-start.84 = (bf16[2,2,920,128]{3,2,0,1:T(8,128)(2,1)S(1)}, bf16[2,2,920,128]{3,2,0,1:T(8,128)(2,1)S(1)}, u32[]{:S(2)}, u32[]{:S(2)}) collective-permute-start(bf16[2,2,920,128]{3,2,0,1:T(8,128)(2,1)S(1)} %fusion.80), channel_id=1, source_target_pairs={{0,4},{1,5},{2,6},{3,7},{4,0},{5,1},{6,2},{7,3},{8,12},{9,13},{10,... | collective-permute-start | bytes 2826248 | tf_op jit(solution)/shard_map/ppermute | solution.py:46
  934.3 20.8 %collective-permute-start.87 = (bf16[2,920,128]{2,1,0:T(8,128)(2,1)S(1)}, bf16[2,920,128]{2,1,0:T(8,128)(2,1)S(1)}, u32[]{:S(2)}, u32[]{:S(2)}) collective-permute-start(bf16[2,920,128]{2,1,0:T(8,128)(2,1)S(1)} %fusion.109), channel_id=1, source_target_pairs={{0,4},{1,5},{2,6},{3,7},{4,0},{5,1},{6,2},{7,3},{8,12},{9,13},{10,... | collective-permute-start | bytes 1413128 | tf_op jit(solution)/shard_map/ppermute | solution.py:46
  940.4 28.4 %collective-permute-start.82 = (f32[912,128]{1,0:T(8,128)S(1)}, f32[912,128]{1,0:T(8,128)S(1)}, u32[]{:S(2)}, u32[]{:S(2)}) collective-permute-start(f32[912,128]{1,0:T(8,128)S(1)} %fusion.116), channel_id=1, source_target_pairs={{0,8},{8,16},{16,24},{24,0},{1,9},{9,17},{17,25},{25,1},{2,10},{10... | collective-permute-start | bytes 1400840 | tf_op jit(solution)/shard_map/ppermute | solution.py:51
  978.4 39.3 %collective-permute-start.90 = (f32[920,128]{1,0:T(8,128)S(1)}, f32[920,128]{1,0:T(8,128)S(1)}, u32[]{:S(2)}, u32[]{:S(2)}) collective-permute-start(f32[920,128]{1,0:T(8,128)S(1)} %fusion.111), channel_id=1, source_target_pairs={{0,8},{8,16},{16,24},{24,0},{1,9},{9,17},{17,25},{25,1},{2,10},{10... | collective-permute-start | bytes 1413128 | tf_op jit(solution)/shard_map/ppermute | solution.py:51
  (213 other events, 2808.1 us)
Sparse Core Ops, SparseCore 0:
  10.2 63.0 all-gather.3
  76.2 144.1 all-gather.5
  617.0 115.3 reduce-scatter.1
  734.7 48.7 all-gather.7

commit v3 on v2

--- a/solution.py
+++ b/solution.py
@@ -58,15 +58,25 @@
     return value
 
 
-def scatter_near(value_far, value_near):
-    half = value_near.shape[2] // 2
-    value = value_near + swap(value_far, CORE)
+def plane_hop(value):
+    half = value.shape[2] // 2
     upper, lower = value[:, :, :half], value[:, :, half:]
-    upper = upper[:, 0] + swap(upper[:, 1], ACROSS)
-    lower = lower[0] + swap(lower[1], DEEP)
-    upper = upper[0] + swap(upper[1], DEEP)
-    lower = lower[0] + swap(lower[1], ACROSS)
-    return jnp.concatenate([upper, lower])
+    return upper[:, 0] + swap(upper[:, 1], ACROSS), lower[0] + swap(lower[1], DEEP)
+
+
+def plane_end(upper, lower):
+    return jnp.concatenate([upper[0] + swap(upper[1], DEEP), lower[0] + swap(lower[1], ACROSS)])
+
+
+def together(*values):
+    return lax.optimization_barrier(values)
+
+
+def ring_sum(value):
+    moving = shift(value[3], 1)
+    moving = shift(value[2] + moving, 1)
+    moving = shift(value[1] + moving, 1)
+    return value[0] + moving
 
 
 def sum_everywhere(value):
@@ -88,7 +98,7 @@
 def rolled(table, downward):
     z = lax.axis_index("dp")
     order = (z - jnp.arange(4)) % 4 if downward else (z + jnp.arange(4)) % 4
-    return jnp.stack([lax.dynamic_index_in_dim(table, order[k], keepdims=False) for k in range(4)])
+    return [lax.dynamic_index_in_dim(table, order[k], keepdims=False) for k in range(4)]
 
 
 def rows_of_tiles(tiles):
@@ -116,7 +126,7 @@
 
 def unpack_matrix(tiles, piece):
     first, height, across = piece
-    lines = 64 if across > 6 else 128
+    lines = min(height, 384 if across > 6 else 768)
     block = lines * across
     return pl.pallas_call(
         functools.partial(unpack_kernel, across=across),
@@ -134,6 +144,7 @@
     targets = refs[len(places) : len(places) + 5]
     tail = refs[len(places) + 5]
     landed, stage, full, packed, in_sems, out_sems, tail_sem = refs[len(places) + 6 :]
+    slots = packed.shape[0]
     copies = []
     for n, (arrival, place) in enumerate(zip(arrivals, places)):
         target = landed if place is None else landed.at[place[0], pl.ds(place[1], place[2])]
@@ -180,11 +191,11 @@
             )
 
         def one_column(n, carry, first=first, size=size, out_copy=out_copy):
-            slot = n % 2
-
-            @pl.when(n >= 2)
+            slot = n % slots
+
+            @pl.when(n >= slots)
             def _():
-                out_copy(n - 2, slot).wait()
+                out_copy(n - slots, slot).wait()
 
             packed[slot, pl.ds(0, size), :] = full[pl.ds(pl.multiple_of(first + n * size, 128), size), :].astype(
                 jnp.bfloat16
@@ -194,8 +205,8 @@
 
         total = across * parts
         lax.fori_loop(0, total, one_column, 0)
-        for n in (total - 2, total - 1):
-            out_copy(n, n % 2).wait()
+        for n in range(total - slots, total):
+            out_copy(n, n % slots).wait()
     tail_copy.wait()
 
 
@@ -210,9 +221,9 @@
             pltpu.VMEM((count, per, TILE), jnp.bfloat16),
             pltpu.VMEM((128, TILE), jnp.float32),
             pltpu.VMEM((count * per, TILE), jnp.float32),
-            pltpu.VMEM((2, D, TILE), jnp.bfloat16),
+            pltpu.VMEM((6, D, TILE), jnp.bfloat16),
             pltpu.SemaphoreType.DMA((len(arrivals),)),
-            pltpu.SemaphoreType.DMA((2,)),
+            pltpu.SemaphoreType.DMA((6,)),
             pltpu.SemaphoreType.DMA,
         ],
         compiler_params=pltpu.CompilerParams(vmem_limit_bytes=VMEM_LIMIT),
@@ -394,10 +405,8 @@
     return (final_lines, saved)
 
 
-def layer_backward(pieces, saved, grad_final, lengths):
-    small_rows = pieces["small"].astype(jnp.float32)
-    seqs_count = lengths.shape[0]
-    rows_here = seqs_count * LEN
+def feed_backward(pieces, saved, grad_final):
+    small_rows = pieces["small"]
     grad_sum_two, grad_gain_two, grad_shift_two = norm_backward(
         grad_final, saved["normed_two"], saved["inverse_two"], small_rows[8]
     )
@@ -410,6 +419,16 @@
     grad_sum_one, grad_gain_one, grad_shift_one = norm_backward(
         grad_middle, saved["normed_one"], saved["inverse_one"], small_rows[6]
     )
+    grad_small = [jnp.sum(grad_out.astype(jnp.float32), axis=0), grad_gain_one, grad_shift_one, grad_gain_two, grad_shift_two]
+    grad_upbias = jnp.sum(grad_hidden.astype(jnp.float32), axis=0)
+    return grad_sum_one, (grad_up, grad_down, grad_small, grad_upbias)
+
+
+def attention_backward(pieces, saved, grad_sum_one, feed_grads, lengths):
+    small_rows = pieces["small"]
+    seqs_count = lengths.shape[0]
+    rows_here = seqs_count * LEN
+    grad_up, grad_down, grad_small, grad_upbias = feed_grads
     grad_att = grad_sum_one.astype(jnp.bfloat16)
     grad_outw = matmul_left(saved["context"], grad_att)
     grad_context = (
@@ -455,16 +474,12 @@
             grad_bias_all[:D],
             grad_bias_all[2 * D :],
             jnp.sum(grad_att.astype(jnp.float32), axis=0),
-            jnp.sum(grad_out.astype(jnp.float32), axis=0),
+            grad_small[0],
             grad_gain_zero,
             grad_shift_zero,
-            grad_gain_one,
-            grad_shift_one,
-            grad_gain_two,
-            grad_shift_two,
+            *grad_small[1:],
         ]
     )
-    grad_upbias = jnp.sum(grad_hidden.astype(jnp.float32), axis=0)
     tail = jnp.concatenate(
         [grad_small.reshape(60, TILE), grad_upbias.reshape(24, TILE), jnp.zeros((4, TILE), jnp.float32)]
     )
@@ -524,18 +539,18 @@
     return swap(value.astype(jnp.bfloat16), bit).astype(jnp.float32)
 
 
-def reduce_chunk(value):
-    lines = value.shape[1]
-    value = value.reshape(4, 2, 2, lines, TILE)
+def plane_first(value):
+    value = value.reshape(4, 2, 2, value.shape[1], TILE)
     first, second = value[2:], value[:2]
     first = first[:, :, 0] + sent_low(first[:, :, 1], ACROSS)
     second = second[:, 0] + sent_low(second[:, 1], DEEP)
+    return first, second
+
+
+def plane_second(first, second):
     first = first[:, 0] + sent_low(first[:, 1], DEEP)
     second = second[:, 0] + sent_low(second[:, 1], ACROSS)
-    moving = shift(first[1], 1)
-    moving = shift(first[0] + moving, 1)
-    moving = shift(second[1] + moving, 1)
-    return second[0] + moving
+    return [second[0], second[1], first[0], first[1]]
 
 
 def on_device(
@@ -566,61 +581,73 @@
     target_rows = rows_of_tiles(owner_order)
     student_low = student_flat.astype(jnp.bfloat16)
     table_low = lax.all_gather(student_embed.T.astype(jnp.bfloat16), "dp", axis=0, tiled=True)
-    teacher_tiles = lax.all_gather(teacher_flat, ("dp", "vocab"), axis=0, tiled=True)
+    words = jnp.arange(vocab_rows, dtype=jnp.int32)
+
+    def chosen(ids):
+        return (ids.reshape(-1, 1) - here * vocab_rows == words[None]).astype(jnp.bfloat16)
+
+    def rows_t(ids):
+        return array_multiply(chosen(ids), mentor_lexicon_weights).astype(jnp.bfloat16)
+
+    def rows_s(ids):
+        return trailing_array_multiply(chosen(ids), table_low).astype(jnp.bfloat16)
+
     if near:
         plane_facts = gather_near(facts)
         by_plane = [facts, shift(facts, 1), shift(facts, 2), shift(facts, 3)]
         other_facts = gather_near(jnp.stack(by_plane[1:]))
         all_facts = jnp.concatenate([plane_facts[:, None], other_facts], axis=1)
         relative = relative_order(target_rows, per)
-        downward = rolled(relative, True).reshape(-1)
-        upward = rolled(relative.transpose(3, 0, 1, 2, 4).swapaxes(0, 1), False).swapaxes(0, 1).reshape(-1)
+        downward = jnp.stack(rolled(relative, True)).reshape(-1)
+        upward = jnp.stack(rolled(relative.transpose(0, 3, 1, 2, 4), False), axis=1).reshape(-1)
+        arrivals, places = gather_student(student_low)
+        far_ids, close_ids = plane_facts[4:, :LEN], plane_facts[:4, :LEN]
+        shape = (2, 2, LEN, D)
+        looked_t = rows_t(close_ids).reshape(shape) + swap(rows_t(far_ids).reshape(shape), CORE)
+        looked_s = rows_s(close_ids).reshape(shape) + swap(rows_s(far_ids).reshape(shape), CORE)
+        arrivals, teacher_flat, looked_t, looked_s = lax.optimization_barrier(
+            (arrivals, teacher_flat, looked_t, looked_s)
+        )
+        teacher_tiles = lax.all_gather(teacher_flat, ("dp", "vocab"), axis=0, tiled=True)
+        looked_t, looked_s = plane_hop(looked_t), plane_hop(looked_s)
+        matrices = place_tiles(downward, arrivals, tuple(places), planes * group, per)
+        matrices, looked_t, looked_s = together(matrices, looked_t, looked_s)
+        looked_s = plane_end(*looked_s).astype(jnp.float32)
+        looked_t = plane_end(*looked_t).astype(jnp.float32)
     else:
         by_plane = lax.all_gather(facts, "dp", axis=0)
         all_facts = lax.all_gather(by_plane, "vocab", axis=0)
         plane_facts = lax.dynamic_index_in_dim(all_facts, lax.axis_index("dp"), 1, keepdims=False)
+        teacher_tiles = lax.all_gather(teacher_flat, ("dp", "vocab"), axis=0, tiled=True)
         student_tiles = lax.all_gather(student_low, ("dp", "vocab"), axis=0, tiled=True)
-    token_total = jnp.sum(all_facts[:, :, LEN]).astype(jnp.float32)
-    masked_total = jnp.sum(all_facts[:, :, LEN + 1]).astype(jnp.float32)
-
-    words = jnp.arange(vocab_rows, dtype=jnp.int32)
-
-    def chosen(ids):
-        return (ids.reshape(-1, 1) - here * vocab_rows == words[None]).astype(jnp.bfloat16)
-
-    def looked_up(multiply):
-        if near:
-            far = multiply(chosen(plane_facts[4:, :LEN])).astype(jnp.bfloat16)
-            close = multiply(chosen(plane_facts[:4, :LEN])).astype(jnp.bfloat16)
-            total = scatter_near(far.reshape(2, 2, LEN, D), close.reshape(2, 2, LEN, D))
-        else:
-            rows = multiply(chosen(plane_facts[:, :LEN])).astype(jnp.bfloat16)
-            total = lax.psum_scatter(rows, "vocab", scatter_dimension=0, tiled=True)
-        return total.astype(jnp.float32)
-
-    looked_t = looked_up(lambda pick: array_multiply(pick, mentor_lexicon_weights))
-    looked_s = looked_up(lambda pick: trailing_array_multiply(pick, table_low))
-    if near:
-        arrivals, places = gather_student(student_low)
-        arrivals, looked_t, looked_s = lax.optimization_barrier((arrivals, looked_t, looked_s))
-        matrices = place_tiles(downward, arrivals, tuple(places), planes * group, per)
-    else:
+        plane_ids = plane_facts[:, :LEN]
+        looked_t, looked_s = (
+            lax.psum_scatter(rows, "vocab", scatter_dimension=0, tiled=True).astype(jnp.float32)
+            for rows in (rows_t(plane_ids), rows_s(plane_ids))
+        )
         matrices = place_tiles(
             target_rows, [student_tiles.reshape(planes * group, per, TILE)], (None,), planes * group, per
         )
     student = pieces_of(matrices[:5], matrices[5])
+    final_s, saved = layer_forward(student, looked_s, lengths)
+    final_s, teacher_tiles, looked_t, all_facts = together(final_s, teacher_tiles, looked_t, all_facts)
     teacher = pieces_of(
         [unpack_matrix(teacher_tiles, piece) for piece in MATRICES],
         teacher_tiles[TAIL : TAIL + TAIL_TILES].astype(jnp.float32),
     )
-    final_s, saved = layer_forward(student, looked_s, lengths)
-    final_t = layer_forward(teacher, looked_t, lengths)[0]
+    token_total = jnp.sum(all_facts[:, :, LEN]).astype(jnp.float32)
+    masked_total = jnp.sum(all_facts[:, :, LEN + 1]).astype(jnp.float32)
 
     offsets = jnp.concatenate([mask_pos.reshape(CAP), jnp.zeros((SLOTS - CAP,), jnp.int32)])
     picked_s = final_s[offsets].astype(jnp.bfloat16)
+    if near:
+        learner_picked = gather_near(picked_s).reshape(-1, D)
+    final_t = layer_forward(teacher, looked_t, lengths)[0]
+    if near:
+        final_t, learner_picked = together(final_t, learner_picked)
+
     picked_t = final_t[offsets].astype(jnp.bfloat16)
     if near:
-        learner_picked = gather_near(picked_s).reshape(-1, D)
         mentor_picked = gather_near(picked_t).reshape(-1, D)
     else:
         learner_picked = lax.all_gather(picked_s, "vocab", axis=0, tiled=True)
@@ -672,14 +699,15 @@
         half = grad_logit.shape[0] // 2
         far = trailing_array_multiply(grad_logit[half:], table_low).reshape(2, 2, SLOTS, D)
         close = trailing_array_multiply(grad_logit[:half], table_low).reshape(2, 2, SLOTS, D)
-        grad_rows = scatter_near(far, close)
+        grad_rows = plane_end(*plane_hop(close + swap(far, CORE)))
     else:
         grad_rows = lax.psum_scatter(
             trailing_array_multiply(grad_logit, table_low), "vocab", scatter_dimension=0, tiled=True
         )
     head_grad = matmul_left(learner_picked, grad_logit)
-    head_grad, grad_rows = lax.optimization_barrier((head_grad, grad_rows))
-    head_part = lax.psum_scatter(head_grad, "dp", scatter_dimension=0, tiled=True)
+    head_grad, grad_rows = together(head_grad, grad_rows)
+    if not near:
+        head_part = lax.psum_scatter(head_grad, "dp", scatter_dimension=0, tiled=True)
     products = jnp.sum(final_s * final_t, axis=1)
     inverse_s = lax.rsqrt(jnp.sum(final_s * final_s, axis=1) + cosine_eps)
     inverse_t = lax.rsqrt(jnp.sum(final_t * final_t, axis=1) + cosine_eps)
@@ -691,13 +719,22 @@
         final_t - (products * inverse_s * inverse_s)[:, None] * final_s
     )
     grad_final = grad_final.at[offsets].add(grad_rows)
-    layer_grads, grad_embedded = layer_backward(student, saved, grad_final, lengths)
-    layer_grads, head_part = lax.optimization_barrier((layer_grads, head_part))
+    if near:
+        heads = rolled(head_grad.reshape(4, width_share, vocab_rows), False)
+        moving = shift(heads[3], 1)
+        grad_sum_one, feed_grads = feed_backward(student, saved, grad_final)
+        grad_sum_one, moving = together(grad_sum_one, moving)
+        moving = shift(heads[2] + moving, 1)
+        layer_grads, grad_embedded = attention_backward(student, saved, grad_sum_one, feed_grads, lengths)
+        grad_embedded, moving = together(grad_embedded, moving)
+        moving = shift(heads[1] + moving, 1)
+    else:
+        grad_sum_one, feed_grads = feed_backward(student, saved, grad_final)
+        layer_grads, grad_embedded = attention_backward(student, saved, grad_sum_one, feed_grads, lengths)
 
     shares = grad_embedded.astype(jnp.bfloat16).reshape(LEN, planes, width_share).transpose(1, 0, 2)
     if near:
-        z = lax.axis_index("dp")
-        own = [lax.dynamic_index_in_dim(shares, (z + k) % 4, keepdims=False) for k in range(4)]
+        own = rolled(shares, False)
         shares = jnp.stack([own[0]] + [shift(own[k], k) for k in (1, 2, 3)])
         ids = all_facts[:, :, :LEN].reshape(2, 2, 2, planes, LEN)
         for axis, bit in ((0, CORE), (1, DEEP), (2, ACROSS)):
@@ -708,20 +745,43 @@
         ids = all_facts[:, :, :LEN]
     token_grads = lax.all_gather(shares.reshape(-1, width_share), "vocab", axis=0, tiled=True)
     if near:
-        split = per // 16 * 8
-        sums = []
-        for begin, end in ((0, split), (split, per)):
-            own_tiles, other_tiles = collect_tiles(upward, layer_grads, tiles_all, per, 2, begin, end - begin)
-            chip = own_tiles + swap(other_tiles, CORE)
-            chip, upward, token_grads = lax.optimization_barrier((chip, upward, token_grads))
-            sums.append(reduce_chunk(chip))
+        step = per // 32 * 8
+        edges = (0, step, 2 * step, 3 * step, per)
+
+        def collect(n):
+            return collect_tiles(upward, layer_grads, tiles_all, per, 2, edges[n], edges[n + 1] - edges[n])
+
+        one = collect(0)
+        one, moving, shares = together(one, moving, shares)
+        token_grads = lax.all_gather(shares.reshape(-1, width_share), "vocab", axis=0, tiled=True)
+        head_part = heads[0] + moving
+        chip_one = one[0] + swap(one[1], CORE)
+        chip_one, two = together(chip_one, collect(1))
+        first_one = plane_first(chip_one)
+        chip_two = two[0] + swap(two[1], CORE)
+        first_one, chip_two, three = together(first_one, chip_two, collect(2))
+        blocks_one = plane_second(*first_one)
+        first_two = plane_first(chip_two)
+        chip_three = three[0] + swap(three[1], CORE)
+        blocks_one, first_two, chip_three, token_grads, four = together(
+            blocks_one, first_two, chip_three, token_grads, collect(3)
+        )
+        token_part = matmul_left(token_grads, chosen(ids))
+        blocks_two = plane_second(*first_two)
+        first_three = plane_first(chip_three)
+        chip_four = four[0] + swap(four[1], CORE)
+        blocks_two, first_three, chip_four, token_part = together(blocks_two, first_three, chip_four, token_part)
+        blocks_three = plane_second(*first_three)
+        blocks_four = plane_second(*plane_first(chip_four))
+        sums = [ring_sum(blocks) for blocks in (blocks_one, blocks_two, blocks_three, blocks_four)]
         flat_grad = jnp.concatenate(sums)
     else:
+        token_grads = lax.all_gather(shares.reshape(-1, width_share), "vocab", axis=0, tiled=True)
+        token_part = matmul_left(token_grads, chosen(ids))
         (grad_tiles,) = collect_tiles(target_rows, layer_grads, tiles_all, per, 1, 0, per)
         flat_grad = lax.psum_scatter(
             grad_tiles.reshape(tiles_all, TILE), ("dp", "vocab"), scatter_dimension=0, tiled=True
         )
-    token_part = matmul_left(token_grads, chosen(ids))
     table_grad = (head_part + token_part).T
     loss_term = (
         mixing_coefficient * smoothing_heat_scale**2 * divergence_part / masked_total

time: 1060 us -> 994 us (0.938)
  waiting for transfers between devices: 305 us -> 237 us
  starting transfers between devices: 79.6 us -> 99.4 us
    ppermute x79 -> x89, waiting for transfers between devices: 170 us -> 101 us  [swap(): return lax.ppermute(value, 'vocab', [(i, i ^ bit) for i in range(8)])]
    pallas_call x2 -> x4, Pallas kernels: 82.3 us -> 119 us  [collect_tiles(): pl.pallas_call(functools.partial(collect_kernel, outs=outs, blocks=blocks...]
    all_gather x1, waiting for transfers between devices: 32.4 us -> 0.01 us  [on_device(): lax.all_gather(student_embed.T.astype(jnp.bfloat16), 'dp', axis=0, tiled=...]
    ppermute x15 -> x24, waiting for transfers between devices: 96.3 us -> 128 us  [shift(): lax.ppermute(value, 'dp', [(i, (i + steps) % size) for i in range(size)])]
    pallas_call x5, Pallas kernels: 41.5 us -> 21.2 us  [unpack_matrix(): pl.pallas_call(functools.partial(unpack_kernel, across=across), grid=(hei...]
    pallas_call x1, Pallas kernels: 88.7 us -> 71.5 us  [place_tiles(): pl.pallas_call(functools.partial(place_kernel, places=places, count=count...]
    ppermute x15 -> x24, starting transfers between devices: 16.1 us -> 30.5 us  [shift(): lax.ppermute(value, 'dp', [(i, (i + steps) % size) for i in range(size)])]
    add x28 -> x50, other arithmetic: 31.1 us -> 39.7 us  [the longest x1 4.56 us: on_device(): rows_t(close_ids).reshape(shape)]
  transfers between devices with their start and end apart: 100 -> 118, of which waited for: 46 -> 48; matrix products, arithmetic and copies ran while one was open for 25% -> 29% of each run, Pallas kernels for 12% -> 19%
where the time goes in v3:
time: 994 us; the launch traced here: 983 us
  waiting for transfers between devices  237 us (24%)
  matrix products  224 us (23%)
  Pallas kernels  211 us (21%)
  other arithmetic  103 us (10%)
  starting transfers between devices  99.4 us (10%)
  local copies, waits for them, and re-layouts  67.4 us (7%)
  between operations  40.5 us (4%)
    ppermute x24, waiting for transfers between devices, shift(): lax.ppermute(value, 'dp', [(i, (i + steps) % size) for i in range(size)])  128 us
    pallas_call x4, Pallas kernels, collect_tiles(): pl.pallas_call(functools.partial(collect_kernel, outs=outs, blocks=blocks...  119 us
    ppermute x89, waiting for transfers between devices, swap(): return lax.ppermute(value, 'vocab', [(i, i ^ bit) for i in range(8)])  101 us
    dot_general x10, matrix products, array_multiply(): return jnp.dot(left_side, right_side, preferred_element_type=jnp.float32)  78.6 us
    pallas_call x1, Pallas kernels, place_tiles(): pl.pallas_call(functools.partial(place_kernel, places=places, count=count...  71.5 us
    ppermute x89, starting transfers between devices, swap(): return lax.ppermute(value, 'vocab', [(i, i ^ bit) for i in range(8)])  68.8 us
    dot_general x6, matrix products, matmul_left(): lax.dot_general(left_side, right_side, (((0,), (0,)), ((), ())), preferre...  61.6 us
    dot_general x9, matrix products, trailing_array_multiply(): lax.dot_general(left_side, right_side, (((1,), (1,)), ((), ())), preferre...  41.1 us
  transfers between devices with their start and end apart: 118, of which 48 were waited for; matrix products, arithmetic and copies ran while one was open for 29% of the time, Pallas kernels for 19%

profile of v3, /device:TPU:0, one launch (start us, length us, event | category | flops | bytes accessed | tf_op | source)
XLA Modules:
  0.0 983.5 jit_solution(17915103187554910275)
XLA Ops:
  19.1 5.8 collective-permute-done.1.refs_2_
  40.0 5.1 collective-permute-start.19
  54.2 14.8 %collective-permute-done.19.refs_20_ = bf16[1832,128]{1,0:T(8,128)(2,1)} collective-permute-done((bf16[1832,128]{1,0:T(8,128)(2,1)}, bf16[1832,128]{1,0:T(8,128)(2,1)}, u32[]{:S(2)}, u32[]{:S(2)}) %collective-permute-start.19) | collective-permute-done | bytes 469024 | tf_op jit(solution)/shard_map/ppermute | solution.py:51
  69.7 10.1 %collective-permute-start.29 = (bf16[1832,128]{1,0:T(8,128)(2,1)}, bf16[1832,128]{1,0:T(8,128)(2,1)}, u32[]{:S(2)}, u32[]{:S(2)}) collective-permute-start(bf16[1832,128]{1,0:T(8,128)(2,1)} %collective-permute-done.19.refs_20_), channel_id=1, source_target_pairs={{0,8},{8,16},{16,24},{24,0},{1,9},{9,17},{17,25},{25,1},{2,10},{10... | collective-permute-start | bytes 1406984 | tf_op jit(solution)/shard_map/ppermute | solution.py:51
  81.2 8.5 fusion.53
  96.7 9.2 fusion.54
  113.4 11.0 %collective-permute-done.25.refs_26_ = bf16[912,128]{1,0:T(8,128)(2,1)S(1)} collective-permute-done((bf16[912,128]{1,0:T(8,128)(2,1)S(1)}, bf16[912,128]{1,0:T(8,128)(2,1)S(1)}, u32[]{:S(2)}, u32[]{:S(2)}) %collective-permute-start.25) | collective-permute-done | bytes 233504 | tf_op jit(solution)/shard_map/ppermute | solution.py:46
  126.3 7.3 collective-permute-done.27.refs_28_
  136.2 7.5 fusion.51
  149.6 7.3 fusion.52
  177.8 5.6 rev.32
  208.6 71.5 %place_tiles.1 = (bf16[768,2304]{1,0:T(8,128)(2,1)}, bf16[768,768]{1,0:T(8,128)(2,1)}, bf16[768,3072]{1,0:T(8,128)(2,1)}, bf16[3072,768]{1,0:T(8,128)(2,1)}, bf1...) custom-call(s32[58624]{0:T(1024)} %reshape.763.rows, bf16[1832,128]{1,0:T(8,128)(2,1)} %copy-done.48, ...), custom_call_target="tpu_custom_call" | custom-call | bytes 180000000 | tf_op jit(solution)/shard_map/place_tiles/pallas_call | solution.py:215
  292.0 6.3 collective-permute-done.49
  327.1 19.7 %fusion.17 = (bf16[512,3072]{1,0:T(8,128)(2,1)S(1)}, f32[512,3072]{1,0:T(8,128)}) fusion(f32[3072]{0:T(1024)S(1)} %slice_bitcast_fusion.60, bf16[768,3072]{1,0:T(8,128)(2,1)} %get-tuple-element.171, f32[512,768]{1,0:T(8,128)S(1)} %get-tuple-element.357, f32[768]{0:T(1024)S(1)} %get-tuple-element.311, f32[768]{0:T(1024)S(1)} %get-tuple-element.312, ...), kind=kOutput, calls=%fused_computation.41 | convolution fusion | flops 2521694208 | bytes 15751168 | tf_op jit(solution)/shard_map/dot_general | solution.py:293
  362.4 6.2 unpack_matrix.9
  368.6 5.7 unpack_matrix.8
  379.7 5.7 fusion.50
  390.0 10.9 %fusion.259 = (f32[12,512]{1,0:T(8,128)S(1)}, f32[12,512,512]{1,2,0:T(8,128)}) fusion(pred[512]{0:T(512)(128)(4,1)S(1)} %iota_compare_fusion.17, bf16[1,512,3,12,64]{1,4,3,2,0:T(8,128)(2,1)} %bitcast.521), kind=kOutput, calls=%fused_computation.581 | convolution fusion | flops 415236608 | bytes 14180864 | tf_op jit(solution)/shard_map/sub | solution.py:371
  401.0 6.2 fusion.68
  411.8 23.2 %fusion.261 = (f32[512]{0:T(512)S(1)}, f32[512,768]{1,0:T(8,128)}) fusion(f32[768]{0:T(1024)S(1)} %get-tuple-element.300, bf16[3072,768]{1,0:T(8,128)(2,1)} %unpack_matrix.9, bf16[768,3072]{1,0:T(8,128)(2,1)} %unpack_matrix.8, f32[3072]{0:T(1024)S(1)} %slice_bitcast_fusion.59, f32[512,768]{1,0:T(8,128)} %copy-done.51, f32[768]{0:T(1024)S(1)} %get-tuple-element.301, ...), kind=kOutput, calls=%fused_computation.583 | convolution fusion | flops 4940365312 | bytes 12610560 | tf_op jit(solution)/shard_map/dot_general | solution.py:293
  444.0 6.3 collective-permute-done.61
  450.8 9.9 %collective-permute-done.62 = bf16[2,128,768]{2,1,0:T(8,128)(2,1)S(1)} collective-permute-done((bf16[2,128,768]{2,1,0:T(8,128)(2,1)S(1)}, bf16[2,128,768]{2,1,0:T(8,128)(2,1)S(1)}, u32[]{:S(2)}, u32[]{:S(2)}) %collective-permute-start.62) | collective-permute-done | bytes 393248 | tf_op jit(solution)/shard_map/ppermute | solution.py:46
  460.9 5.3 multiply_reduce_fusion.3
  484.0 7.7 multiply_convert_fusion.1
  507.9 5.3 fusion.264
  530.6 7.3 convert_reduce_fusion
  538.0 5.5 multiply_reduce_fusion.5
  548.0 5.2 fusion.197.refs_3_
  553.2 5.5 fusion.234.refs_2_
  558.7 20.5 %collective-permute-done.72 = f32[192,1920]{1,0:T(8,128)S(1)} collective-permute-done((f32[192,1920]{1,0:T(8,128)S(1)}, f32[192,1920]{1,0:T(8,128)S(1)}, u32[]{:S(2)}, u32[]{:S(2)}) %collective-permute-start.72) | collective-permute-done | bytes 1474592 | tf_op jit(solution)/shard_map/ppermute | solution.py:51
  582.5 7.0 fusion.60
  589.5 9.0 multiply_reduce_fusion
  598.5 6.8 multiply_convert_fusion
  617.2 26.7 %collective-permute-done.73 = f32[192,1920]{1,0:T(8,128)S(1)} collective-permute-done((f32[192,1920]{1,0:T(8,128)S(1)}, f32[192,1920]{1,0:T(8,128)S(1)}, u32[]{:S(2)}, u32[]{:S(2)}) %collective-permute-start.73) | collective-permute-done | bytes 1474592 | tf_op jit(solution)/shard_map/ppermute | solution.py:51
  649.4 5.3 fusion.167.refs_0_
  660.6 28.4 %collect_tiles.4 = (f32[16,456,128]{2,1,0:T(8,128)}, f32[16,456,128]{2,1,0:T(8,128)}) custom-call(s32[58624]{0:T(1024)} %reshape.762.rows, f32[768,2304]{1,0:T(8,128)} %fusion.167.refs_0_, f32[768,768]{1,0:T(8,128)} %fusion.194.refs_1_, f32[768,3072]{1,0:T(8,128)} %fusion.234.refs_2_, f32[3072,768]{1,0:T(8,128)} %fusion.197.refs_3_, f32[512,768]{1,0:T(8,128)} %copy-done.3, ...), custom_call_target="tpu_custom_call" | custom-call | bytes 80000000 | tf_op jit(solution)/shard_map/collect_tiles/pallas_call | solution.py:279
  689.1 5.4 collective-permute-done.76
  695.7 28.7 %collect_tiles.5 = (f32[16,456,128]{2,1,0:T(8,128)}, f32[16,456,128]{2,1,0:T(8,128)}) custom-call(s32[58624]{0:T(1024)} %reshape.762.rows, f32[768,2304]{1,0:T(8,128)} %fusion.167.refs_0_, f32[768,768]{1,0:T(8,128)} %fusion.194.refs_1_, f32[768,3072]{1,0:T(8,128)} %fusion.234.refs_2_, f32[3072,768]{1,0:T(8,128)} %fusion.197.refs_3_, f32[512,768]{1,0:T(8,128)} %copy-done.3, ...), custom_call_target="tpu_custom_call" | custom-call | bytes 80000000 | tf_op jit(solution)/shard_map/collect_tiles/pallas_call | solution.py:279
  732.5 28.5 %collect_tiles.6 = (f32[16,456,128]{2,1,0:T(8,128)}, f32[16,456,128]{2,1,0:T(8,128)}) custom-call(s32[58624]{0:T(1024)} %reshape.762.rows, f32[768,2304]{1,0:T(8,128)} %fusion.167.refs_0_, f32[768,768]{1,0:T(8,128)} %fusion.194.refs_1_, f32[768,3072]{1,0:T(8,128)} %fusion.234.refs_2_, f32[3072,768]{1,0:T(8,128)} %fusion.197.refs_3_, f32[512,768]{1,0:T(8,128)} %copy-done.3, ...), custom_call_target="tpu_custom_call" | custom-call | bytes 80000000 | tf_op jit(solution)/shard_map/collect_tiles/pallas_call | solution.py:279
  770.8 32.9 %collect_tiles.7 = (f32[16,464,128]{2,1,0:T(8,128)}, f32[16,464,128]{2,1,0:T(8,128)}) custom-call(s32[58624]{0:T(1024)} %reshape.762.rows, f32[768,2304]{1,0:T(8,128)} %fusion.167.refs_0_, f32[768,768]{1,0:T(8,128)} %fusion.194.refs_1_, f32[768,3072]{1,0:T(8,128)} %fusion.234.refs_2_, f32[3072,768]{1,0:T(8,128)} %fusion.197.refs_3_, f32[512,768]{1,0:T(8,128)} %copy-done.3, ...), custom_call_target="tpu_custom_call" | custom-call | bytes 80000000 | tf_op jit(solution)/shard_map/collect_tiles/pallas_call | solution.py:279
  814.1 7.9 collective-permute-done.85
  834.8 36.2 %fusion.1 = f32[192,1920]{1,0:T(8,128)S(1)} fusion(bf16[16384,192]{0,1:T(8,128)(2,1)S(1)} %copy-done.121, s32[16384]{0:T(1024)S(1)} %bitcast.549), kind=kOutput, calls=%fused_computation.5 | convolution fusion | flops 12111052800 | bytes 7831552 | tf_op jit(solution)/shard_map/dot_general | solution.py:297
  872.8 9.4 collective-permute-done.88
  884.3 6.9 collective-permute-done.89
  902.4 8.0 collective-permute-done.100
  925.9 5.1 collective-permute-done.107
  931.6 8.7 collective-permute-done.108
  940.5 7.8 collective-permute-done.109
  (781 shorter events, 348.3 us)
Async XLA Ops:
  7.2 89.5 %all-gather.4.cloned.1.call-start = ((), (), s32[]{:S(2)}) async-start(), calls=%async_computation | async-start | bytes 3686400 | tf_op jit(solution)/shard_map/all_gather | solution.py:583
  9.7 342.6 %all-gather.6.cloned.1.call-start = ((), (), s32[]{:S(2)}) async-start(), calls=%async_computation.1 | async-start | bytes 15476736 | tf_op jit(solution)/shard_map/all_gather | solution.py:611
  14.0 18.3 %collective-permute-start.9 = (bf16[1832,128]{1,0:T(8,128)(2,1)S(1)}, bf16[1832,128]{1,0:T(8,128)(2,1)}, u32[]{:S(2)}, u32[]{:S(2)}) collective-permute-start(bf16[1832,128]{1,0:T(8,128)(2,1)S(1)} %convert_element_type.315.refs_0_), channel_id=1, source_target_pairs={{0,8},{8,16},{16,24},{24,0},{1,9},{9,17},{17,25},{25,1},{2,10},{10... | collective-permute-start | bytes 1406984 | tf_op jit(solution)/shard_map/ppermute | solution.py:51
  15.6 20.5 %collective-permute-start.3 = (bf16[1832,128]{1,0:T(8,128)(2,1)S(1)}, bf16[1832,128]{1,0:T(8,128)(2,1)S(1)}, u32[]{:S(2)}, u32[]{:S(2)}) collective-permute-start(bf16[1832,128]{1,0:T(8,128)(2,1)S(1)} %convert_element_type.315.refs_0_), channel_id=1, source_target_pairs={{0,4},{1,5},{2,6},{3,7},{4,0},{5,1},{6,2},{7,3},{8,12},{9,13},{10,... | collective-permute-start | bytes 1406984 | tf_op jit(solution)/shard_map/ppermute | solution.py:46
  19.1 20.9 %collective-permute-start = (bf16[1832,128]{1,0:T(8,128)(2,1)S(1)}, bf16[1832,128]{1,0:T(8,128)(2,1)S(1)}, u32[]{:S(2)}, u32[]{:S(2)}) collective-permute-start(bf16[1832,128]{1,0:T(8,128)(2,1)S(1)} %convert_element_type.315.refs_0_), channel_id=1, source_target_pairs={{0,1},{1,0},{2,3},{3,2},{4,5},{5,4},{6,7},{7,6},{8,9},{9,8},{10,11... | collective-permute-start | bytes 1406984 | tf_op jit(solution)/shard_map/ppermute | solution.py:46
  40.0 29.0 %collective-permute-start.19 = (bf16[1832,128]{1,0:T(8,128)(2,1)}, bf16[1832,128]{1,0:T(8,128)(2,1)}, u32[]{:S(2)}, u32[]{:S(2)}) collective-permute-start(bf16[1832,128]{1,0:T(8,128)(2,1)} %collective-permute-done.9.refs_10_), channel_id=1, source_target_pairs={{0,8},{8,16},{16,24},{24,0},{1,9},{9,17},{17,25},{25,1},{2,10},{10... | collective-permute-start | bytes 1406984 | tf_op jit(solution)/shard_map/ppermute | solution.py:51
  46.1 22.8 %collective-permute-start.10 = (bf16[1832,128]{1,0:T(8,128)(2,1)}, bf16[1832,128]{1,0:T(8,128)(2,1)}, u32[]{:S(2)}, u32[]{:S(2)}) collective-permute-start(bf16[1832,128]{1,0:T(8,128)(2,1)} %collective-permute-done.9.refs_10_), channel_id=1, source_target_pairs={{0,1},{1,0},{2,3},{3,2},{4,5},{5,4},{6,7},{7,6},{8,9},{9,8},{10,11... | collective-permute-start | bytes 1406984 | tf_op jit(solution)/shard_map/ppermute | solution.py:46
  46.8 22.9 %collective-permute-start.4 = (bf16[1832,128]{1,0:T(8,128)(2,1)S(1)}, bf16[1832,128]{1,0:T(8,128)(2,1)}, u32[]{:S(2)}, u32[]{:S(2)}) collective-permute-start(bf16[1832,128]{1,0:T(8,128)(2,1)S(1)} %collective-permute-done.3.refs_4_), channel_id=1, source_target_pairs={{0,1},{1,0},{2,3},{3,2},{4,5},{5,4},{6,7},{7,6},{8,9},{9,8},{10,11... | collective-permute-start | bytes 1406984 | tf_op jit(solution)/shard_map/ppermute | solution.py:46
  47.5 32.3 %collective-permute-start.2 = (bf16[1832,128]{1,0:T(8,128)(2,1)}, bf16[1832,128]{1,0:T(8,128)(2,1)}, u32[]{:S(2)}, u32[]{:S(2)}) collective-permute-start(bf16[1832,128]{1,0:T(8,128)(2,1)} %collective-permute-done.1.refs_2_), channel_id=1, source_target_pairs={{0,1},{1,0},{2,3},{3,2},{4,5},{5,4},{6,7},{7,6},{8,9},{9,8},{10,11... | collective-permute-start | bytes 1406984 | tf_op jit(solution)/shard_map/ppermute | solution.py:46
  51.7 29.5 %collective-permute-start.15 = (bf16[912,128]{1,0:T(8,128)(2,1)}, bf16[912,128]{1,0:T(8,128)(2,1)}, u32[]{:S(2)}, u32[]{:S(2)}) collective-permute-start(bf16[912,128]{1,0:T(8,128)(2,1)} %slice.821), channel_id=1, source_target_pairs={{0,4},{1,5},{2,6},{3,7},{4,0},{5,1},{6,2},{7,3},{8,12},{9,13},{10,... | collective-permute-start | bytes 700424 | tf_op jit(solution)/shard_map/ppermute | solution.py:46
  69.0 20.8 %collective-permute-start.8 = (bf16[920,128]{1,0:T(8,128)(2,1)}, bf16[920,128]{1,0:T(8,128)(2,1)S(1)}, u32[]{:S(2)}, u32[]{:S(2)}) collective-permute-start(bf16[920,128]{1,0:T(8,128)(2,1)} %copy-done.77), channel_id=1, source_target_pairs={{0,1},{1,0},{2,3},{3,2},{4,5},{5,4},{6,7},{7,6},{8,9},{9,8},{10,11... | collective-permute-start | bytes 706568 | tf_op jit(solution)/shard_map/ppermute | solution.py:46
  69.0 21.4 %collective-permute-start.17 = (bf16[920,128]{1,0:T(8,128)(2,1)S(1)}, bf16[920,128]{1,0:T(8,128)(2,1)S(1)}, u32[]{:S(2)}, u32[]{:S(2)}) collective-permute-start(bf16[920,128]{1,0:T(8,128)(2,1)S(1)} %slice.822), channel_id=1, source_target_pairs={{0,2},{1,3},{2,0},{3,1},{4,6},{5,7},{6,4},{7,5},{8,10},{9,11},{10,... | collective-permute-start | bytes 706568 | tf_op jit(solution)/shard_map/ppermute | solution.py:46
  69.7 26.4 %collective-permute-start.29 = (bf16[1832,128]{1,0:T(8,128)(2,1)}, bf16[1832,128]{1,0:T(8,128)(2,1)}, u32[]{:S(2)}, u32[]{:S(2)}) collective-permute-start(bf16[1832,128]{1,0:T(8,128)(2,1)} %collective-permute-done.19.refs_20_), channel_id=1, source_target_pairs={{0,8},{8,16},{16,24},{24,0},{1,9},{9,17},{17,25},{25,1},{2,10},{10... | collective-permute-start | bytes 1406984 | tf_op jit(solution)/shard_map/ppermute | solution.py:51
  89.7 45.0 %collective-permute-start.42 = (bf16[2,2,512,768]{3,2,1,0:T(8,128)(2,1)}, bf16[2,2,512,768]{3,2,1,0:T(8,128)(2,1)}, u32[]{:S(2)}, u32[]{:S(2)}) collective-permute-start(bf16[2,2,512,768]{3,2,1,0:T(8,128)(2,1)} %bitcast.18), channel_id=1, source_target_pairs={{0,1},{1,0},{2,3},{3,2},{4,5},{5,4},{6,7},{7,6},{8,9},{9,8},{10,11... | collective-permute-start | bytes 9437192 | tf_op jit(solution)/shard_map/ppermute | solution.py:46
  105.9 43.7 %collective-permute-start.43 = (bf16[2,2,512,768]{3,2,1,0:T(8,128)(2,1)S(1)}, bf16[2,2,512,768]{3,2,1,0:T(8,128)(2,1)S(1)}, u32[]{:S(2)}, u32[]{:S(2)}) collective-permute-start(bf16[2,2,512,768]{3,2,1,0:T(8,128)(2,1)S(1)} %bitcast.571), channel_id=1, source_target_pairs={{0,1},{1,0},{2,3},{3,2},{4,5},{5,4},{6,7},{7,6},{8,9},{9,8},{10,11... | collective-permute-start | bytes 9437192 | tf_op jit(solution)/shard_map/ppermute | solution.py:46
  106.4 19.0 %collective-permute-start.33 = (bf16[1832,128]{1,0:T(8,128)(2,1)}, bf16[1832,128]{1,0:T(8,128)(2,1)S(1)}, u32[]{:S(2)}, u32[]{:S(2)}) collective-permute-start(bf16[1832,128]{1,0:T(8,128)(2,1)} %collective-permute-done.29.refs_30_), channel_id=1, source_target_pairs={{0,4},{1,5},{2,6},{3,7},{4,0},{5,1},{6,2},{7,3},{8,12},{9,13},{10,... | collective-permute-start | bytes 1406984 | tf_op jit(solution)/shard_map/ppermute | solution.py:46
  107.9 18.2 %collective-permute-start.31 = (bf16[1832,128]{1,0:T(8,128)(2,1)}, bf16[1832,128]{1,0:T(8,128)(2,1)S(1)}, u32[]{:S(2)}, u32[]{:S(2)}) collective-permute-start(bf16[1832,128]{1,0:T(8,128)(2,1)} %collective-permute-done.29.refs_30_), channel_id=1, source_target_pairs={{0,2},{1,3},{2,0},{3,1},{4,6},{5,7},{6,4},{7,5},{8,10},{9,11},{10,... | collective-permute-start | bytes 1406984 | tf_op jit(solution)/shard_map/ppermute | solution.py:46
  161.3 666.9 %all-gather.8.cloned.1.call-start = ((), (), s32[]{:S(2)}) async-start(), calls=%async_computation.2 | async-start | bytes 7077888 | tf_op jit(solution)/shard_map/all_gather | solution.py:756
  161.4 28.2 %collective-permute-start.54 = (s32[640]{0:T(1024)S(1)}, s32[640]{0:T(1024)S(1)}, u32[]{:S(2)}, u32[]{:S(2)}) collective-permute-start(s32[640]{0:T(1024)S(1)} %pad_add_fusion.7), channel_id=1, source_target_pairs={{0,24},{8,0},{16,8},{24,16},{1,25},{9,1},{17,9},{25,17},{2,26},{10... | collective-permute-start | bytes 7688 | tf_op jit(solution)/shard_map/ppermute | solution.py:51
  162.8 26.8 %collective-permute-start.53 = (s32[640]{0:T(1024)S(1)}, s32[640]{0:T(1024)S(1)}, u32[]{:S(2)}, u32[]{:S(2)}) collective-permute-start(s32[640]{0:T(1024)S(1)} %pad_add_fusion.7), channel_id=1, source_target_pairs={{0,16},{8,24},{16,0},{24,8},{1,17},{9,25},{17,1},{25,9},{2,18},{10... | collective-permute-start | bytes 7688 | tf_op jit(solution)/shard_map/ppermute | solution.py:51
  164.3 25.3 %collective-permute-start.52 = (s32[640]{0:T(1024)S(1)}, s32[640]{0:T(1024)S(1)}, u32[]{:S(2)}, u32[]{:S(2)}) collective-permute-start(s32[640]{0:T(1024)S(1)} %pad_add_fusion.7), channel_id=1, source_target_pairs={{0,8},{8,16},{16,24},{24,0},{1,9},{9,17},{17,25},{25,1},{2,10},{10... | collective-permute-start | bytes 7688 | tf_op jit(solution)/shard_map/ppermute | solution.py:51
  201.4 78.7 %collective-permute-start.46 = (bf16[2,256,768]{2,1,0:T(8,128)(2,1)}, bf16[2,256,768]{2,1,0:T(8,128)(2,1)}, u32[]{:S(2)}, u32[]{:S(2)}) collective-permute-start(bf16[2,256,768]{2,1,0:T(8,128)(2,1)} %slice_bitcast_fusion.10), channel_id=1, source_target_pairs={{0,2},{1,3},{2,0},{3,1},{4,6},{5,7},{6,4},{7,5},{8,10},{9,11},{10,... | collective-permute-start | bytes 2359304 | tf_op jit(solution)/shard_map/ppermute | solution.py:46
  204.7 77.1 %collective-permute-start.47 = (bf16[2,256,768]{2,1,0:T(8,128)(2,1)}, bf16[2,256,768]{2,1,0:T(8,128)(2,1)}, u32[]{:S(2)}, u32[]{:S(2)}) collective-permute-start(bf16[2,256,768]{2,1,0:T(8,128)(2,1)} %slice_bitcast_fusion.9), channel_id=1, source_target_pairs={{0,4},{1,5},{2,6},{3,7},{4,0},{5,1},{6,2},{7,3},{8,12},{9,13},{10,... | collective-permute-start | bytes 2359304 | tf_op jit(solution)/shard_map/ppermute | solution.py:46
  206.3 76.9 %collective-permute-start.44 = (bf16[2,256,768]{2,1,0:T(8,128)(2,1)}, bf16[2,256,768]{2,1,0:T(8,128)(2,1)}, u32[]{:S(2)}, u32[]{:S(2)}) collective-permute-start(bf16[2,256,768]{2,1,0:T(8,128)(2,1)} %slice_bitcast_fusion.12), channel_id=1, source_target_pairs={{0,2},{1,3},{2,0},{3,1},{4,6},{5,7},{6,4},{7,5},{8,10},{9,11},{10,... | collective-permute-start | bytes 2359304 | tf_op jit(solution)/shard_map/ppermute | solution.py:46
  207.8 76.8 %collective-permute-start.45 = (bf16[2,256,768]{2,1,0:T(8,128)(2,1)S(1)}, bf16[2,256,768]{2,1,0:T(8,128)(2,1)}, u32[]{:S(2)}, u32[]{:S(2)}) collective-permute-start(bf16[2,256,768]{2,1,0:T(8,128)(2,1)S(1)} %slice_bitcast_fusion.11), channel_id=1, source_target_pairs={{0,4},{1,5},{2,6},{3,7},{4,0},{5,1},{6,2},{7,3},{8,12},{9,13},{10,... | collective-permute-start | bytes 2359304 | tf_op jit(solution)/shard_map/ppermute | solution.py:46
  290.0 20.2 %collective-permute-start.51 = (bf16[256,768]{1,0:T(8,128)(2,1)}, bf16[256,768]{1,0:T(8,128)(2,1)}, u32[]{:S(2)}, u32[]{:S(2)}) collective-permute-start(bf16[256,768]{1,0:T(8,128)(2,1)} %slice_bitcast_fusion.35), channel_id=1, source_target_pairs={{0,2},{1,3},{2,0},{3,1},{4,6},{5,7},{6,4},{7,5},{8,10},{9,11},{10,... | collective-permute-start | bytes 1179656 | tf_op jit(solution)/shard_map/ppermute | solution.py:46
  291.5 19.9 %collective-permute-start.50 = (bf16[256,768]{1,0:T(8,128)(2,1)}, bf16[256,768]{1,0:T(8,128)(2,1)}, u32[]{:S(2)}, u32[]{:S(2)}) collective-permute-start(bf16[256,768]{1,0:T(8,128)(2,1)} %slice_bitcast_fusion.36), channel_id=1, source_target_pairs={{0,4},{1,5},{2,6},{3,7},{4,0},{5,1},{6,2},{7,3},{8,12},{9,13},{10,... | collective-permute-start | bytes 1179656 | tf_op jit(solution)/shard_map/ppermute | solution.py:46
  376.7 32.0 %collective-permute-start.58 = (bf16[1,128,768]{2,1,0:T(8,128)(2,1)S(1)}, bf16[1,128,768]{2,1,0:T(8,128)(2,1)S(1)}, u32[]{:S(2)}, u32[]{:S(2)}) collective-permute-start(bf16[1,128,768]{2,1,0:T(8,128)(2,1)S(1)} %bitcast.509), channel_id=1, source_target_pairs={{0,2},{1,3},{2,0},{3,1},{4,6},{5,7},{6,4},{7,5},{8,10},{9,11},{10,... | collective-permute-start | bytes 589832 | tf_op jit(solution)/shard_map/ppermute | solution.py:46
  410.3 24.7 %collective-permute-start.59 = (bf16[2,128,768]{2,1,0:T(8,128)(2,1)}, bf16[2,128,768]{2,1,0:T(8,128)(2,1)}, u32[]{:S(2)}, u32[]{:S(2)}) collective-permute-start(bf16[2,128,768]{2,1,0:T(8,128)(2,1)} %pad_maximum_fusion.7), channel_id=1, source_target_pairs={{0,4},{1,5},{2,6},{3,7},{4,0},{5,1},{6,2},{7,3},{8,12},{9,13},{10,... | collective-permute-start | bytes 1179656 | tf_op jit(solution)/shard_map/ppermute | solution.py:46
  545.0 34.2 %collective-permute-start.72 = (f32[192,1920]{1,0:T(8,128)S(1)}, f32[192,1920]{1,0:T(8,128)S(1)}, u32[]{:S(2)}, u32[]{:S(2)}) collective-permute-start(f32[192,1920]{1,0:T(8,128)S(1)} %dynamic-slice_bitcast_fusion), channel_id=1, source_target_pairs={{0,8},{8,16},{16,24},{24,0},{1,9},{9,17},{17,25},{25,1},{2,10},{10... | collective-permute-start | bytes 4423688 | tf_op jit(solution)/shard_map/ppermute | solution.py:51
  610.3 33.5 %collective-permute-start.73 = (f32[192,1920]{1,0:T(8,128)S(1)}, f32[192,1920]{1,0:T(8,128)S(1)}, u32[]{:S(2)}, u32[]{:S(2)}) collective-permute-start(f32[192,1920]{1,0:T(8,128)S(1)} %bitcast_add_fusion.1), channel_id=1, source_target_pairs={{0,8},{8,16},{16,24},{24,0},{1,9},{9,17},{17,25},{25,1},{2,10},{10... | collective-permute-start | bytes 4423688 | tf_op jit(solution)/shard_map/ppermute | solution.py:51
  645.1 49.5 %collective-permute-start.74 = (f32[192,1920]{1,0:T(8,128)}, f32[192,1920]{1,0:T(8,128)}, u32[]{:S(2)}, u32[]{:S(2)}) collective-permute-start(f32[192,1920]{1,0:T(8,128)} %bitcast_add_fusion.2), channel_id=1, source_target_pairs={{0,8},{8,16},{16,24},{24,0},{1,9},{9,17},{17,25},{25,1},{2,10},{10... | collective-permute-start | bytes 4423688 | tf_op jit(solution)/shard_map/ppermute | solution.py:51
  655.2 33.9 %collective-permute-start.77 = (bf16[512,192]{0,1:T(8,128)(2,1)S(1)}, bf16[512,192]{0,1:T(8,128)(2,1)S(1)}, u32[]{:S(2)}, u32[]{:S(2)}) collective-permute-start(bf16[512,192]{0,1:T(8,128)(2,1)S(1)} %get-tuple-element.279), channel_id=1, source_target_pairs={{0,24},{8,0},{16,8},{24,16},{1,25},{9,1},{17,9},{25,17},{2,26},{10... | collective-permute-start | bytes 589832 | tf_op jit(solution)/shard_map/ppermute | solution.py:51
  659.1 35.4 %collective-permute-start.76 = (bf16[512,192]{0,1:T(8,128)(2,1)S(1)}, bf16[512,192]{0,1:T(8,128)(2,1)S(1)}, u32[]{:S(2)}, u32[]{:S(2)}) collective-permute-start(bf16[512,192]{0,1:T(8,128)(2,1)S(1)} %get-tuple-element.280), channel_id=1, source_target_pairs={{0,16},{8,24},{16,0},{24,8},{1,17},{9,25},{17,1},{25,9},{2,18},{10... | collective-permute-start | bytes 589832 | tf_op jit(solution)/shard_map/ppermute | solution.py:51
  659.1 35.4 %collective-permute-start.75 = (bf16[512,192]{0,1:T(8,128)(2,1)S(1)}, bf16[512,192]{0,1:T(8,128)(2,1)S(1)}, u32[]{:S(2)}, u32[]{:S(2)}) collective-permute-start(bf16[512,192]{0,1:T(8,128)(2,1)S(1)} %get-tuple-element.281), channel_id=1, source_target_pairs={{0,8},{8,16},{16,24},{24,0},{1,9},{9,17},{17,25},{25,1},{2,10},{10... | collective-permute-start | bytes 589832 | tf_op jit(solution)/shard_map/ppermute | solution.py:51
  694.6 29.8 %collective-permute-start.78 = (f32[16,456,128]{2,1,0:T(8,128)}, f32[16,456,128]{2,1,0:T(8,128)}, u32[]{:S(2)}, u32[]{:S(2)}) collective-permute-start(f32[16,456,128]{2,1,0:T(8,128)} %get-tuple-element.191), channel_id=1, source_target_pairs={{0,1},{1,0},{2,3},{3,2},{4,5},{5,4},{6,7},{7,6},{8,9},{9,8},{10,11... | collective-permute-start | bytes 11206664 | tf_op jit(solution)/shard_map/ppermute | solution.py:46
  728.1 35.5 %collective-permute-start.81 = (f32[16,456,128]{2,1,0:T(8,128)}, f32[16,456,128]{2,1,0:T(8,128)}, u32[]{:S(2)}, u32[]{:S(2)}) collective-permute-start(f32[16,456,128]{2,1,0:T(8,128)} %get-tuple-element.196), channel_id=1, source_target_pairs={{0,1},{1,0},{2,3},{3,2},{4,5},{5,4},{6,7},{7,6},{8,9},{9,8},{10,11... | collective-permute-start | bytes 11206664 | tf_op jit(solution)/shard_map/ppermute | solution.py:46
  730.1 30.9 %collective-permute-start.80 = (bf16[2,2,456,128]{3,2,0,1:T(8,128)(2,1)S(1)}, bf16[2,2,456,128]{3,2,0,1:T(8,128)(2,1)}, u32[]{:S(2)}, u32[]{:S(2)}) collective-permute-start(bf16[2,2,456,128]{3,2,0,1:T(8,128)(2,1)S(1)} %fusion.110), channel_id=1, source_target_pairs={{0,4},{1,5},{2,6},{3,7},{4,0},{5,1},{6,2},{7,3},{8,12},{9,13},{10,... | collective-permute-start | bytes 1400840 | tf_op jit(solution)/shard_map/ppermute | solution.py:46
  731.8 30.7 %collective-permute-start.79 = (bf16[2,2,456,128]{3,2,0,1:T(8,128)(2,1)S(1)}, bf16[2,2,456,128]{3,2,0,1:T(8,128)(2,1)S(1)}, u32[]{:S(2)}, u32[]{:S(2)}) collective-permute-start(bf16[2,2,456,128]{3,2,0,1:T(8,128)(2,1)S(1)} %fusion.109), channel_id=1, source_target_pairs={{0,2},{1,3},{2,0},{3,1},{4,6},{5,7},{6,4},{7,5},{8,10},{9,11},{10,... | collective-permute-start | bytes 1400840 | tf_op jit(solution)/shard_map/ppermute | solution.py:46
  768.0 55.8 %collective-permute-start.86 = (f32[16,456,128]{2,1,0:T(8,128)}, f32[16,456,128]{2,1,0:T(8,128)}, u32[]{:S(2)}, u32[]{:S(2)}) collective-permute-start(f32[16,456,128]{2,1,0:T(8,128)} %get-tuple-element.203), channel_id=1, source_target_pairs={{0,1},{1,0},{2,3},{3,2},{4,5},{5,4},{6,7},{7,6},{8,9},{9,8},{10,11... | collective-permute-start | bytes 11206664 | tf_op jit(solution)/shard_map/ppermute | solution.py:46
  829.3 43.1 %collective-permute-start.91 = (bf16[2,456,128]{2,1,0:T(8,128)(2,1)S(1)}, bf16[2,456,128]{2,1,0:T(8,128)(2,1)S(1)}, u32[]{:S(2)}, u32[]{:S(2)}) collective-permute-start(bf16[2,456,128]{2,1,0:T(8,128)(2,1)S(1)} %fusion.161), channel_id=1, source_target_pairs={{0,4},{1,5},{2,6},{3,7},{4,0},{5,1},{6,2},{7,3},{8,12},{9,13},{10,... | collective-permute-start | bytes 700424 | tf_op jit(solution)/shard_map/ppermute | solution.py:46
  830.4 42.2 %collective-permute-start.90 = (bf16[2,456,128]{2,1,0:T(8,128)(2,1)S(1)}, bf16[2,456,128]{2,1,0:T(8,128)(2,1)S(1)}, u32[]{:S(2)}, u32[]{:S(2)}) collective-permute-start(bf16[2,456,128]{2,1,0:T(8,128)(2,1)S(1)} %fusion.160), channel_id=1, source_target_pairs={{0,2},{1,3},{2,0},{3,1},{4,6},{5,7},{6,4},{7,5},{8,10},{9,11},{10,... | collective-permute-start | bytes 700424 | tf_op jit(solution)/shard_map/ppermute | solution.py:46
  831.8 39.2 %collective-permute-start.87 = (f32[456,128]{1,0:T(8,128)}, f32[456,128]{1,0:T(8,128)S(1)}, u32[]{:S(2)}, u32[]{:S(2)}) collective-permute-start(f32[456,128]{1,0:T(8,128)} %get-tuple-element.210), channel_id=1, source_target_pairs={{0,8},{8,16},{16,24},{24,0},{1,9},{9,17},{17,25},{25,1},{2,10},{10... | collective-permute-start | bytes 700424 | tf_op jit(solution)/shard_map/ppermute | solution.py:51
  834.2 48.1 %collective-permute-start.93 = (bf16[2,2,456,128]{3,2,0,1:T(8,128)(2,1)S(1)}, bf16[2,2,456,128]{3,2,0,1:T(8,128)(2,1)S(1)}, u32[]{:S(2)}, u32[]{:S(2)}) collective-permute-start(bf16[2,2,456,128]{3,2,0,1:T(8,128)(2,1)S(1)} %fusion.114), channel_id=1, source_target_pairs={{0,4},{1,5},{2,6},{3,7},{4,0},{5,1},{6,2},{7,3},{8,12},{9,13},{10,... | collective-permute-start | bytes 1400840 | tf_op jit(solution)/shard_map/ppermute | solution.py:46
  834.7 56.4 %collective-permute-start.94 = (f32[16,464,128]{2,1,0:T(8,128)}, f32[16,464,128]{2,1,0:T(8,128)S(1)}, u32[]{:S(2)}, u32[]{:S(2)}) collective-permute-start(f32[16,464,128]{2,1,0:T(8,128)} %get-tuple-element.215), channel_id=1, source_target_pairs={{0,1},{1,0},{2,3},{3,2},{4,5},{5,4},{6,7},{7,6},{8,9},{9,8},{10,11... | collective-permute-start | bytes 11403272 | tf_op jit(solution)/shard_map/ppermute | solution.py:46
  894.8 22.3 %collective-permute-start.103 = (bf16[2,2,464,128]{3,2,0,1:T(8,128)(2,1)S(1)}, bf16[2,2,464,128]{3,2,0,1:T(8,128)(2,1)S(1)}, u32[]{:S(2)}, u32[]{:S(2)}) collective-permute-start(bf16[2,2,464,128]{3,2,0,1:T(8,128)(2,1)S(1)} %fusion.105), channel_id=1, source_target_pairs={{0,4},{1,5},{2,6},{3,7},{4,0},{5,1},{6,2},{7,3},{8,12},{9,13},{10,... | collective-permute-start | bytes 1425416 | tf_op jit(solution)/shard_map/ppermute | solution.py:46
  895.3 20.2 %collective-permute-start.105 = (bf16[2,2,464,128]{3,2,0,1:T(8,128)(2,1)S(1)}, bf16[2,2,464,128]{3,2,0,1:T(8,128)(2,1)S(1)}, u32[]{:S(2)}, u32[]{:S(2)}) collective-permute-start(bf16[2,2,464,128]{3,2,0,1:T(8,128)(2,1)S(1)} %fusion.106), channel_id=1, source_target_pairs={{0,2},{1,3},{2,0},{3,1},{4,6},{5,7},{6,4},{7,5},{8,10},{9,11},{10,... | collective-permute-start | bytes 1425416 | tf_op jit(solution)/shard_map/ppermute | solution.py:46
  923.0 17.5 %collective-permute-start.102 = (f32[456,128]{1,0:T(8,128)S(1)}, f32[456,128]{1,0:T(8,128)S(1)}, u32[]{:S(2)}, u32[]{:S(2)}) collective-permute-start(f32[456,128]{1,0:T(8,128)S(1)} %fusion.165), channel_id=1, source_target_pairs={{0,8},{8,16},{16,24},{24,0},{1,9},{9,17},{17,25},{25,1},{2,10},{10... | collective-permute-start | bytes 700424 | tf_op jit(solution)/shard_map/ppermute | solution.py:51
  (208 other events, 2204.7 us)
Sparse Core Ops, SparseCore 0:
  10.2 78.9 all-gather.3
  161.4 126.1 all-gather.5
  695.8 46.8 all-gather.7

commit v4 on v3

--- a/solution.py
+++ b/solution.py
@@ -87,18 +87,9 @@
     return value
 
 
-def relative_order(table, per_device):
-    here = lax.axis_index("vocab")
-    table = table.reshape(4, 2, 2, 2, per_device)
-    for axis, bit in ((1, DEEP), (2, ACROSS), (3, CORE)):
-        table = jnp.where((here & bit) != 0, jnp.flip(table, axis), table)
-    return table
-
-
-def rolled(table, downward):
+def upward(table):
     z = lax.axis_index("dp")
-    order = (z - jnp.arange(4)) % 4 if downward else (z + jnp.arange(4)) % 4
-    return [lax.dynamic_index_in_dim(table, order[k], keepdims=False) for k in range(4)]
+    return [lax.dynamic_index_in_dim(table, (z + k) % 4, keepdims=False) for k in range(4)]
 
 
 def rows_of_tiles(tiles):
@@ -139,7 +130,7 @@
     )(tiles)
 
 
-def place_kernel(rows, *refs, places, count, per):
+def place_kernel(spot, rows, *refs, places, count, per):
     arrivals = refs[: len(places)]
     targets = refs[len(places) : len(places) + 5]
     tail = refs[len(places) + 5]
@@ -156,7 +147,11 @@
 
     def lines(block, start, size):
         stage[pl.ds(0, size), :] = landed[block, pl.ds(start, size), :].astype(jnp.float32)
-        base = block * per + start
+        if places[0] is None:
+            owner = block
+        else:
+            owner = ((spot[0] + 4 - block // 8) % 4) * 8 + (spot[1] ^ (block % 8))
+        base = owner * per + start
         for u in range(size):
             full[pl.ds(rows[base + u], 1), :] = stage[pl.ds(u, 1), :]
 
@@ -210,11 +205,11 @@
     tail_copy.wait()
 
 
-def place_tiles(rows, arrivals, places, count, per):
+def place_tiles(spot, rows, arrivals, places, count, per):
     shapes = [jax.ShapeDtypeStruct((h, a * TILE), jnp.bfloat16) for _, h, a in MATRICES]
     return pl.pallas_call(
         functools.partial(place_kernel, places=places, count=count, per=per),
-        in_specs=[pl.BlockSpec(memory_space=pltpu.SMEM)] + [pl.BlockSpec(memory_space=pl.ANY)] * len(arrivals),
+        in_specs=[pl.BlockSpec(memory_space=pltpu.SMEM)] * 2 + [pl.BlockSpec(memory_space=pl.ANY)] * len(arrivals),
         out_specs=[pl.BlockSpec(memory_space=pl.ANY)] * 6,
         out_shape=shapes + [jax.ShapeDtypeStruct((TAIL_TILES, TILE), jnp.float32)],
         scratch_shapes=[
@@ -229,14 +224,14 @@
         compiler_params=pltpu.CompilerParams(vmem_limit_bytes=VMEM_LIMIT),
         cost_estimate=pl.CostEstimate(flops=0, bytes_accessed=180_000_000, transcendentals=0),
         name="place_tiles",
-    )(rows, *arrivals)
+    )(spot, rows, *arrivals)
 
 
 def step_size(rows):
     return max(n for n in range(8, 193, 8) if rows % n == 0)
 
 
-def collect_kernel(rows, *refs, outs, blocks, per, begin):
+def collect_kernel(spot, rows, *refs, outs, blocks, per, begin):
     sources, targets = refs[:6], refs[6 : 6 + outs]
     full, sems = refs[6 + outs :]
     block = pl.program_id(0)
@@ -263,7 +258,11 @@
 
     size = step_size(targets[0].shape[1])
     for n, target in enumerate(targets):
-        base = (n * blocks + block) * per + begin
+        if outs == 1:
+            owner = block
+        else:
+            owner = ((spot[0] + block // 4) % 4) * 8 + (spot[1] ^ ((block % 4) * 2 + n))
+        base = owner * per + begin
 
         def one_step(i, carry, target=target, base=base):
             start = pl.multiple_of(i * size, 8)
@@ -274,19 +273,19 @@
         lax.fori_loop(0, target.shape[1] // size, one_step, 0)
 
 
-def collect_tiles(rows, sources, tiles_all, per, outs, begin, lines):
+def collect_tiles(spot, rows, sources, tiles_all, per, outs, begin, lines):
     blocks = tiles_all // per // outs
     return pl.pallas_call(
         functools.partial(collect_kernel, outs=outs, blocks=blocks, per=per, begin=begin),
         grid=(blocks,),
-        in_specs=[pl.BlockSpec(memory_space=pltpu.SMEM)] + [pl.BlockSpec(memory_space=pl.ANY)] * 6,
+        in_specs=[pl.BlockSpec(memory_space=pltpu.SMEM)] * 2 + [pl.BlockSpec(memory_space=pl.ANY)] * 6,
         out_specs=[pl.BlockSpec((1, lines, TILE), lambda i: (i, 0, 0))] * outs,
         out_shape=[jax.ShapeDtypeStruct((blocks, lines, TILE), jnp.float32)] * outs,
         scratch_shapes=[pltpu.VMEM((tiles_all, TILE), jnp.float32), pltpu.SemaphoreType.DMA((61,))],
         compiler_params=pltpu.CompilerParams(vmem_limit_bytes=VMEM_LIMIT),
         cost_estimate=pl.CostEstimate(flops=0, bytes_accessed=80_000_000, transcendentals=0),
         name="collect_tiles",
-    )(rows, *sources)
+    )(spot, rows, *sources)
 
 
 def array_multiply(left_side, right_side):
@@ -513,7 +512,7 @@
     return (weight - learn_rate * (update + weight_decay * weight), new_first, new_second)
 
 
-def gather_student(tiles):
+def gather_student(tiles, beside):
     per = tiles.shape[0]
     half = per // 16 * 8
     arrivals, places = [], []
@@ -525,6 +524,8 @@
 
     for plane in range(4):
         across, deep = swap(tiles, ACROSS), swap(tiles, DEEP)
+        if plane == 3:
+            across, deep, beside = together(across, deep, beside)
         keep(tiles, plane, 0, 0)
         keep(across, plane, 1, 0)
         keep(deep, plane, 2, 0)
@@ -532,7 +533,7 @@
         keep(swap(deep[half:], ACROSS), plane, 3, half)
         if plane < 3:
             tiles = shift(tiles, 1)
-    return arrivals, places
+    return arrivals, places, beside
 
 
 def sent_low(value, bit):
@@ -576,6 +577,7 @@
     planes = lax.axis_size("dp")
     group = lax.axis_size("vocab")
     here = lax.axis_index("vocab")
+    spot = jnp.stack([lax.axis_index("dp"), here]).astype(jnp.int32)
 
     facts = jnp.concatenate([token_ids.reshape(LEN), lengths, mask_count, jnp.zeros((TILE - 2,), jnp.int32)])
     target_rows = rows_of_tiles(owner_order)
@@ -594,24 +596,25 @@
 
     if near:
         plane_facts = gather_near(facts)
-        by_plane = [facts, shift(facts, 1), shift(facts, 2), shift(facts, 3)]
-        other_facts = gather_near(jnp.stack(by_plane[1:]))
-        all_facts = jnp.concatenate([plane_facts[:, None], other_facts], axis=1)
-        relative = relative_order(target_rows, per)
-        downward = jnp.stack(rolled(relative, True)).reshape(-1)
-        upward = jnp.stack(rolled(relative.transpose(0, 3, 1, 2, 4), False), axis=1).reshape(-1)
-        arrivals, places = gather_student(student_low)
         far_ids, close_ids = plane_facts[4:, :LEN], plane_facts[:4, :LEN]
         shape = (2, 2, LEN, D)
-        looked_t = rows_t(close_ids).reshape(shape) + swap(rows_t(far_ids).reshape(shape), CORE)
-        looked_s = rows_s(close_ids).reshape(shape) + swap(rows_s(far_ids).reshape(shape), CORE)
-        arrivals, teacher_flat, looked_t, looked_s = lax.optimization_barrier(
-            (arrivals, teacher_flat, looked_t, looked_s)
+        beside = [
+            rows_t(close_ids).reshape(shape) + swap(rows_t(far_ids).reshape(shape), CORE),
+            rows_s(close_ids).reshape(shape),
+            rows_s(far_ids).reshape(shape),
+        ]
+        arrivals, places, beside = gather_student(student_low, beside)
+        looked_t = beside[0]
+        looked_s = beside[1] + swap(beside[2], CORE)
+        arrivals, teacher_flat, looked_t, looked_s, target_rows = together(
+            arrivals, teacher_flat, looked_t, looked_s, target_rows
         )
         teacher_tiles = lax.all_gather(teacher_flat, ("dp", "vocab"), axis=0, tiled=True)
         looked_t, looked_s = plane_hop(looked_t), plane_hop(looked_s)
-        matrices = place_tiles(downward, arrivals, tuple(places), planes * group, per)
-        matrices, looked_t, looked_s = together(matrices, looked_t, looked_s)
+        matrices = place_tiles(spot, target_rows, arrivals, tuple(places), planes * group, per)
+        matrices, looked_t, looked_s, facts = together(matrices, looked_t, looked_s, facts)
+        other_facts = gather_near(jnp.stack([shift(facts, 1), shift(facts, 2), shift(facts, 3)]))
+        all_facts = jnp.concatenate([plane_facts[:, None], other_facts], axis=1)
         looked_s = plane_end(*looked_s).astype(jnp.float32)
         looked_t = plane_end(*looked_t).astype(jnp.float32)
     else:
@@ -626,7 +629,7 @@
             for rows in (rows_t(plane_ids), rows_s(plane_ids))
         )
         matrices = place_tiles(
-            target_rows, [student_tiles.reshape(planes * group, per, TILE)], (None,), planes * group, per
+            spot, target_rows, [student_tiles.reshape(planes * group, per, TILE)], (None,), planes * group, per
         )
     student = pieces_of(matrices[:5], matrices[5])
     final_s, saved = layer_forward(student, looked_s, lengths)
@@ -720,21 +723,18 @@
     )
     grad_final = grad_final.at[offsets].add(grad_rows)
     if near:
-        heads = rolled(head_grad.reshape(4, width_share, vocab_rows), False)
+        heads = upward(head_grad.reshape(4, width_share, vocab_rows))
         moving = shift(heads[3], 1)
         grad_sum_one, feed_grads = feed_backward(student, saved, grad_final)
-        grad_sum_one, moving = together(grad_sum_one, moving)
-        moving = shift(heads[2] + moving, 1)
         layer_grads, grad_embedded = attention_backward(student, saved, grad_sum_one, feed_grads, lengths)
         grad_embedded, moving = together(grad_embedded, moving)
-        moving = shift(heads[1] + moving, 1)
     else:
         grad_sum_one, feed_grads = feed_backward(student, saved, grad_final)
         layer_grads, grad_embedded = attention_backward(student, saved, grad_sum_one, feed_grads, lengths)
 
     shares = grad_embedded.astype(jnp.bfloat16).reshape(LEN, planes, width_share).transpose(1, 0, 2)
     if near:
-        own = rolled(shares, False)
+        own = upward(shares)
         shares = jnp.stack([own[0]] + [shift(own[k], k) for k in (1, 2, 3)])
         ids = all_facts[:, :, :LEN].reshape(2, 2, 2, planes, LEN)
         for axis, bit in ((0, CORE), (1, DEEP), (2, ACROSS)):
@@ -745,40 +745,36 @@
         ids = all_facts[:, :, :LEN]
     token_grads = lax.all_gather(shares.reshape(-1, width_share), "vocab", axis=0, tiled=True)
     if near:
-        step = per // 32 * 8
-        edges = (0, step, 2 * step, 3 * step, per)
+        edges = (0, 640, 1256, per)
 
         def collect(n):
-            return collect_tiles(upward, layer_grads, tiles_all, per, 2, edges[n], edges[n + 1] - edges[n])
-
-        one = collect(0)
-        one, moving, shares = together(one, moving, shares)
+            return collect_tiles(spot, target_rows, layer_grads, tiles_all, per, 2, edges[n], edges[n + 1] - edges[n])
+
+        one, shares = together(collect(0), shares)
+        moving = shift(heads[2] + moving, 1)
         token_grads = lax.all_gather(shares.reshape(-1, width_share), "vocab", axis=0, tiled=True)
-        head_part = heads[0] + moving
         chip_one = one[0] + swap(one[1], CORE)
-        chip_one, two = together(chip_one, collect(1))
+        chip_one, two, moving = together(chip_one, collect(1), moving)
+        moving = shift(heads[1] + moving, 1)
         first_one = plane_first(chip_one)
         chip_two = two[0] + swap(two[1], CORE)
-        first_one, chip_two, three = together(first_one, chip_two, collect(2))
+        first_one, chip_two, three, token_grads = together(first_one, chip_two, collect(2), token_grads)
+        token_part = matmul_left(token_grads, chosen(ids))
         blocks_one = plane_second(*first_one)
         first_two = plane_first(chip_two)
         chip_three = three[0] + swap(three[1], CORE)
-        blocks_one, first_two, chip_three, token_grads, four = together(
-            blocks_one, first_two, chip_three, token_grads, collect(3)
+        blocks_one, first_two, chip_three, token_part, moving = together(
+            blocks_one, first_two, chip_three, token_part, moving
         )
-        token_part = matmul_left(token_grads, chosen(ids))
+        head_part = heads[0] + moving
         blocks_two = plane_second(*first_two)
-        first_three = plane_first(chip_three)
-        chip_four = four[0] + swap(four[1], CORE)
-        blocks_two, first_three, chip_four, token_part = together(blocks_two, first_three, chip_four, token_part)
-        blocks_three = plane_second(*first_three)
-        blocks_four = plane_second(*plane_first(chip_four))
-        sums = [ring_sum(blocks) for blocks in (blocks_one, blocks_two, blocks_three, blocks_four)]
+        blocks_three = plane_second(*plane_first(chip_three))
+        sums = [ring_sum(blocks) for blocks in (blocks_one, blocks_two, blocks_three)]
         flat_grad = jnp.concatenate(sums)
     else:
         token_grads = lax.all_gather(shares.reshape(-1, width_share), "vocab", axis=0, tiled=True)
         token_part = matmul_left(token_grads, chosen(ids))
-        (grad_tiles,) = collect_tiles(target_rows, layer_grads, tiles_all, per, 1, 0, per)
+        (grad_tiles,) = collect_tiles(spot, target_rows, layer_grads, tiles_all, per, 1, 0, per)
         flat_grad = lax.psum_scatter(
             grad_tiles.reshape(tiles_all, TILE), ("dp", "vocab"), scatter_dimension=0, tiled=True
         )

time: 994 us -> 1010 us (1.016)
  waiting for transfers between devices: 237 us -> 286 us
  between operations: 40.5 us -> 24.7 us
  Pallas kernels: 211 us -> 197 us
  local copies, waits for them, and re-layouts: 67.4 us -> 54 us
    ppermute x89 -> x84, waiting for transfers between devices: 101 us -> 170 us  [swap(): return lax.ppermute(value, 'vocab', [(i, i ^ bit) for i in range(8)])]
    ppermute x24 -> x21, waiting for transfers between devices: 128 us -> 108 us  [shift(): lax.ppermute(value, 'dp', [(i, (i + steps) % size) for i in range(size)])]
    pallas_call x4 -> x3, Pallas kernels: 119 us -> 98.9 us  [collect_tiles(): pl.pallas_call(functools.partial(collect_kernel, outs=outs, blocks=blocks...]
    ppermute x24 -> x21, starting transfers between devices: 30.5 us -> 38.8 us  [shift(): lax.ppermute(value, 'dp', [(i, (i + steps) % size) for i in range(size)])]
    ppermute x89 -> x84, starting transfers between devices: 68.8 us -> 62.8 us  [swap(): return lax.ppermute(value, 'vocab', [(i, i ^ bit) for i in range(8)])]
  transfers between devices with their start and end apart: 118 -> 110, of which waited for: 48 -> 48; matrix products, arithmetic and copies ran while one was open for 29% -> 27% of each run, Pallas kernels for 19% -> 17%
where the time goes in v4:
time: 1010 us; the launch traced here: 1000 us
  waiting for transfers between devices  286 us (28%)
  matrix products  228 us (23%)
  Pallas kernels  197 us (20%)
  other arithmetic  113 us (11%)
  starting transfers between devices  102 us (10%)
  local copies, waits for them, and re-layouts  54 us (5%)
  between operations  24.7 us (2%)
    ppermute x84, waiting for transfers between devices, swap(): return lax.ppermute(value, 'vocab', [(i, i ^ bit) for i in range(8)])  170 us
    ppermute x21, waiting for transfers between devices, shift(): lax.ppermute(value, 'dp', [(i, (i + steps) % size) for i in range(size)])  108 us
    pallas_call x3, Pallas kernels, collect_tiles(): pl.pallas_call(functools.partial(collect_kernel, outs=outs, blocks=blocks...  98.9 us
    dot_general x10, matrix products, array_multiply(): return jnp.dot(left_side, right_side, preferred_element_type=jnp.float32)  77.6 us
    pallas_call x1, Pallas kernels, place_tiles(): pl.pallas_call(functools.partial(place_kernel, places=places, count=count...  76.4 us
    ppermute x84, starting transfers between devices, swap(): return lax.ppermute(value, 'vocab', [(i, i ^ bit) for i in range(8)])  62.8 us
    dot_general x6, matrix products, matmul_left(): lax.dot_general(left_side, right_side, (((0,), (0,)), ((), ())), preferre...  59.3 us
    dot_general x9, matrix products, trailing_array_multiply(): lax.dot_general(left_side, right_side, (((1,), (1,)), ((), ())), preferre...  47.9 us
  transfers between devices with their start and end apart: 110, of which 48 were waited for; matrix products, arithmetic and copies ran while one was open for 27% of the time, Pallas kernels for 17%

profile of v4, /device:TPU:0, one launch (start us, length us, event | category | flops | bytes accessed | tf_op | source)
XLA Modules:
  0.0 1004.2 jit_solution(1346095322623018465)
XLA Ops:
  20.3 7.3 fusion.53
  30.4 22.3 %collective-permute-done.9.refs_10_ = bf16[1832,128]{1,0:T(8,128)(2,1)S(1)} collective-permute-done((bf16[1832,128]{1,0:T(8,128)(2,1)S(1)}, bf16[1832,128]{1,0:T(8,128)(2,1)S(1)}, u32[]{:S(2)}, u32[]{:S(2)}) %collective-permute-start.9) | collective-permute-done | bytes 469024 | tf_op jit(solution)/shard_map/ppermute | solution.py:51
  52.7 9.4 collective-permute-start.19
  62.1 24.0 %collective-permute-done.19.refs_20_ = bf16[1832,128]{1,0:T(8,128)(2,1)S(1)} collective-permute-done((bf16[1832,128]{1,0:T(8,128)(2,1)S(1)}, bf16[1832,128]{1,0:T(8,128)(2,1)S(1)}, u32[]{:S(2)}, u32[]{:S(2)}) %collective-permute-start.19) | collective-permute-done | bytes 469024 | tf_op jit(solution)/shard_map/ppermute | solution.py:51
  86.1 10.2 %collective-permute-start.29 = (bf16[1832,128]{1,0:T(8,128)(2,1)S(1)}, bf16[1832,128]{1,0:T(8,128)(2,1)}, u32[]{:S(2)}, u32[]{:S(2)}) collective-permute-start(bf16[1832,128]{1,0:T(8,128)(2,1)S(1)} %collective-permute-done.19.refs_20_), channel_id=1, source_target_pairs={{0,8},{8,16},{16,24},{24,0},{1,9},{9,17},{17,25},{25,1},{2,10},{10... | collective-permute-start | bytes 1406984 | tf_op jit(solution)/shard_map/ppermute | solution.py:51
  96.3 7.3 fusion.51
  103.7 7.6 collective-permute-done.29.refs_30_
  116.8 9.3 fusion.54
  126.1 7.9 fusion.52
  136.9 10.5 %collective-permute-done.1.refs_2_ = bf16[1832,128]{1,0:T(8,128)(2,1)S(1)} collective-permute-done((bf16[1832,128]{1,0:T(8,128)(2,1)S(1)}, bf16[1832,128]{1,0:T(8,128)(2,1)S(1)}, u32[]{:S(2)}, u32[]{:S(2)}) %collective-permute-start.1) | collective-permute-done | bytes 469024 | tf_op jit(solution)/shard_map/ppermute | solution.py:46
  149.9 12.7 %collective-permute-done.5.refs_6_ = bf16[912,128]{1,0:T(8,128)(2,1)S(1)} collective-permute-done((bf16[912,128]{1,0:T(8,128)(2,1)S(1)}, bf16[912,128]{1,0:T(8,128)(2,1)S(1)}, u32[]{:S(2)}, u32[]{:S(2)}) %collective-permute-start.5) | collective-permute-done | bytes 233504 | tf_op jit(solution)/shard_map/ppermute | solution.py:46
  164.9 10.9 %collective-permute-done.11.refs_12_ = bf16[1832,128]{1,0:T(8,128)(2,1)S(1)} collective-permute-done((bf16[1832,128]{1,0:T(8,128)(2,1)S(1)}, bf16[1832,128]{1,0:T(8,128)(2,1)S(1)}, u32[]{:S(2)}, u32[]{:S(2)}) %collective-permute-start.11) | collective-permute-done | bytes 469024 | tf_op jit(solution)/shard_map/ppermute | solution.py:46
  179.5 13.6 %collective-permute-done.15.refs_16_ = bf16[912,128]{1,0:T(8,128)(2,1)S(1)} collective-permute-done((bf16[912,128]{1,0:T(8,128)(2,1)S(1)}, bf16[912,128]{1,0:T(8,128)(2,1)S(1)}, u32[]{:S(2)}, u32[]{:S(2)}) %collective-permute-start.15) | collective-permute-done | bytes 233504 | tf_op jit(solution)/shard_map/ppermute | solution.py:46
  195.6 10.8 %collective-permute-done.21.refs_22_ = bf16[1832,128]{1,0:T(8,128)(2,1)S(1)} collective-permute-done((bf16[1832,128]{1,0:T(8,128)(2,1)S(1)}, bf16[1832,128]{1,0:T(8,128)(2,1)S(1)}, u32[]{:S(2)}, u32[]{:S(2)}) %collective-permute-start.21) | collective-permute-done | bytes 469024 | tf_op jit(solution)/shard_map/ppermute | solution.py:46
  209.1 6.7 collective-permute-done.25.refs_26_
  220.8 6.4 collective-permute-done.39.refs_36_
  244.7 76.4 %place_tiles.1 = (bf16[768,2304]{1,0:T(8,128)(2,1)}, bf16[768,768]{1,0:T(8,128)(2,1)}, bf16[768,3072]{1,0:T(8,128)(2,1)}, bf16[3072,768]{1,0:T(8,128)(2,1)}, bf1...) custom-call(s32[2]{0:T(128)} %pad_add_fusion.6.spot, s32[58624]{0:T(1024)} %fusion.128.rows, bf16[1832,128]{1,0:T(8,128)(2,1)} %copy-done.48, ...), custom_call_target="tpu_custom_call" | custom-call | bytes 180000000 | tf_op jit(solution)/shard_map/place_tiles/pallas_call | solution.py:210
  347.9 8.5 collective-permute-done.48
  382.2 19.8 %fusion.17 = (bf16[512,3072]{1,0:T(8,128)(2,1)S(1)}, f32[512,3072]{1,0:T(8,128)}) fusion(f32[3072]{0:T(1024)S(1)} %slice_bitcast_fusion.56, bf16[768,3072]{1,0:T(8,128)(2,1)} %get-tuple-element.172, f32[512,768]{1,0:T(8,128)S(1)} %get-tuple-element.327, f32[768]{0:T(1024)S(1)} %get-tuple-element.289, f32[768]{0:T(1024)S(1)} %get-tuple-element.290, ...), kind=kOutput, calls=%fused_computation.41 | convolution fusion | flops 2521694208 | bytes 15751168 | tf_op jit(solution)/shard_map/dot_general | solution.py:292
  417.6 6.2 unpack_matrix.9
  423.8 5.8 unpack_matrix.8
  434.9 5.7 fusion.50
  445.4 10.9 %fusion.248 = (f32[12,512]{1,0:T(8,128)S(1)}, f32[12,512,512]{1,2,0:T(8,128)}) fusion(pred[512]{0:T(512)(128)(4,1)S(1)} %iota_compare_fusion.17, bf16[1,512,3,12,64]{1,4,3,2,0:T(8,128)(2,1)} %bitcast.467), kind=kOutput, calls=%fused_computation.540 | convolution fusion | flops 415236608 | bytes 14180864 | tf_op jit(solution)/shard_map/sub | solution.py:370
  456.3 6.2 fusion.68
  467.1 23.3 %fusion.250 = (f32[512]{0:T(512)S(1)}, f32[512,768]{1,0:T(8,128)}) fusion(f32[768]{0:T(1024)S(1)} %get-tuple-element.278, bf16[3072,768]{1,0:T(8,128)(2,1)} %unpack_matrix.9, bf16[768,3072]{1,0:T(8,128)(2,1)} %unpack_matrix.8, f32[3072]{0:T(1024)S(1)} %slice_bitcast_fusion.55, f32[512,768]{1,0:T(8,128)} %copy-done.51, f32[768]{0:T(1024)S(1)} %get-tuple-element.279, ...), kind=kOutput, calls=%fused_computation.542 | convolution fusion | flops 4940365312 | bytes 12610560 | tf_op jit(solution)/shard_map/dot_general | solution.py:292
  500.1 5.5 collective-permute-done.61
  506.3 9.8 collective-permute-done.62
  539.9 7.7 multiply_convert_fusion.1
  590.4 8.4 convert_reduce_fusion
  598.8 6.6 multiply_reduce_fusion.5
  613.0 7.0 fusion.60
  620.0 9.0 multiply_reduce_fusion
  629.0 7.0 multiply_convert_fusion
  645.1 5.3 fusion.161.refs_0_
  661.7 5.5 fusion.226.refs_2_
  667.2 20.4 %collective-permute-done.72 = f32[192,1920]{1,0:T(8,128)} collective-permute-done((f32[192,1920]{1,0:T(8,128)}, f32[192,1920]{1,0:T(8,128)}, u32[]{:S(2)}, u32[]{:S(2)}) %collective-permute-start.72) | collective-permute-done | bytes 1474592 | tf_op jit(solution)/shard_map/ppermute | solution.py:51
  695.5 33.9 %collect_tiles.3 = (f32[16,640,128]{2,1,0:T(8,128)}, f32[16,640,128]{2,1,0:T(8,128)}) custom-call(s32[2]{0:T(128)} %pad_add_fusion.6.spot, s32[58624]{0:T(1024)} %fusion.128.rows, f32[768,2304]{1,0:T(8,128)} %fusion.161.refs_0_, f32[768,768]{1,0:T(8,128)} %fusion.186.refs_1_, f32[768,3072]{1,0:T(8,128)} %fusion.226.refs_2_, f32[3072,768]{1,0:T(8,128)} %fusion.189.refs_3_, ...), custom_call_target="tpu_custom_call" | custom-call | bytes 80000000 | tf_op jit(solution)/shard_map/collect_tiles/pallas_call | solution.py:278
  736.1 33.3 %collect_tiles.4 = (f32[16,616,128]{2,1,0:T(8,128)}, f32[16,616,128]{2,1,0:T(8,128)}) custom-call(s32[2]{0:T(128)} %pad_add_fusion.6.spot, s32[58624]{0:T(1024)} %fusion.128.rows, f32[768,2304]{1,0:T(8,128)} %fusion.161.refs_0_, f32[768,768]{1,0:T(8,128)} %fusion.186.refs_1_, f32[768,3072]{1,0:T(8,128)} %fusion.226.refs_2_, f32[3072,768]{1,0:T(8,128)} %fusion.189.refs_3_, ...), custom_call_target="tpu_custom_call" | custom-call | bytes 80000000 | tf_op jit(solution)/shard_map/collect_tiles/pallas_call | solution.py:278
  769.4 7.1 add.734
  780.3 31.7 %collect_tiles.5 = (f32[16,576,128]{2,1,0:T(8,128)}, f32[16,576,128]{2,1,0:T(8,128)}) custom-call(s32[2]{0:T(128)} %pad_add_fusion.6.spot, s32[58624]{0:T(1024)} %fusion.128.rows, f32[768,2304]{1,0:T(8,128)} %fusion.161.refs_0_, f32[768,768]{1,0:T(8,128)} %fusion.186.refs_1_, f32[768,3072]{1,0:T(8,128)} %fusion.226.refs_2_, f32[3072,768]{1,0:T(8,128)} %fusion.189.refs_3_, ...), custom_call_target="tpu_custom_call" | custom-call | bytes 80000000 | tf_op jit(solution)/shard_map/collect_tiles/pallas_call | solution.py:278
  822.4 9.7 collective-permute-done.79
  845.0 35.9 %fusion.1 = f32[192,1920]{1,0:T(8,128)S(1)} fusion(bf16[16384,192]{0,1:T(8,128)(2,1)S(1)} %copy-done.125, s32[16384]{0:T(1024)S(1)} %bitcast.494), kind=kOutput, calls=%fused_computation.5 | convolution fusion | flops 12111052800 | bytes 7831552 | tf_op jit(solution)/shard_map/dot_general | solution.py:296
  883.3 14.2 %collective-permute-done.84 = bf16[2,2,616,128]{3,2,0,1:T(8,128)(2,1)S(1)} collective-permute-done((bf16[2,2,616,128]{3,2,0,1:T(8,128)(2,1)S(1)}, bf16[2,2,616,128]{3,2,0,1:T(8,128)(2,1)S(1)}, u32[]{:S(2)}, u32[]{:S(2)}) %collective-permute-start.84) | collective-permute-done | bytes 630816 | tf_op jit(solution)/shard_map/ppermute | solution.py:46
  912.6 8.3 collective-permute-done.97
  922.5 5.4 collective-permute-done.98
  932.6 7.2 collective-permute-done.99
  940.2 6.4 collective-permute-done.93
  946.9 13.1 %collective-permute-done.100 = f32[576,128]{1,0:T(8,128)S(1)} collective-permute-done((f32[576,128]{1,0:T(8,128)S(1)}, f32[576,128]{1,0:T(8,128)S(1)}, u32[]{:S(2)}, u32[]{:S(2)}) %collective-permute-start.100) | collective-permute-done | bytes 294944 | tf_op jit(solution)/shard_map/ppermute | solution.py:51
  (749 shorter events, 341.4 us)
Async XLA Ops:
  7.2 109.6 %all-gather.4.cloned.1.call-start = ((), (), s32[]{:S(2)}) async-start(), calls=%async_computation | async-start | bytes 3686400 | tf_op jit(solution)/shard_map/all_gather | solution.py:585
  20.2 387.3 %all-gather.6.cloned.1.call-start = ((), (), s32[]{:S(2)}) async-start(), calls=%async_computation.1 | async-start | bytes 15476736 | tf_op jit(solution)/shard_map/all_gather | solution.py:612
  27.6 86.7 %collective-permute-start.36 = (bf16[2,2,512,768]{3,2,1,0:T(8,128)(2,1)S(1)}, bf16[2,2,512,768]{3,2,1,0:T(8,128)(2,1)S(1)}, u32[]{:S(2)}, u32[]{:S(2)}) collective-permute-start(bf16[2,2,512,768]{3,2,1,0:T(8,128)(2,1)S(1)} %bitcast.517), channel_id=1, source_target_pairs={{0,1},{1,0},{2,3},{3,2},{4,5},{5,4},{6,7},{7,6},{8,9},{9,8},{10,11... | collective-permute-start | bytes 9437192 | tf_op jit(solution)/shard_map/ppermute | solution.py:46
  28.2 24.5 %collective-permute-start.9 = (bf16[1832,128]{1,0:T(8,128)(2,1)S(1)}, bf16[1832,128]{1,0:T(8,128)(2,1)S(1)}, u32[]{:S(2)}, u32[]{:S(2)}) collective-permute-start(bf16[1832,128]{1,0:T(8,128)(2,1)S(1)} %convert_element_type.287.refs_0_), channel_id=1, source_target_pairs={{0,8},{8,16},{16,24},{24,0},{1,9},{9,17},{17,25},{25,1},{2,10},{10... | collective-permute-start | bytes 1406984 | tf_op jit(solution)/shard_map/ppermute | solution.py:51
  52.7 33.4 %collective-permute-start.19 = (bf16[1832,128]{1,0:T(8,128)(2,1)S(1)}, bf16[1832,128]{1,0:T(8,128)(2,1)S(1)}, u32[]{:S(2)}, u32[]{:S(2)}) collective-permute-start(bf16[1832,128]{1,0:T(8,128)(2,1)S(1)} %collective-permute-done.9.refs_10_), channel_id=1, source_target_pairs={{0,8},{8,16},{16,24},{24,0},{1,9},{9,17},{17,25},{25,1},{2,10},{10... | collective-permute-start | bytes 1406984 | tf_op jit(solution)/shard_map/ppermute | solution.py:51
  86.1 25.2 %collective-permute-start.29 = (bf16[1832,128]{1,0:T(8,128)(2,1)S(1)}, bf16[1832,128]{1,0:T(8,128)(2,1)}, u32[]{:S(2)}, u32[]{:S(2)}) collective-permute-start(bf16[1832,128]{1,0:T(8,128)(2,1)S(1)} %collective-permute-done.19.refs_20_), channel_id=1, source_target_pairs={{0,8},{8,16},{16,24},{24,0},{1,9},{9,17},{17,25},{25,1},{2,10},{10... | collective-permute-start | bytes 1406984 | tf_op jit(solution)/shard_map/ppermute | solution.py:51
  111.3 22.8 %collective-permute-start.32 = (bf16[1832,128]{1,0:T(8,128)(2,1)}, bf16[1832,128]{1,0:T(8,128)(2,1)}, u32[]{:S(2)}, u32[]{:S(2)}) collective-permute-start(bf16[1832,128]{1,0:T(8,128)(2,1)} %collective-permute-done.29.refs_30_), channel_id=1, source_target_pairs={{0,4},{1,5},{2,6},{3,7},{4,0},{5,1},{6,2},{7,3},{8,12},{9,13},{10,... | collective-permute-start | bytes 1406984 | tf_op jit(solution)/shard_map/ppermute | solution.py:46
  112.8 21.2 %collective-permute-start.31 = (bf16[1832,128]{1,0:T(8,128)(2,1)}, bf16[1832,128]{1,0:T(8,128)(2,1)}, u32[]{:S(2)}, u32[]{:S(2)}) collective-permute-start(bf16[1832,128]{1,0:T(8,128)(2,1)} %collective-permute-done.29.refs_30_), channel_id=1, source_target_pairs={{0,2},{1,3},{2,0},{3,1},{4,6},{5,7},{6,4},{7,5},{8,10},{9,11},{10,... | collective-permute-start | bytes 1406984 | tf_op jit(solution)/shard_map/ppermute | solution.py:46
  134.1 93.7 %collective-permute-start.43 = (bf16[2,2,512,768]{3,2,1,0:T(8,128)(2,1)S(1)}, bf16[2,2,512,768]{3,2,1,0:T(8,128)(2,1)S(1)}, u32[]{:S(2)}, u32[]{:S(2)}) collective-permute-start(bf16[2,2,512,768]{3,2,1,0:T(8,128)(2,1)S(1)} %bitcast.516), channel_id=1, source_target_pairs={{0,1},{1,0},{2,3},{3,2},{4,5},{5,4},{6,7},{7,6},{8,9},{9,8},{10,11... | collective-permute-start | bytes 9437192 | tf_op jit(solution)/shard_map/ppermute | solution.py:46
  135.3 27.4 %collective-permute-start = (bf16[1832,128]{1,0:T(8,128)(2,1)S(1)}, bf16[1832,128]{1,0:T(8,128)(2,1)S(1)}, u32[]{:S(2)}, u32[]{:S(2)}) collective-permute-start(bf16[1832,128]{1,0:T(8,128)(2,1)S(1)} %convert_element_type.287.refs_0_), channel_id=1, source_target_pairs={{0,1},{1,0},{2,3},{3,2},{4,5},{5,4},{6,7},{7,6},{8,9},{9,8},{10,11... | collective-permute-start | bytes 1406984 | tf_op jit(solution)/shard_map/ppermute | solution.py:46
  135.3 29.5 %collective-permute-start.13 = (bf16[1832,128]{1,0:T(8,128)(2,1)S(1)}, bf16[1832,128]{1,0:T(8,128)(2,1)S(1)}, u32[]{:S(2)}, u32[]{:S(2)}) collective-permute-start(bf16[1832,128]{1,0:T(8,128)(2,1)S(1)} %copy-done.64), channel_id=1, source_target_pairs={{0,4},{1,5},{2,6},{3,7},{4,0},{5,1},{6,2},{7,3},{8,12},{9,13},{10,... | collective-permute-start | bytes 1406984 | tf_op jit(solution)/shard_map/ppermute | solution.py:46
  147.3 15.3 %collective-permute-start.5 = (bf16[912,128]{1,0:T(8,128)(2,1)S(1)}, bf16[912,128]{1,0:T(8,128)(2,1)S(1)}, u32[]{:S(2)}, u32[]{:S(2)}) collective-permute-start(bf16[912,128]{1,0:T(8,128)(2,1)S(1)} %slice.711), channel_id=1, source_target_pairs={{0,4},{1,5},{2,6},{3,7},{4,0},{5,1},{6,2},{7,3},{8,12},{9,13},{10,... | collective-permute-start | bytes 700424 | tf_op jit(solution)/shard_map/ppermute | solution.py:46
  148.4 15.8 %collective-permute-start.7 = (bf16[920,128]{1,0:T(8,128)(2,1)S(1)}, bf16[920,128]{1,0:T(8,128)(2,1)S(1)}, u32[]{:S(2)}, u32[]{:S(2)}) collective-permute-start(bf16[920,128]{1,0:T(8,128)(2,1)S(1)} %slice.712), channel_id=1, source_target_pairs={{0,2},{1,3},{2,0},{3,1},{4,6},{5,7},{6,4},{7,5},{8,10},{9,11},{10,... | collective-permute-start | bytes 706568 | tf_op jit(solution)/shard_map/ppermute | solution.py:46
  175.8 19.5 %collective-permute-start.23 = (bf16[1832,128]{1,0:T(8,128)(2,1)S(1)}, bf16[1832,128]{1,0:T(8,128)(2,1)S(1)}, u32[]{:S(2)}, u32[]{:S(2)}) collective-permute-start(bf16[1832,128]{1,0:T(8,128)(2,1)S(1)} %copy-done.66), channel_id=1, source_target_pairs={{0,4},{1,5},{2,6},{3,7},{4,0},{5,1},{6,2},{7,3},{8,12},{9,13},{10,... | collective-permute-start | bytes 1406984 | tf_op jit(solution)/shard_map/ppermute | solution.py:46
  176.3 16.8 %collective-permute-start.15 = (bf16[912,128]{1,0:T(8,128)(2,1)S(1)}, bf16[912,128]{1,0:T(8,128)(2,1)S(1)}, u32[]{:S(2)}, u32[]{:S(2)}) collective-permute-start(bf16[912,128]{1,0:T(8,128)(2,1)S(1)} %slice.713), channel_id=1, source_target_pairs={{0,4},{1,5},{2,6},{3,7},{4,0},{5,1},{6,2},{7,3},{8,12},{9,13},{10,... | collective-permute-start | bytes 700424 | tf_op jit(solution)/shard_map/ppermute | solution.py:46
  178.0 16.7 %collective-permute-start.17 = (bf16[920,128]{1,0:T(8,128)(2,1)S(1)}, bf16[920,128]{1,0:T(8,128)(2,1)S(1)}, u32[]{:S(2)}, u32[]{:S(2)}) collective-permute-start(bf16[920,128]{1,0:T(8,128)(2,1)S(1)} %slice.714), channel_id=1, source_target_pairs={{0,2},{1,3},{2,0},{3,1},{4,6},{5,7},{6,4},{7,5},{8,10},{9,11},{10,... | collective-permute-start | bytes 706568 | tf_op jit(solution)/shard_map/ppermute | solution.py:46
  234.0 605.5 %all-gather.8.cloned.1.call-start = ((), (), s32[]{:S(2)}) async-start(), calls=%async_computation.2 | async-start | bytes 7077888 | tf_op jit(solution)/shard_map/all_gather | solution.py:755
  237.5 83.6 %collective-permute-start.46 = (bf16[2,256,768]{2,1,0:T(8,128)(2,1)}, bf16[2,256,768]{2,1,0:T(8,128)(2,1)}, u32[]{:S(2)}, u32[]{:S(2)}) collective-permute-start(bf16[2,256,768]{2,1,0:T(8,128)(2,1)} %slice_bitcast_fusion.10), channel_id=1, source_target_pairs={{0,2},{1,3},{2,0},{3,1},{4,6},{5,7},{6,4},{7,5},{8,10},{9,11},{10,... | collective-permute-start | bytes 2359304 | tf_op jit(solution)/shard_map/ppermute | solution.py:46
  241.1 81.7 %collective-permute-start.47 = (bf16[2,256,768]{2,1,0:T(8,128)(2,1)}, bf16[2,256,768]{2,1,0:T(8,128)(2,1)}, u32[]{:S(2)}, u32[]{:S(2)}) collective-permute-start(bf16[2,256,768]{2,1,0:T(8,128)(2,1)} %slice_bitcast_fusion.9), channel_id=1, source_target_pairs={{0,4},{1,5},{2,6},{3,7},{4,0},{5,1},{6,2},{7,3},{8,12},{9,13},{10,... | collective-permute-start | bytes 2359304 | tf_op jit(solution)/shard_map/ppermute | solution.py:46
  242.5 81.8 %collective-permute-start.44 = (bf16[2,256,768]{2,1,0:T(8,128)(2,1)}, bf16[2,256,768]{2,1,0:T(8,128)(2,1)}, u32[]{:S(2)}, u32[]{:S(2)}) collective-permute-start(bf16[2,256,768]{2,1,0:T(8,128)(2,1)} %slice_bitcast_fusion.12), channel_id=1, source_target_pairs={{0,2},{1,3},{2,0},{3,1},{4,6},{5,7},{6,4},{7,5},{8,10},{9,11},{10,... | collective-permute-start | bytes 2359304 | tf_op jit(solution)/shard_map/ppermute | solution.py:46
  243.1 82.5 %collective-permute-start.45 = (bf16[2,256,768]{2,1,0:T(8,128)(2,1)S(1)}, bf16[2,256,768]{2,1,0:T(8,128)(2,1)}, u32[]{:S(2)}, u32[]{:S(2)}) collective-permute-start(bf16[2,256,768]{2,1,0:T(8,128)(2,1)S(1)} %slice_bitcast_fusion.11), channel_id=1, source_target_pairs={{0,4},{1,5},{2,6},{3,7},{4,0},{5,1},{6,2},{7,3},{8,12},{9,13},{10,... | collective-permute-start | bytes 2359304 | tf_op jit(solution)/shard_map/ppermute | solution.py:46
  338.5 26.9 %collective-permute-start.51 = (bf16[256,768]{1,0:T(8,128)(2,1)}, bf16[256,768]{1,0:T(8,128)(2,1)}, u32[]{:S(2)}, u32[]{:S(2)}) collective-permute-start(bf16[256,768]{1,0:T(8,128)(2,1)} %slice_bitcast_fusion.35), channel_id=1, source_target_pairs={{0,2},{1,3},{2,0},{3,1},{4,6},{5,7},{6,4},{7,5},{8,10},{9,11},{10,... | collective-permute-start | bytes 1179656 | tf_op jit(solution)/shard_map/ppermute | solution.py:46
  340.1 26.7 %collective-permute-start.50 = (bf16[256,768]{1,0:T(8,128)(2,1)}, bf16[256,768]{1,0:T(8,128)(2,1)}, u32[]{:S(2)}, u32[]{:S(2)}) collective-permute-start(bf16[256,768]{1,0:T(8,128)(2,1)} %slice_bitcast_fusion.36), channel_id=1, source_target_pairs={{0,4},{1,5},{2,6},{3,7},{4,0},{5,1},{6,2},{7,3},{8,12},{9,13},{10,... | collective-permute-start | bytes 1179656 | tf_op jit(solution)/shard_map/ppermute | solution.py:46
  432.0 32.0 %collective-permute-start.58 = (bf16[1,128,768]{2,1,0:T(8,128)(2,1)S(1)}, bf16[1,128,768]{2,1,0:T(8,128)(2,1)S(1)}, u32[]{:S(2)}, u32[]{:S(2)}) collective-permute-start(bf16[1,128,768]{2,1,0:T(8,128)(2,1)S(1)} %bitcast.455), channel_id=1, source_target_pairs={{0,2},{1,3},{2,0},{3,1},{4,6},{5,7},{6,4},{7,5},{8,10},{9,11},{10,... | collective-permute-start | bytes 589832 | tf_op jit(solution)/shard_map/ppermute | solution.py:46
  465.6 24.8 %collective-permute-start.59 = (bf16[2,128,768]{2,1,0:T(8,128)(2,1)}, bf16[2,128,768]{2,1,0:T(8,128)(2,1)}, u32[]{:S(2)}, u32[]{:S(2)}) collective-permute-start(bf16[2,128,768]{2,1,0:T(8,128)(2,1)} %pad_maximum_fusion.7), channel_id=1, source_target_pairs={{0,4},{1,5},{2,6},{3,7},{4,0},{5,1},{6,2},{7,3},{8,12},{9,13},{10,... | collective-permute-start | bytes 1179656 | tf_op jit(solution)/shard_map/ppermute | solution.py:46
  653.1 34.5 %collective-permute-start.72 = (f32[192,1920]{1,0:T(8,128)}, f32[192,1920]{1,0:T(8,128)}, u32[]{:S(2)}, u32[]{:S(2)}) collective-permute-start(f32[192,1920]{1,0:T(8,128)} %dynamic-slice_bitcast_fusion), channel_id=1, source_target_pairs={{0,8},{8,16},{16,24},{24,0},{1,9},{9,17},{17,25},{25,1},{2,10},{10... | collective-permute-start | bytes 4423688 | tf_op jit(solution)/shard_map/ppermute | solution.py:51
  692.8 36.6 %collective-permute-start.75 = (bf16[512,192]{0,1:T(8,128)(2,1)}, bf16[512,192]{0,1:T(8,128)(2,1)S(1)}, u32[]{:S(2)}, u32[]{:S(2)}) collective-permute-start(bf16[512,192]{0,1:T(8,128)(2,1)} %get-tuple-element.269), channel_id=1, source_target_pairs={{0,24},{8,0},{16,8},{24,16},{1,25},{9,1},{17,9},{25,17},{2,26},{10... | collective-permute-start | bytes 589832 | tf_op jit(solution)/shard_map/ppermute | solution.py:51
  692.8 36.6 %collective-permute-start.74 = (bf16[512,192]{0,1:T(8,128)(2,1)S(1)}, bf16[512,192]{0,1:T(8,128)(2,1)S(1)}, u32[]{:S(2)}, u32[]{:S(2)}) collective-permute-start(bf16[512,192]{0,1:T(8,128)(2,1)S(1)} %get-tuple-element.270), channel_id=1, source_target_pairs={{0,16},{8,24},{16,0},{24,8},{1,17},{9,25},{17,1},{25,9},{2,18},{10... | collective-permute-start | bytes 589832 | tf_op jit(solution)/shard_map/ppermute | solution.py:51
  692.8 36.6 %collective-permute-start.73 = (bf16[512,192]{0,1:T(8,128)(2,1)S(1)}, bf16[512,192]{0,1:T(8,128)(2,1)}, u32[]{:S(2)}, u32[]{:S(2)}) collective-permute-start(bf16[512,192]{0,1:T(8,128)(2,1)S(1)} %get-tuple-element.271), channel_id=1, source_target_pairs={{0,8},{8,16},{16,24},{24,0},{1,9},{9,17},{17,25},{25,1},{2,10},{10... | collective-permute-start | bytes 589832 | tf_op jit(solution)/shard_map/ppermute | solution.py:51
  731.5 37.9 %collective-permute-start.76 = (f32[16,640,128]{2,1,0:T(8,128)}, f32[16,640,128]{2,1,0:T(8,128)}, u32[]{:S(2)}, u32[]{:S(2)}) collective-permute-start(f32[16,640,128]{2,1,0:T(8,128)} %get-tuple-element.190), channel_id=1, source_target_pairs={{0,1},{1,0},{2,3},{3,2},{4,5},{5,4},{6,7},{7,6},{8,9},{9,8},{10,11... | collective-permute-start | bytes 15728648 | tf_op jit(solution)/shard_map/ppermute | solution.py:46
  734.6 41.9 %collective-permute-start.77 = (f32[192,1920]{1,0:T(8,128)}, f32[192,1920]{1,0:T(8,128)}, u32[]{:S(2)}, u32[]{:S(2)}) collective-permute-start(f32[192,1920]{1,0:T(8,128)} %bitcast_add_fusion.2), channel_id=1, source_target_pairs={{0,8},{8,16},{16,24},{24,0},{1,9},{9,17},{17,25},{25,1},{2,10},{10... | collective-permute-start | bytes 4423688 | tf_op jit(solution)/shard_map/ppermute | solution.py:51
  776.5 57.9 %collective-permute-start.80 = (f32[16,616,128]{2,1,0:T(8,128)}, f32[16,616,128]{2,1,0:T(8,128)}, u32[]{:S(2)}, u32[]{:S(2)}) collective-permute-start(f32[16,616,128]{2,1,0:T(8,128)} %get-tuple-element.196), channel_id=1, source_target_pairs={{0,1},{1,0},{2,3},{3,2},{4,5},{5,4},{6,7},{7,6},{8,9},{9,8},{10,11... | collective-permute-start | bytes 15138824 | tf_op jit(solution)/shard_map/ppermute | solution.py:46
  815.0 17.0 %collective-permute-start.79 = (bf16[2,2,640,128]{3,2,0,1:T(8,128)(2,1)S(1)}, bf16[2,2,640,128]{3,2,0,1:T(8,128)(2,1)S(1)}, u32[]{:S(2)}, u32[]{:S(2)}) collective-permute-start(bf16[2,2,640,128]{3,2,0,1:T(8,128)(2,1)S(1)} %fusion.104), channel_id=1, source_target_pairs={{0,4},{1,5},{2,6},{3,7},{4,0},{5,1},{6,2},{7,3},{8,12},{9,13},{10,... | collective-permute-start | bytes 1966088 | tf_op jit(solution)/shard_map/ppermute | solution.py:46
  816.0 17.2 %collective-permute-start.78 = (bf16[2,2,640,128]{3,2,0,1:T(8,128)(2,1)S(1)}, bf16[2,2,640,128]{3,2,0,1:T(8,128)(2,1)S(1)}, u32[]{:S(2)}, u32[]{:S(2)}) collective-permute-start(bf16[2,2,640,128]{3,2,0,1:T(8,128)(2,1)S(1)} %fusion.103), channel_id=1, source_target_pairs={{0,2},{1,3},{2,0},{3,1},{4,6},{5,7},{6,4},{7,5},{8,10},{9,11},{10,... | collective-permute-start | bytes 1966088 | tf_op jit(solution)/shard_map/ppermute | solution.py:46
  820.6 78.6 %collective-permute-start.86 = (f32[192,1920]{1,0:T(8,128)}, f32[192,1920]{1,0:T(8,128)}, u32[]{:S(2)}, u32[]{:S(2)}) collective-permute-start(f32[192,1920]{1,0:T(8,128)} %bitcast_add_fusion.1), channel_id=1, source_target_pairs={{0,8},{8,16},{16,24},{24,0},{1,9},{9,17},{17,25},{25,1},{2,10},{10... | collective-permute-start | bytes 4423688 | tf_op jit(solution)/shard_map/ppermute | solution.py:51
  842.6 39.8 %collective-permute-start.82 = (bf16[2,640,128]{2,1,0:T(8,128)(2,1)S(1)}, bf16[2,640,128]{2,1,0:T(8,128)(2,1)S(1)}, u32[]{:S(2)}, u32[]{:S(2)}) collective-permute-start(bf16[2,640,128]{2,1,0:T(8,128)(2,1)S(1)} %fusion.114), channel_id=1, source_target_pairs={{0,4},{1,5},{2,6},{3,7},{4,0},{5,1},{6,2},{7,3},{8,12},{9,13},{10,... | collective-permute-start | bytes 983048 | tf_op jit(solution)/shard_map/ppermute | solution.py:46
  843.4 55.1 %collective-permute-start.85 = (f32[16,576,128]{2,1,0:T(8,128)}, f32[16,576,128]{2,1,0:T(8,128)S(1)}, u32[]{:S(2)}, u32[]{:S(2)}) collective-permute-start(f32[16,576,128]{2,1,0:T(8,128)} %get-tuple-element.204), channel_id=1, source_target_pairs={{0,1},{1,0},{2,3},{3,2},{4,5},{5,4},{6,7},{7,6},{8,9},{9,8},{10,11... | collective-permute-start | bytes 14155784 | tf_op jit(solution)/shard_map/ppermute | solution.py:46
  843.5 39.6 %collective-permute-start.81 = (bf16[2,640,128]{2,1,0:T(8,128)(2,1)S(1)}, bf16[2,640,128]{2,1,0:T(8,128)(2,1)S(1)}, u32[]{:S(2)}, u32[]{:S(2)}) collective-permute-start(bf16[2,640,128]{2,1,0:T(8,128)(2,1)S(1)} %fusion.113), channel_id=1, source_target_pairs={{0,2},{1,3},{2,0},{3,1},{4,6},{5,7},{6,4},{7,5},{8,10},{9,11},{10,... | collective-permute-start | bytes 983048 | tf_op jit(solution)/shard_map/ppermute | solution.py:46
  881.1 16.4 %collective-permute-start.84 = (bf16[2,2,616,128]{3,2,0,1:T(8,128)(2,1)S(1)}, bf16[2,2,616,128]{3,2,0,1:T(8,128)(2,1)S(1)}, u32[]{:S(2)}, u32[]{:S(2)}) collective-permute-start(bf16[2,2,616,128]{3,2,0,1:T(8,128)(2,1)S(1)} %fusion.106), channel_id=1, source_target_pairs={{0,4},{1,5},{2,6},{3,7},{4,0},{5,1},{6,2},{7,3},{8,12},{9,13},{10,... | collective-permute-start | bytes 1892360 | tf_op jit(solution)/shard_map/ppermute | solution.py:46
  882.4 16.1 %collective-permute-start.83 = (bf16[2,2,616,128]{3,2,0,1:T(8,128)(2,1)S(1)}, bf16[2,2,616,128]{3,2,0,1:T(8,128)(2,1)S(1)}, u32[]{:S(2)}, u32[]{:S(2)}) collective-permute-start(bf16[2,2,616,128]{3,2,0,1:T(8,128)(2,1)S(1)} %fusion.105), channel_id=1, source_target_pairs={{0,2},{1,3},{2,0},{3,1},{4,6},{5,7},{6,4},{7,5},{8,10},{9,11},{10,... | collective-permute-start | bytes 1892360 | tf_op jit(solution)/shard_map/ppermute | solution.py:46
  903.1 19.2 %collective-permute-start.95 = (bf16[2,2,576,128]{3,2,0,1:T(8,128)(2,1)S(1)}, bf16[2,2,576,128]{3,2,0,1:T(8,128)(2,1)S(1)}, u32[]{:S(2)}, u32[]{:S(2)}) collective-permute-start(bf16[2,2,576,128]{3,2,0,1:T(8,128)(2,1)S(1)} %fusion.107), channel_id=1, source_target_pairs={{0,4},{1,5},{2,6},{3,7},{4,0},{5,1},{6,2},{7,3},{8,12},{9,13},{10,... | collective-permute-start | bytes 1769480 | tf_op jit(solution)/shard_map/ppermute | solution.py:46
  904.5 16.4 %collective-permute-start.97 = (bf16[2,2,576,128]{3,2,0,1:T(8,128)(2,1)S(1)}, bf16[2,2,576,128]{3,2,0,1:T(8,128)(2,1)S(1)}, u32[]{:S(2)}, u32[]{:S(2)}) collective-permute-start(bf16[2,2,576,128]{3,2,0,1:T(8,128)(2,1)S(1)} %fusion.108), channel_id=1, source_target_pairs={{0,2},{1,3},{2,0},{3,1},{4,6},{5,7},{6,4},{7,5},{8,10},{9,11},{10,... | collective-permute-start | bytes 1769480 | tf_op jit(solution)/shard_map/ppermute | solution.py:46
  909.8 20.9 %collective-permute-start.92 = (f32[616,128]{1,0:T(8,128)S(1)}, f32[616,128]{1,0:T(8,128)S(1)}, u32[]{:S(2)}, u32[]{:S(2)}) collective-permute-start(f32[616,128]{1,0:T(8,128)S(1)} %slice_bitcast_fusion.43), channel_id=1, source_target_pairs={{0,8},{8,16},{16,24},{24,0},{1,9},{9,17},{17,25},{25,1},{2,10},{10... | collective-permute-start | bytes 946184 | tf_op jit(solution)/shard_map/ppermute | solution.py:51
  912.0 18.9 %collective-permute-start.88 = (f32[640,128]{1,0:T(8,128)S(1)}, f32[640,128]{1,0:T(8,128)S(1)}, u32[]{:S(2)}, u32[]{:S(2)}) collective-permute-start(f32[640,128]{1,0:T(8,128)S(1)} %add.745), channel_id=1, source_target_pairs={{0,8},{8,16},{16,24},{24,0},{1,9},{9,17},{17,25},{25,1},{2,10},{10... | collective-permute-start | bytes 983048 | tf_op jit(solution)/shard_map/ppermute | solution.py:51
  930.8 15.8 %collective-permute-start.93 = (f32[616,128]{1,0:T(8,128)S(1)}, f32[616,128]{1,0:T(8,128)S(1)}, u32[]{:S(2)}, u32[]{:S(2)}) collective-permute-start(f32[616,128]{1,0:T(8,128)S(1)} %fusion.117), channel_id=1, source_target_pairs={{0,8},{8,16},{16,24},{24,0},{1,9},{9,17},{17,25},{25,1},{2,10},{10... | collective-permute-start | bytes 946184 | tf_op jit(solution)/shard_map/ppermute | solution.py:51
  931.0 33.4 %collective-permute-start.89 = (f32[640,128]{1,0:T(8,128)S(1)}, f32[640,128]{1,0:T(8,128)S(1)}, u32[]{:S(2)}, u32[]{:S(2)}) collective-permute-start(f32[640,128]{1,0:T(8,128)S(1)} %add.746), channel_id=1, source_target_pairs={{0,8},{8,16},{16,24},{24,0},{1,9},{9,17},{17,25},{25,1},{2,10},{10... | collective-permute-start | bytes 983048 | tf_op jit(solution)/shard_map/ppermute | solution.py:51
  939.9 20.1 %collective-permute-start.100 = (f32[576,128]{1,0:T(8,128)S(1)}, f32[576,128]{1,0:T(8,128)S(1)}, u32[]{:S(2)}, u32[]{:S(2)}) collective-permute-start(f32[576,128]{1,0:T(8,128)S(1)} %fusion.122), channel_id=1, source_target_pairs={{0,8},{8,16},{16,24},{24,0},{1,9},{9,17},{17,25},{25,1},{2,10},{10... | collective-permute-start | bytes 884744 | tf_op jit(solution)/shard_map/ppermute | solution.py:51
  946.7 19.1 %collective-permute-start.94 = (f32[616,128]{1,0:T(8,128)S(1)}, f32[616,128]{1,0:T(8,128)S(1)}, u32[]{:S(2)}, u32[]{:S(2)}) collective-permute-start(f32[616,128]{1,0:T(8,128)S(1)} %fusion.118), channel_id=1, source_target_pairs={{0,8},{8,16},{16,24},{24,0},{1,9},{9,17},{17,25},{25,1},{2,10},{10... | collective-permute-start | bytes 946184 | tf_op jit(solution)/shard_map/ppermute | solution.py:51
  (207 other events, 2733.3 us)
Sparse Core Ops, SparseCore 0:
  20.3 83.0 all-gather.3
  234.2 118.7 all-gather.5
  731.6 45.0 all-gather.7

commit v5 on v4

--- a/solution.py
+++ b/solution.py
@@ -1,4 +1,5 @@
 import functools
+import math
 
 import jax
 import jax.numpy as jnp
@@ -24,6 +25,7 @@
 MATRICES = (QKV, OUT, UP, DOWN, PLACE)
 TAIL = 58368
 TAIL_TILES = 88
+HOME_ORDER = (UP, DOWN, QKV, OUT, PLACE)
 
 VMEM_LIMIT = 60 * 1024 * 1024
 
@@ -72,11 +74,9 @@
     return lax.optimization_barrier(values)
 
 
-def ring_sum(value):
-    moving = shift(value[3], 1)
-    moving = shift(value[2] + moving, 1)
-    moving = shift(value[1] + moving, 1)
-    return value[0] + moving
+def ring_hop(blocks):
+    moving = shift(blocks[-1], 1)
+    return [*blocks[:-2], blocks[-2] + moving]
 
 
 def sum_everywhere(value):
@@ -92,13 +92,229 @@
     return [lax.dynamic_index_in_dim(table, (z + k) % 4, keepdims=False) for k in range(4)]
 
 
-def rows_of_tiles(tiles):
-    rows = tiles
-    for first, height, across in MATRICES:
-        inside = (tiles >= first) & (tiles < first + height * across)
+def shares_of(tiles_all, devices):
+    sizes = [height * across // devices for _, height, across in HOME_ORDER]
+    sizes.append((tiles_all - TAIL) // devices)
+    starts = [sum(sizes[:n]) for n in range(len(sizes))]
+    return sizes, starts
+
+
+def homes_of(tiles, tiles_all, devices):
+    per = tiles_all // devices
+    sizes, starts = shares_of(tiles_all, devices)
+    homes = ((tiles - TAIL) // sizes[-1]) * per + starts[-1] + (tiles - TAIL) % sizes[-1]
+    for (first, height, across), size, start in zip(HOME_ORDER, sizes, starts):
         at = tiles - first
-        rows = jnp.where(inside, first + (at % across) * height + at // across, rows)
-    return rows
+        line = (at % across) * height + at // across
+        inside = (at >= 0) & (at < height * across)
+        homes = jnp.where(inside, (line // size) * per + start + line % size, homes)
+    return homes
+
+
+def room(per, devices):
+    mean = per / devices
+    return int(-(-(mean + 5.0 * mean**0.5) // 8) * 8)
+
+
+def row_steps(total, size, step):
+    whole, rest = divmod(total, size)
+
+    def body(i, carry):
+        step(i * size, size)
+        return carry
+
+    lax.fori_loop(0, whole, body, 0)
+    if rest:
+        step(whole * size, rest)
+
+
+def send_kernel(slots, lines, tiles, packed, index, stage, *, per):
+    slot_count = packed.shape[0]
+
+    def clear(start, size):
+        for u in range(size):
+            index[start + u] = per
+
+    row_steps(slot_count + 8, 64, clear)
+    stage[...] = jnp.zeros_like(stage)
+
+    def place(start, size):
+        for u in range(size):
+            slot = slots[start + u]
+            stage[pl.ds(slot, 1), :] = tiles[pl.ds(start + u, 1), :]
+            index[slot] = lines[start + u]
+
+    row_steps(per, 64, place)
+    packed[...] = stage[pl.ds(0, slot_count), :].astype(packed.dtype)
+
+
+def send_tiles(slots, lines, tiles, slot_count):
+    per = tiles.shape[0]
+    return pl.pallas_call(
+        functools.partial(send_kernel, per=per),
+        in_specs=[pl.BlockSpec(memory_space=pltpu.SMEM)] * 2 + [pl.BlockSpec(memory_space=pltpu.VMEM)],
+        out_specs=[pl.BlockSpec(memory_space=pltpu.VMEM), pl.BlockSpec(memory_space=pltpu.SMEM)],
+        out_shape=[
+            jax.ShapeDtypeStruct((slot_count, TILE), jnp.bfloat16),
+            jax.ShapeDtypeStruct((slot_count + 8,), jnp.int32),
+        ],
+        scratch_shapes=[pltpu.VMEM((slot_count + 8, TILE), jnp.float32)],
+        name="send_tiles",
+    )(slots, lines, tiles)
+
+
+def land_kernel(index, packed, tiles, stage, full):
+    stage[...] = packed[...].astype(jnp.float32)
+
+    def place(start, size):
+        for u in range(size):
+            full[pl.ds(index[start + u], 1), :] = stage[pl.ds(start + u, 1), :]
+
+    row_steps(packed.shape[0], 128, place)
+    tiles[...] = full[pl.ds(0, tiles.shape[0]), :].astype(tiles.dtype)
+
+
+def land_tiles(index, packed, per):
+    slot_count = packed.shape[0]
+    return pl.pallas_call(
+        land_kernel,
+        in_specs=[pl.BlockSpec(memory_space=pltpu.SMEM), pl.BlockSpec(memory_space=pltpu.VMEM)],
+        out_specs=pl.BlockSpec(memory_space=pltpu.VMEM),
+        out_shape=jax.ShapeDtypeStruct((per, TILE), jnp.bfloat16),
+        scratch_shapes=[pltpu.VMEM((slot_count, TILE), jnp.float32), pltpu.VMEM((per + 8, TILE), jnp.float32)],
+        name="land_tiles",
+    )(index, packed)
+
+
+def pick_kernel(index, source, target, *, count):
+    def pick(start, size):
+        for u in range(size):
+            target[pl.ds(start + u, 1), :] = source[pl.ds(index[start + u], 1), :]
+
+    row_steps(count, 128, pick)
+
+
+def pick_tiles(index, source, count):
+    return pl.pallas_call(
+        functools.partial(pick_kernel, count=count),
+        in_specs=[pl.BlockSpec(memory_space=pltpu.SMEM), pl.BlockSpec(memory_space=pltpu.VMEM)],
+        out_specs=pl.BlockSpec(memory_space=pltpu.VMEM),
+        out_shape=jax.ShapeDtypeStruct((count, TILE), source.dtype),
+        name="pick_tiles",
+    )(index, source)
+
+
+def assemble_kernel(spot, *refs, places, sizes, starts):
+    arrivals = refs[: len(places)]
+    targets = refs[len(places) : len(places) + 5]
+    tail = refs[len(places) + 5]
+    landed, sems = refs[len(places) + 6 :]
+    copies = []
+    for n, (arrival, place) in enumerate(zip(arrivals, places)):
+        target = landed.at[place[0], pl.ds(place[1], place[2])]
+        copies.append(pltpu.make_async_copy(arrival, target, sems.at[n]))
+    for copy in copies:
+        copy.start()
+    for copy in copies:
+        copy.wait()
+
+    def one_device(block, carry):
+        owner = ((spot[0] + 4 - block // 8) % 4) * 8 + (spot[1] ^ (block % 8))
+        for target, (_, height, _), size, start in zip(targets, HOME_ORDER, sizes, starts):
+            unit = math.gcd(size, height)
+            for part in range(size // unit):
+                line = owner * size + part * unit
+                column = line // height
+                target[
+                    pl.ds(pl.multiple_of(line - column * height, 16), unit),
+                    pl.ds(pl.multiple_of(column * TILE, TILE), TILE),
+                ] = landed[block, pl.ds(start + part * unit, unit), :]
+        tail[owner] = landed[block, pl.ds(starts[-1], sizes[-1]), :].astype(jnp.float32)
+        return carry
+
+    lax.fori_loop(0, landed.shape[0], one_device, 0)
+
+
+def assemble_layer(spot, arrivals, places, tiles_all, devices):
+    sizes, starts = shares_of(tiles_all, devices)
+    return pl.pallas_call(
+        functools.partial(assemble_kernel, places=places, sizes=sizes, starts=starts),
+        in_specs=[pl.BlockSpec(memory_space=pltpu.SMEM)] + [pl.BlockSpec(memory_space=pl.ANY)] * len(arrivals),
+        out_specs=[pl.BlockSpec(memory_space=pltpu.VMEM)] * 6,
+        out_shape=[jax.ShapeDtypeStruct((h, a * TILE), jnp.bfloat16) for _, h, a in HOME_ORDER]
+        + [jax.ShapeDtypeStruct((devices, sizes[-1], TILE), jnp.float32)],
+        scratch_shapes=[
+            pltpu.VMEM((devices, tiles_all // devices, TILE), jnp.bfloat16),
+            pltpu.SemaphoreType.DMA((len(arrivals),)),
+        ],
+        compiler_params=pltpu.CompilerParams(vmem_limit_bytes=VMEM_LIMIT),
+        cost_estimate=pl.CostEstimate(flops=0, bytes_accessed=60_000_000, transcendentals=0),
+        name="assemble_layer",
+    )(spot, *arrivals)
+
+
+def split_kernel(spot, *refs, count, sizes):
+    near, far = refs[2 * count :]
+    start = 0
+    for n in range(count):
+        near[0, pl.ds(start, sizes[n]), :] = refs[n][0]
+        far[0, pl.ds(start, sizes[n]), :] = refs[count + n][0]
+        start += sizes[n]
+
+
+def split_cores(spot, parts):
+    sizes = [part.shape[1] for part in parts]
+    total = sum(sizes)
+
+    def owner(block, spot, core):
+        return ((spot[0] + block // 4) % 4) * 8 + (spot[1] ^ ((block % 4) * 2 + core))
+
+    specs = [
+        pl.BlockSpec((1, size, TILE), lambda i, spot, core=core: (owner(i, spot, core), 0, 0))
+        for core in (0, 1)
+        for size in sizes
+    ]
+    return pl.pallas_call(
+        functools.partial(split_kernel, count=len(parts), sizes=sizes),
+        grid_spec=pltpu.PrefetchScalarGridSpec(
+            num_scalar_prefetch=1,
+            grid=(16,),
+            in_specs=specs,
+            out_specs=[pl.BlockSpec((1, total, TILE), lambda i, spot: (i, 0, 0))] * 2,
+        ),
+        out_shape=[jax.ShapeDtypeStruct((16, total, TILE), jnp.float32)] * 2,
+        cost_estimate=pl.CostEstimate(flops=0, bytes_accessed=32 * total * TILE * 8, transcendentals=0),
+        name="split_cores",
+    )(spot, *parts, *parts)
+
+
+def weight_grad_kernel(left, right, target):
+    product = lax.dot_general(
+        left[...], right[...], (((0,), (0,)), ((), ())), preferred_element_type=jnp.float32
+    )
+    for column in range(target.shape[0]):
+        target[column] = product[:, column * TILE : (column + 1) * TILE]
+
+
+def weight_grad(left, right, columns):
+    rows, height = left.shape
+    across = right.shape[1] // TILE
+    return pl.pallas_call(
+        weight_grad_kernel,
+        grid=(height // D, across // columns),
+        in_specs=[
+            pl.BlockSpec((rows, D), lambda i, j: (0, i)),
+            pl.BlockSpec((rows, columns * TILE), lambda i, j: (0, j)),
+        ],
+        out_specs=pl.BlockSpec((columns, D, TILE), lambda i, j: (j, i, 0)),
+        out_shape=jax.ShapeDtypeStruct((across, height, TILE), jnp.float32),
+        cost_estimate=pl.CostEstimate(
+            flops=2 * rows * height * across * TILE,
+            bytes_accessed=rows * (height + across * TILE) * 2 + height * across * TILE * 4,
+            transcendentals=0,
+        ),
+        name="weight_grad",
+    )(left, right)
 
 
 def unpack_kernel(source, target, stage, *, across):
@@ -128,164 +344,6 @@
         scratch_shapes=[pltpu.VMEM((block, TILE), jnp.float32)],
         name="unpack_matrix",
     )(tiles)
-
-
-def place_kernel(spot, rows, *refs, places, count, per):
-    arrivals = refs[: len(places)]
-    targets = refs[len(places) : len(places) + 5]
-    tail = refs[len(places) + 5]
-    landed, stage, full, packed, in_sems, out_sems, tail_sem = refs[len(places) + 6 :]
-    slots = packed.shape[0]
-    copies = []
-    for n, (arrival, place) in enumerate(zip(arrivals, places)):
-        target = landed if place is None else landed.at[place[0], pl.ds(place[1], place[2])]
-        copies.append(pltpu.make_async_copy(arrival, target, in_sems.at[n]))
-    for copy in copies:
-        copy.start()
-    for copy in copies:
-        copy.wait()
-
-    def lines(block, start, size):
-        stage[pl.ds(0, size), :] = landed[block, pl.ds(start, size), :].astype(jnp.float32)
-        if places[0] is None:
-            owner = block
-        else:
-            owner = ((spot[0] + 4 - block // 8) % 4) * 8 + (spot[1] ^ (block % 8))
-        base = owner * per + start
-        for u in range(size):
-            full[pl.ds(rows[base + u], 1), :] = stage[pl.ds(u, 1), :]
-
-    whole, rest = divmod(per, 128)
-
-    def one_block(block, carry):
-        def one_step(i, inner):
-            lines(block, pl.multiple_of(i * 128, 128), 128)
-            return inner
-
-        lax.fori_loop(0, whole, one_step, 0)
-        if rest:
-            lines(block, whole * 128, rest)
-        return carry
-
-    lax.fori_loop(0, count, one_block, 0)
-    tail_copy = pltpu.make_async_copy(full.at[pl.ds(TAIL, TAIL_TILES)], tail, tail_sem)
-    tail_copy.start()
-    for target, (first, height, across) in zip(targets, MATRICES):
-        size = min(height, D)
-        parts = height // size
-
-        def out_copy(n, slot, target=target, size=size, parts=parts):
-            column, part = n // parts, n % parts
-            return pltpu.make_async_copy(
-                packed.at[slot, pl.ds(0, size)],
-                target.at[
-                    pl.ds(pl.multiple_of(part * size, 256), size),
-                    pl.ds(pl.multiple_of(column * TILE, TILE), TILE),
-                ],
-                out_sems.at[slot],
-            )
-
-        def one_column(n, carry, first=first, size=size, out_copy=out_copy):
-            slot = n % slots
-
-            @pl.when(n >= slots)
-            def _():
-                out_copy(n - slots, slot).wait()
-
-            packed[slot, pl.ds(0, size), :] = full[pl.ds(pl.multiple_of(first + n * size, 128), size), :].astype(
-                jnp.bfloat16
-            )
-            out_copy(n, slot).start()
-            return carry
-
-        total = across * parts
-        lax.fori_loop(0, total, one_column, 0)
-        for n in range(total - slots, total):
-            out_copy(n, n % slots).wait()
-    tail_copy.wait()
-
-
-def place_tiles(spot, rows, arrivals, places, count, per):
-    shapes = [jax.ShapeDtypeStruct((h, a * TILE), jnp.bfloat16) for _, h, a in MATRICES]
-    return pl.pallas_call(
-        functools.partial(place_kernel, places=places, count=count, per=per),
-        in_specs=[pl.BlockSpec(memory_space=pltpu.SMEM)] * 2 + [pl.BlockSpec(memory_space=pl.ANY)] * len(arrivals),
-        out_specs=[pl.BlockSpec(memory_space=pl.ANY)] * 6,
-        out_shape=shapes + [jax.ShapeDtypeStruct((TAIL_TILES, TILE), jnp.float32)],
-        scratch_shapes=[
-            pltpu.VMEM((count, per, TILE), jnp.bfloat16),
-            pltpu.VMEM((128, TILE), jnp.float32),
-            pltpu.VMEM((count * per, TILE), jnp.float32),
-            pltpu.VMEM((6, D, TILE), jnp.bfloat16),
-            pltpu.SemaphoreType.DMA((len(arrivals),)),
-            pltpu.SemaphoreType.DMA((6,)),
-            pltpu.SemaphoreType.DMA,
-        ],
-        compiler_params=pltpu.CompilerParams(vmem_limit_bytes=VMEM_LIMIT),
-        cost_estimate=pl.CostEstimate(flops=0, bytes_accessed=180_000_000, transcendentals=0),
-        name="place_tiles",
-    )(spot, rows, *arrivals)
-
-
-def step_size(rows):
-    return max(n for n in range(8, 193, 8) if rows % n == 0)
-
-
-def collect_kernel(spot, rows, *refs, outs, blocks, per, begin):
-    sources, targets = refs[:6], refs[6 : 6 + outs]
-    full, sems = refs[6 + outs :]
-    block = pl.program_id(0)
-
-    @pl.when(block == 0)
-    def _():
-        copies = []
-        for source, (first, height, across) in zip(sources, MATRICES):
-            for column in range(across):
-                copies.append(
-                    pltpu.make_async_copy(
-                        source.at[:, pl.ds(column * TILE, TILE)],
-                        full.at[pl.ds(first + column * height, height)],
-                        sems.at[len(copies)],
-                    )
-                )
-        copies.append(pltpu.make_async_copy(sources[5], full.at[pl.ds(TAIL, TAIL_TILES)], sems.at[len(copies)]))
-        for copy in copies:
-            copy.start()
-        unused = full.shape[0] - TAIL - TAIL_TILES
-        full[pl.ds(TAIL + TAIL_TILES, unused), :] = jnp.zeros((unused, TILE), jnp.float32)
-        for copy in copies:
-            copy.wait()
-
-    size = step_size(targets[0].shape[1])
-    for n, target in enumerate(targets):
-        if outs == 1:
-            owner = block
-        else:
-            owner = ((spot[0] + block // 4) % 4) * 8 + (spot[1] ^ ((block % 4) * 2 + n))
-        base = owner * per + begin
-
-        def one_step(i, carry, target=target, base=base):
-            start = pl.multiple_of(i * size, 8)
-            for u in range(size):
-                target[0, pl.ds(start + u, 1), :] = full[pl.ds(rows[base + start + u], 1), :]
-            return carry
-
-        lax.fori_loop(0, target.shape[1] // size, one_step, 0)
-
-
-def collect_tiles(spot, rows, sources, tiles_all, per, outs, begin, lines):
-    blocks = tiles_all // per // outs
-    return pl.pallas_call(
-        functools.partial(collect_kernel, outs=outs, blocks=blocks, per=per, begin=begin),
-        grid=(blocks,),
-        in_specs=[pl.BlockSpec(memory_space=pltpu.SMEM)] * 2 + [pl.BlockSpec(memory_space=pl.ANY)] * 6,
-        out_specs=[pl.BlockSpec((1, lines, TILE), lambda i: (i, 0, 0))] * outs,
-        out_shape=[jax.ShapeDtypeStruct((blocks, lines, TILE), jnp.float32)] * outs,
-        scratch_shapes=[pltpu.VMEM((tiles_all, TILE), jnp.float32), pltpu.SemaphoreType.DMA((61,))],
-        compiler_params=pltpu.CompilerParams(vmem_limit_bytes=VMEM_LIMIT),
-        cost_estimate=pl.CostEstimate(flops=0, bytes_accessed=80_000_000, transcendentals=0),
-        name="collect_tiles",
-    )(spot, rows, *sources)
 
 
 def array_multiply(left_side, right_side):
@@ -404,32 +462,36 @@
     return (final_lines, saved)
 
 
-def feed_backward(pieces, saved, grad_final):
+def feed_backward(pieces, saved, grad_final, flow):
     small_rows = pieces["small"]
     grad_sum_two, grad_gain_two, grad_shift_two = norm_backward(
         grad_final, saved["normed_two"], saved["inverse_two"], small_rows[8]
     )
     grad_out = grad_sum_two.astype(jnp.bfloat16)
-    grad_down = matmul_left(saved["activated"], grad_out)
+    flow.add(weight_grad(saved["activated"], grad_out, 6))
     grad_act = trailing_array_multiply(grad_out, pieces["down"])
     grad_hidden = (grad_act * gelu_slope(saved["hidden"])).astype(jnp.bfloat16)
-    grad_up = matmul_left(saved["middle_low"], grad_hidden)
+    (grad_hidden,) = flow.advance(grad_hidden)
+    flow.add(weight_grad(saved["middle_low"], grad_hidden, 6))
     grad_middle = grad_sum_two + trailing_array_multiply(grad_hidden, pieces["up"])
     grad_sum_one, grad_gain_one, grad_shift_one = norm_backward(
         grad_middle, saved["normed_one"], saved["inverse_one"], small_rows[6]
     )
-    grad_small = [jnp.sum(grad_out.astype(jnp.float32), axis=0), grad_gain_one, grad_shift_one, grad_gain_two, grad_shift_two]
     grad_upbias = jnp.sum(grad_hidden.astype(jnp.float32), axis=0)
-    return grad_sum_one, (grad_up, grad_down, grad_small, grad_upbias)
-
-
-def attention_backward(pieces, saved, grad_sum_one, feed_grads, lengths):
+    (grad_sum_one,) = flow.advance(grad_sum_one)
+    return (
+        grad_sum_one,
+        [jnp.sum(grad_out.astype(jnp.float32), axis=0), grad_gain_one, grad_shift_one, grad_gain_two, grad_shift_two],
+        grad_upbias,
+    )
+
+
+def attention_backward(pieces, saved, grad_sum_one, grad_small, grad_upbias, lengths, tail_rows, flow):
     small_rows = pieces["small"]
     seqs_count = lengths.shape[0]
     rows_here = seqs_count * LEN
-    grad_up, grad_down, grad_small, grad_upbias = feed_grads
     grad_att = grad_sum_one.astype(jnp.bfloat16)
-    grad_outw = matmul_left(saved["context"], grad_att)
+    grad_outw = weight_grad(saved["context"], grad_att, 6)
     grad_context = (
         trailing_array_multiply(grad_att, pieces["out"])
         .astype(jnp.bfloat16)
@@ -446,10 +508,11 @@
         grad_context,
         preferred_element_type=jnp.float32,
     )
+    grad_values, grad_probs = flow.advance(grad_values, grad_probs)
     grad_scores = probabilities * (
         grad_probs - jnp.sum(grad_probs * probabilities, axis=-1, keepdims=True)
     )
-    grad_scores = grad_scores.astype(jnp.bfloat16)
+    (grad_scores,) = flow.advance(grad_scores.astype(jnp.bfloat16))
     grad_queries = jnp.einsum(
         "shqk,skhd->sqhd", grad_scores, split_heads[:, :, 1], preferred_element_type=jnp.float32
     ) * HEAD_DIM ** (-0.5)
@@ -461,7 +524,8 @@
         .reshape(rows_here, 3 * D)
         .astype(jnp.bfloat16)
     )
-    grad_qkv = matmul_left(saved["inputs"], grad_proj)
+    (grad_proj,) = flow.advance(grad_proj)
+    grad_qkv = weight_grad(saved["inputs"], grad_proj, 6)
     grad_bias_all = jnp.sum(grad_proj.astype(jnp.float32), axis=0)
     grad_first = grad_sum_one + trailing_array_multiply(grad_proj, pieces["qkv"])
     grad_embedded, grad_gain_zero, grad_shift_zero = norm_backward(
@@ -480,9 +544,15 @@
         ]
     )
     tail = jnp.concatenate(
-        [grad_small.reshape(60, TILE), grad_upbias.reshape(24, TILE), jnp.zeros((4, TILE), jnp.float32)]
-    )
-    return ((grad_qkv, grad_outw, grad_up, grad_down, grad_place, tail), grad_embedded)
+        [
+            grad_small.reshape(60, TILE),
+            grad_upbias.reshape(24, TILE),
+            jnp.zeros((tail_rows - 84, TILE), jnp.float32),
+        ]
+    )
+    (grad_embedded,) = flow.advance(grad_embedded)
+    flow.add(grad_qkv, grad_outw, grad_place.reshape(LEN, 6, TILE).transpose(1, 0, 2), tail)
+    return grad_embedded
 
 
 def combine_stats(earlier, later):
@@ -512,28 +582,91 @@
     return (weight - learn_rate * (update + weight_decay * weight), new_first, new_second)
 
 
-def gather_student(tiles, beside):
+def gather_layer(tiles, fillers):
     per = tiles.shape[0]
     half = per // 16 * 8
     arrivals, places = [], []
-
-    def keep(value, plane, near, start):
-        for core in (0, 1):
-            arrivals.append(swap(value, CORE) if core else value)
-            places.append((plane * 8 + near * 2 + core, start, value.shape[0]))
-
-    for plane in range(4):
-        across, deep = swap(tiles, ACROSS), swap(tiles, DEEP)
-        if plane == 3:
-            across, deep, beside = together(across, deep, beside)
-        keep(tiles, plane, 0, 0)
-        keep(across, plane, 1, 0)
-        keep(deep, plane, 2, 0)
-        keep(swap(across[:half], DEEP), plane, 3, 0)
-        keep(swap(deep[half:], ACROSS), plane, 3, half)
-        if plane < 3:
-            tiles = shift(tiles, 1)
-    return arrivals, places, beside
+    waiting = [(tiles, 0, 0, 0)]
+    crossed = None
+    done = []
+    for stage in range(6):
+        moved = []
+        for value, plane, near, start in waiting:
+            arrivals.append(value)
+            places.append((plane * 8 + near * 2, start, value.shape[0]))
+            moved.append((swap(value, CORE), plane, near, start))
+        landed = []
+        if crossed is not None:
+            across, deep, plane = crossed
+            landed.append((swap(across[:half], DEEP), plane, 3, 0))
+            landed.append((swap(deep[half:], ACROSS), plane, 3, half))
+            crossed = None
+        if stage < 4:
+            across, deep = swap(tiles, ACROSS), swap(tiles, DEEP)
+            landed.append((across, stage, 1, 0))
+            landed.append((deep, stage, 2, 0))
+            crossed = (across, deep, stage)
+        ahead = shift(tiles, 1) if stage < 3 else tiles
+        extra = fillers[stage](done) if stage < len(fillers) else []
+        values, landed_values, ahead, extra = together(
+            [entry[0] for entry in moved], [entry[0] for entry in landed], ahead, extra
+        )
+        done = done + list(extra)
+        for value, (_, plane, near, start) in zip(values, moved):
+            arrivals.append(value)
+            places.append((plane * 8 + near * 2 + 1, start, value.shape[0]))
+        landed = [(value, *entry[1:]) for value, entry in zip(landed_values, landed)]
+        if stage < 4:
+            crossed = (landed_values[-2], landed_values[-1], stage)
+        waiting = landed
+        if stage < 3:
+            tiles = ahead
+            waiting = waiting + [(tiles, stage + 1, 0, 0)]
+    return arrivals, places, done
+
+
+def reduce_steps(near, far):
+    chip = yield [near + swap(far, CORE)]
+    first, second = yield list(plane_first(chip[0]))
+    blocks = yield plane_second(first, second)
+    for _ in range(3):
+        blocks = yield ring_hop(blocks)
+    return blocks[0]
+
+
+class Flow:
+    def __init__(self, spot, devices):
+        self.spot, self.devices = spot, devices
+        self.lines, self.waiting, self.sums = [], [], []
+
+    def add(self, *parts):
+        near, far = split_cores(self.spot, [part.reshape(self.devices, -1, TILE) for part in parts])
+        self.lines.append(reduce_steps(near, far))
+        self.waiting.append(next(self.lines[-1]))
+        self.sums.append(None)
+
+    def advance(self, *values):
+        tied, values = together([moved for moved in self.waiting if moved is not None], list(values))
+        tied = list(tied)
+        for n, moved in enumerate(self.waiting):
+            if moved is not None:
+                try:
+                    self.waiting[n] = self.lines[n].send(tied.pop(0))
+                except StopIteration as stop:
+                    self.waiting[n], self.sums[n] = None, stop.value
+        return values
+
+
+class PlainFlow:
+    def __init__(self, devices):
+        self.devices, self.sums = devices, []
+
+    def add(self, *parts):
+        whole = jnp.concatenate([part.reshape(self.devices, -1, TILE) for part in parts], axis=1)
+        self.sums.append(lax.psum_scatter(whole, ("dp", "vocab"), scatter_dimension=0, tiled=False))
+
+    def advance(self, *values):
+        return values
 
 
 def sent_low(value, bit):
@@ -578,11 +711,40 @@
     group = lax.axis_size("vocab")
     here = lax.axis_index("vocab")
     spot = jnp.stack([lax.axis_index("dp"), here]).astype(jnp.int32)
+    devices = planes * group
+    everywhere = ("dp", "vocab")
+    device = lax.axis_index(everywhere)
+    capacity = room(per, devices)
+    slot_count = devices * capacity
 
     facts = jnp.concatenate([token_ids.reshape(LEN), lengths, mask_count, jnp.zeros((TILE - 2,), jnp.int32)])
-    target_rows = rows_of_tiles(owner_order)
-    student_low = student_flat.astype(jnp.bfloat16)
     table_low = lax.all_gather(student_embed.T.astype(jnp.bfloat16), "dp", axis=0, tiled=True)
+
+    homes = homes_of(owner_order, tiles_all, devices)
+    one_of = jnp.arange(devices, dtype=jnp.int32)
+    pairs = jnp.sum((homes.reshape(devices, per, 1) // per == one_of).astype(jnp.int32), axis=1)
+    crowded = jnp.max(pairs) > capacity
+    own_homes = lax.dynamic_slice_in_dim(homes, device * per, per)
+    own_target = own_homes // per
+    chosen_target = (own_target[:, None] == one_of).astype(jnp.bfloat16)
+    lines = jnp.arange(per, dtype=jnp.int32)
+    earlier = (lines[None] < lines[:, None]).astype(jnp.bfloat16)
+    rank = jnp.sum(array_multiply(earlier, chosen_target) * chosen_target.astype(jnp.float32), axis=1)
+    rank = rank.astype(jnp.int32)
+    slots = jnp.where(rank < capacity, own_target * capacity + rank, slot_count)
+    packed, home_line = send_tiles(slots, own_homes % per, student_flat, slot_count)
+    packed = lax.all_to_all(packed.reshape(devices, capacity, TILE), everywhere, 0, 0)
+    home_line = lax.all_to_all(home_line[:slot_count].reshape(devices, 1, capacity), everywhere, 0, 0)
+    home_line = home_line.reshape(slot_count)
+    home_tiles = land_tiles(home_line, packed.reshape(slot_count, TILE), per)
+
+    def every_tile(tiles):
+        stored = lax.all_gather(student_flat.astype(jnp.bfloat16), everywhere, axis=0, tiled=True)
+        sources = jnp.zeros((tiles_all,), jnp.int32).at[homes].set(jnp.arange(tiles_all, dtype=jnp.int32))
+        return stored[lax.dynamic_slice_in_dim(sources, device * per, per)]
+
+    home_tiles = lax.cond(crowded, every_tile, lambda tiles: tiles, home_tiles)
+
     words = jnp.arange(vocab_rows, dtype=jnp.int32)
 
     def chosen(ids):
@@ -596,23 +758,26 @@
 
     if near:
         plane_facts = gather_near(facts)
-        far_ids, close_ids = plane_facts[4:, :LEN], plane_facts[:4, :LEN]
         shape = (2, 2, LEN, D)
-        beside = [
-            rows_t(close_ids).reshape(shape) + swap(rows_t(far_ids).reshape(shape), CORE),
-            rows_s(close_ids).reshape(shape),
-            rows_s(far_ids).reshape(shape),
+
+        def ids(far):
+            return plane_facts[4:, :LEN] if far else plane_facts[:4, :LEN]
+
+        fillers = [
+            lambda done: [],
+            lambda done: [rows_t(ids(True)).reshape(shape)],
+            lambda done: [rows_t(ids(False)).reshape(shape), swap(done[0], CORE)],
+            lambda done: [done[1] + done[2], rows_s(ids(True)).reshape(shape)],
+            lambda done: [rows_s(ids(False)).reshape(shape), swap(done[4], CORE)],
+            lambda done: [done[5] + done[6], *plane_hop(done[3])],
         ]
-        arrivals, places, beside = gather_student(student_low, beside)
-        looked_t = beside[0]
-        looked_s = beside[1] + swap(beside[2], CORE)
-        arrivals, teacher_flat, looked_t, looked_s, target_rows = together(
-            arrivals, teacher_flat, looked_t, looked_s, target_rows
-        )
-        teacher_tiles = lax.all_gather(teacher_flat, ("dp", "vocab"), axis=0, tiled=True)
-        looked_t, looked_s = plane_hop(looked_t), plane_hop(looked_s)
-        matrices = place_tiles(spot, target_rows, arrivals, tuple(places), planes * group, per)
-        matrices, looked_t, looked_s, facts = together(matrices, looked_t, looked_s, facts)
+        teacher_flat, plane_facts = together(teacher_flat, plane_facts)
+        teacher_tiles = lax.all_gather(teacher_flat, everywhere, axis=0, tiled=True)
+        arrivals, places, done = gather_layer(home_tiles, fillers)
+        looked_s, looked_t = done[7], (done[8], done[9])
+        looked_s = plane_hop(looked_s)
+        matrices = assemble_layer(spot, arrivals, tuple(places), tiles_all, devices)
+        matrices, looked_s, facts = together(matrices, looked_s, facts)
         other_facts = gather_near(jnp.stack([shift(facts, 1), shift(facts, 2), shift(facts, 3)]))
         all_facts = jnp.concatenate([plane_facts[:, None], other_facts], axis=1)
         looked_s = plane_end(*looked_s).astype(jnp.float32)
@@ -621,17 +786,21 @@
         by_plane = lax.all_gather(facts, "dp", axis=0)
         all_facts = lax.all_gather(by_plane, "vocab", axis=0)
         plane_facts = lax.dynamic_index_in_dim(all_facts, lax.axis_index("dp"), 1, keepdims=False)
-        teacher_tiles = lax.all_gather(teacher_flat, ("dp", "vocab"), axis=0, tiled=True)
-        student_tiles = lax.all_gather(student_low, ("dp", "vocab"), axis=0, tiled=True)
+        teacher_tiles = lax.all_gather(teacher_flat, everywhere, axis=0, tiled=True)
+        layer = lax.all_gather(home_tiles, everywhere, axis=0)
+        sizes, starts = shares_of(tiles_all, devices)
+        matrices = [
+            layer[:, start : start + size].reshape(across, height, TILE).transpose(1, 0, 2).reshape(height, -1)
+            for (_, height, across), size, start in zip(HOME_ORDER, sizes, starts)
+        ]
+        matrices.append(layer[:, starts[-1] :].astype(jnp.float32))
         plane_ids = plane_facts[:, :LEN]
         looked_t, looked_s = (
             lax.psum_scatter(rows, "vocab", scatter_dimension=0, tiled=True).astype(jnp.float32)
             for rows in (rows_t(plane_ids), rows_s(plane_ids))
         )
-        matrices = place_tiles(
-            spot, target_rows, [student_tiles.reshape(planes * group, per, TILE)], (None,), planes * group, per
-        )
-    student = pieces_of(matrices[:5], matrices[5])
+    up, down, qkv, out, place = matrices[:5]
+    student = pieces_of((qkv, out, up, down, place), matrices[5].reshape(-1, TILE))
     final_s, saved = layer_forward(student, looked_s, lengths)
     final_s, teacher_tiles, looked_t, all_facts = together(final_s, teacher_tiles, looked_t, all_facts)
     teacher = pieces_of(
@@ -709,8 +878,7 @@
         )
     head_grad = matmul_left(learner_picked, grad_logit)
     head_grad, grad_rows = together(head_grad, grad_rows)
-    if not near:
-        head_part = lax.psum_scatter(head_grad, "dp", scatter_dimension=0, tiled=True)
+    head_part = lax.psum_scatter(head_grad, "dp", scatter_dimension=0, tiled=True)
     products = jnp.sum(final_s * final_t, axis=1)
     inverse_s = lax.rsqrt(jnp.sum(final_s * final_s, axis=1) + cosine_eps)
     inverse_t = lax.rsqrt(jnp.sum(final_t * final_t, axis=1) + cosine_eps)
@@ -722,15 +890,11 @@
         final_t - (products * inverse_s * inverse_s)[:, None] * final_s
     )
     grad_final = grad_final.at[offsets].add(grad_rows)
-    if near:
-        heads = upward(head_grad.reshape(4, width_share, vocab_rows))
-        moving = shift(heads[3], 1)
-        grad_sum_one, feed_grads = feed_backward(student, saved, grad_final)
-        layer_grads, grad_embedded = attention_backward(student, saved, grad_sum_one, feed_grads, lengths)
-        grad_embedded, moving = together(grad_embedded, moving)
-    else:
-        grad_sum_one, feed_grads = feed_backward(student, saved, grad_final)
-        layer_grads, grad_embedded = attention_backward(student, saved, grad_sum_one, feed_grads, lengths)
+    flow = Flow(spot, devices) if near else PlainFlow(devices)
+    grad_sum_one, grad_small, grad_upbias = feed_backward(student, saved, grad_final, flow)
+    grad_embedded = attention_backward(
+        student, saved, grad_sum_one, grad_small, grad_upbias, lengths, tiles_all - TAIL, flow
+    )
 
     shares = grad_embedded.astype(jnp.bfloat16).reshape(LEN, planes, width_share).transpose(1, 0, 2)
     if near:
@@ -744,40 +908,30 @@
         shares = lax.all_to_all(shares, "dp", 0, 0)
         ids = all_facts[:, :, :LEN]
     token_grads = lax.all_gather(shares.reshape(-1, width_share), "vocab", axis=0, tiled=True)
-    if near:
-        edges = (0, 640, 1256, per)
-
-        def collect(n):
-            return collect_tiles(spot, target_rows, layer_grads, tiles_all, per, 2, edges[n], edges[n + 1] - edges[n])
-
-        one, shares = together(collect(0), shares)
-        moving = shift(heads[2] + moving, 1)
-        token_grads = lax.all_gather(shares.reshape(-1, width_share), "vocab", axis=0, tiled=True)
-        chip_one = one[0] + swap(one[1], CORE)
-        chip_one, two, moving = together(chip_one, collect(1), moving)
-        moving = shift(heads[1] + moving, 1)
-        first_one = plane_first(chip_one)
-        chip_two = two[0] + swap(two[1], CORE)
-        first_one, chip_two, three, token_grads = together(first_one, chip_two, collect(2), token_grads)
-        token_part = matmul_left(token_grads, chosen(ids))
-        blocks_one = plane_second(*first_one)
-        first_two = plane_first(chip_two)
-        chip_three = three[0] + swap(three[1], CORE)
-        blocks_one, first_two, chip_three, token_part, moving = together(
-            blocks_one, first_two, chip_three, token_part, moving
-        )
-        head_part = heads[0] + moving
-        blocks_two = plane_second(*first_two)
-        blocks_three = plane_second(*plane_first(chip_three))
-        sums = [ring_sum(blocks) for blocks in (blocks_one, blocks_two, blocks_three)]
-        flat_grad = jnp.concatenate(sums)
-    else:
-        token_grads = lax.all_gather(shares.reshape(-1, width_share), "vocab", axis=0, tiled=True)
-        token_part = matmul_left(token_grads, chosen(ids))
-        (grad_tiles,) = collect_tiles(spot, target_rows, layer_grads, tiles_all, per, 1, 0, per)
-        flat_grad = lax.psum_scatter(
-            grad_tiles.reshape(tiles_all, TILE), ("dp", "vocab"), scatter_dimension=0, tiled=True
-        )
+    def token_sum(n):
+        third = token_grads.shape[0] // 8 * 3
+        begin, end = (n * third, (n + 1) * third) if n < 2 else (n * third, token_grads.shape[0])
+        return matmul_left(token_grads[begin:end], chosen(ids.reshape(-1)[begin:end]))
+
+    shares, head_part = flow.advance(shares, head_part)
+    token_grads = lax.all_gather(shares.reshape(-1, width_share), "vocab", axis=0, tiled=True)
+    flow.advance()
+    flow.advance()
+    (token_grads,) = flow.advance(token_grads)
+    (token_part,) = flow.advance(token_sum(0))
+    flow.advance()
+    sum_down, sum_up, sum_rest = flow.sums
+    home_grads = jnp.concatenate([sum_up, sum_down, sum_rest])
+    returned = pick_tiles(jnp.minimum(home_line, per - 1), home_grads, slot_count)
+    returned = lax.all_to_all(returned.reshape(devices, capacity, TILE), everywhere, 0, 0)
+    flat_grad = pick_tiles(jnp.minimum(slots, slot_count - 1), returned.reshape(slot_count, TILE), per)
+    flat_grad = lax.cond(
+        crowded,
+        lambda grads: lax.all_gather(home_grads, everywhere, axis=0, tiled=True)[own_homes],
+        lambda grads: grads,
+        flat_grad,
+    )
+    token_part = token_part + token_sum(1) + token_sum(2)
     table_grad = (head_part + token_part).T
     loss_term = (
         mixing_coefficient * smoothing_heat_scale**2 * divergence_part / masked_total

time: 1010 us -> 1010 us (level)
  Pallas kernels: 197 us -> 125 us
  waiting for transfers between devices: 286 us -> 309 us
  local copies, waits for them, and re-layouts: 54 us -> 76.7 us
  other arithmetic: 113 us -> 132 us
  matrix products: 228 us -> 210 us
  blocking collectives: 0 us -> 14.2 us
    pallas_call x4 -> x12, Pallas kernels: 175 us -> 104 us  [the longest x3 40.8 us: split_cores(): pl.pallas_call(functools.partial(split_kernel, count=len(parts), sizes=si...]
    all_to_all x0 -> x2, waiting for transfers between devices: none -> 20.2 us  [the longest x1 12.4 us: on_device(): lax.all_to_all(packed.reshape(devices, capacity, TILE), everywhere, 0, 0)]
    dot_general x6 -> x4, matrix products: 59.3 us -> 40.7 us  [matmul_left(): lax.dot_general(left_side, right_side, (((0,), (0,)), ((), ())), preferre...]
    ppermute x21 -> x18, waiting for transfers between devices: 108 us -> 127 us  [shift(): lax.ppermute(value, 'dp', [(i, (i + steps) % size) for i in range(size)])]
    ppermute x84, waiting for transfers between devices: 170 us -> 155 us  [swap(): return lax.ppermute(value, 'vocab', [(i, i ^ bit) for i in range(8)])]
    reduce_sum x0 -> x3, other arithmetic: none -> 14.6 us  [the longest x1 12.8 us: attention_backward(): jnp.sum(grad_probs * probabilities, axis=-1, keepdims=True)]
    all_to_all x0 -> x1, blocking collectives: none -> 14.2 us  [on_device(): lax.all_to_all(home_line[:slot_count].reshape(devices, 1, capacity), ever...]
    ppermute x21 -> x18, starting transfers between devices: 38.8 us -> 32.5 us  [shift(): lax.ppermute(value, 'dp', [(i, (i + steps) % size) for i in range(size)])]
  transfers between devices with their start and end apart: 110 -> 110, of which waited for: 48 -> 54; matrix products, arithmetic and copies ran while one was open for 27% -> 34% of each run, Pallas kernels for 17% -> 4%
where the time goes in v5:
time: 1010 us; the launch traced here: 998 us
  waiting for transfers between devices  309 us (31%)
  matrix products  210 us (21%)
  other arithmetic  132 us (13%)
  Pallas kernels  125 us (12%)
  starting transfers between devices  104 us (10%)
  local copies, waits for them, and re-layouts  76.7 us (8%)
  between operations  27.6 us (3%)
  blocking collectives  14.2 us (1%)
    ppermute x84, waiting for transfers between devices, swap(): return lax.ppermute(value, 'vocab', [(i, i ^ bit) for i in range(8)])  155 us
    ppermute x18, waiting for transfers between devices, shift(): lax.ppermute(value, 'dp', [(i, (i + steps) % size) for i in range(size)])  127 us
    dot_general x11, matrix products, array_multiply(): return jnp.dot(left_side, right_side, preferred_element_type=jnp.float32)  78 us
    ppermute x84, starting transfers between devices, swap(): return lax.ppermute(value, 'vocab', [(i, i ^ bit) for i in range(8)])  63.9 us
    dot_general x9, matrix products, trailing_array_multiply(): lax.dot_general(left_side, right_side, (((1,), (1,)), ((), ())), preferre...  48.7 us
    pallas_call x3, Pallas kernels, split_cores(): pl.pallas_call(functools.partial(split_kernel, count=len(parts), sizes=si...  40.8 us
    dot_general x4, matrix products, matmul_left(): lax.dot_general(left_side, right_side, (((0,), (0,)), ((), ())), preferre...  40.7 us
    ppermute x18, starting transfers between devices, shift(): lax.ppermute(value, 'dp', [(i, (i + steps) % size) for i in range(size)])  32.5 us
  transfers between devices with their start and end apart: 110, of which 54 were waited for; matrix products, arithmetic and copies ran while one was open for 34% of the time, Pallas kernels for 4%

profile of v5, /device:TPU:0, one launch (start us, length us, event | category | flops | bytes accessed | tf_op | source)
XLA Modules:
  0.0 998.4 jit_solution(4010486937387488520)
XLA Ops:
  15.2 7.2 send_tiles.1
  23.3 14.2 %all_to_all.15 = s32[32,1,96]{2,1,0:T(1,128)} all-to-all(s32[32,1,96]{2,1,0:T(1,128)S(1)} %reshape.730), channel_id=1, replica_groups=mesh['dp'=4,'vocab'=8] {'dp','vocab'}, dimensions={0} | all-to-all | bytes 24576 | tf_op jit(solution)/shard_map/all_to_all | solution.py:737
  49.0 12.4 %all-to-all-done.1 = bf16[32,96,128]{2,1,0:T(8,128)(2,1)} async-done(((bf16[32,96,128]{2,1,0:T(8,128)(2,1)}), bf16[32,96,128]{2,1,0:T(8,128)(2,1)}, u32[]{:S(2)}, u32[]{:S(2)}) %all-to-all-start.1) | async-done | bytes 786464 | tf_op jit(solution)/shard_map/all_to_all | solution.py:736
  80.4 22.3 %collective-permute-done.3.refs_4_ = bf16[1832,128]{1,0:T(8,128)(2,1)S(1)} collective-permute-done((bf16[1832,128]{1,0:T(8,128)(2,1)}, bf16[1832,128]{1,0:T(8,128)(2,1)S(1)}, u32[]{:S(2)}, u32[]{:S(2)}) %collective-permute-start.3) | collective-permute-done | bytes 469024 | tf_op jit(solution)/shard_map/ppermute | solution.py:53
  117.7 7.3 fusion.64
  125.0 15.4 %collective-permute-done.11.refs_12_ = bf16[1832,128]{1,0:T(8,128)(2,1)S(1)} collective-permute-done((bf16[1832,128]{1,0:T(8,128)(2,1)}, bf16[1832,128]{1,0:T(8,128)(2,1)S(1)}, u32[]{:S(2)}, u32[]{:S(2)}) %collective-permute-start.11) | collective-permute-done | bytes 469024 | tf_op jit(solution)/shard_map/ppermute | solution.py:53
  142.0 6.7 collective-permute-done.20.refs_18_
  149.3 6.7 collective-permute-done.21.refs_19_
  164.9 8.5 fusion.66
  173.3 9.2 collective-permute-done.24.refs_22_
  187.3 11.2 %collective-permute-done.31.refs_28_ = bf16[912,128]{1,0:T(8,128)(2,1)S(1)} collective-permute-done((bf16[912,128]{1,0:T(8,128)(2,1)S(1)}, bf16[912,128]{1,0:T(8,128)(2,1)S(1)}, u32[]{:S(2)}, u32[]{:S(2)}) %collective-permute-start.31) | collective-permute-done | bytes 233504 | tf_op jit(solution)/shard_map/ppermute | solution.py:48
  201.2 9.3 fusion.65
  220.9 11.0 %collective-permute-done.39.refs_36_ = bf16[912,128]{1,0:T(8,128)(2,1)S(1)} collective-permute-done((bf16[912,128]{1,0:T(8,128)(2,1)S(1)}, bf16[912,128]{1,0:T(8,128)(2,1)S(1)}, u32[]{:S(2)}, u32[]{:S(2)}) %collective-permute-start.39) | collective-permute-done | bytes 233504 | tf_op jit(solution)/shard_map/ppermute | solution.py:48
  234.2 7.7 fusion.67
  241.9 26.8 %collective-permute-done.44 = bf16[2,256,768]{2,1,0:T(8,128)(2,1)S(1)} collective-permute-done((bf16[2,256,768]{2,1,0:T(8,128)(2,1)S(1)}, bf16[2,256,768]{2,1,0:T(8,128)(2,1)S(1)}, u32[]{:S(2)}, u32[]{:S(2)}) %collective-permute-start.44) | collective-permute-done | bytes 786464 | tf_op jit(solution)/shard_map/ppermute | solution.py:48
  279.3 19.1 %assemble_layer.1 = (bf16[768,3072]{1,0:T(8,128)(2,1)}, bf16[3072,768]{1,0:T(8,128)(2,1)}, bf16[768,2304]{1,0:T(8,128)(2,1)}, bf16[768,768]{1,0:T(8,128)(2,1)}, ...) custom-call(s32[2]{0:T(128)} %pad_add_fusion.6.spot, bf16[1832,128]{1,0:T(8,128)(2,1)} %get-tuple-element.443.refs_0_, ...), custom_call_target="tpu_custom_call" | custom-call | bytes 60000000 | tf_op jit(solution)/shard_map/assemble_layer/pallas_call | solution.py:240
  350.2 18.2 %fusion.26 = (bf16[512,3072]{1,0:T(8,128)(2,1)S(1)}, f32[512,3072]{1,0:T(8,128)}) fusion(f32[3072]{0:T(1024)S(1)} %slice_bitcast_fusion.54, bf16[512,768]{1,0:T(8,128)(2,1)S(1)} %fusion.94.left, bf16[768,3072]{1,0:T(8,128)(2,1)S(1)} %bitcast.537), kind=kOutput, calls=%fused_computation.63 | convolution fusion | flops 2519728128 | bytes 14954496 | tf_op jit(solution)/shard_map/dot_general | solution.py:350
  384.1 6.2 unpack_matrix.9
  390.3 5.8 unpack_matrix.8
  412.5 10.9 %fusion.265 = (f32[12,512]{1,0:T(8,128)S(1)}, f32[12,512,512]{1,2,0:T(8,128)}) fusion(pred[512]{0:T(512)(128)(4,1)S(1)} %copy-done.141, bf16[1,512,3,12,64]{1,4,3,2,0:T(8,128)(2,1)} %bitcast.483), kind=kOutput, calls=%fused_computation.617 | convolution fusion | flops 415236608 | bytes 14180864 | tf_op jit(solution)/shard_map/sub | solution.py:428
  423.4 6.2 fusion.88
  433.3 23.1 %fusion.267 = (f32[512]{0:T(512)S(1)}, f32[512,768]{1,0:T(8,128)}) fusion(f32[768]{0:T(1024)S(1)} %get-tuple-element.386, bf16[3072,768]{1,0:T(8,128)(2,1)} %unpack_matrix.9, bf16[768,3072]{1,0:T(8,128)(2,1)} %unpack_matrix.8, f32[3072]{0:T(1024)S(1)} %slice_bitcast_fusion.53, f32[512,768]{1,0:T(8,128)} %copy-done.55, f32[768]{0:T(1024)S(1)} %get-tuple-element.387, ...), kind=kOutput, calls=%fused_computation.619 | convolution fusion | flops 4940365312 | bytes 12610560 | tf_op jit(solution)/shard_map/dot_general | solution.py:350
  473.4 8.9 collective-permute-done.62
  506.1 7.7 multiply_convert_fusion
  555.0 7.5 weight_grad.4
  562.5 13.1 %split_cores.3 = (f32[16,576,128]{2,1,0:T(8,128)}, f32[16,576,128]{2,1,0:T(8,128)}) custom-call(s32[2]{0:T(128)} %pad_add_fusion.6.spot, f32[32,576,128]{2,1,0:T(8,128)} %bitcast.430, f32[32,576,128]{2,1,0:T(8,128)} %bitcast.431), custom_call_target="tpu_custom_call" | custom-call | bytes 18874368 | tf_op jit(solution)/shard_map/split_cores/pallas_call | solution.py:277
  575.7 10.7 %fusion.35.right = bf16[512,3072]{1,0:T(8,128)(2,1)} fusion(f32[512,3072]{1,0:T(8,128)} %get-tuple-element.427, bf16[512,768]{1,0:T(8,128)(2,1)S(1)} %copy-done.51, bf16[3072,768]{1,0:T(8,128)(2,1)} %get-tuple-element.231, f32[3072]{0:T(1024)S(1)} %copy-done.136), kind=kOutput, calls=%fused_computation.72 | convolution fusion | flops 2433220608 | bytes 14954496 | tf_op jit(solution)/shard_map/dot_general | solution.py:360
  589.0 7.5 weight_grad.5
  596.6 13.1 %split_cores.4 = (f32[16,576,128]{2,1,0:T(8,128)}, f32[16,576,128]{2,1,0:T(8,128)}) custom-call(s32[2]{0:T(128)} %pad_add_fusion.6.spot, f32[32,576,128]{2,1,0:T(8,128)} %bitcast.432, f32[32,576,128]{2,1,0:T(8,128)} %bitcast.433), custom_call_target="tpu_custom_call" | custom-call | bytes 18874368 | tf_op jit(solution)/shard_map/split_cores/pallas_call | solution.py:277
  646.0 7.9 fusion.77
  654.5 6.4 convolution_bitcast_fusion
  671.3 12.8 %fusion.14 = f32[12,512]{1,0:T(8,128)S(1)} fusion(f32[1,12,512,512]{2,3,1,0:T(8,128)} %convolution_bitcast_fusion, f32[12,512,512]{1,2,0:T(8,128)} %copy-done.2, f32[12,512]{1,0:T(8,128)S(1)} %copy-done.71), kind=kLoop, calls=%fused_computation.33 | loop fusion | flops 9431040 | bytes 25214976 | tf_op jit(solution)/shard_map/reduce_sum | solution.py:513
  695.3 14.5 %collective-permute-done.80 = f32[576,128]{1,0:T(8,128)S(1)} collective-permute-done((f32[576,128]{1,0:T(8,128)}, f32[576,128]{1,0:T(8,128)S(1)}, u32[]{:S(2)}, u32[]{:S(2)}) %collective-permute-start.80) | collective-permute-done | bytes 294944 | tf_op jit(solution)/shard_map/ppermute | solution.py:53
  722.7 8.2 collective-permute-done.83
  738.4 6.4 multiply_reduce_fusion.5
  752.4 6.2 weight_grad.6
  759.5 14.7 %split_cores.5 = (f32[16,680,128]{2,1,0:T(8,128)}, f32[16,680,128]{2,1,0:T(8,128)}) custom-call(s32[2]{0:T(128)} %pad_add_fusion.6.spot, f32[32,432,128]{2,1,0:T(8,128)} %bitcast.434, f32[32,144,128]{2,1,0:T(8,128)} %bitcast.436, f32[32,96,128]{2,1,0:T(8,128)} %bitcast.446, f32[32,8,128]{2,1,0:T(8,128)} %maximum_bitcast_fusion.refs_3_.refs_7_, ...), custom_call_target="tpu_custom_call" | custom-call | bytes 22282240 | tf_op jit(solution)/shard_map/split_cores/pallas_call | solution.py:277
  774.4 11.6 %collective-permute-done.85 = f32[576,128]{1,0:T(8,128)} collective-permute-done((f32[576,128]{1,0:T(8,128)S(1)}, f32[576,128]{1,0:T(8,128)}, u32[]{:S(2)}, u32[]{:S(2)}) %collective-permute-start.85) | collective-permute-done | bytes 294944 | tf_op jit(solution)/shard_map/ppermute | solution.py:53
  799.9 16.6 %collective-permute-done.90 = bf16[512,192]{0,1:T(8,128)(2,1)S(1)} collective-permute-done((bf16[512,192]{0,1:T(8,128)(2,1)S(1)}, bf16[512,192]{0,1:T(8,128)(2,1)S(1)}, u32[]{:S(2)}, u32[]{:S(2)}) %collective-permute-start.90) | collective-permute-done | bytes 196640 | tf_op jit(solution)/shard_map/ppermute | solution.py:53
  816.6 7.2 add.844
  834.2 21.3 %collective-permute-done.93 = bf16[2,2,680,128]{3,2,0,1:T(8,128)(2,1)} collective-permute-done((bf16[2,2,680,128]{3,2,0,1:T(8,128)(2,1)}, bf16[2,2,680,128]{3,2,0,1:T(8,128)(2,1)}, u32[]{:S(2)}, u32[]{:S(2)}) %collective-permute-start.93) | collective-permute-done | bytes 696352 | tf_op jit(solution)/shard_map/ppermute | solution.py:48
  861.6 14.9 %collective-permute-done.95 = bf16[2,680,128]{2,1,0:T(8,128)(2,1)S(1)} collective-permute-done((bf16[2,680,128]{2,1,0:T(8,128)(2,1)S(1)}, bf16[2,680,128]{2,1,0:T(8,128)(2,1)S(1)}, u32[]{:S(2)}, u32[]{:S(2)}) %collective-permute-start.95) | collective-permute-done | bytes 348192 | tf_op jit(solution)/shard_map/ppermute | solution.py:48
  880.2 6.5 collective-permute-done.96
  888.9 12.9 %fusion.3 = f32[192,1920]{1,0:T(8,128)} fusion(s32[6144]{0:T(1024)S(1)} %get-tuple-element.383, bf16[16384,192]{0,1:T(8,128)(2,1)} %all-gather.14.cloned.1.call-done), kind=kOutput, calls=%fused_computation.16 | convolution fusion | flops 4541644800 | bytes 3858432 | tf_op jit(solution)/shard_map/dot_general | solution.py:354
  905.8 7.3 collective-permute-done.98
  923.3 9.3 fusion.5
  932.6 13.2 %fusion.4 = f32[192,1920]{1,0:T(8,128)} fusion(s32[6144]{0:T(1024)S(1)} %get-tuple-element.382, bf16[16384,192]{0,1:T(8,128)(2,1)} %all-gather.14.cloned.1.call-done), kind=kOutput, calls=%fused_computation.17 | convolution fusion | flops 4541644800 | bytes 3858432 | tf_op jit(solution)/shard_map/dot_general | solution.py:354
  950.5 7.7 all-to-all-done.2
  (816 shorter events, 431.3 us)
Async XLA Ops:
  37.5 23.9 %all-to-all-start.1 = ((bf16[32,96,128]{2,1,0:T(8,128)(2,1)}), bf16[32,96,128]{2,1,0:T(8,128)(2,1)}, u32[]{:S(2)}, u32[]{:S(2)}) async-start(bf16[32,96,128]{2,1,0:T(8,128)(2,1)} %bitcast.491), calls=%async_computation.1 | async-start | bytes 1572864 | tf_op jit(solution)/shard_map/all_to_all | solution.py:736
  66.0 135.2 %all-gather.10.cloned.1.call-start = ((), (), s32[]{:S(2)}) async-start(), calls=%async_computation.6 | async-start | bytes 3686400 | tf_op jit(solution)/shard_map/all_gather | solution.py:721
  66.6 307.5 %all-gather.12.cloned.1.call-start = ((), (), s32[]{:S(2)}) async-start(), calls=%async_computation.7 | async-start | bytes 15476736 | tf_op jit(solution)/shard_map/all_gather | solution.py:775
  77.2 746.6 %reduce-scatter.2.cloned.1.call-start = ((), (), s32[]{:S(2)}) async-start(), calls=%async_computation.8 | async-start | bytes 7372800 | tf_op jit(solution)/shard_map/reduce_scatter | solution.py:881
  77.3 25.4 %collective-permute-start.3 = (bf16[1832,128]{1,0:T(8,128)(2,1)}, bf16[1832,128]{1,0:T(8,128)(2,1)S(1)}, u32[]{:S(2)}, u32[]{:S(2)}) collective-permute-start(bf16[1832,128]{1,0:T(8,128)(2,1)} %get-tuple-element.443.refs_0_), channel_id=1, source_target_pairs={{0,8},{8,16},{16,24},{24,0},{1,9},{9,17},{17,25},{25,1},{2,10},{10... | collective-permute-start | bytes 1406984 | tf_op jit(solution)/shard_map/ppermute | solution.py:53
  78.7 24.0 %collective-permute-start.2 = (bf16[1832,128]{1,0:T(8,128)(2,1)}, bf16[1832,128]{1,0:T(8,128)(2,1)S(1)}, u32[]{:S(2)}, u32[]{:S(2)}) collective-permute-start(bf16[1832,128]{1,0:T(8,128)(2,1)} %get-tuple-element.443.refs_0_), channel_id=1, source_target_pairs={{0,4},{1,5},{2,6},{3,7},{4,0},{5,1},{6,2},{7,3},{8,12},{9,13},{10,... | collective-permute-start | bytes 1406984 | tf_op jit(solution)/shard_map/ppermute | solution.py:48
  79.7 23.8 %collective-permute-start.1 = (bf16[1832,128]{1,0:T(8,128)(2,1)}, bf16[1832,128]{1,0:T(8,128)(2,1)}, u32[]{:S(2)}, u32[]{:S(2)}) collective-permute-start(bf16[1832,128]{1,0:T(8,128)(2,1)} %get-tuple-element.443.refs_0_), channel_id=1, source_target_pairs={{0,2},{1,3},{2,0},{3,1},{4,6},{5,7},{6,4},{7,5},{8,10},{9,11},{10,... | collective-permute-start | bytes 1406984 | tf_op jit(solution)/shard_map/ppermute | solution.py:48
  80.4 23.1 %collective-permute-start = (bf16[1832,128]{1,0:T(8,128)(2,1)}, bf16[1832,128]{1,0:T(8,128)(2,1)}, u32[]{:S(2)}, u32[]{:S(2)}) collective-permute-start(bf16[1832,128]{1,0:T(8,128)(2,1)} %get-tuple-element.443.refs_0_), channel_id=1, source_target_pairs={{0,1},{1,0},{2,3},{3,2},{4,5},{5,4},{6,7},{7,6},{8,9},{9,8},{10,11... | collective-permute-start | bytes 1406984 | tf_op jit(solution)/shard_map/ppermute | solution.py:48
  109.0 31.3 %collective-permute-start.11 = (bf16[1832,128]{1,0:T(8,128)(2,1)}, bf16[1832,128]{1,0:T(8,128)(2,1)S(1)}, u32[]{:S(2)}, u32[]{:S(2)}) collective-permute-start(bf16[1832,128]{1,0:T(8,128)(2,1)} %copy-done.72), channel_id=1, source_target_pairs={{0,8},{8,16},{16,24},{24,0},{1,9},{9,17},{17,25},{25,1},{2,10},{10... | collective-permute-start | bytes 1406984 | tf_op jit(solution)/shard_map/ppermute | solution.py:53
  115.5 24.9 %collective-permute-start.10 = (bf16[1832,128]{1,0:T(8,128)(2,1)}, bf16[1832,128]{1,0:T(8,128)(2,1)S(1)}, u32[]{:S(2)}, u32[]{:S(2)}) collective-permute-start(bf16[1832,128]{1,0:T(8,128)(2,1)} %copy-done.72), channel_id=1, source_target_pairs={{0,4},{1,5},{2,6},{3,7},{4,0},{5,1},{6,2},{7,3},{8,12},{9,13},{10,... | collective-permute-start | bytes 1406984 | tf_op jit(solution)/shard_map/ppermute | solution.py:48
  117.0 23.4 %collective-permute-start.9 = (bf16[1832,128]{1,0:T(8,128)(2,1)}, bf16[1832,128]{1,0:T(8,128)(2,1)S(1)}, u32[]{:S(2)}, u32[]{:S(2)}) collective-permute-start(bf16[1832,128]{1,0:T(8,128)(2,1)} %copy-done.72), channel_id=1, source_target_pairs={{0,2},{1,3},{2,0},{3,1},{4,6},{5,7},{6,4},{7,5},{8,10},{9,11},{10,... | collective-permute-start | bytes 1406984 | tf_op jit(solution)/shard_map/ppermute | solution.py:48
  117.6 22.8 %collective-permute-start.6 = (bf16[1832,128]{1,0:T(8,128)(2,1)}, bf16[1832,128]{1,0:T(8,128)(2,1)S(1)}, u32[]{:S(2)}, u32[]{:S(2)}) collective-permute-start(bf16[1832,128]{1,0:T(8,128)(2,1)} %copy-done.72), channel_id=1, source_target_pairs={{0,1},{1,0},{2,3},{3,2},{4,5},{5,4},{6,7},{7,6},{8,9},{9,8},{10,11... | collective-permute-start | bytes 1406984 | tf_op jit(solution)/shard_map/ppermute | solution.py:48
  140.4 42.2 %collective-permute-start.25 = (bf16[2,2,512,768]{3,2,1,0:T(8,128)(2,1)S(1)}, bf16[2,2,512,768]{3,2,1,0:T(8,128)(2,1)}, u32[]{:S(2)}, u32[]{:S(2)}) collective-permute-start(bf16[2,2,512,768]{3,2,1,0:T(8,128)(2,1)S(1)} %bitcast.540), channel_id=1, source_target_pairs={{0,1},{1,0},{2,3},{3,2},{4,5},{5,4},{6,7},{7,6},{8,9},{9,8},{10,11... | collective-permute-start | bytes 9437192 | tf_op jit(solution)/shard_map/ppermute | solution.py:48
  141.5 21.0 %collective-permute-start.17 = (bf16[1832,128]{1,0:T(8,128)(2,1)S(1)}, bf16[1832,128]{1,0:T(8,128)(2,1)S(1)}, u32[]{:S(2)}, u32[]{:S(2)}) collective-permute-start(bf16[1832,128]{1,0:T(8,128)(2,1)S(1)} %collective-permute-done.9.refs_10_), channel_id=1, source_target_pairs={{0,1},{1,0},{2,3},{3,2},{4,5},{5,4},{6,7},{7,6},{8,9},{9,8},{10,11... | collective-permute-start | bytes 1406984 | tf_op jit(solution)/shard_map/ppermute | solution.py:48
  141.8 22.3 %collective-permute-start.18 = (bf16[1832,128]{1,0:T(8,128)(2,1)S(1)}, bf16[1832,128]{1,0:T(8,128)(2,1)S(1)}, u32[]{:S(2)}, u32[]{:S(2)}) collective-permute-start(bf16[1832,128]{1,0:T(8,128)(2,1)S(1)} %collective-permute-done.10.refs_11_), channel_id=1, source_target_pairs={{0,1},{1,0},{2,3},{3,2},{4,5},{5,4},{6,7},{7,6},{8,9},{9,8},{10,11... | collective-permute-start | bytes 1406984 | tf_op jit(solution)/shard_map/ppermute | solution.py:48
  156.1 26.5 %collective-permute-start.24 = (bf16[1832,128]{1,0:T(8,128)(2,1)S(1)}, bf16[1832,128]{1,0:T(8,128)(2,1)}, u32[]{:S(2)}, u32[]{:S(2)}) collective-permute-start(bf16[1832,128]{1,0:T(8,128)(2,1)S(1)} %collective-permute-done.11.refs_12_), channel_id=1, source_target_pairs={{0,8},{8,16},{16,24},{24,0},{1,9},{9,17},{17,25},{25,1},{2,10},{10... | collective-permute-start | bytes 1406984 | tf_op jit(solution)/shard_map/ppermute | solution.py:53
  160.8 21.8 %collective-permute-start.23 = (bf16[1832,128]{1,0:T(8,128)(2,1)S(1)}, bf16[1832,128]{1,0:T(8,128)(2,1)S(1)}, u32[]{:S(2)}, u32[]{:S(2)}) collective-permute-start(bf16[1832,128]{1,0:T(8,128)(2,1)S(1)} %collective-permute-done.11.refs_12_), channel_id=1, source_target_pairs={{0,4},{1,5},{2,6},{3,7},{4,0},{5,1},{6,2},{7,3},{8,12},{9,13},{10,... | collective-permute-start | bytes 1406984 | tf_op jit(solution)/shard_map/ppermute | solution.py:48
  162.5 20.1 %collective-permute-start.22 = (bf16[1832,128]{1,0:T(8,128)(2,1)S(1)}, bf16[1832,128]{1,0:T(8,128)(2,1)}, u32[]{:S(2)}, u32[]{:S(2)}) collective-permute-start(bf16[1832,128]{1,0:T(8,128)(2,1)S(1)} %collective-permute-done.11.refs_12_), channel_id=1, source_target_pairs={{0,2},{1,3},{2,0},{3,1},{4,6},{5,7},{6,4},{7,5},{8,10},{9,11},{10,... | collective-permute-start | bytes 1406984 | tf_op jit(solution)/shard_map/ppermute | solution.py:48
  164.1 18.5 %collective-permute-start.19 = (bf16[1832,128]{1,0:T(8,128)(2,1)S(1)}, bf16[1832,128]{1,0:T(8,128)(2,1)S(1)}, u32[]{:S(2)}, u32[]{:S(2)}) collective-permute-start(bf16[1832,128]{1,0:T(8,128)(2,1)S(1)} %collective-permute-done.11.refs_12_), channel_id=1, source_target_pairs={{0,1},{1,0},{2,3},{3,2},{4,5},{5,4},{6,7},{7,6},{8,9},{9,8},{10,11... | collective-permute-start | bytes 1406984 | tf_op jit(solution)/shard_map/ppermute | solution.py:48
  187.0 26.3 %collective-permute-start.28 = (bf16[1832,128]{1,0:T(8,128)(2,1)}, bf16[1832,128]{1,0:T(8,128)(2,1)}, u32[]{:S(2)}, u32[]{:S(2)}) collective-permute-start(bf16[1832,128]{1,0:T(8,128)(2,1)} %collective-permute-done.22.refs_20_), channel_id=1, source_target_pairs={{0,1},{1,0},{2,3},{3,2},{4,5},{5,4},{6,7},{7,6},{8,9},{9,8},{10,11... | collective-permute-start | bytes 1406984 | tf_op jit(solution)/shard_map/ppermute | solution.py:48
  213.4 56.9 %collective-permute-start.41 = (bf16[2,2,512,768]{3,2,1,0:T(8,128)(2,1)S(1)}, bf16[2,2,512,768]{3,2,1,0:T(8,128)(2,1)S(1)}, u32[]{:S(2)}, u32[]{:S(2)}) collective-permute-start(bf16[2,2,512,768]{3,2,1,0:T(8,128)(2,1)S(1)} %bitcast.541), channel_id=1, source_target_pairs={{0,1},{1,0},{2,3},{3,2},{4,5},{5,4},{6,7},{7,6},{8,9},{9,8},{10,11... | collective-permute-start | bytes 9437192 | tf_op jit(solution)/shard_map/ppermute | solution.py:48
  217.3 53.0 %collective-permute-start.37 = (bf16[1832,128]{1,0:T(8,128)(2,1)}, bf16[1832,128]{1,0:T(8,128)(2,1)S(1)}, u32[]{:S(2)}, u32[]{:S(2)}) collective-permute-start(bf16[1832,128]{1,0:T(8,128)(2,1)} %collective-permute-done.33.refs_30_), channel_id=1, source_target_pairs={{0,1},{1,0},{2,3},{3,2},{4,5},{5,4},{6,7},{7,6},{8,9},{9,8},{10,11... | collective-permute-start | bytes 1406984 | tf_op jit(solution)/shard_map/ppermute | solution.py:48
  231.9 38.5 %collective-permute-start.38 = (bf16[1832,128]{1,0:T(8,128)(2,1)}, bf16[1832,128]{1,0:T(8,128)(2,1)S(1)}, u32[]{:S(2)}, u32[]{:S(2)}) collective-permute-start(bf16[1832,128]{1,0:T(8,128)(2,1)} %collective-permute-done.34.refs_31_), channel_id=1, source_target_pairs={{0,1},{1,0},{2,3},{3,2},{4,5},{5,4},{6,7},{7,6},{8,9},{9,8},{10,11... | collective-permute-start | bytes 1406984 | tf_op jit(solution)/shard_map/ppermute | solution.py:48
  231.9 36.8 %collective-permute-start.44 = (bf16[2,256,768]{2,1,0:T(8,128)(2,1)S(1)}, bf16[2,256,768]{2,1,0:T(8,128)(2,1)S(1)}, u32[]{:S(2)}, u32[]{:S(2)}) collective-permute-start(bf16[2,256,768]{2,1,0:T(8,128)(2,1)S(1)} %slice_bitcast_fusion.12), channel_id=1, source_target_pairs={{0,2},{1,3},{2,0},{3,1},{4,6},{5,7},{6,4},{7,5},{8,10},{9,11},{10,... | collective-permute-start | bytes 2359304 | tf_op jit(solution)/shard_map/ppermute | solution.py:48
  232.8 38.1 %collective-permute-start.45 = (bf16[2,256,768]{2,1,0:T(8,128)(2,1)S(1)}, bf16[2,256,768]{2,1,0:T(8,128)(2,1)S(1)}, u32[]{:S(2)}, u32[]{:S(2)}) collective-permute-start(bf16[2,256,768]{2,1,0:T(8,128)(2,1)S(1)} %slice_bitcast_fusion.11), channel_id=1, source_target_pairs={{0,4},{1,5},{2,6},{3,7},{4,0},{5,1},{6,2},{7,3},{8,12},{9,13},{10,... | collective-permute-start | bytes 2359304 | tf_op jit(solution)/shard_map/ppermute | solution.py:48
  273.3 25.1 %collective-permute-start.51 = (bf16[256,768]{1,0:T(8,128)(2,1)}, bf16[256,768]{1,0:T(8,128)(2,1)}, u32[]{:S(2)}, u32[]{:S(2)}) collective-permute-start(bf16[256,768]{1,0:T(8,128)(2,1)} %slice_bitcast_fusion.33), channel_id=1, source_target_pairs={{0,2},{1,3},{2,0},{3,1},{4,6},{5,7},{6,4},{7,5},{8,10},{9,11},{10,... | collective-permute-start | bytes 1179656 | tf_op jit(solution)/shard_map/ppermute | solution.py:48
  273.8 25.9 %collective-permute-start.50 = (bf16[256,768]{1,0:T(8,128)(2,1)S(1)}, bf16[256,768]{1,0:T(8,128)(2,1)}, u32[]{:S(2)}, u32[]{:S(2)}) collective-permute-start(bf16[256,768]{1,0:T(8,128)(2,1)S(1)} %slice_bitcast_fusion.34), channel_id=1, source_target_pairs={{0,4},{1,5},{2,6},{3,7},{4,0},{5,1},{6,2},{7,3},{8,12},{9,13},{10,... | collective-permute-start | bytes 1179656 | tf_op jit(solution)/shard_map/ppermute | solution.py:48
  276.4 25.7 %collective-permute-start.46 = (bf16[2,256,768]{2,1,0:T(8,128)(2,1)}, bf16[2,256,768]{2,1,0:T(8,128)(2,1)}, u32[]{:S(2)}, u32[]{:S(2)}) collective-permute-start(bf16[2,256,768]{2,1,0:T(8,128)(2,1)} %slice_bitcast_fusion.10), channel_id=1, source_target_pairs={{0,2},{1,3},{2,0},{3,1},{4,6},{5,7},{6,4},{7,5},{8,10},{9,11},{10,... | collective-permute-start | bytes 2359304 | tf_op jit(solution)/shard_map/ppermute | solution.py:48
  278.2 25.2 %collective-permute-start.47 = (bf16[2,256,768]{2,1,0:T(8,128)(2,1)}, bf16[2,256,768]{2,1,0:T(8,128)(2,1)}, u32[]{:S(2)}, u32[]{:S(2)}) collective-permute-start(bf16[2,256,768]{2,1,0:T(8,128)(2,1)} %slice_bitcast_fusion.9), channel_id=1, source_target_pairs={{0,4},{1,5},{2,6},{3,7},{4,0},{5,1},{6,2},{7,3},{8,12},{9,13},{10,... | collective-permute-start | bytes 2359304 | tf_op jit(solution)/shard_map/ppermute | solution.py:48
  398.7 32.5 %collective-permute-start.58 = (bf16[1,128,768]{2,1,0:T(8,128)(2,1)S(1)}, bf16[1,128,768]{2,1,0:T(8,128)(2,1)S(1)}, u32[]{:S(2)}, u32[]{:S(2)}) collective-permute-start(bf16[1,128,768]{2,1,0:T(8,128)(2,1)S(1)} %bitcast.473), channel_id=1, source_target_pairs={{0,2},{1,3},{2,0},{3,1},{4,6},{5,7},{6,4},{7,5},{8,10},{9,11},{10,... | collective-permute-start | bytes 589832 | tf_op jit(solution)/shard_map/ppermute | solution.py:48
  432.8 23.7 %collective-permute-start.59 = (bf16[2,128,768]{2,1,0:T(8,128)(2,1)}, bf16[2,128,768]{2,1,0:T(8,128)(2,1)}, u32[]{:S(2)}, u32[]{:S(2)}) collective-permute-start(bf16[2,128,768]{2,1,0:T(8,128)(2,1)} %pad_maximum_fusion.8), channel_id=1, source_target_pairs={{0,4},{1,5},{2,6},{3,7},{4,0},{5,1},{6,2},{7,3},{8,12},{9,13},{10,... | collective-permute-start | bytes 1179656 | tf_op jit(solution)/shard_map/ppermute | solution.py:48
  609.6 23.5 %collective-permute-start.75 = (f32[16,576,128]{2,1,0:T(8,128)}, f32[16,576,128]{2,1,0:T(8,128)}, u32[]{:S(2)}, u32[]{:S(2)}) collective-permute-start(f32[16,576,128]{2,1,0:T(8,128)} %get-tuple-element.248), channel_id=1, source_target_pairs={{0,1},{1,0},{2,3},{3,2},{4,5},{5,4},{6,7},{7,6},{8,9},{9,8},{10,11... | collective-permute-start | bytes 14155784 | tf_op jit(solution)/shard_map/ppermute | solution.py:48
  611.9 274.9 %all-gather.14.cloned.1.call-start = ((), (), s32[]{:S(2)}) async-start(), calls=%async_computation.9 | async-start | bytes 7077888 | tf_op jit(solution)/shard_map/all_gather | solution.py:917
  637.8 26.7 %collective-permute-start.77 = (bf16[2,576,128]{2,1,0:T(8,128)(2,1)S(1)}, bf16[2,576,128]{2,1,0:T(8,128)(2,1)}, u32[]{:S(2)}, u32[]{:S(2)}) collective-permute-start(bf16[2,576,128]{2,1,0:T(8,128)(2,1)S(1)} %fusion.140), channel_id=1, source_target_pairs={{0,4},{1,5},{2,6},{3,7},{4,0},{5,1},{6,2},{7,3},{8,12},{9,13},{10,... | collective-permute-start | bytes 884744 | tf_op jit(solution)/shard_map/ppermute | solution.py:48
  638.5 27.5 %collective-permute-start.76 = (bf16[2,576,128]{2,1,0:T(8,128)(2,1)}, bf16[2,576,128]{2,1,0:T(8,128)(2,1)}, u32[]{:S(2)}, u32[]{:S(2)}) collective-permute-start(bf16[2,576,128]{2,1,0:T(8,128)(2,1)} %fusion.139), channel_id=1, source_target_pairs={{0,2},{1,3},{2,0},{3,1},{4,6},{5,7},{6,4},{7,5},{8,10},{9,11},{10,... | collective-permute-start | bytes 884744 | tf_op jit(solution)/shard_map/ppermute | solution.py:48
  640.8 28.0 %collective-permute-start.79 = (bf16[2,2,576,128]{3,2,0,1:T(8,128)(2,1)}, bf16[2,2,576,128]{3,2,0,1:T(8,128)(2,1)}, u32[]{:S(2)}, u32[]{:S(2)}) collective-permute-start(bf16[2,2,576,128]{3,2,0,1:T(8,128)(2,1)} %fusion.134), channel_id=1, source_target_pairs={{0,4},{1,5},{2,6},{3,7},{4,0},{5,1},{6,2},{7,3},{8,12},{9,13},{10,... | collective-permute-start | bytes 1769480 | tf_op jit(solution)/shard_map/ppermute | solution.py:48
  641.8 28.2 %collective-permute-start.78 = (bf16[2,2,576,128]{3,2,0,1:T(8,128)(2,1)S(1)}, bf16[2,2,576,128]{3,2,0,1:T(8,128)(2,1)}, u32[]{:S(2)}, u32[]{:S(2)}) collective-permute-start(bf16[2,2,576,128]{3,2,0,1:T(8,128)(2,1)S(1)} %fusion.133), channel_id=1, source_target_pairs={{0,2},{1,3},{2,0},{3,1},{4,6},{5,7},{6,4},{7,5},{8,10},{9,11},{10,... | collective-permute-start | bytes 1769480 | tf_op jit(solution)/shard_map/ppermute | solution.py:48
  692.3 17.4 %collective-permute-start.80 = (f32[576,128]{1,0:T(8,128)}, f32[576,128]{1,0:T(8,128)S(1)}, u32[]{:S(2)}, u32[]{:S(2)}) collective-permute-start(f32[576,128]{1,0:T(8,128)} %get-tuple-element.256), channel_id=1, source_target_pairs={{0,8},{8,16},{16,24},{24,0},{1,9},{9,17},{17,25},{25,1},{2,10},{10... | collective-permute-start | bytes 884744 | tf_op jit(solution)/shard_map/ppermute | solution.py:53
  692.9 17.9 %collective-permute-start.81 = (bf16[2,576,128]{2,1,0:T(8,128)(2,1)S(1)}, bf16[2,576,128]{2,1,0:T(8,128)(2,1)S(1)}, u32[]{:S(2)}, u32[]{:S(2)}) collective-permute-start(bf16[2,576,128]{2,1,0:T(8,128)(2,1)S(1)} %fusion.141), channel_id=1, source_target_pairs={{0,2},{1,3},{2,0},{3,1},{4,6},{5,7},{6,4},{7,5},{8,10},{9,11},{10,... | collective-permute-start | bytes 884744 | tf_op jit(solution)/shard_map/ppermute | solution.py:48
  711.7 19.2 %collective-permute-start.83 = (f32[576,128]{1,0:T(8,128)S(1)}, f32[576,128]{1,0:T(8,128)S(1)}, u32[]{:S(2)}, u32[]{:S(2)}) collective-permute-start(f32[576,128]{1,0:T(8,128)S(1)} %add.835), channel_id=1, source_target_pairs={{0,8},{8,16},{16,24},{24,0},{1,9},{9,17},{17,25},{25,1},{2,10},{10... | collective-permute-start | bytes 884744 | tf_op jit(solution)/shard_map/ppermute | solution.py:53
  716.9 18.1 %collective-permute-start.84 = (f32[576,128]{1,0:T(8,128)S(1)}, f32[576,128]{1,0:T(8,128)S(1)}, u32[]{:S(2)}, u32[]{:S(2)}) collective-permute-start(f32[576,128]{1,0:T(8,128)S(1)} %get-tuple-element.266), channel_id=1, source_target_pairs={{0,8},{8,16},{16,24},{24,0},{1,9},{9,17},{17,25},{25,1},{2,10},{10... | collective-permute-start | bytes 884744 | tf_op jit(solution)/shard_map/ppermute | solution.py:53
  774.1 42.5 %collective-permute-start.88 = (f32[16,680,128]{2,1,0:T(8,128)}, f32[16,680,128]{2,1,0:T(8,128)}, u32[]{:S(2)}, u32[]{:S(2)}) collective-permute-start(f32[16,680,128]{2,1,0:T(8,128)} %get-tuple-element.278), channel_id=1, source_target_pairs={{0,1},{1,0},{2,3},{3,2},{4,5},{5,4},{6,7},{7,6},{8,9},{9,8},{10,11... | collective-permute-start | bytes 16711688 | tf_op jit(solution)/shard_map/ppermute | solution.py:48
  792.9 23.5 %collective-permute-start.90 = (bf16[512,192]{0,1:T(8,128)(2,1)S(1)}, bf16[512,192]{0,1:T(8,128)(2,1)S(1)}, u32[]{:S(2)}, u32[]{:S(2)}) collective-permute-start(bf16[512,192]{0,1:T(8,128)(2,1)S(1)} %get-tuple-element.358), channel_id=1, source_target_pairs={{0,16},{8,24},{16,0},{24,8},{1,17},{9,25},{17,1},{25,9},{2,18},{10... | collective-permute-start | bytes 589832 | tf_op jit(solution)/shard_map/ppermute | solution.py:53
  793.0 23.5 %collective-permute-start.89 = (bf16[512,192]{0,1:T(8,128)(2,1)S(1)}, bf16[512,192]{0,1:T(8,128)(2,1)S(1)}, u32[]{:S(2)}, u32[]{:S(2)}) collective-permute-start(bf16[512,192]{0,1:T(8,128)(2,1)S(1)} %get-tuple-element.359), channel_id=1, source_target_pairs={{0,8},{8,16},{16,24},{24,0},{1,9},{9,17},{17,25},{25,1},{2,10},{10... | collective-permute-start | bytes 589832 | tf_op jit(solution)/shard_map/ppermute | solution.py:53
  795.0 21.6 %collective-permute-start.87 = (f32[576,128]{1,0:T(8,128)S(1)}, f32[576,128]{1,0:T(8,128)S(1)}, u32[]{:S(2)}, u32[]{:S(2)}) collective-permute-start(f32[576,128]{1,0:T(8,128)S(1)} %copy-done.86), channel_id=1, source_target_pairs={{0,8},{8,16},{16,24},{24,0},{1,9},{9,17},{17,25},{25,1},{2,10},{10... | collective-permute-start | bytes 884744 | tf_op jit(solution)/shard_map/ppermute | solution.py:53
  830.3 25.2 %collective-permute-start.93 = (bf16[2,2,680,128]{3,2,0,1:T(8,128)(2,1)}, bf16[2,2,680,128]{3,2,0,1:T(8,128)(2,1)}, u32[]{:S(2)}, u32[]{:S(2)}) collective-permute-start(bf16[2,2,680,128]{3,2,0,1:T(8,128)(2,1)} %fusion.129), channel_id=1, source_target_pairs={{0,4},{1,5},{2,6},{3,7},{4,0},{5,1},{6,2},{7,3},{8,12},{9,13},{10,... | collective-permute-start | bytes 2088968 | tf_op jit(solution)/shard_map/ppermute | solution.py:48
  832.7 25.0 %collective-permute-start.92 = (bf16[2,2,680,128]{3,2,0,1:T(8,128)(2,1)}, bf16[2,2,680,128]{3,2,0,1:T(8,128)(2,1)}, u32[]{:S(2)}, u32[]{:S(2)}) collective-permute-start(bf16[2,2,680,128]{3,2,0,1:T(8,128)(2,1)} %fusion.128), channel_id=1, source_target_pairs={{0,2},{1,3},{2,0},{3,1},{4,6},{5,7},{6,4},{7,5},{8,10},{9,11},{10,... | collective-permute-start | bytes 2088968 | tf_op jit(solution)/shard_map/ppermute | solution.py:48
  917.7 40.5 %all-to-all-start.2 = ((f32[32,96,128]{2,1,0:T(8,128)}), f32[32,96,128]{2,1,0:T(8,128)S(1)}, u32[]{:S(2)}, u32[]{:S(2)}) async-start(f32[32,96,128]{2,1,0:T(8,128)} %bitcast.463), calls=%async_computation.3 | async-start | bytes 3145728 | tf_op jit(solution)/shard_map/all_to_all | solution.py:926
  (222 other events, 2467.3 us)
Sparse Core Ops, SparseCore 1:
  68.6 78.8 all-gather.9
  150.3 138.0 all-gather.11
  612.0 113.6 reduce-scatter.1
  824.9 61.4 all-gather.13

commit v6 on v5

--- a/solution.py
+++ b/solution.py
@@ -1,5 +1,4 @@
 import functools
-import math
 
 import jax
 import jax.numpy as jnp
@@ -41,6 +40,10 @@
 norm_eps = 1e-12
 cosine_eps = 1e-06
 
+CHIPS = 16
+SLABS = ((0, 48, 1, 12, 0), (48, 48, 4, 3, 0), (96, 48, 1, 9, 0), (96, 48, 1, 3, 9), (144, 16, 2, 3, 0))
+SHARE = (160, 1536)
+TAIL_AT = (144, 6)
 CORE, ACROSS, DEEP = 1, 2, 4
 
 
@@ -99,15 +102,21 @@
     return sizes, starts
 
 
-def homes_of(tiles, tiles_all, devices):
+def homes_of(tiles, tiles_all, devices, near):
     per = tiles_all // devices
     sizes, starts = shares_of(tiles_all, devices)
     homes = ((tiles - TAIL) // sizes[-1]) * per + starts[-1] + (tiles - TAIL) % sizes[-1]
     for (first, height, across), size, start in zip(HOME_ORDER, sizes, starts):
         at = tiles - first
-        line = (at % across) * height + at // across
         inside = (at >= 0) & (at < height * across)
-        homes = jnp.where(inside, (line // size) * per + start + line % size, homes)
+        if near:
+            row, column = at // across, at % across
+            slab, half = height // CHIPS, across // 2
+            owner = row // slab * 2 + column // half
+            line = column % half * slab + row % slab
+        else:
+            owner, line = at // size, at % size
+        homes = jnp.where(inside, owner * per + start + line, homes)
     return homes
 
 
@@ -163,7 +172,14 @@
     )(slots, lines, tiles)
 
 
-def land_kernel(index, packed, tiles, stage, full):
+def slab_pieces(starts):
+    for (row, lines, groups, columns, offset), start in zip(SLABS, starts):
+        for column in range(columns):
+            for part in range(groups):
+                yield row, offset + part * columns + column, lines, start + (column * groups + part) * lines
+
+
+def land_kernel(index, packed, tiles, stage, full, *, starts):
     stage[...] = packed[...].astype(jnp.float32)
 
     def place(start, size):
@@ -171,19 +187,48 @@
             full[pl.ds(index[start + u], 1), :] = stage[pl.ds(start + u, 1), :]
 
     row_steps(packed.shape[0], 128, place)
-    tiles[...] = full[pl.ds(0, tiles.shape[0]), :].astype(tiles.dtype)
-
-
-def land_tiles(index, packed, per):
+    if starts is None:
+        tiles[...] = full[pl.ds(0, tiles.shape[0]), :].astype(tiles.dtype)
+    else:
+        tiles[...] = jnp.zeros_like(tiles)
+        for row, column, lines, line in (*slab_pieces(starts), (*TAIL_AT, 16, starts[-1])):
+            tiles[pl.ds(row, lines), column * TILE : (column + 1) * TILE] = full[pl.ds(line, lines), :].astype(
+                tiles.dtype
+            )
+
+
+def land_tiles(index, packed, per, starts):
     slot_count = packed.shape[0]
     return pl.pallas_call(
-        land_kernel,
+        functools.partial(land_kernel, starts=starts),
         in_specs=[pl.BlockSpec(memory_space=pltpu.SMEM), pl.BlockSpec(memory_space=pltpu.VMEM)],
         out_specs=pl.BlockSpec(memory_space=pltpu.VMEM),
-        out_shape=jax.ShapeDtypeStruct((per, TILE), jnp.bfloat16),
+        out_shape=jax.ShapeDtypeStruct((per, TILE) if starts is None else SHARE, jnp.bfloat16),
         scratch_shapes=[pltpu.VMEM((slot_count, TILE), jnp.float32), pltpu.VMEM((per + 8, TILE), jnp.float32)],
         name="land_tiles",
     )(index, packed)
+
+
+def share_lines_kernel(up, down, qkv, rest, lines, *, starts):
+    slabs = (up, down, qkv, rest, rest)
+    first = (0, 0, 0, 0, 48)
+    for n, (source, (_, _, _, columns, _), begin, start) in enumerate(zip(slabs, SLABS, first, starts)):
+        height = HOME_ORDER[n][1] // CHIPS
+        for column in range(columns):
+            lines[pl.ds(start + column * height, height), :] = source[
+                pl.ds(begin, height), column * TILE : (column + 1) * TILE
+            ]
+    lines[pl.ds(starts[-1], 8), :] = rest[pl.ds(80, 8), :TILE]
+
+
+def share_lines(up, down, qkv, rest, per, starts):
+    return pl.pallas_call(
+        functools.partial(share_lines_kernel, starts=starts),
+        in_specs=[pl.BlockSpec(memory_space=pltpu.VMEM)] * 4,
+        out_specs=pl.BlockSpec(memory_space=pltpu.VMEM),
+        out_shape=jax.ShapeDtypeStruct((per, TILE), jnp.float32),
+        name="share_lines",
+    )(up, down, qkv, rest)
 
 
 def pick_kernel(index, source, target, *, count):
@@ -204,14 +249,12 @@
     )(index, source)
 
 
-def assemble_kernel(spot, *refs, places, sizes, starts):
+def assemble_kernel(spot, *refs, places):
     arrivals = refs[: len(places)]
-    targets = refs[len(places) : len(places) + 5]
-    tail = refs[len(places) + 5]
-    landed, sems = refs[len(places) + 6 :]
+    up, down, qkv, out, place, tail, landed, sems = refs[len(places) :]
     copies = []
-    for n, (arrival, place) in enumerate(zip(arrivals, places)):
-        target = landed.at[place[0], pl.ds(place[1], place[2])]
+    for n, (arrival, where) in enumerate(zip(arrivals, places)):
+        target = landed.at[where[0], pl.ds(where[1], where[2])]
         copies.append(pltpu.make_async_copy(arrival, target, sems.at[n]))
     for copy in copies:
         copy.start()
@@ -220,101 +263,43 @@
 
     def one_device(block, carry):
         owner = ((spot[0] + 4 - block // 8) % 4) * 8 + (spot[1] ^ (block % 8))
-        for target, (_, height, _), size, start in zip(targets, HOME_ORDER, sizes, starts):
-            unit = math.gcd(size, height)
-            for part in range(size // unit):
-                line = owner * size + part * unit
-                column = line // height
-                target[
-                    pl.ds(pl.multiple_of(line - column * height, 16), unit),
-                    pl.ds(pl.multiple_of(column * TILE, TILE), TILE),
-                ] = landed[block, pl.ds(start + part * unit, unit), :]
-        tail[owner] = landed[block, pl.ds(starts[-1], sizes[-1]), :].astype(jnp.float32)
+        chip, core = owner // 2, owner % 2
+
+        def put(target, row, lines, width, source_row, source_column):
+            target[
+                pl.ds(pl.multiple_of(row, 16), lines), pl.ds(pl.multiple_of(core * width, TILE), width)
+            ] = landed[block, pl.ds(source_row, lines), source_column : source_column + width]
+
+        put(up, chip * 48, 48, 1536, 0, 0)
+        for part in range(4):
+            put(down, chip * 192 + part * 48, 48, 384, 48, part * 384)
+        put(qkv, chip * 48, 48, 1152, 96, 0)
+        put(out, chip * 48, 48, 384, 96, 1152)
+        for part in range(2):
+            put(place, chip * 32 + part * 16, 16, 384, 144, part * 384)
+        tail[owner] = landed[block, pl.ds(TAIL_AT[0], 16), TAIL_AT[1] * TILE : (TAIL_AT[1] + 1) * TILE].astype(
+            jnp.float32
+        )[:8]
         return carry
 
     lax.fori_loop(0, landed.shape[0], one_device, 0)
 
 
-def assemble_layer(spot, arrivals, places, tiles_all, devices):
-    sizes, starts = shares_of(tiles_all, devices)
+def assemble_layer(spot, arrivals, places, devices):
     return pl.pallas_call(
-        functools.partial(assemble_kernel, places=places, sizes=sizes, starts=starts),
+        functools.partial(assemble_kernel, places=places),
         in_specs=[pl.BlockSpec(memory_space=pltpu.SMEM)] + [pl.BlockSpec(memory_space=pl.ANY)] * len(arrivals),
         out_specs=[pl.BlockSpec(memory_space=pltpu.VMEM)] * 6,
         out_shape=[jax.ShapeDtypeStruct((h, a * TILE), jnp.bfloat16) for _, h, a in HOME_ORDER]
-        + [jax.ShapeDtypeStruct((devices, sizes[-1], TILE), jnp.float32)],
+        + [jax.ShapeDtypeStruct((devices, 8, TILE), jnp.float32)],
         scratch_shapes=[
-            pltpu.VMEM((devices, tiles_all // devices, TILE), jnp.bfloat16),
+            pltpu.VMEM((devices, *SHARE), jnp.bfloat16),
             pltpu.SemaphoreType.DMA((len(arrivals),)),
         ],
         compiler_params=pltpu.CompilerParams(vmem_limit_bytes=VMEM_LIMIT),
         cost_estimate=pl.CostEstimate(flops=0, bytes_accessed=60_000_000, transcendentals=0),
         name="assemble_layer",
     )(spot, *arrivals)
-
-
-def split_kernel(spot, *refs, count, sizes):
-    near, far = refs[2 * count :]
-    start = 0
-    for n in range(count):
-        near[0, pl.ds(start, sizes[n]), :] = refs[n][0]
-        far[0, pl.ds(start, sizes[n]), :] = refs[count + n][0]
-        start += sizes[n]
-
-
-def split_cores(spot, parts):
-    sizes = [part.shape[1] for part in parts]
-    total = sum(sizes)
-
-    def owner(block, spot, core):
-        return ((spot[0] + block // 4) % 4) * 8 + (spot[1] ^ ((block % 4) * 2 + core))
-
-    specs = [
-        pl.BlockSpec((1, size, TILE), lambda i, spot, core=core: (owner(i, spot, core), 0, 0))
-        for core in (0, 1)
-        for size in sizes
-    ]
-    return pl.pallas_call(
-        functools.partial(split_kernel, count=len(parts), sizes=sizes),
-        grid_spec=pltpu.PrefetchScalarGridSpec(
-            num_scalar_prefetch=1,
-            grid=(16,),
-            in_specs=specs,
-            out_specs=[pl.BlockSpec((1, total, TILE), lambda i, spot: (i, 0, 0))] * 2,
-        ),
-        out_shape=[jax.ShapeDtypeStruct((16, total, TILE), jnp.float32)] * 2,
-        cost_estimate=pl.CostEstimate(flops=0, bytes_accessed=32 * total * TILE * 8, transcendentals=0),
-        name="split_cores",
-    )(spot, *parts, *parts)
-
-
-def weight_grad_kernel(left, right, target):
-    product = lax.dot_general(
-        left[...], right[...], (((0,), (0,)), ((), ())), preferred_element_type=jnp.float32
-    )
-    for column in range(target.shape[0]):
-        target[column] = product[:, column * TILE : (column + 1) * TILE]
-
-
-def weight_grad(left, right, columns):
-    rows, height = left.shape
-    across = right.shape[1] // TILE
-    return pl.pallas_call(
-        weight_grad_kernel,
-        grid=(height // D, across // columns),
-        in_specs=[
-            pl.BlockSpec((rows, D), lambda i, j: (0, i)),
-            pl.BlockSpec((rows, columns * TILE), lambda i, j: (0, j)),
-        ],
-        out_specs=pl.BlockSpec((columns, D, TILE), lambda i, j: (j, i, 0)),
-        out_shape=jax.ShapeDtypeStruct((across, height, TILE), jnp.float32),
-        cost_estimate=pl.CostEstimate(
-            flops=2 * rows * height * across * TILE,
-            bytes_accessed=rows * (height + across * TILE) * 2 + height * across * TILE * 4,
-            transcendentals=0,
-        ),
-        name="weight_grad",
-    )(left, right)
 
 
 def unpack_kernel(source, target, stage, *, across):
@@ -468,11 +453,11 @@
         grad_final, saved["normed_two"], saved["inverse_two"], small_rows[8]
     )
     grad_out = grad_sum_two.astype(jnp.bfloat16)
-    flow.add(weight_grad(saved["activated"], grad_out, 6))
+    flow.add_product(saved["activated"], grad_out)
     grad_act = trailing_array_multiply(grad_out, pieces["down"])
     grad_hidden = (grad_act * gelu_slope(saved["hidden"])).astype(jnp.bfloat16)
     (grad_hidden,) = flow.advance(grad_hidden)
-    flow.add(weight_grad(saved["middle_low"], grad_hidden, 6))
+    flow.add_product(saved["middle_low"], grad_hidden)
     grad_middle = grad_sum_two + trailing_array_multiply(grad_hidden, pieces["up"])
     grad_sum_one, grad_gain_one, grad_shift_one = norm_backward(
         grad_middle, saved["normed_one"], saved["inverse_one"], small_rows[6]
@@ -491,7 +476,7 @@
     seqs_count = lengths.shape[0]
     rows_here = seqs_count * LEN
     grad_att = grad_sum_one.astype(jnp.bfloat16)
-    grad_outw = weight_grad(saved["context"], grad_att, 6)
+    grad_outw = matmul_left(saved["context"], grad_att)
     grad_context = (
         trailing_array_multiply(grad_att, pieces["out"])
         .astype(jnp.bfloat16)
@@ -525,7 +510,7 @@
         .astype(jnp.bfloat16)
     )
     (grad_proj,) = flow.advance(grad_proj)
-    grad_qkv = weight_grad(saved["inputs"], grad_proj, 6)
+    flow.add_product(saved["inputs"], grad_proj)
     grad_bias_all = jnp.sum(grad_proj.astype(jnp.float32), axis=0)
     grad_first = grad_sum_one + trailing_array_multiply(grad_proj, pieces["qkv"])
     grad_embedded, grad_gain_zero, grad_shift_zero = norm_backward(
@@ -551,7 +536,7 @@
         ]
     )
     (grad_embedded,) = flow.advance(grad_embedded)
-    flow.add(grad_qkv, grad_outw, grad_place.reshape(LEN, 6, TILE).transpose(1, 0, 2), tail)
+    flow.add_rest(grad_outw, grad_place, tail)
     return grad_embedded
 
 
@@ -625,25 +610,62 @@
     return arrivals, places, done
 
 
+def at(value, index, axis):
+    return lax.dynamic_index_in_dim(value, index, axis, keepdims=False)
+
+
+def sent_low(value, bit):
+    return swap(value.astype(jnp.bfloat16), bit).astype(jnp.float32)
+
+
+def bit_of(bit):
+    return lax.axis_index("vocab") // bit % 2
+
+
+def halved(value, axis, bit):
+    mine = bit_of(bit)
+    return at(value, mine, axis) + sent_low(at(value, 1 - mine, axis), bit)
+
+
 def reduce_steps(near, far):
-    chip = yield [near + swap(far, CORE)]
-    first, second = yield list(plane_first(chip[0]))
-    blocks = yield plane_second(first, second)
+    (chip,) = yield [near + swap(far, CORE)]
+    chip = chip.reshape(4, 2, 2, chip.shape[0] // CHIPS, chip.shape[1])
+    first, second = yield [halved(chip[:2], 2, ACROSS), halved(chip[2:], 1, DEEP)]
+    first, second = yield [halved(first, 1, DEEP), halved(second, 1, ACROSS)]
+    z = lax.axis_index("dp")
+    blocks = [
+        jnp.where((z + k) % 4 < 2, at(first, (z + k) % 2, 0), at(second, (z + k) % 2, 0)) for k in range(4)
+    ]
     for _ in range(3):
         blocks = yield ring_hop(blocks)
     return blocks[0]
 
 
 class Flow:
-    def __init__(self, spot, devices):
-        self.spot, self.devices = spot, devices
+    def __init__(self):
         self.lines, self.waiting, self.sums = [], [], []
 
-    def add(self, *parts):
-        near, far = split_cores(self.spot, [part.reshape(self.devices, -1, TILE) for part in parts])
+    def add(self, near, far):
         self.lines.append(reduce_steps(near, far))
         self.waiting.append(next(self.lines[-1]))
         self.sums.append(None)
+
+    def add_product(self, left, right):
+        width = right.shape[1] // 2
+        core = bit_of(CORE)
+        far = matmul_left(left, lax.dynamic_slice_in_dim(right, (1 - core) * width, width, 1))
+        near = matmul_left(left, lax.dynamic_slice_in_dim(right, core * width, width, 1))
+        self.add(near, far)
+
+    def add_rest(self, out, place, tail):
+        def half(core):
+            columns = [
+                lax.dynamic_slice_in_dim(whole, core * 384, 384, 1).reshape(CHIPS, -1, 384) for whole in (out, place)
+            ]
+            ends = jnp.pad(at(tail.reshape(CHIPS, 2, 8, TILE), core, 1), ((0, 0), (0, 0), (0, 256)))
+            return jnp.concatenate([*columns, ends], axis=1).reshape(-1, 384)
+
+        self.add(half(bit_of(CORE)), half(1 - bit_of(CORE)))
 
     def advance(self, *values):
         tied, values = together([moved for moved in self.waiting if moved is not None], list(values))
@@ -661,30 +683,17 @@
     def __init__(self, devices):
         self.devices, self.sums = devices, []
 
-    def add(self, *parts):
-        whole = jnp.concatenate([part.reshape(self.devices, -1, TILE) for part in parts], axis=1)
-        self.sums.append(lax.psum_scatter(whole, ("dp", "vocab"), scatter_dimension=0, tiled=False))
+    def add_product(self, left, right):
+        parts = matmul_left(left, right).reshape(self.devices, -1, TILE)
+        self.sums.append(lax.psum_scatter(parts, ("dp", "vocab"), scatter_dimension=0, tiled=False))
+
+    def add_rest(self, out, place, tail):
+        parts = [part.reshape(self.devices, -1, TILE) for part in (out, place, tail)]
+        parts = jnp.concatenate(parts, axis=1)
+        self.sums.append(lax.psum_scatter(parts, ("dp", "vocab"), scatter_dimension=0, tiled=False))
 
     def advance(self, *values):
         return values
-
-
-def sent_low(value, bit):
-    return swap(value.astype(jnp.bfloat16), bit).astype(jnp.float32)
-
-
-def plane_first(value):
-    value = value.reshape(4, 2, 2, value.shape[1], TILE)
-    first, second = value[2:], value[:2]
-    first = first[:, :, 0] + sent_low(first[:, :, 1], ACROSS)
-    second = second[:, 0] + sent_low(second[:, 1], DEEP)
-    return first, second
-
-
-def plane_second(first, second):
-    first = first[:, 0] + sent_low(first[:, 1], DEEP)
-    second = second[:, 0] + sent_low(second[:, 1], ACROSS)
-    return [second[0], second[1], first[0], first[1]]
 
 
 def on_device(
@@ -720,7 +729,8 @@
     facts = jnp.concatenate([token_ids.reshape(LEN), lengths, mask_count, jnp.zeros((TILE - 2,), jnp.int32)])
     table_low = lax.all_gather(student_embed.T.astype(jnp.bfloat16), "dp", axis=0, tiled=True)
 
-    homes = homes_of(owner_order, tiles_all, devices)
+    homes = homes_of(owner_order, tiles_all, devices, near)
+    sizes, starts = shares_of(tiles_all, devices)
     one_of = jnp.arange(devices, dtype=jnp.int32)
     pairs = jnp.sum((homes.reshape(devices, per, 1) // per == one_of).astype(jnp.int32), axis=1)
     crowded = jnp.max(pairs) > capacity
@@ -736,12 +746,16 @@
     packed = lax.all_to_all(packed.reshape(devices, capacity, TILE), everywhere, 0, 0)
     home_line = lax.all_to_all(home_line[:slot_count].reshape(devices, 1, capacity), everywhere, 0, 0)
     home_line = home_line.reshape(slot_count)
-    home_tiles = land_tiles(home_line, packed.reshape(slot_count, TILE), per)
+    home_tiles = land_tiles(home_line, packed.reshape(slot_count, TILE), per, starts if near else None)
+    home_tiles, table_low = together(home_tiles, table_low)
 
     def every_tile(tiles):
         stored = lax.all_gather(student_flat.astype(jnp.bfloat16), everywhere, axis=0, tiled=True)
         sources = jnp.zeros((tiles_all,), jnp.int32).at[homes].set(jnp.arange(tiles_all, dtype=jnp.int32))
-        return stored[lax.dynamic_slice_in_dim(sources, device * per, per)]
+        stored = stored[lax.dynamic_slice_in_dim(sources, device * per, per)]
+        if near:
+            return land_tiles(lines, stored, per, starts)
+        return stored
 
     home_tiles = lax.cond(crowded, every_tile, lambda tiles: tiles, home_tiles)
 
@@ -776,7 +790,7 @@
         arrivals, places, done = gather_layer(home_tiles, fillers)
         looked_s, looked_t = done[7], (done[8], done[9])
         looked_s = plane_hop(looked_s)
-        matrices = assemble_layer(spot, arrivals, tuple(places), tiles_all, devices)
+        matrices = assemble_layer(spot, arrivals, tuple(places), devices)
         matrices, looked_s, facts = together(matrices, looked_s, facts)
         other_facts = gather_near(jnp.stack([shift(facts, 1), shift(facts, 2), shift(facts, 3)]))
         all_facts = jnp.concatenate([plane_facts[:, None], other_facts], axis=1)
@@ -788,9 +802,8 @@
         plane_facts = lax.dynamic_index_in_dim(all_facts, lax.axis_index("dp"), 1, keepdims=False)
         teacher_tiles = lax.all_gather(teacher_flat, everywhere, axis=0, tiled=True)
         layer = lax.all_gather(home_tiles, everywhere, axis=0)
-        sizes, starts = shares_of(tiles_all, devices)
         matrices = [
-            layer[:, start : start + size].reshape(across, height, TILE).transpose(1, 0, 2).reshape(height, -1)
+            layer[:, start : start + size].reshape(height, across * TILE)
             for (_, height, across), size, start in zip(HOME_ORDER, sizes, starts)
         ]
         matrices.append(layer[:, starts[-1] :].astype(jnp.float32))
@@ -890,7 +903,7 @@
         final_t - (products * inverse_s * inverse_s)[:, None] * final_s
     )
     grad_final = grad_final.at[offsets].add(grad_rows)
-    flow = Flow(spot, devices) if near else PlainFlow(devices)
+    flow = Flow() if near else PlainFlow(devices)
     grad_sum_one, grad_small, grad_upbias = feed_backward(student, saved, grad_final, flow)
     grad_embedded = attention_backward(
         student, saved, grad_sum_one, grad_small, grad_upbias, lengths, tiles_all - TAIL, flow
@@ -920,8 +933,11 @@
     (token_grads,) = flow.advance(token_grads)
     (token_part,) = flow.advance(token_sum(0))
     flow.advance()
-    sum_down, sum_up, sum_rest = flow.sums
-    home_grads = jnp.concatenate([sum_up, sum_down, sum_rest])
+    sum_down, sum_up, sum_qkv, sum_rest = flow.sums
+    if near:
+        home_grads = share_lines(sum_up, sum_down, sum_qkv, sum_rest, per, starts)
+    else:
+        home_grads = jnp.concatenate([sum_up, sum_down, sum_qkv, sum_rest])
     returned = pick_tiles(jnp.minimum(home_line, per - 1), home_grads, slot_count)
     returned = lax.all_to_all(returned.reshape(devices, capacity, TILE), everywhere, 0, 0)
     flat_grad = pick_tiles(jnp.minimum(slots, slot_count - 1), returned.reshape(slot_count, TILE), per)

time: 1010 us -> 919 us (0.910)
  Pallas kernels: 125 us -> 55.7 us
  local copies, waits for them, and re-layouts: 76.7 us -> 54.6 us
  matrix products: 210 us -> 231 us
  blocking collectives: 14.2 us -> 0 us
  other arithmetic: 132 us -> 119 us
    pallas_call x9 -> x3, Pallas kernels: 89.4 us -> 19.6 us  [the longest x1 13.7 us: assemble_layer(): pl.pallas_call(functools.partial(assemble_kernel, places=places), in_spec...]
    dot_general x4 -> x11, matrix products: 40.7 us -> 73.9 us  [matmul_left(): lax.dot_general(left_side, right_side, (((0,), (0,)), ((), ())), preferre...]
    ppermute x18 -> x21, waiting for transfers between devices: 127 us -> 100 us  [shift(): lax.ppermute(value, 'dp', [(i, (i + steps) % size) for i in range(size)])]
    all_to_all x1, waiting for transfers between devices: 12.4 us -> 28.9 us  [on_device(): lax.all_to_all(packed.reshape(devices, capacity, TILE), everywhere, 0, 0)]
    all_to_all x1 -> x0, blocking collectives: 14.2 us -> none  [on_device(): lax.all_to_all(home_line[:slot_count].reshape(devices, 1, capacity), ever...]
    add x15 -> x17, other arithmetic: 23.2 us -> 9.28 us  [the longest x16 5.95 us: halved(): return at(value, mine, axis) + sent_low(at(value, 1 - mine, axis), bit)]
    ppermute x18 -> x21, starting transfers between devices: 32.5 us -> 22.3 us  [shift(): lax.ppermute(value, 'dp', [(i, (i + steps) % size) for i in range(size)])]
    ppermute x84 -> x89, waiting for transfers between devices: 155 us -> 163 us  [swap(): return lax.ppermute(value, 'vocab', [(i, i ^ bit) for i in range(8)])]
  transfers between devices with their start and end apart: 110 -> 119, of which waited for: 54 -> 71; matrix products, arithmetic and copies ran while one was open for 34% -> 36% of each run, Pallas kernels for 4% -> 3%
where the time goes in v6:
time: 919 us; the launch traced here: 909 us
  waiting for transfers between devices  317 us (34%)
  matrix products  231 us (25%)
  other arithmetic  119 us (13%)
  starting transfers between devices  105 us (11%)
  Pallas kernels  55.7 us (6%)
  local copies, waits for them, and re-layouts  54.6 us (6%)
  between operations  27.3 us (3%)
    ppermute x89, waiting for transfers between devices, swap(): return lax.ppermute(value, 'vocab', [(i, i ^ bit) for i in range(8)])  163 us
    ppermute x21, waiting for transfers between devices, shift(): lax.ppermute(value, 'dp', [(i, (i + steps) % size) for i in range(size)])  100 us
    dot_general x11, matrix products, array_multiply(): return jnp.dot(left_side, right_side, preferred_element_type=jnp.float32)  78.6 us
    dot_general x11, matrix products, matmul_left(): lax.dot_general(left_side, right_side, (((0,), (0,)), ((), ())), preferre...  73.9 us
    ppermute x89, starting transfers between devices, swap(): return lax.ppermute(value, 'vocab', [(i, i ^ bit) for i in range(8)])  67.2 us
    dot_general x9, matrix products, trailing_array_multiply(): lax.dot_general(left_side, right_side, (((1,), (1,)), ((), ())), preferre...  42 us
    all_to_all x1, waiting for transfers between devices, on_device(): lax.all_to_all(packed.reshape(devices, capacity, TILE), everywhere, 0, 0)  28.9 us
    ppermute x21, starting transfers between devices, shift(): lax.ppermute(value, 'dp', [(i, (i + steps) % size) for i in range(size)])  22.3 us
  transfers between devices with their start and end apart: 119, of which 71 were waited for; matrix products, arithmetic and copies ran while one was open for 36% of the time, Pallas kernels for 3%

profile of v6, /device:TPU:0, one launch (start us, length us, event | category | flops | bytes accessed | tf_op | source)
XLA Modules:
  0.0 908.8 jit_solution(5538782627280079147)
XLA Ops:
  17.9 7.2 send_tiles.1
  26.6 7.4 all-to-all-start
  57.0 28.9 %all-to-all-done.1 = bf16[32,96,128]{2,1,0:T(8,128)(2,1)} async-done(((bf16[32,96,128]{2,1,0:T(8,128)(2,1)}), bf16[32,96,128]{2,1,0:T(8,128)(2,1)}, u32[]{:S(2)}, u32[]{:S(2)}) %all-to-all-start.1) | async-done | bytes 786464 | tf_op jit(solution)/shard_map/all_to_all | solution.py:746
  94.6 12.5 %collective-permute-done.3.refs_4_ = bf16[160,1536]{1,0:T(8,128)(2,1)S(1)} collective-permute-done((bf16[160,1536]{1,0:T(8,128)(2,1)}, bf16[160,1536]{1,0:T(8,128)(2,1)S(1)}, u32[]{:S(2)}, u32[]{:S(2)}) %collective-permute-start.3) | collective-permute-done | bytes 491552 | tf_op jit(solution)/shard_map/ppermute | solution.py:56
  122.2 7.3 fusion.64
  132.7 6.2 collective-permute-done.10.refs_11_
  138.9 6.1 collective-permute-done.9.refs_10_
  146.4 7.2 collective-permute-done.21.refs_19_
  158.2 7.3 fusion.66
  165.5 9.9 %collective-permute-done.24.refs_22_ = bf16[160,1536]{1,0:T(8,128)(2,1)S(1)} collective-permute-done((bf16[160,1536]{1,0:T(8,128)(2,1)S(1)}, bf16[160,1536]{1,0:T(8,128)(2,1)S(1)}, u32[]{:S(2)}, u32[]{:S(2)}) %collective-permute-start.24) | collective-permute-done | bytes 491552 | tf_op jit(solution)/shard_map/ppermute | solution.py:56
  180.1 8.5 collective-permute-done.32.refs_29_
  192.1 7.3 fusion.65
  200.4 10.9 %collective-permute-done.34.refs_31_ = bf16[160,1536]{1,0:T(8,128)(2,1)S(1)} collective-permute-done((bf16[160,1536]{1,0:T(8,128)(2,1)S(1)}, bf16[160,1536]{1,0:T(8,128)(2,1)S(1)}, u32[]{:S(2)}, u32[]{:S(2)}) %collective-permute-start.34) | collective-permute-done | bytes 491552 | tf_op jit(solution)/shard_map/ppermute | solution.py:51
  226.2 7.5 fusion.67
  233.7 9.1 collective-permute-done.44
  253.3 13.7 %assemble_layer.1 = (bf16[768,3072]{1,0:T(8,128)(2,1)}, bf16[3072,768]{1,0:T(8,128)(2,1)}, bf16[768,2304]{1,0:T(8,128)(2,1)}, bf16[768,768]{1,0:T(8,128)(2,1)}, ...) custom-call(s32[2]{0:T(128)} %pad_add_fusion.6.spot, bf16[160,1536]{1,0:T(8,128)(2,1)} %get-tuple-element.454.refs_0_, ...), custom_call_target="tpu_custom_call" | custom-call | bytes 60000000 | tf_op jit(solution)/shard_map/assemble_layer/pallas_call | solution.py:289
  324.5 19.7 %fusion.26 = (bf16[512,3072]{1,0:T(8,128)(2,1)S(1)}, f32[512,3072]{1,0:T(8,128)}) fusion(f32[3072]{0:T(1024)S(1)} %slice_bitcast_fusion.42, bf16[768,3072]{1,0:T(8,128)(2,1)} %get-tuple-element.236, f32[512,768]{1,0:T(8,128)S(1)} %get-tuple-element.436, f32[768]{0:T(1024)S(1)} %get-tuple-element.386, f32[768]{0:T(1024)S(1)} %get-tuple-element.387, ...), kind=kOutput, calls=%fused_computation.63 | convolution fusion | flops 2521694208 | bytes 15751168 | tf_op jit(solution)/shard_map/dot_general | solution.py:335
  359.8 6.2 unpack_matrix.9
  366.0 5.8 unpack_matrix.8
  378.2 5.7 fusion.63
  388.6 10.9 %fusion.303 = (f32[12,512]{1,0:T(8,128)S(1)}, f32[12,512,512]{1,2,0:T(8,128)}) fusion(pred[512]{0:T(512)(128)(4,1)S(1)} %copy-done.136, bf16[1,512,3,12,64]{1,4,3,2,0:T(8,128)(2,1)} %bitcast.495), kind=kOutput, calls=%fused_computation.714 | convolution fusion | flops 415236608 | bytes 14180864 | tf_op jit(solution)/shard_map/sub | solution.py:413
  399.5 6.2 fusion.91
  409.2 23.3 %fusion.305 = (f32[512]{0:T(512)S(1)}, f32[512,768]{1,0:T(8,128)}) fusion(f32[768]{0:T(1024)S(1)} %get-tuple-element.397, bf16[3072,768]{1,0:T(8,128)(2,1)} %unpack_matrix.9, bf16[768,3072]{1,0:T(8,128)(2,1)} %unpack_matrix.8, f32[3072]{0:T(1024)S(1)} %slice_bitcast_fusion.41, f32[512,768]{1,0:T(8,128)} %copy-done.55, f32[768]{0:T(1024)S(1)} %get-tuple-element.398, ...), kind=kOutput, calls=%fused_computation.716 | convolution fusion | flops 4940365312 | bytes 12610560 | tf_op jit(solution)/shard_map/dot_general | solution.py:335
  441.5 6.3 collective-permute-done.61
  449.7 8.6 collective-permute-done.62
  482.1 7.5 multiply_convert_fusion
  535.4 7.0 fusion.35
  543.6 6.8 convolution_add_fusion.2
  555.4 7.2 multiply_reduce_fusion.4
  566.5 11.7 %collective-permute-done.74 = bf16[2,2,192,384]{3,2,0,1:T(8,128)(2,1)S(1)} collective-permute-done((bf16[2,2,192,384]{3,2,0,1:T(8,128)(2,1)S(1)}, bf16[2,2,192,384]{3,2,0,1:T(8,128)(2,1)S(1)}, u32[]{:S(2)}, u32[]{:S(2)}) %collective-permute-start.74) | collective-permute-done | bytes 589856 | tf_op jit(solution)/shard_map/ppermute | solution.py:51
  580.8 6.3 convolution_add_fusion.4
  601.2 6.4 convolution_bitcast_fusion
  616.4 6.6 fusion.14
  623.1 6.9 fusion.15
  636.9 13.3 %collective-permute-done.80 = f32[192,384]{1,0:T(8,128)S(1)} collective-permute-done((f32[192,384]{1,0:T(8,128)S(1)}, f32[192,384]{1,0:T(8,128)S(1)}, u32[]{:S(2)}, u32[]{:S(2)}) %collective-permute-start.80) | collective-permute-done | bytes 294944 | tf_op jit(solution)/shard_map/ppermute | solution.py:56
  663.1 6.0 collective-permute-done.83
  669.8 7.3 collective-permute-done.84
  693.7 10.2 %collective-permute-done.85 = f32[192,384]{1,0:T(8,128)} collective-permute-done((f32[192,384]{1,0:T(8,128)}, f32[192,384]{1,0:T(8,128)}, u32[]{:S(2)}, u32[]{:S(2)}) %collective-permute-start.85) | collective-permute-done | bytes 294944 | tf_op jit(solution)/shard_map/ppermute | solution.py:56
  714.3 5.3 convolution_add_fusion.3
  728.5 5.5 collective-permute-done.94
  735.5 11.1 %collective-permute-done.93 = bf16[512,192]{0,1:T(8,128)(2,1)S(1)} collective-permute-done((bf16[512,192]{0,1:T(8,128)(2,1)S(1)}, bf16[512,192]{0,1:T(8,128)(2,1)S(1)}, u32[]{:S(2)}, u32[]{:S(2)}) %collective-permute-start.93) | collective-permute-done | bytes 196640 | tf_op jit(solution)/shard_map/ppermute | solution.py:56
  768.1 8.2 collective-permute-done.98
  777.6 6.6 collective-permute-done.101
  785.6 6.7 collective-permute-done.103
  801.6 12.9 %fusion.3 = f32[192,1920]{1,0:T(8,128)} fusion(s32[6144]{0:T(1024)S(1)} %get-tuple-element.394, bf16[16384,192]{0,1:T(8,128)(2,1)} %all-gather.14.cloned.1.call-done), kind=kOutput, calls=%fused_computation.16 | convolution fusion | flops 4541644800 | bytes 3858432 | tf_op jit(solution)/shard_map/dot_general | solution.py:339
  834.3 9.3 %fusion.5 = f32[192,1920]{1,0:T(8,128)} fusion(s32[4096]{0:T(1024)S(1)} %slice_subtract_fusion.2, bf16[16384,192]{0,1:T(8,128)(2,1)} %all-gather.14.cloned.1.call-done), kind=kOutput, calls=%fused_computation.19 | convolution fusion | flops 3027763200 | bytes 3063808 | tf_op jit(solution)/shard_map/dot_general | solution.py:339
  843.6 13.1 %fusion.4 = f32[192,1920]{1,0:T(8,128)} fusion(s32[6144]{0:T(1024)S(1)} %get-tuple-element.393, bf16[16384,192]{0,1:T(8,128)(2,1)} %all-gather.14.cloned.1.call-done), kind=kOutput, calls=%fused_computation.17 | convolution fusion | flops 4541644800 | bytes 3858432 | tf_op jit(solution)/shard_map/dot_general | solution.py:339
  861.5 7.6 all-to-all-done.2
  (823 shorter events, 442.3 us)
Async XLA Ops:
  8.0 82.9 %all-gather.10.cloned.1.call-start = ((), (), s32[]{:S(2)}) async-start(), calls=%async_computation.6 | async-start | bytes 3686400 | tf_op jit(solution)/shard_map/all_gather | solution.py:730
  41.2 44.6 %all-to-all-start.1 = ((bf16[32,96,128]{2,1,0:T(8,128)(2,1)}), bf16[32,96,128]{2,1,0:T(8,128)(2,1)}, u32[]{:S(2)}, u32[]{:S(2)}) async-start(bf16[32,96,128]{2,1,0:T(8,128)(2,1)} %bitcast.503), calls=%async_computation.1 | async-start | bytes 1572864 | tf_op jit(solution)/shard_map/all_to_all | solution.py:746
  90.9 258.8 %all-gather.12.cloned.1.call-start = ((), (), s32[]{:S(2)}) async-start(), calls=%async_computation.7 | async-start | bytes 15476736 | tf_op jit(solution)/shard_map/all_gather | solution.py:789
  91.5 658.0 %reduce-scatter.2.cloned.1.call-start = ((), (), s32[]{:S(2)}) async-start(), calls=%async_computation.8 | async-start | bytes 7372800 | tf_op jit(solution)/shard_map/reduce_scatter | solution.py:894
  93.1 16.3 %collective-permute-start.1 = (bf16[160,1536]{1,0:T(8,128)(2,1)}, bf16[160,1536]{1,0:T(8,128)(2,1)}, u32[]{:S(2)}, u32[]{:S(2)}) collective-permute-start(bf16[160,1536]{1,0:T(8,128)(2,1)} %get-tuple-element.454.refs_0_), channel_id=1, source_target_pairs={{0,2},{1,3},{2,0},{3,1},{4,6},{5,7},{6,4},{7,5},{8,10},{9,11},{10,... | collective-permute-start | bytes 1474568 | tf_op jit(solution)/shard_map/ppermute | solution.py:51
  113.8 15.8 %collective-permute-start.5 = (bf16[160,1536]{1,0:T(8,128)(2,1)S(1)}, bf16[160,1536]{1,0:T(8,128)(2,1)S(1)}, u32[]{:S(2)}, u32[]{:S(2)}) collective-permute-start(bf16[160,1536]{1,0:T(8,128)(2,1)S(1)} %collective-permute-done.2.refs_3_), channel_id=1, source_target_pairs={{0,1},{1,0},{2,3},{3,2},{4,5},{5,4},{6,7},{7,6},{8,9},{9,8},{10,11... | collective-permute-start | bytes 1474568 | tf_op jit(solution)/shard_map/ppermute | solution.py:51
  113.9 18.8 %collective-permute-start.11 = (bf16[160,1536]{1,0:T(8,128)(2,1)}, bf16[160,1536]{1,0:T(8,128)(2,1)S(1)}, u32[]{:S(2)}, u32[]{:S(2)}) collective-permute-start(bf16[160,1536]{1,0:T(8,128)(2,1)} %copy-done.71), channel_id=1, source_target_pairs={{0,8},{8,16},{16,24},{24,0},{1,9},{9,17},{17,25},{25,1},{2,10},{10... | collective-permute-start | bytes 1474568 | tf_op jit(solution)/shard_map/ppermute | solution.py:56
  118.8 20.0 %collective-permute-start.10 = (bf16[160,1536]{1,0:T(8,128)(2,1)}, bf16[160,1536]{1,0:T(8,128)(2,1)S(1)}, u32[]{:S(2)}, u32[]{:S(2)}) collective-permute-start(bf16[160,1536]{1,0:T(8,128)(2,1)} %copy-done.71), channel_id=1, source_target_pairs={{0,4},{1,5},{2,6},{3,7},{4,0},{5,1},{6,2},{7,3},{8,12},{9,13},{10,... | collective-permute-start | bytes 1474568 | tf_op jit(solution)/shard_map/ppermute | solution.py:51
  121.9 23.1 %collective-permute-start.9 = (bf16[160,1536]{1,0:T(8,128)(2,1)}, bf16[160,1536]{1,0:T(8,128)(2,1)S(1)}, u32[]{:S(2)}, u32[]{:S(2)}) collective-permute-start(bf16[160,1536]{1,0:T(8,128)(2,1)} %copy-done.71), channel_id=1, source_target_pairs={{0,2},{1,3},{2,0},{3,1},{4,6},{5,7},{6,4},{7,5},{8,10},{9,11},{10,... | collective-permute-start | bytes 1474568 | tf_op jit(solution)/shard_map/ppermute | solution.py:51
  122.2 22.8 %collective-permute-start.6 = (bf16[160,1536]{1,0:T(8,128)(2,1)}, bf16[160,1536]{1,0:T(8,128)(2,1)S(1)}, u32[]{:S(2)}, u32[]{:S(2)}) collective-permute-start(bf16[160,1536]{1,0:T(8,128)(2,1)} %copy-done.71), channel_id=1, source_target_pairs={{0,1},{1,0},{2,3},{3,2},{4,5},{5,4},{6,7},{7,6},{8,9},{9,8},{10,11... | collective-permute-start | bytes 1474568 | tf_op jit(solution)/shard_map/ppermute | solution.py:51
  145.0 30.5 %collective-permute-start.25 = (bf16[2,2,512,768]{3,2,1,0:T(8,128)(2,1)S(1)}, bf16[2,2,512,768]{3,2,1,0:T(8,128)(2,1)S(1)}, u32[]{:S(2)}, u32[]{:S(2)}) collective-permute-start(bf16[2,2,512,768]{3,2,1,0:T(8,128)(2,1)S(1)} %bitcast.551), channel_id=1, source_target_pairs={{0,1},{1,0},{2,3},{3,2},{4,5},{5,4},{6,7},{7,6},{8,9},{9,8},{10,11... | collective-permute-start | bytes 9437192 | tf_op jit(solution)/shard_map/ppermute | solution.py:51
  155.2 20.2 %collective-permute-start.24 = (bf16[160,1536]{1,0:T(8,128)(2,1)S(1)}, bf16[160,1536]{1,0:T(8,128)(2,1)S(1)}, u32[]{:S(2)}, u32[]{:S(2)}) collective-permute-start(bf16[160,1536]{1,0:T(8,128)(2,1)S(1)} %collective-permute-done.11.refs_12_), channel_id=1, source_target_pairs={{0,8},{8,16},{16,24},{24,0},{1,9},{9,17},{17,25},{25,1},{2,10},{10... | collective-permute-start | bytes 1474568 | tf_op jit(solution)/shard_map/ppermute | solution.py:56
  155.6 19.9 %collective-permute-start.23 = (bf16[160,1536]{1,0:T(8,128)(2,1)S(1)}, bf16[160,1536]{1,0:T(8,128)(2,1)S(1)}, u32[]{:S(2)}, u32[]{:S(2)}) collective-permute-start(bf16[160,1536]{1,0:T(8,128)(2,1)S(1)} %collective-permute-done.11.refs_12_), channel_id=1, source_target_pairs={{0,4},{1,5},{2,6},{3,7},{4,0},{5,1},{6,2},{7,3},{8,12},{9,13},{10,... | collective-permute-start | bytes 1474568 | tf_op jit(solution)/shard_map/ppermute | solution.py:51
  155.9 19.6 %collective-permute-start.22 = (bf16[160,1536]{1,0:T(8,128)(2,1)S(1)}, bf16[160,1536]{1,0:T(8,128)(2,1)S(1)}, u32[]{:S(2)}, u32[]{:S(2)}) collective-permute-start(bf16[160,1536]{1,0:T(8,128)(2,1)S(1)} %collective-permute-done.11.refs_12_), channel_id=1, source_target_pairs={{0,2},{1,3},{2,0},{3,1},{4,6},{5,7},{6,4},{7,5},{8,10},{9,11},{10,... | collective-permute-start | bytes 1474568 | tf_op jit(solution)/shard_map/ppermute | solution.py:51
  157.4 18.1 %collective-permute-start.19 = (bf16[160,1536]{1,0:T(8,128)(2,1)S(1)}, bf16[160,1536]{1,0:T(8,128)(2,1)S(1)}, u32[]{:S(2)}, u32[]{:S(2)}) collective-permute-start(bf16[160,1536]{1,0:T(8,128)(2,1)S(1)} %collective-permute-done.11.refs_12_), channel_id=1, source_target_pairs={{0,1},{1,0},{2,3},{3,2},{4,5},{5,4},{6,7},{7,6},{8,9},{9,8},{10,11... | collective-permute-start | bytes 1474568 | tf_op jit(solution)/shard_map/ppermute | solution.py:51
  180.0 20.4 %collective-permute-start.28 = (bf16[160,1536]{1,0:T(8,128)(2,1)S(1)}, bf16[160,1536]{1,0:T(8,128)(2,1)S(1)}, u32[]{:S(2)}, u32[]{:S(2)}) collective-permute-start(bf16[160,1536]{1,0:T(8,128)(2,1)S(1)} %collective-permute-done.22.refs_20_), channel_id=1, source_target_pairs={{0,1},{1,0},{2,3},{3,2},{4,5},{5,4},{6,7},{7,6},{8,9},{9,8},{10,11... | collective-permute-start | bytes 1474568 | tf_op jit(solution)/shard_map/ppermute | solution.py:51
  190.2 21.1 %collective-permute-start.34 = (bf16[160,1536]{1,0:T(8,128)(2,1)S(1)}, bf16[160,1536]{1,0:T(8,128)(2,1)S(1)}, u32[]{:S(2)}, u32[]{:S(2)}) collective-permute-start(bf16[160,1536]{1,0:T(8,128)(2,1)S(1)} %collective-permute-done.24.refs_22_), channel_id=1, source_target_pairs={{0,4},{1,5},{2,6},{3,7},{4,0},{5,1},{6,2},{7,3},{8,12},{9,13},{10,... | collective-permute-start | bytes 1474568 | tf_op jit(solution)/shard_map/ppermute | solution.py:51
  192.0 19.7 %collective-permute-start.33 = (bf16[160,1536]{1,0:T(8,128)(2,1)S(1)}, bf16[160,1536]{1,0:T(8,128)(2,1)S(1)}, u32[]{:S(2)}, u32[]{:S(2)}) collective-permute-start(bf16[160,1536]{1,0:T(8,128)(2,1)S(1)} %collective-permute-done.24.refs_22_), channel_id=1, source_target_pairs={{0,2},{1,3},{2,0},{3,1},{4,6},{5,7},{6,4},{7,5},{8,10},{9,11},{10,... | collective-permute-start | bytes 1474568 | tf_op jit(solution)/shard_map/ppermute | solution.py:51
  192.1 19.5 %collective-permute-start.30 = (bf16[160,1536]{1,0:T(8,128)(2,1)S(1)}, bf16[160,1536]{1,0:T(8,128)(2,1)S(1)}, u32[]{:S(2)}, u32[]{:S(2)}) collective-permute-start(bf16[160,1536]{1,0:T(8,128)(2,1)S(1)} %collective-permute-done.24.refs_22_), channel_id=1, source_target_pairs={{0,1},{1,0},{2,3},{3,2},{4,5},{5,4},{6,7},{7,6},{8,9},{9,8},{10,11... | collective-permute-start | bytes 1474568 | tf_op jit(solution)/shard_map/ppermute | solution.py:51
  211.6 32.7 %collective-permute-start.41 = (bf16[2,2,512,768]{3,2,1,0:T(8,128)(2,1)S(1)}, bf16[2,2,512,768]{3,2,1,0:T(8,128)(2,1)S(1)}, u32[]{:S(2)}, u32[]{:S(2)}) collective-permute-start(bf16[2,2,512,768]{3,2,1,0:T(8,128)(2,1)S(1)} %bitcast.552), channel_id=1, source_target_pairs={{0,1},{1,0},{2,3},{3,2},{4,5},{5,4},{6,7},{7,6},{8,9},{9,8},{10,11... | collective-permute-start | bytes 9437192 | tf_op jit(solution)/shard_map/ppermute | solution.py:51
  214.2 30.1 %collective-permute-start.37 = (bf16[160,1536]{1,0:T(8,128)(2,1)S(1)}, bf16[160,1536]{1,0:T(8,128)(2,1)S(1)}, u32[]{:S(2)}, u32[]{:S(2)}) collective-permute-start(bf16[160,1536]{1,0:T(8,128)(2,1)S(1)} %collective-permute-done.33.refs_30_), channel_id=1, source_target_pairs={{0,1},{1,0},{2,3},{3,2},{4,5},{5,4},{6,7},{7,6},{8,9},{9,8},{10,11... | collective-permute-start | bytes 1474568 | tf_op jit(solution)/shard_map/ppermute | solution.py:51
  222.8 21.6 %collective-permute-start.38 = (bf16[160,1536]{1,0:T(8,128)(2,1)S(1)}, bf16[160,1536]{1,0:T(8,128)(2,1)S(1)}, u32[]{:S(2)}, u32[]{:S(2)}) collective-permute-start(bf16[160,1536]{1,0:T(8,128)(2,1)S(1)} %collective-permute-done.34.refs_31_), channel_id=1, source_target_pairs={{0,1},{1,0},{2,3},{3,2},{4,5},{5,4},{6,7},{7,6},{8,9},{9,8},{10,11... | collective-permute-start | bytes 1474568 | tf_op jit(solution)/shard_map/ppermute | solution.py:51
  223.9 18.9 %collective-permute-start.44 = (bf16[2,256,768]{2,1,0:T(8,128)(2,1)S(1)}, bf16[2,256,768]{2,1,0:T(8,128)(2,1)S(1)}, u32[]{:S(2)}, u32[]{:S(2)}) collective-permute-start(bf16[2,256,768]{2,1,0:T(8,128)(2,1)S(1)} %slice_bitcast_fusion.12), channel_id=1, source_target_pairs={{0,2},{1,3},{2,0},{3,1},{4,6},{5,7},{6,4},{7,5},{8,10},{9,11},{10,... | collective-permute-start | bytes 2359304 | tf_op jit(solution)/shard_map/ppermute | solution.py:51
  224.5 20.4 %collective-permute-start.45 = (bf16[2,256,768]{2,1,0:T(8,128)(2,1)S(1)}, bf16[2,256,768]{2,1,0:T(8,128)(2,1)S(1)}, u32[]{:S(2)}, u32[]{:S(2)}) collective-permute-start(bf16[2,256,768]{2,1,0:T(8,128)(2,1)S(1)} %slice_bitcast_fusion.11), channel_id=1, source_target_pairs={{0,4},{1,5},{2,6},{3,7},{4,0},{5,1},{6,2},{7,3},{8,12},{9,13},{10,... | collective-permute-start | bytes 2359304 | tf_op jit(solution)/shard_map/ppermute | solution.py:51
  247.3 19.8 %collective-permute-start.51 = (bf16[256,768]{1,0:T(8,128)(2,1)}, bf16[256,768]{1,0:T(8,128)(2,1)}, u32[]{:S(2)}, u32[]{:S(2)}) collective-permute-start(bf16[256,768]{1,0:T(8,128)(2,1)} %slice_bitcast_fusion.33), channel_id=1, source_target_pairs={{0,2},{1,3},{2,0},{3,1},{4,6},{5,7},{6,4},{7,5},{8,10},{9,11},{10,... | collective-permute-start | bytes 1179656 | tf_op jit(solution)/shard_map/ppermute | solution.py:51
  248.8 19.6 %collective-permute-start.50 = (bf16[256,768]{1,0:T(8,128)(2,1)S(1)}, bf16[256,768]{1,0:T(8,128)(2,1)}, u32[]{:S(2)}, u32[]{:S(2)}) collective-permute-start(bf16[256,768]{1,0:T(8,128)(2,1)S(1)} %slice_bitcast_fusion.34), channel_id=1, source_target_pairs={{0,4},{1,5},{2,6},{3,7},{4,0},{5,1},{6,2},{7,3},{8,12},{9,13},{10,... | collective-permute-start | bytes 1179656 | tf_op jit(solution)/shard_map/ppermute | solution.py:51
  251.5 24.2 %collective-permute-start.46 = (bf16[2,256,768]{2,1,0:T(8,128)(2,1)}, bf16[2,256,768]{2,1,0:T(8,128)(2,1)}, u32[]{:S(2)}, u32[]{:S(2)}) collective-permute-start(bf16[2,256,768]{2,1,0:T(8,128)(2,1)} %slice_bitcast_fusion.10), channel_id=1, source_target_pairs={{0,2},{1,3},{2,0},{3,1},{4,6},{5,7},{6,4},{7,5},{8,10},{9,11},{10,... | collective-permute-start | bytes 2359304 | tf_op jit(solution)/shard_map/ppermute | solution.py:51
  253.0 24.0 %collective-permute-start.47 = (bf16[2,256,768]{2,1,0:T(8,128)(2,1)}, bf16[2,256,768]{2,1,0:T(8,128)(2,1)}, u32[]{:S(2)}, u32[]{:S(2)}) collective-permute-start(bf16[2,256,768]{2,1,0:T(8,128)(2,1)} %slice_bitcast_fusion.9), channel_id=1, source_target_pairs={{0,4},{1,5},{2,6},{3,7},{4,0},{5,1},{6,2},{7,3},{8,12},{9,13},{10,... | collective-permute-start | bytes 2359304 | tf_op jit(solution)/shard_map/ppermute | solution.py:51
  374.4 32.9 %collective-permute-start.58 = (bf16[1,128,768]{2,1,0:T(8,128)(2,1)S(1)}, bf16[1,128,768]{2,1,0:T(8,128)(2,1)S(1)}, u32[]{:S(2)}, u32[]{:S(2)}) collective-permute-start(bf16[1,128,768]{2,1,0:T(8,128)(2,1)S(1)} %bitcast.485), channel_id=1, source_target_pairs={{0,2},{1,3},{2,0},{3,1},{4,6},{5,7},{6,4},{7,5},{8,10},{9,11},{10,... | collective-permute-start | bytes 589832 | tf_op jit(solution)/shard_map/ppermute | solution.py:51
  408.8 23.7 %collective-permute-start.59 = (bf16[2,128,768]{2,1,0:T(8,128)(2,1)}, bf16[2,128,768]{2,1,0:T(8,128)(2,1)}, u32[]{:S(2)}, u32[]{:S(2)}) collective-permute-start(bf16[2,128,768]{2,1,0:T(8,128)(2,1)} %pad_maximum_fusion.7), channel_id=1, source_target_pairs={{0,4},{1,5},{2,6},{3,7},{4,0},{5,1},{6,2},{7,3},{8,12},{9,13},{10,... | collective-permute-start | bytes 1179656 | tf_op jit(solution)/shard_map/ppermute | solution.py:51
  554.3 26.5 %collective-permute-start.75 = (f32[768,1536]{1,0:T(8,128)}, f32[768,1536]{1,0:T(8,128)}, u32[]{:S(2)}, u32[]{:S(2)}) collective-permute-start(f32[768,1536]{1,0:T(8,128)} %fusion.77), channel_id=1, source_target_pairs={{0,1},{1,0},{2,3},{3,2},{4,5},{5,4},{6,7},{7,6},{8,9},{9,8},{10,11... | collective-permute-start | bytes 14155784 | tf_op jit(solution)/shard_map/ppermute | solution.py:51
  554.9 245.1 %all-gather.14.cloned.1.call-start = ((), (), s32[]{:S(2)}) async-start(), calls=%async_computation.9 | async-start | bytes 7077888 | tf_op jit(solution)/shard_map/all_gather | solution.py:930
  596.6 19.5 %collective-permute-start.79 = (bf16[2,2,48,1536]{3,2,0,1:T(8,128)(2,1)S(1)}, bf16[2,2,48,1536]{3,2,0,1:T(8,128)(2,1)S(1)}, u32[]{:S(2)}, u32[]{:S(2)}) collective-permute-start(bf16[2,2,48,1536]{3,2,0,1:T(8,128)(2,1)S(1)} %fusion.132), channel_id=1, source_target_pairs={{0,4},{1,5},{2,6},{3,7},{4,0},{5,1},{6,2},{7,3},{8,12},{9,13},{10,... | collective-permute-start | bytes 1769480 | tf_op jit(solution)/shard_map/ppermute | solution.py:51
  598.2 18.0 %collective-permute-start.78 = (bf16[2,2,48,1536]{3,2,0,1:T(8,128)(2,1)S(1)}, bf16[2,2,48,1536]{3,2,0,1:T(8,128)(2,1)S(1)}, u32[]{:S(2)}, u32[]{:S(2)}) collective-permute-start(bf16[2,2,48,1536]{3,2,0,1:T(8,128)(2,1)S(1)} %fusion.131), channel_id=1, source_target_pairs={{0,2},{1,3},{2,0},{3,1},{4,6},{5,7},{6,4},{7,5},{8,10},{9,11},{10,... | collective-permute-start | bytes 1769480 | tf_op jit(solution)/shard_map/ppermute | solution.py:51
  631.5 18.8 %collective-permute-start.81 = (bf16[2,48,1536]{2,1,0:T(8,128)(2,1)S(1)}, bf16[2,48,1536]{2,1,0:T(8,128)(2,1)S(1)}, u32[]{:S(2)}, u32[]{:S(2)}) collective-permute-start(bf16[2,48,1536]{2,1,0:T(8,128)(2,1)S(1)} %fusion.142), channel_id=1, source_target_pairs={{0,4},{1,5},{2,6},{3,7},{4,0},{5,1},{6,2},{7,3},{8,12},{9,13},{10,... | collective-permute-start | bytes 884744 | tf_op jit(solution)/shard_map/ppermute | solution.py:51
  633.1 17.1 %collective-permute-start.80 = (f32[192,384]{1,0:T(8,128)S(1)}, f32[192,384]{1,0:T(8,128)S(1)}, u32[]{:S(2)}, u32[]{:S(2)}) collective-permute-start(f32[192,384]{1,0:T(8,128)S(1)} %get-tuple-element.368), channel_id=1, source_target_pairs={{0,8},{8,16},{16,24},{24,0},{1,9},{9,17},{17,25},{25,1},{2,10},{10... | collective-permute-start | bytes 884744 | tf_op jit(solution)/shard_map/ppermute | solution.py:56
  650.3 18.8 %collective-permute-start.83 = (f32[192,384]{1,0:T(8,128)S(1)}, f32[192,384]{1,0:T(8,128)S(1)}, u32[]{:S(2)}, u32[]{:S(2)}) collective-permute-start(f32[192,384]{1,0:T(8,128)S(1)} %bitcast_add_fusion.22), channel_id=1, source_target_pairs={{0,8},{8,16},{16,24},{24,0},{1,9},{9,17},{17,25},{25,1},{2,10},{10... | collective-permute-start | bytes 884744 | tf_op jit(solution)/shard_map/ppermute | solution.py:56
  655.5 21.6 %collective-permute-start.84 = (f32[48,1536]{1,0:T(8,128)S(1)}, f32[48,1536]{1,0:T(8,128)S(1)}, u32[]{:S(2)}, u32[]{:S(2)}) collective-permute-start(f32[48,1536]{1,0:T(8,128)S(1)} %get-tuple-element.365), channel_id=1, source_target_pairs={{0,8},{8,16},{16,24},{24,0},{1,9},{9,17},{17,25},{25,1},{2,10},{10... | collective-permute-start | bytes 884744 | tf_op jit(solution)/shard_map/ppermute | solution.py:56
  687.2 27.1 %collective-permute-start.87 = (f32[768,1152]{1,0:T(8,128)}, f32[768,1152]{1,0:T(8,128)}, u32[]{:S(2)}, u32[]{:S(2)}) collective-permute-start(f32[768,1152]{1,0:T(8,128)} %fusion.108), channel_id=1, source_target_pairs={{0,1},{1,0},{2,3},{3,2},{4,5},{5,4},{6,7},{7,6},{8,9},{9,8},{10,11... | collective-permute-start | bytes 10616840 | tf_op jit(solution)/shard_map/ppermute | solution.py:51
  691.0 20.0 %collective-permute-start.91 = (f32[1408,384]{1,0:T(8,128)}, f32[1408,384]{1,0:T(8,128)}, u32[]{:S(2)}, u32[]{:S(2)}) collective-permute-start(f32[1408,384]{1,0:T(8,128)} %bitcast.154), channel_id=1, source_target_pairs={{0,1},{1,0},{2,3},{3,2},{4,5},{5,4},{6,7},{7,6},{8,9},{9,8},{10,11... | collective-permute-start | bytes 6488072 | tf_op jit(solution)/shard_map/ppermute | solution.py:51
  691.9 17.3 %collective-permute-start.86 = (f32[48,1536]{1,0:T(8,128)}, f32[48,1536]{1,0:T(8,128)}, u32[]{:S(2)}, u32[]{:S(2)}) collective-permute-start(f32[48,1536]{1,0:T(8,128)} %bitcast_add_fusion.21), channel_id=1, source_target_pairs={{0,8},{8,16},{16,24},{24,0},{1,9},{9,17},{17,25},{25,1},{2,10},{10... | collective-permute-start | bytes 884744 | tf_op jit(solution)/shard_map/ppermute | solution.py:56
  719.6 27.0 %collective-permute-start.88 = (f32[48,1536]{1,0:T(8,128)}, f32[48,1536]{1,0:T(8,128)S(1)}, u32[]{:S(2)}, u32[]{:S(2)}) collective-permute-start(f32[48,1536]{1,0:T(8,128)} %add.1198), channel_id=1, source_target_pairs={{0,8},{8,16},{16,24},{24,0},{1,9},{9,17},{17,25},{25,1},{2,10},{10... | collective-permute-start | bytes 884744 | tf_op jit(solution)/shard_map/ppermute | solution.py:56
  722.3 25.1 %collective-permute-start.90 = (bf16[2,2,48,1152]{3,2,0,1:T(8,128)(2,1)S(1)}, bf16[2,2,48,1152]{3,2,0,1:T(8,128)(2,1)S(1)}, u32[]{:S(2)}, u32[]{:S(2)}) collective-permute-start(bf16[2,2,48,1152]{3,2,0,1:T(8,128)(2,1)S(1)} %fusion.134), channel_id=1, source_target_pairs={{0,4},{1,5},{2,6},{3,7},{4,0},{5,1},{6,2},{7,3},{8,12},{9,13},{10,... | collective-permute-start | bytes 1327112 | tf_op jit(solution)/shard_map/ppermute | solution.py:51
  727.8 18.8 %collective-permute-start.93 = (bf16[512,192]{0,1:T(8,128)(2,1)S(1)}, bf16[512,192]{0,1:T(8,128)(2,1)S(1)}, u32[]{:S(2)}, u32[]{:S(2)}) collective-permute-start(bf16[512,192]{0,1:T(8,128)(2,1)S(1)} %get-tuple-element.376), channel_id=1, source_target_pairs={{0,16},{8,24},{16,0},{24,8},{1,17},{9,25},{17,1},{25,9},{2,18},{10... | collective-permute-start | bytes 589832 | tf_op jit(solution)/shard_map/ppermute | solution.py:56
  727.8 18.8 %collective-permute-start.92 = (bf16[512,192]{0,1:T(8,128)(2,1)S(1)}, bf16[512,192]{0,1:T(8,128)(2,1)S(1)}, u32[]{:S(2)}, u32[]{:S(2)}) collective-permute-start(bf16[512,192]{0,1:T(8,128)(2,1)S(1)} %get-tuple-element.377), channel_id=1, source_target_pairs={{0,8},{8,16},{16,24},{24,0},{1,9},{9,17},{17,25},{25,1},{2,10},{10... | collective-permute-start | bytes 589832 | tf_op jit(solution)/shard_map/ppermute | solution.py:56
  756.1 20.2 %collective-permute-start.98 = (bf16[2,2,88,384]{3,2,0,1:T(8,128)(2,1)S(1)}, bf16[2,2,88,384]{3,2,0,1:T(8,128)(2,1)S(1)}, u32[]{:S(2)}, u32[]{:S(2)}) collective-permute-start(bf16[2,2,88,384]{3,2,0,1:T(8,128)(2,1)S(1)} %fusion.145), channel_id=1, source_target_pairs={{0,4},{1,5},{2,6},{3,7},{4,0},{5,1},{6,2},{7,3},{8,12},{9,13},{10,... | collective-permute-start | bytes 811016 | tf_op jit(solution)/shard_map/ppermute | solution.py:51
  757.4 19.0 %collective-permute-start.97 = (bf16[2,2,88,384]{3,2,0,1:T(8,128)(2,1)S(1)}, bf16[2,2,88,384]{3,2,0,1:T(8,128)(2,1)S(1)}, u32[]{:S(2)}, u32[]{:S(2)}) collective-permute-start(bf16[2,2,88,384]{3,2,0,1:T(8,128)(2,1)S(1)} %fusion.144), channel_id=1, source_target_pairs={{0,2},{1,3},{2,0},{3,1},{4,6},{5,7},{6,4},{7,5},{8,10},{9,11},{10,... | collective-permute-start | bytes 811016 | tf_op jit(solution)/shard_map/ppermute | solution.py:51
  828.7 40.3 %all-to-all-start.2 = ((f32[32,96,128]{2,1,0:T(8,128)}), f32[32,96,128]{2,1,0:T(8,128)S(1)}, u32[]{:S(2)}, u32[]{:S(2)}) async-start(f32[32,96,128]{2,1,0:T(8,128)} %bitcast.468), calls=%async_computation.3 | async-start | bytes 3145728 | tf_op jit(solution)/shard_map/all_to_all | solution.py:942
  (223 other events, 2688.2 us)
Sparse Core Ops, SparseCore 0:
  11.0 79.8 all-gather.9
  555.0 117.4 reduce-scatter.1
Sparse Core Ops, SparseCore 1:
  94.3 133.4 all-gather.11
  750.5 49.5 all-gather.13

commit v7 on v6

--- a/solution.py
+++ b/solution.py
@@ -75,11 +75,6 @@
 
 def together(*values):
     return lax.optimization_barrier(values)
-
-
-def ring_hop(blocks):
-    moving = shift(blocks[-1], 1)
-    return [*blocks[:-2], blocks[-2] + moving]
 
 
 def sum_everywhere(value):
@@ -249,21 +244,13 @@
     )(index, source)
 
 
-def assemble_kernel(spot, *refs, places):
-    arrivals = refs[: len(places)]
-    up, down, qkv, out, place, tail, landed, sems = refs[len(places) :]
-    copies = []
-    for n, (arrival, where) in enumerate(zip(arrivals, places)):
-        target = landed.at[where[0], pl.ds(where[1], where[2])]
-        copies.append(pltpu.make_async_copy(arrival, target, sems.at[n]))
-    for copy in copies:
-        copy.start()
-    for copy in copies:
-        copy.wait()
+def assemble_kernel(arrived, up, down, qkv, out, place, tail, landed, sem):
+    copy = pltpu.make_async_copy(arrived, landed, sem)
+    copy.start()
+    copy.wait()
 
     def one_device(block, carry):
-        owner = ((spot[0] + 4 - block // 8) % 4) * 8 + (spot[1] ^ (block % 8))
-        chip, core = owner // 2, owner % 2
+        chip, core = block // 2, block % 2
 
         def put(target, row, lines, width, source_row, source_column):
             target[
@@ -277,7 +264,7 @@
         put(out, chip * 48, 48, 384, 96, 1152)
         for part in range(2):
             put(place, chip * 32 + part * 16, 16, 384, 144, part * 384)
-        tail[owner] = landed[block, pl.ds(TAIL_AT[0], 16), TAIL_AT[1] * TILE : (TAIL_AT[1] + 1) * TILE].astype(
+        tail[block] = landed[block, pl.ds(TAIL_AT[0], 16), TAIL_AT[1] * TILE : (TAIL_AT[1] + 1) * TILE].astype(
             jnp.float32
         )[:8]
         return carry
@@ -285,21 +272,22 @@
     lax.fori_loop(0, landed.shape[0], one_device, 0)
 
 
-def assemble_layer(spot, arrivals, places, devices):
+def assemble_layer(arrived):
+    devices = arrived.shape[0]
     return pl.pallas_call(
-        functools.partial(assemble_kernel, places=places),
-        in_specs=[pl.BlockSpec(memory_space=pltpu.SMEM)] + [pl.BlockSpec(memory_space=pl.ANY)] * len(arrivals),
+        assemble_kernel,
+        in_specs=[pl.BlockSpec(memory_space=pl.ANY)],
         out_specs=[pl.BlockSpec(memory_space=pltpu.VMEM)] * 6,
         out_shape=[jax.ShapeDtypeStruct((h, a * TILE), jnp.bfloat16) for _, h, a in HOME_ORDER]
         + [jax.ShapeDtypeStruct((devices, 8, TILE), jnp.float32)],
         scratch_shapes=[
             pltpu.VMEM((devices, *SHARE), jnp.bfloat16),
-            pltpu.SemaphoreType.DMA((len(arrivals),)),
+            pltpu.SemaphoreType.DMA,
         ],
         compiler_params=pltpu.CompilerParams(vmem_limit_bytes=VMEM_LIMIT),
         cost_estimate=pl.CostEstimate(flops=0, bytes_accessed=60_000_000, transcendentals=0),
         name="assemble_layer",
-    )(spot, *arrivals)
+    )(arrived)
 
 
 def unpack_kernel(source, target, stage, *, across):
@@ -397,7 +385,7 @@
     return (jnp.where(live_keys[:, None, None, :], scores, -1000000000.0), split_heads)
 
 
-def layer_forward(pieces, looked, lengths):
+def attention_forward(pieces, looked, lengths):
     small_rows = pieces["small"].astype(jnp.float32)
     seqs_count = lengths.shape[0]
     rows_here = seqs_count * LEN
@@ -422,6 +410,21 @@
     middle, normed_one, inverse_one = norm_forward(
         first_norm + attended, small_rows[6], small_rows[7]
     )
+    saved = {
+        "inputs": inputs,
+        "projected": projected,
+        "logsum": logsum,
+        "context": context,
+        "normed_zero": normed_zero,
+        "inverse_zero": inverse_zero,
+        "normed_one": normed_one,
+        "inverse_one": inverse_one,
+    }
+    return middle, saved
+
+
+def feed_forward(pieces, middle, saved):
+    small_rows = pieces["small"]
     middle_low = middle.astype(jnp.bfloat16)
     hidden = array_multiply(middle_low, pieces["up"]) + pieces["upbias"].astype(jnp.float32)
     activated = jax.nn.gelu(hidden, approximate=False).astype(jnp.bfloat16)
@@ -430,17 +433,10 @@
         middle + output, small_rows[8], small_rows[9]
     )
     saved = {
-        "inputs": inputs,
-        "projected": projected,
-        "logsum": logsum,
-        "context": context,
+        **saved,
         "middle_low": middle_low,
         "hidden": hidden,
         "activated": activated,
-        "normed_zero": normed_zero,
-        "inverse_zero": inverse_zero,
-        "normed_one": normed_one,
-        "inverse_one": inverse_one,
         "normed_two": normed_two,
         "inverse_two": inverse_two,
     }
@@ -456,7 +452,6 @@
     flow.add_product(saved["activated"], grad_out)
     grad_act = trailing_array_multiply(grad_out, pieces["down"])
     grad_hidden = (grad_act * gelu_slope(saved["hidden"])).astype(jnp.bfloat16)
-    (grad_hidden,) = flow.advance(grad_hidden)
     flow.add_product(saved["middle_low"], grad_hidden)
     grad_middle = grad_sum_two + trailing_array_multiply(grad_hidden, pieces["up"])
     grad_sum_one, grad_gain_one, grad_shift_one = norm_backward(
@@ -471,7 +466,7 @@
     )
 
 
-def attention_backward(pieces, saved, grad_sum_one, grad_small, grad_upbias, lengths, tail_rows, flow):
+def attention_backward(pieces, saved, grad_sum_one, grad_small, grad_upbias, lengths, tail_rows, flow, head_part):
     small_rows = pieces["small"]
     seqs_count = lengths.shape[0]
     rows_here = seqs_count * LEN
@@ -493,7 +488,6 @@
         grad_context,
         preferred_element_type=jnp.float32,
     )
-    grad_values, grad_probs = flow.advance(grad_values, grad_probs)
     grad_scores = probabilities * (
         grad_probs - jnp.sum(grad_probs * probabilities, axis=-1, keepdims=True)
     )
@@ -509,8 +503,6 @@
         .reshape(rows_here, 3 * D)
         .astype(jnp.bfloat16)
     )
-    (grad_proj,) = flow.advance(grad_proj)
-    flow.add_product(saved["inputs"], grad_proj)
     grad_bias_all = jnp.sum(grad_proj.astype(jnp.float32), axis=0)
     grad_first = grad_sum_one + trailing_array_multiply(grad_proj, pieces["qkv"])
     grad_embedded, grad_gain_zero, grad_shift_zero = norm_backward(
@@ -535,9 +527,10 @@
             jnp.zeros((tail_rows - 84, TILE), jnp.float32),
         ]
     )
-    (grad_embedded,) = flow.advance(grad_embedded)
+    grad_embedded, head_part = flow.advance(grad_embedded, head_part)
+    flow.add_product(saved["inputs"], grad_proj)
     flow.add_rest(grad_outw, grad_place, tail)
-    return grad_embedded
+    return grad_embedded, head_part
 
 
 def combine_stats(earlier, later):
@@ -567,49 +560,6 @@
     return (weight - learn_rate * (update + weight_decay * weight), new_first, new_second)
 
 
-def gather_layer(tiles, fillers):
-    per = tiles.shape[0]
-    half = per // 16 * 8
-    arrivals, places = [], []
-    waiting = [(tiles, 0, 0, 0)]
-    crossed = None
-    done = []
-    for stage in range(6):
-        moved = []
-        for value, plane, near, start in waiting:
-            arrivals.append(value)
-            places.append((plane * 8 + near * 2, start, value.shape[0]))
-            moved.append((swap(value, CORE), plane, near, start))
-        landed = []
-        if crossed is not None:
-            across, deep, plane = crossed
-            landed.append((swap(across[:half], DEEP), plane, 3, 0))
-            landed.append((swap(deep[half:], ACROSS), plane, 3, half))
-            crossed = None
-        if stage < 4:
-            across, deep = swap(tiles, ACROSS), swap(tiles, DEEP)
-            landed.append((across, stage, 1, 0))
-            landed.append((deep, stage, 2, 0))
-            crossed = (across, deep, stage)
-        ahead = shift(tiles, 1) if stage < 3 else tiles
-        extra = fillers[stage](done) if stage < len(fillers) else []
-        values, landed_values, ahead, extra = together(
-            [entry[0] for entry in moved], [entry[0] for entry in landed], ahead, extra
-        )
-        done = done + list(extra)
-        for value, (_, plane, near, start) in zip(values, moved):
-            arrivals.append(value)
-            places.append((plane * 8 + near * 2 + 1, start, value.shape[0]))
-        landed = [(value, *entry[1:]) for value, entry in zip(landed_values, landed)]
-        if stage < 4:
-            crossed = (landed_values[-2], landed_values[-1], stage)
-        waiting = landed
-        if stage < 3:
-            tiles = ahead
-            waiting = waiting + [(tiles, stage + 1, 0, 0)]
-    return arrivals, places, done
-
-
 def at(value, index, axis):
     return lax.dynamic_index_in_dim(value, index, axis, keepdims=False)
 
@@ -636,9 +586,8 @@
     blocks = [
         jnp.where((z + k) % 4 < 2, at(first, (z + k) % 2, 0), at(second, (z + k) % 2, 0)) for k in range(4)
     ]
-    for _ in range(3):
-        blocks = yield ring_hop(blocks)
-    return blocks[0]
+    blocks = yield [blocks[0], *(shift(blocks[k], k) for k in (1, 2, 3))]
+    return blocks[0] + blocks[1] + blocks[2] + blocks[3]
 
 
 class Flow:
@@ -727,7 +676,23 @@
     slot_count = devices * capacity
 
     facts = jnp.concatenate([token_ids.reshape(LEN), lengths, mask_count, jnp.zeros((TILE - 2,), jnp.int32)])
-    table_low = lax.all_gather(student_embed.T.astype(jnp.bfloat16), "dp", axis=0, tiled=True)
+    columns_low = student_embed.T.astype(jnp.bfloat16)
+    words = jnp.arange(vocab_rows, dtype=jnp.int32)
+
+    def chosen(ids):
+        return (ids.reshape(-1, 1) - here * vocab_rows == words[None]).astype(jnp.bfloat16)
+
+    def rows_t(ids):
+        return array_multiply(chosen(ids), mentor_lexicon_weights).astype(jnp.bfloat16)
+
+    def rows_s(ids, table):
+        return trailing_array_multiply(chosen(ids), table).astype(jnp.bfloat16)
+
+    def teacher_pieces(tiles):
+        return pieces_of(
+            [unpack_matrix(tiles, piece) for piece in MATRICES],
+            tiles[TAIL : TAIL + TAIL_TILES].astype(jnp.float32),
+        )
 
     homes = homes_of(owner_order, tiles_all, devices, near)
     sizes, starts = shares_of(tiles_all, devices)
@@ -743,14 +708,31 @@
     rank = rank.astype(jnp.int32)
     slots = jnp.where(rank < capacity, own_target * capacity + rank, slot_count)
     packed, home_line = send_tiles(slots, own_homes % per, student_flat, slot_count)
+    if near:
+        teacher_tiles = lax.all_gather(teacher_flat, everywhere, axis=0, tiled=True)
+        plane_facts = gather_near(facts)
+        shape = (2, 2, LEN, D)
+        far = rows_t(plane_facts[4:, :LEN]).reshape(shape)
+        columns = [columns_low, shift(columns_low, 1)]
+        packed, home_line, far, columns = together(packed, home_line, far, columns)
     packed = lax.all_to_all(packed.reshape(devices, capacity, TILE), everywhere, 0, 0)
     home_line = lax.all_to_all(home_line[:slot_count].reshape(devices, 1, capacity), everywhere, 0, 0)
     home_line = home_line.reshape(slot_count)
+    if near:
+        looked_t = rows_t(plane_facts[:4, :LEN]).reshape(shape) + swap(far, CORE)
+        packed, home_line, looked_t, ahead = together(packed, home_line, looked_t, shift(columns[1], 1))
+        columns = [*columns, ahead]
     home_tiles = land_tiles(home_line, packed.reshape(slot_count, TILE), per, starts if near else None)
-    home_tiles, table_low = together(home_tiles, table_low)
+    if near:
+        home_tiles, looked_t, ahead = together(home_tiles, plane_hop(looked_t), shift(columns[2], 1))
+        columns = [*columns, ahead]
+
+    def from_everywhere(part):
+        copies = jnp.broadcast_to(part[None], (devices, *part.shape))
+        return lax.all_to_all(copies, everywhere, 0, 0).reshape(-1, TILE)
 
     def every_tile(tiles):
-        stored = lax.all_gather(student_flat.astype(jnp.bfloat16), everywhere, axis=0, tiled=True)
+        stored = from_everywhere(student_flat.astype(jnp.bfloat16))
         sources = jnp.zeros((tiles_all,), jnp.int32).at[homes].set(jnp.arange(tiles_all, dtype=jnp.int32))
         stored = stored[lax.dynamic_slice_in_dim(sources, device * per, per)]
         if near:
@@ -759,44 +741,28 @@
 
     home_tiles = lax.cond(crowded, every_tile, lambda tiles: tiles, home_tiles)
 
-    words = jnp.arange(vocab_rows, dtype=jnp.int32)
-
-    def chosen(ids):
-        return (ids.reshape(-1, 1) - here * vocab_rows == words[None]).astype(jnp.bfloat16)
-
-    def rows_t(ids):
-        return array_multiply(chosen(ids), mentor_lexicon_weights).astype(jnp.bfloat16)
-
-    def rows_s(ids):
-        return trailing_array_multiply(chosen(ids), table_low).astype(jnp.bfloat16)
-
-    if near:
-        plane_facts = gather_near(facts)
-        shape = (2, 2, LEN, D)
-
-        def ids(far):
-            return plane_facts[4:, :LEN] if far else plane_facts[:4, :LEN]
-
-        fillers = [
-            lambda done: [],
-            lambda done: [rows_t(ids(True)).reshape(shape)],
-            lambda done: [rows_t(ids(False)).reshape(shape), swap(done[0], CORE)],
-            lambda done: [done[1] + done[2], rows_s(ids(True)).reshape(shape)],
-            lambda done: [rows_s(ids(False)).reshape(shape), swap(done[4], CORE)],
-            lambda done: [done[5] + done[6], *plane_hop(done[3])],
-        ]
-        teacher_flat, plane_facts = together(teacher_flat, plane_facts)
-        teacher_tiles = lax.all_gather(teacher_flat, everywhere, axis=0, tiled=True)
-        arrivals, places, done = gather_layer(home_tiles, fillers)
-        looked_s, looked_t = done[7], (done[8], done[9])
-        looked_s = plane_hop(looked_s)
-        matrices = assemble_layer(spot, arrivals, tuple(places), devices)
-        matrices, looked_s, facts = together(matrices, looked_s, facts)
+    if near:
+        layer = lax.all_gather(home_tiles, everywhere, axis=0)
+        z = lax.axis_index("dp")
+        table_low = jnp.zeros((D, vocab_rows), jnp.bfloat16)
+        for k, part in enumerate(columns):
+            table_low = lax.dynamic_update_slice(table_low, part, ((z + 4 - k) % 4 * width_share, 0))
+        far = rows_s(plane_facts[4:, :LEN], table_low).reshape(shape)
+        looked_t, far = together(plane_end(*looked_t).astype(jnp.float32), far)
+        close = rows_s(plane_facts[:4, :LEN], table_low).reshape(shape)
+        looked_s, teacher_tiles = together(close + swap(far, CORE), teacher_tiles)
+        teacher = teacher_pieces(teacher_tiles)
+        teacher, looked_s = together(teacher, plane_hop(looked_s))
+        middle, _ = attention_forward(teacher, looked_t, lengths)
+        middle, looked_s = together(middle, plane_end(*looked_s).astype(jnp.float32))
+        final_t = feed_forward(teacher, middle, {})[0]
+        final_t, layer = together(final_t, layer)
+        matrices = assemble_layer(layer)
+        matrices, facts = together(matrices, facts)
         other_facts = gather_near(jnp.stack([shift(facts, 1), shift(facts, 2), shift(facts, 3)]))
         all_facts = jnp.concatenate([plane_facts[:, None], other_facts], axis=1)
-        looked_s = plane_end(*looked_s).astype(jnp.float32)
-        looked_t = plane_end(*looked_t).astype(jnp.float32)
     else:
+        table_low = lax.all_gather(columns_low, "dp", axis=0, tiled=True)
         by_plane = lax.all_gather(facts, "dp", axis=0)
         all_facts = lax.all_gather(by_plane, "vocab", axis=0)
         plane_facts = lax.dynamic_index_in_dim(all_facts, lax.axis_index("dp"), 1, keepdims=False)
@@ -810,42 +776,40 @@
         plane_ids = plane_facts[:, :LEN]
         looked_t, looked_s = (
             lax.psum_scatter(rows, "vocab", scatter_dimension=0, tiled=True).astype(jnp.float32)
-            for rows in (rows_t(plane_ids), rows_s(plane_ids))
+            for rows in (rows_t(plane_ids), rows_s(plane_ids, table_low))
         )
+        teacher = teacher_pieces(teacher_tiles)
+        middle, _ = attention_forward(teacher, looked_t, lengths)
+        final_t = feed_forward(teacher, middle, {})[0]
     up, down, qkv, out, place = matrices[:5]
     student = pieces_of((qkv, out, up, down, place), matrices[5].reshape(-1, TILE))
-    final_s, saved = layer_forward(student, looked_s, lengths)
-    final_s, teacher_tiles, looked_t, all_facts = together(final_s, teacher_tiles, looked_t, all_facts)
-    teacher = pieces_of(
-        [unpack_matrix(teacher_tiles, piece) for piece in MATRICES],
-        teacher_tiles[TAIL : TAIL + TAIL_TILES].astype(jnp.float32),
-    )
+    middle, saved = attention_forward(student, looked_s, lengths)
+    final_s, saved = feed_forward(student, middle, saved)
+
+    offsets = jnp.concatenate([mask_pos.reshape(CAP), jnp.zeros((SLOTS - CAP,), jnp.int32)])
+    picked_t = final_t[offsets].astype(jnp.bfloat16)
+    if near:
+        mentor_picked = gather_near(picked_t).reshape(-1, D)
+        final_s, mentor_picked, all_facts = together(final_s, mentor_picked, all_facts)
+    else:
+        mentor_picked = lax.all_gather(picked_t, "vocab", axis=0, tiled=True)
     token_total = jnp.sum(all_facts[:, :, LEN]).astype(jnp.float32)
     masked_total = jnp.sum(all_facts[:, :, LEN + 1]).astype(jnp.float32)
-
-    offsets = jnp.concatenate([mask_pos.reshape(CAP), jnp.zeros((SLOTS - CAP,), jnp.int32)])
+    teacher_logit = (
+        trailing_array_multiply(mentor_picked, mentor_lexicon_weights) / smoothing_heat_scale
+    )
+    peak_t = jnp.max(teacher_logit, axis=1)
     picked_s = final_s[offsets].astype(jnp.bfloat16)
     if near:
         learner_picked = gather_near(picked_s).reshape(-1, D)
-    final_t = layer_forward(teacher, looked_t, lengths)[0]
-    if near:
-        final_t, learner_picked = together(final_t, learner_picked)
-
-    picked_t = final_t[offsets].astype(jnp.bfloat16)
-    if near:
-        mentor_picked = gather_near(picked_t).reshape(-1, D)
+        learner_picked, teacher_logit, peak_t = together(learner_picked, teacher_logit, peak_t)
     else:
         learner_picked = lax.all_gather(picked_s, "vocab", axis=0, tiled=True)
-        mentor_picked = lax.all_gather(picked_t, "vocab", axis=0, tiled=True)
     live_weighting = (
         (jnp.arange(SLOTS)[None] < plane_facts[:, LEN + 1, None]).astype(jnp.float32).reshape(-1)
     )
     learner_energy = array_multiply(learner_picked, table_low) / smoothing_heat_scale
-    teacher_logit = (
-        trailing_array_multiply(mentor_picked, mentor_lexicon_weights) / smoothing_heat_scale
-    )
     peak_s = jnp.max(learner_energy, axis=1)
-    peak_t = jnp.max(teacher_logit, axis=1)
     teacher_exps = jnp.exp(teacher_logit - peak_t[:, None])
     stats = jnp.stack(
         [
@@ -905,8 +869,8 @@
     grad_final = grad_final.at[offsets].add(grad_rows)
     flow = Flow() if near else PlainFlow(devices)
     grad_sum_one, grad_small, grad_upbias = feed_backward(student, saved, grad_final, flow)
-    grad_embedded = attention_backward(
-        student, saved, grad_sum_one, grad_small, grad_upbias, lengths, tiles_all - TAIL, flow
+    grad_embedded, head_part = attention_backward(
+        student, saved, grad_sum_one, grad_small, grad_upbias, lengths, tiles_all - TAIL, flow, head_part
     )
 
     shares = grad_embedded.astype(jnp.bfloat16).reshape(LEN, planes, width_share).transpose(1, 0, 2)
@@ -921,18 +885,11 @@
         shares = lax.all_to_all(shares, "dp", 0, 0)
         ids = all_facts[:, :, :LEN]
     token_grads = lax.all_gather(shares.reshape(-1, width_share), "vocab", axis=0, tiled=True)
-    def token_sum(n):
-        third = token_grads.shape[0] // 8 * 3
-        begin, end = (n * third, (n + 1) * third) if n < 2 else (n * third, token_grads.shape[0])
-        return matmul_left(token_grads[begin:end], chosen(ids.reshape(-1)[begin:end]))
-
-    shares, head_part = flow.advance(shares, head_part)
+    (shares,) = flow.advance(shares)
     token_grads = lax.all_gather(shares.reshape(-1, width_share), "vocab", axis=0, tiled=True)
     flow.advance()
     flow.advance()
     (token_grads,) = flow.advance(token_grads)
-    (token_part,) = flow.advance(token_sum(0))
-    flow.advance()
     sum_down, sum_up, sum_qkv, sum_rest = flow.sums
     if near:
         home_grads = share_lines(sum_up, sum_down, sum_qkv, sum_rest, per, starts)
@@ -940,14 +897,15 @@
         home_grads = jnp.concatenate([sum_up, sum_down, sum_qkv, sum_rest])
     returned = pick_tiles(jnp.minimum(home_line, per - 1), home_grads, slot_count)
     returned = lax.all_to_all(returned.reshape(devices, capacity, TILE), everywhere, 0, 0)
+    token_part = matmul_left(token_grads, chosen(ids))
+    returned, token_part = together(returned, token_part)
     flat_grad = pick_tiles(jnp.minimum(slots, slot_count - 1), returned.reshape(slot_count, TILE), per)
     flat_grad = lax.cond(
         crowded,
-        lambda grads: lax.all_gather(home_grads, everywhere, axis=0, tiled=True)[own_homes],
+        lambda grads: from_everywhere(home_grads)[own_homes],
         lambda grads: grads,
         flat_grad,
     )
-    token_part = token_part + token_sum(1) + token_sum(2)
     table_grad = (head_part + token_part).T
     loss_term = (
         mixing_coefficient * smoothing_heat_scale**2 * divergence_part / masked_total

time: 919 us -> 879 us (0.956)
  waiting for transfers between devices: 317 us -> 221 us
  local copies, waits for them, and re-layouts: 54.6 us -> 82.2 us
  matrix products: 231 us -> 250 us
    ppermute x21, waiting for transfers between devices: 100 us -> 57.8 us  [shift(): lax.ppermute(value, 'dp', [(i, (i + steps) % size) for i in range(size)])]
    ppermute x89 -> x53, waiting for transfers between devices: 163 us -> 124 us  [swap(): return lax.ppermute(value, 'vocab', [(i, i ^ bit) for i in range(8)])]
    ppermute x21, starting transfers between devices: 22.3 us -> 52.9 us  [shift(): lax.ppermute(value, 'dp', [(i, (i + steps) % size) for i in range(size)])]
    ppermute x89 -> x53, starting transfers between devices: 67.2 us -> 47.1 us  [swap(): return lax.ppermute(value, 'vocab', [(i, i ^ bit) for i in range(8)])]
    sub x1 -> x2, matrix products: 10.9 us -> 30.4 us  [the longest x1 18.8 us: attention_backward(): grad_probs - jnp.sum(grad_probs * probabilities, axis=-1, keepdims=True)]
    all_to_all x1, waiting for transfers between devices: 28.9 us -> 15.8 us  [on_device(): lax.all_to_all(packed.reshape(devices, capacity, TILE), everywhere, 0, 0)]
    unnamed x309 -> x277, local copies, waits for them, and re-layouts: 12.1 us -> 19.8 us
    dot_general x11 -> x9, matrix products: 73.9 us -> 66.5 us  [matmul_left(): lax.dot_general(left_side, right_side, (((0,), (0,)), ((), ())), preferre...]
  transfers between devices with their start and end apart: 119 -> 83, of which waited for: 71 -> 42; matrix products, arithmetic and copies ran while one was open for 36% -> 43% of each run, Pallas kernels for 3% -> 4%
where the time goes in v7:
time: 879 us; the launch traced here: 869 us
  matrix products  250 us (28%)
  waiting for transfers between devices  221 us (25%)
  other arithmetic  122 us (14%)
  starting transfers between devices  111 us (13%)
  local copies, waits for them, and re-layouts  82.2 us (9%)
  Pallas kernels  56.5 us (6%)
  between operations  25.3 us (3%)
    ppermute x53, waiting for transfers between devices, swap(): return lax.ppermute(value, 'vocab', [(i, i ^ bit) for i in range(8)])  124 us
    dot_general x11, matrix products, array_multiply(): return jnp.dot(left_side, right_side, preferred_element_type=jnp.float32)  79.8 us
    dot_general x9, matrix products, matmul_left(): lax.dot_general(left_side, right_side, (((0,), (0,)), ((), ())), preferre...  66.5 us
    ppermute x21, waiting for transfers between devices, shift(): lax.ppermute(value, 'dp', [(i, (i + steps) % size) for i in range(size)])  57.8 us
    ppermute x21, starting transfers between devices, shift(): lax.ppermute(value, 'dp', [(i, (i + steps) % size) for i in range(size)])  52.9 us
    ppermute x53, starting transfers between devices, swap(): return lax.ppermute(value, 'vocab', [(i, i ^ bit) for i in range(8)])  47.1 us
    dot_general x9, matrix products, trailing_array_multiply(): lax.dot_general(left_side, right_side, (((1,), (1,)), ((), ())), preferre...  45.7 us
    pallas_call x5, Pallas kernels, unpack_matrix(): pl.pallas_call(functools.partial(unpack_kernel, across=across), grid=(hei...  21.4 us
  transfers between devices with their start and end apart: 83, of which 42 were waited for; matrix products, arithmetic and copies ran while one was open for 43% of the time, Pallas kernels for 4%

profile of v7, /device:TPU:0, one launch (start us, length us, event | category | flops | bytes accessed | tf_op | source)
XLA Modules:
  0.0 869.1 jit_solution(9203734900336626415)
XLA Ops:
  17.5 4.7 broadcast_divide_fusion
  28.0 7.2 send_tiles.1
  35.3 8.5 fusion.67
  55.2 4.7 all-to-all-done.3
  63.6 8.5 fusion.69
  73.9 5.2 add.1074
  79.2 10.5 %collective-permute-done.5 = bf16[192,1920]{1,0:T(8,128)(2,1)} collective-permute-done((bf16[192,1920]{1,0:T(8,128)(2,1)}, bf16[192,1920]{1,0:T(8,128)(2,1)}, u32[]{:S(2)}, u32[]{:S(2)}) %collective-permute-start.5) | collective-permute-done | bytes 737312 | tf_op jit(solution)/shard_map/ppermute | solution.py:56
  89.7 15.8 %all-to-all-done.2 = bf16[32,96,128]{2,1,0:T(8,128)(2,1)} async-done(((bf16[32,96,128]{2,1,0:T(8,128)(2,1)}), bf16[32,96,128]{2,1,0:T(8,128)(2,1)}, u32[]{:S(2)}, u32[]{:S(2)}) %all-to-all-start.2) | async-done | bytes 786464 | tf_op jit(solution)/shard_map/all_to_all | solution.py:718
  115.3 4.7 land_tiles.3
  119.9 25.1 %collective-permute-done.6 = bf16[2,256,768]{2,1,0:T(8,128)(2,1)} collective-permute-done((bf16[2,256,768]{2,1,0:T(8,128)(2,1)}, bf16[2,256,768]{2,1,0:T(8,128)(2,1)}, u32[]{:S(2)}, u32[]{:S(2)}) %collective-permute-start.6) | collective-permute-done | bytes 786464 | tf_op jit(solution)/shard_map/ppermute | solution.py:51
  159.0 7.4 fusion.68
  168.4 7.3 fusion.70
  195.4 5.8 unpack_matrix.9
  201.2 6.4 unpack_matrix.5
  219.1 4.3 copy.101
  228.4 11.6 %fusion.297 = (f32[12,512]{1,0:T(8,128)S(1)}, f32[12,512,512]{1,2,0:T(8,128)}) fusion(pred[512]{0:T(512)(128)(4,1)S(1)} %iota_compare_fusion.27, bf16[1,512,3,12,64]{1,4,3,2,0:T(8,128)(2,1)} %bitcast.466), kind=kOutput, calls=%fused_computation.715 | convolution fusion | flops 415236608 | bytes 14180864 | tf_op jit(solution)/shard_map/sub | solution.py:401
  240.0 7.2 fusion.92
  253.6 23.4 %fusion.299 = (f32[512]{0:T(512)S(1)}, f32[512,768]{1,0:T(8,128)}) fusion(f32[512,768]{1,0:T(8,128)} %multiply_add_fusion.4, f32[768]{0:T(1024)S(1)} %get-tuple-element.256, bf16[3072,768]{1,0:T(8,128)(2,1)} %unpack_matrix.5, bf16[768,3072]{1,0:T(8,128)(2,1)} %unpack_matrix.9, f32[3072]{0:T(1024)S(1)} %slice_bitcast_fusion.47), kind=kOutput, calls=%fused_computation.717 | convolution fusion | flops 4937219584 | bytes 12600320 | tf_op jit(solution)/shard_map/dot_general | solution.py:323
  280.6 8.4 all-gather.9.cloned.1.call-done
  289.1 12.3 %assemble_layer.1 = (bf16[768,3072]{1,0:T(8,128)(2,1)}, bf16[3072,768]{1,0:T(8,128)(2,1)}, bf16[768,2304]{1,0:T(8,128)(2,1)}, bf16[768,768]{1,0:T(8,128)(2,1)}, ...) custom-call(bf16[32,160,1536]{2,1,0:T(8,128)(2,1)} %bitcast.428), custom_call_target="tpu_custom_call" | custom-call | bytes 60000000 | tf_op jit(solution)/shard_map/assemble_layer/pallas_call | solution.py:277
  313.8 6.0 fusion.66
  332.9 4.6 fusion.93
  339.0 20.1 %fusion.28 = (bf16[512,3072]{1,0:T(8,128)(2,1)S(1)}, f32[512,3072]{1,0:T(8,128)}) fusion(f32[3072]{0:T(1024)S(1)} %slice_bitcast_fusion.46, bf16[768,3072]{1,0:T(8,128)(2,1)} %get-tuple-element.178, f32[512,768]{1,0:T(8,128)S(1)} %get-tuple-element.378, f32[768]{0:T(1024)S(1)} %get-tuple-element.334, f32[768]{0:T(1024)S(1)} %get-tuple-element.335, ...), kind=kOutput, calls=%fused_computation.60 | convolution fusion | flops 2521694208 | bytes 15751168 | tf_op jit(solution)/shard_map/dot_general | solution.py:323
  364.6 7.6 collective-permute-done.17
  382.3 6.7 collective-permute-done.25
  389.7 10.1 %collective-permute-done.26 = bf16[2,128,768]{2,1,0:T(8,128)(2,1)S(1)} collective-permute-done((bf16[2,128,768]{2,1,0:T(8,128)(2,1)S(1)}, bf16[2,128,768]{2,1,0:T(8,128)(2,1)S(1)}, u32[]{:S(2)}, u32[]{:S(2)}) %collective-permute-start.26) | collective-permute-done | bytes 393248 | tf_op jit(solution)/shard_map/ppermute | solution.py:51
  425.3 7.3 multiply_convert_fusion.1
  451.6 5.4 fusion.311
  457.0 4.3 collective-permute-done.32
  483.9 7.1 convert_reduce_fusion.1
  498.3 8.2 multiply_reduce_fusion.4
  530.5 8.6 fusion.83
  539.0 18.8 %fusion.71 = bf16[1,12,512,512]{2,3,1,0:T(8,128)(2,1)} fusion(f32[12,512,512]{1,2,0:T(8,128)} %copy-done.1, f32[12,512]{1,0:T(8,128)} %log_add_fusion, pred[512]{0:T(512)(128)(4,1)S(1)} %iota_compare_fusion.27, bf16[512,12,64]{0,2,1:T(8,128)(2,1)} %bitcast.477, bf16[1,512,3,12,64]{1,4,3,2,0:T(8,128)(2,1)} %bitcast.425), kind=kOutput, calls=%fused_computation.127 | convolution fusion | flops 836770304 | bytes 34669568 | tf_op jit(solution)/shard_map/sub | solution.py:492
  589.6 5.2 fusion.101
  601.7 6.2 collective-permute-done.45
  609.2 4.4 collective-permute-done.43
  634.4 23.0 %collective-permute-start.46 = (f32[192,384]{1,0:T(8,128)S(1)}, f32[192,384]{1,0:T(8,128)S(1)}, u32[]{:S(2)}, u32[]{:S(2)}) collective-permute-start(f32[192,384]{1,0:T(8,128)S(1)} %copy-done.82), channel_id=1, source_target_pairs={{0,8},{8,16},{16,24},{24,0},{1,9},{9,17},{17,25},{25,1},{2,10},{10... | collective-permute-start | bytes 884744 | tf_op jit(solution)/shard_map/ppermute | solution.py:56
  663.5 5.4 convolution_add_fusion.3
  669.0 11.2 %collective-permute-done.47 = f32[192,384]{1,0:T(8,128)S(1)} collective-permute-done((f32[192,384]{1,0:T(8,128)S(1)}, f32[192,384]{1,0:T(8,128)S(1)}, u32[]{:S(2)}, u32[]{:S(2)}) %collective-permute-start.47) | collective-permute-done | bytes 294944 | tf_op jit(solution)/shard_map/ppermute | solution.py:56
  680.2 10.3 %collective-permute-done.50 = f32[48,1536]{1,0:T(8,128)S(1)} collective-permute-done((f32[48,1536]{1,0:T(8,128)S(1)}, f32[48,1536]{1,0:T(8,128)S(1)}, u32[]{:S(2)}, u32[]{:S(2)}) %collective-permute-start.50) | collective-permute-done | bytes 294944 | tf_op jit(solution)/shard_map/ppermute | solution.py:56
  700.3 7.0 collective-permute-done.60
  711.0 8.5 collective-permute-done.58
  729.5 7.1 collective-permute-done.61
  736.9 6.7 collective-permute-start.69
  752.6 6.8 collective-permute-done.69
  759.4 12.4 %collective-permute-done.66 = f32[48,1152]{1,0:T(8,128)S(1)} collective-permute-done((f32[48,1152]{1,0:T(8,128)S(1)}, f32[48,1152]{1,0:T(8,128)S(1)}, u32[]{:S(2)}, u32[]{:S(2)}) %collective-permute-start.66) | collective-permute-done | bytes 221216 | tf_op jit(solution)/shard_map/ppermute | solution.py:56
  778.2 4.9 pick_tiles.2
  789.4 32.3 %fusion.4 = f32[192,1920]{1,0:T(8,128)} fusion(bf16[16384,192]{0,1:T(8,128)(2,1)} %all-gather.7.cloned.1.call-done, s32[16384]{0:T(1024)S(1)} %bitcast.499), kind=kOutput, calls=%fused_computation.16 | convolution fusion | flops 12111052800 | bytes 7831552 | tf_op jit(solution)/shard_map/dot_general | solution.py:327
  (704 shorter events, 388.8 us)
Async XLA Ops:
  7.2 171.2 %all-gather.5.cloned.1.call-start = ((), (), s32[]{:S(2)}) async-start(), calls=%async_computation.6 | async-start | bytes 15476736 | tf_op jit(solution)/shard_map/all_gather | solution.py:712
  15.9 30.2 %collective-permute-start.3 = (bf16[192,1920]{1,0:T(8,128)(2,1)}, bf16[192,1920]{1,0:T(8,128)(2,1)}, u32[]{:S(2)}, u32[]{:S(2)}) collective-permute-start(bf16[192,1920]{1,0:T(8,128)(2,1)} %convert_bitcast_fusion), channel_id=1, source_target_pairs={{0,8},{8,16},{16,24},{24,0},{1,9},{9,17},{17,25},{25,1},{2,10},{10... | collective-permute-start | bytes 2211848 | tf_op jit(solution)/shard_map/ppermute | solution.py:56
  46.1 27.8 %collective-permute-start.4 = (bf16[2,2,512,768]{3,2,1,0:T(8,128)(2,1)}, bf16[2,2,512,768]{3,2,1,0:T(8,128)(2,1)}, u32[]{:S(2)}, u32[]{:S(2)}) collective-permute-start(bf16[2,2,512,768]{3,2,1,0:T(8,128)(2,1)} %bitcast.3), channel_id=1, source_target_pairs={{0,1},{1,0},{2,3},{3,2},{4,5},{5,4},{6,7},{7,6},{8,9},{9,8},{10,11... | collective-permute-start | bytes 9437192 | tf_op jit(solution)/shard_map/ppermute | solution.py:51
  53.5 36.2 %collective-permute-start.5 = (bf16[192,1920]{1,0:T(8,128)(2,1)}, bf16[192,1920]{1,0:T(8,128)(2,1)}, u32[]{:S(2)}, u32[]{:S(2)}) collective-permute-start(bf16[192,1920]{1,0:T(8,128)(2,1)} %collective-permute-done.3), channel_id=1, source_target_pairs={{0,8},{8,16},{16,24},{24,0},{1,9},{9,17},{17,25},{25,1},{2,10},{10... | collective-permute-start | bytes 2211848 | tf_op jit(solution)/shard_map/ppermute | solution.py:56
  60.0 45.5 %all-to-all-start.2 = ((bf16[32,96,128]{2,1,0:T(8,128)(2,1)}), bf16[32,96,128]{2,1,0:T(8,128)(2,1)}, u32[]{:S(2)}, u32[]{:S(2)}) async-start(bf16[32,96,128]{2,1,0:T(8,128)(2,1)} %bitcast.475), calls=%async_computation.2 | async-start | bytes 1572864 | tf_op jit(solution)/shard_map/all_to_all | solution.py:718
  63.3 225.7 %all-gather.9.cloned.1.call-start = ((), (), s32[]{:S(2)}) async-start(), calls=%async_computation.9 | async-start | bytes 16220160 | tf_op jit(solution)/shard_map/all_gather | solution.py:745
  107.8 37.2 %collective-permute-start.6 = (bf16[2,256,768]{2,1,0:T(8,128)(2,1)}, bf16[2,256,768]{2,1,0:T(8,128)(2,1)}, u32[]{:S(2)}, u32[]{:S(2)}) collective-permute-start(bf16[2,256,768]{2,1,0:T(8,128)(2,1)} %slice_bitcast_fusion.12), channel_id=1, source_target_pairs={{0,2},{1,3},{2,0},{3,1},{4,6},{5,7},{6,4},{7,5},{8,10},{9,11},{10,... | collective-permute-start | bytes 2359304 | tf_op jit(solution)/shard_map/ppermute | solution.py:51
  111.3 37.1 %collective-permute-start.7 = (bf16[2,256,768]{2,1,0:T(8,128)(2,1)}, bf16[2,256,768]{2,1,0:T(8,128)(2,1)}, u32[]{:S(2)}, u32[]{:S(2)}) collective-permute-start(bf16[2,256,768]{2,1,0:T(8,128)(2,1)} %slice_bitcast_fusion.11), channel_id=1, source_target_pairs={{0,4},{1,5},{2,6},{3,7},{4,0},{5,1},{6,2},{7,3},{8,12},{9,13},{10,... | collective-permute-start | bytes 2359304 | tf_op jit(solution)/shard_map/ppermute | solution.py:51
  112.8 38.0 %collective-permute-start.8 = (bf16[192,1920]{1,0:T(8,128)(2,1)}, bf16[192,1920]{1,0:T(8,128)(2,1)}, u32[]{:S(2)}, u32[]{:S(2)}) collective-permute-start(bf16[192,1920]{1,0:T(8,128)(2,1)} %collective-permute-done.5), channel_id=1, source_target_pairs={{0,8},{8,16},{16,24},{24,0},{1,9},{9,17},{17,25},{25,1},{2,10},{10... | collective-permute-start | bytes 2211848 | tf_op jit(solution)/shard_map/ppermute | solution.py:56
  151.2 467.8 %reduce-scatter.2.cloned.1.call-start = ((), (), s32[]{:S(2)}) async-start(), calls=%async_computation.7 | async-start | bytes 7372800 | tf_op jit(solution)/shard_map/reduce_scatter | solution.py:858
  180.5 27.9 %collective-permute-start.12 = (bf16[2,256,768]{2,1,0:T(8,128)(2,1)}, bf16[2,256,768]{2,1,0:T(8,128)(2,1)}, u32[]{:S(2)}, u32[]{:S(2)}) collective-permute-start(bf16[2,256,768]{2,1,0:T(8,128)(2,1)} %slice_bitcast_fusion.10), channel_id=1, source_target_pairs={{0,2},{1,3},{2,0},{3,1},{4,6},{5,7},{6,4},{7,5},{8,10},{9,11},{10,... | collective-permute-start | bytes 2359304 | tf_op jit(solution)/shard_map/ppermute | solution.py:51
  184.0 27.0 %collective-permute-start.13 = (bf16[2,256,768]{2,1,0:T(8,128)(2,1)}, bf16[2,256,768]{2,1,0:T(8,128)(2,1)}, u32[]{:S(2)}, u32[]{:S(2)}) collective-permute-start(bf16[2,256,768]{2,1,0:T(8,128)(2,1)} %slice_bitcast_fusion.9), channel_id=1, source_target_pairs={{0,4},{1,5},{2,6},{3,7},{4,0},{5,1},{6,2},{7,3},{8,12},{9,13},{10,... | collective-permute-start | bytes 2359304 | tf_op jit(solution)/shard_map/ppermute | solution.py:51
  225.2 25.0 %collective-permute-start.15 = (bf16[256,768]{1,0:T(8,128)(2,1)}, bf16[256,768]{1,0:T(8,128)(2,1)}, u32[]{:S(2)}, u32[]{:S(2)}) collective-permute-start(bf16[256,768]{1,0:T(8,128)(2,1)} %slice_bitcast_fusion.38), channel_id=1, source_target_pairs={{0,2},{1,3},{2,0},{3,1},{4,6},{5,7},{6,4},{7,5},{8,10},{9,11},{10,... | collective-permute-start | bytes 1179656 | tf_op jit(solution)/shard_map/ppermute | solution.py:51
  227.1 24.1 %collective-permute-start.14 = (bf16[256,768]{1,0:T(8,128)(2,1)S(1)}, bf16[256,768]{1,0:T(8,128)(2,1)}, u32[]{:S(2)}, u32[]{:S(2)}) collective-permute-start(bf16[256,768]{1,0:T(8,128)(2,1)S(1)} %slice_bitcast_fusion.39), channel_id=1, source_target_pairs={{0,4},{1,5},{2,6},{3,7},{4,0},{5,1},{6,2},{7,3},{8,12},{9,13},{10,... | collective-permute-start | bytes 1179656 | tf_op jit(solution)/shard_map/ppermute | solution.py:51
  302.9 60.0 %collective-permute-start.21 = (s32[640]{0:T(1024)S(1)}, s32[640]{0:T(1024)S(1)}, u32[]{:S(2)}, u32[]{:S(2)}) collective-permute-start(s32[640]{0:T(1024)S(1)} %copy-done.112), channel_id=1, source_target_pairs={{0,24},{8,0},{16,8},{24,16},{1,25},{9,1},{17,9},{25,17},{2,26},{10... | collective-permute-start | bytes 7688 | tf_op jit(solution)/shard_map/ppermute | solution.py:56
  304.4 58.5 %collective-permute-start.20 = (s32[640]{0:T(1024)S(1)}, s32[640]{0:T(1024)S(1)}, u32[]{:S(2)}, u32[]{:S(2)}) collective-permute-start(s32[640]{0:T(1024)S(1)} %copy-done.112), channel_id=1, source_target_pairs={{0,16},{8,24},{16,0},{24,8},{1,17},{9,25},{17,1},{25,9},{2,18},{10... | collective-permute-start | bytes 7688 | tf_op jit(solution)/shard_map/ppermute | solution.py:56
  304.9 58.0 %collective-permute-start.19 = (s32[640]{0:T(1024)S(1)}, s32[640]{0:T(1024)S(1)}, u32[]{:S(2)}, u32[]{:S(2)}) collective-permute-start(s32[640]{0:T(1024)S(1)} %copy-done.112), channel_id=1, source_target_pairs={{0,8},{8,16},{16,24},{24,0},{1,9},{9,17},{17,25},{25,1},{2,10},{10... | collective-permute-start | bytes 7688 | tf_op jit(solution)/shard_map/ppermute | solution.py:56
  312.3 49.5 %collective-permute-start.16 = (bf16[1,128,768]{2,1,0:T(8,128)(2,1)S(1)}, bf16[1,128,768]{2,1,0:T(8,128)(2,1)S(1)}, u32[]{:S(2)}, u32[]{:S(2)}) collective-permute-start(bf16[1,128,768]{2,1,0:T(8,128)(2,1)S(1)} %bitcast.456), channel_id=1, source_target_pairs={{0,2},{1,3},{2,0},{3,1},{4,6},{5,7},{6,4},{7,5},{8,10},{9,11},{10,... | collective-permute-start | bytes 589832 | tf_op jit(solution)/shard_map/ppermute | solution.py:51
  483.8 25.0 %collective-permute-start.36 = (f32[3072,384]{1,0:T(8,128)}, f32[3072,384]{1,0:T(8,128)}, u32[]{:S(2)}, u32[]{:S(2)}) collective-permute-start(f32[3072,384]{1,0:T(8,128)} %fusion.126), channel_id=1, source_target_pairs={{0,1},{1,0},{2,3},{3,2},{4,5},{5,4},{6,7},{7,6},{8,9},{9,8},{10,11... | collective-permute-start | bytes 14155784 | tf_op jit(solution)/shard_map/ppermute | solution.py:51
  494.9 20.4 %collective-permute-start.37 = (f32[768,1536]{1,0:T(8,128)}, f32[768,1536]{1,0:T(8,128)}, u32[]{:S(2)}, u32[]{:S(2)}) collective-permute-start(f32[768,1536]{1,0:T(8,128)} %fusion.80), channel_id=1, source_target_pairs={{0,1},{1,0},{2,3},{3,2},{4,5},{5,4},{6,7},{7,6},{8,9},{9,8},{10,11... | collective-permute-start | bytes 14155784 | tf_op jit(solution)/shard_map/ppermute | solution.py:51
  496.7 275.9 %all-gather.7.cloned.1.call-start = ((), (), s32[]{:S(2)}) async-start(), calls=%async_computation.8 | async-start | bytes 7077888 | tf_op jit(solution)/shard_map/all_gather | solution.py:889
  520.5 46.0 %collective-permute-start.39 = (bf16[2,2,192,384]{3,2,0,1:T(8,128)(2,1)}, bf16[2,2,192,384]{3,2,0,1:T(8,128)(2,1)}, u32[]{:S(2)}, u32[]{:S(2)}) collective-permute-start(bf16[2,2,192,384]{3,2,0,1:T(8,128)(2,1)} %fusion.119), channel_id=1, source_target_pairs={{0,4},{1,5},{2,6},{3,7},{4,0},{5,1},{6,2},{7,3},{8,12},{9,13},{10,... | collective-permute-start | bytes 1769480 | tf_op jit(solution)/shard_map/ppermute | solution.py:51
  520.6 48.1 %collective-permute-start.38 = (bf16[2,2,192,384]{3,2,0,1:T(8,128)(2,1)S(1)}, bf16[2,2,192,384]{3,2,0,1:T(8,128)(2,1)}, u32[]{:S(2)}, u32[]{:S(2)}) collective-permute-start(bf16[2,2,192,384]{3,2,0,1:T(8,128)(2,1)S(1)} %fusion.118), channel_id=1, source_target_pairs={{0,2},{1,3},{2,0},{3,1},{4,6},{5,7},{6,4},{7,5},{8,10},{9,11},{10,... | collective-permute-start | bytes 1769480 | tf_op jit(solution)/shard_map/ppermute | solution.py:51
  559.4 14.8 %collective-permute-start.41 = (bf16[2,2,48,1536]{3,2,0,1:T(8,128)(2,1)S(1)}, bf16[2,2,48,1536]{3,2,0,1:T(8,128)(2,1)S(1)}, u32[]{:S(2)}, u32[]{:S(2)}) collective-permute-start(bf16[2,2,48,1536]{3,2,0,1:T(8,128)(2,1)S(1)} %fusion.121), channel_id=1, source_target_pairs={{0,4},{1,5},{2,6},{3,7},{4,0},{5,1},{6,2},{7,3},{8,12},{9,13},{10,... | collective-permute-start | bytes 1769480 | tf_op jit(solution)/shard_map/ppermute | solution.py:51
  564.5 14.4 %collective-permute-start.40 = (bf16[2,2,48,1536]{3,2,0,1:T(8,128)(2,1)S(1)}, bf16[2,2,48,1536]{3,2,0,1:T(8,128)(2,1)S(1)}, u32[]{:S(2)}, u32[]{:S(2)}) collective-permute-start(bf16[2,2,48,1536]{3,2,0,1:T(8,128)(2,1)S(1)} %fusion.120), channel_id=1, source_target_pairs={{0,2},{1,3},{2,0},{3,1},{4,6},{5,7},{6,4},{7,5},{8,10},{9,11},{10,... | collective-permute-start | bytes 1769480 | tf_op jit(solution)/shard_map/ppermute | solution.py:51
  594.7 36.9 %collective-permute-start.52 = (f32[768,1152]{1,0:T(8,128)}, f32[768,1152]{1,0:T(8,128)}, u32[]{:S(2)}, u32[]{:S(2)}) collective-permute-start(f32[768,1152]{1,0:T(8,128)} %fusion.101), channel_id=1, source_target_pairs={{0,1},{1,0},{2,3},{3,2},{4,5},{5,4},{6,7},{7,6},{8,9},{9,8},{10,11... | collective-permute-start | bytes 10616840 | tf_op jit(solution)/shard_map/ppermute | solution.py:51
  597.4 20.0 %collective-permute-start.53 = (f32[1408,384]{1,0:T(8,128)S(1)}, f32[1408,384]{1,0:T(8,128)S(1)}, u32[]{:S(2)}, u32[]{:S(2)}) collective-permute-start(f32[1408,384]{1,0:T(8,128)S(1)} %bitcast.468), channel_id=1, source_target_pairs={{0,1},{1,0},{2,3},{3,2},{4,5},{5,4},{6,7},{7,6},{8,9},{9,8},{10,11... | collective-permute-start | bytes 6488072 | tf_op jit(solution)/shard_map/ppermute | solution.py:51
  600.1 16.4 %collective-permute-start.44 = (bf16[2,48,1536]{2,1,0:T(8,128)(2,1)S(1)}, bf16[2,48,1536]{2,1,0:T(8,128)(2,1)S(1)}, u32[]{:S(2)}, u32[]{:S(2)}) collective-permute-start(bf16[2,48,1536]{2,1,0:T(8,128)(2,1)S(1)} %fusion.131), channel_id=1, source_target_pairs={{0,4},{1,5},{2,6},{3,7},{4,0},{5,1},{6,2},{7,3},{8,12},{9,13},{10,... | collective-permute-start | bytes 884744 | tf_op jit(solution)/shard_map/ppermute | solution.py:51
  600.3 13.3 %collective-permute-start.43 = (bf16[2,192,384]{2,1,0:T(8,128)(2,1)S(1)}, bf16[2,192,384]{2,1,0:T(8,128)(2,1)S(1)}, u32[]{:S(2)}, u32[]{:S(2)}) collective-permute-start(bf16[2,192,384]{2,1,0:T(8,128)(2,1)S(1)} %fusion.130), channel_id=1, source_target_pairs={{0,2},{1,3},{2,0},{3,1},{4,6},{5,7},{6,4},{7,5},{8,10},{9,11},{10,... | collective-permute-start | bytes 884744 | tf_op jit(solution)/shard_map/ppermute | solution.py:51
  621.8 39.4 %collective-permute-start.48 = (f32[192,384]{1,0:T(8,128)}, f32[192,384]{1,0:T(8,128)}, u32[]{:S(2)}, u32[]{:S(2)}) collective-permute-start(f32[192,384]{1,0:T(8,128)} %get-tuple-element.313), channel_id=1, source_target_pairs={{0,24},{8,0},{16,8},{24,16},{1,25},{9,1},{17,9},{25,17},{2,26},{10... | collective-permute-start | bytes 884744 | tf_op jit(solution)/shard_map/ppermute | solution.py:56
  628.9 32.3 %collective-permute-start.55 = (bf16[512,192]{0,1:T(8,128)(2,1)S(1)}, bf16[512,192]{0,1:T(8,128)(2,1)S(1)}, u32[]{:S(2)}, u32[]{:S(2)}) collective-permute-start(bf16[512,192]{0,1:T(8,128)(2,1)S(1)} %get-tuple-element.323), channel_id=1, source_target_pairs={{0,16},{8,24},{16,0},{24,8},{1,17},{9,25},{17,1},{25,9},{2,18},{10... | collective-permute-start | bytes 589832 | tf_op jit(solution)/shard_map/ppermute | solution.py:56
  630.0 31.2 %collective-permute-start.54 = (bf16[512,192]{0,1:T(8,128)(2,1)S(1)}, bf16[512,192]{0,1:T(8,128)(2,1)S(1)}, u32[]{:S(2)}, u32[]{:S(2)}) collective-permute-start(bf16[512,192]{0,1:T(8,128)(2,1)S(1)} %get-tuple-element.324), channel_id=1, source_target_pairs={{0,8},{8,16},{16,24},{24,0},{1,9},{9,17},{17,25},{25,1},{2,10},{10... | collective-permute-start | bytes 589832 | tf_op jit(solution)/shard_map/ppermute | solution.py:56
  631.6 48.5 %collective-permute-start.47 = (f32[192,384]{1,0:T(8,128)S(1)}, f32[192,384]{1,0:T(8,128)S(1)}, u32[]{:S(2)}, u32[]{:S(2)}) collective-permute-start(f32[192,384]{1,0:T(8,128)S(1)} %copy-done.83), channel_id=1, source_target_pairs={{0,16},{8,24},{16,0},{24,8},{1,17},{9,25},{17,1},{25,9},{2,18},{10... | collective-permute-start | bytes 884744 | tf_op jit(solution)/shard_map/ppermute | solution.py:56
  634.4 45.7 %collective-permute-start.46 = (f32[192,384]{1,0:T(8,128)S(1)}, f32[192,384]{1,0:T(8,128)S(1)}, u32[]{:S(2)}, u32[]{:S(2)}) collective-permute-start(f32[192,384]{1,0:T(8,128)S(1)} %copy-done.82), channel_id=1, source_target_pairs={{0,8},{8,16},{16,24},{24,0},{1,9},{9,17},{17,25},{25,1},{2,10},{10... | collective-permute-start | bytes 884744 | tf_op jit(solution)/shard_map/ppermute | solution.py:56
  661.2 19.0 %collective-permute-start.51 = (f32[48,1536]{1,0:T(8,128)S(1)}, f32[48,1536]{1,0:T(8,128)S(1)}, u32[]{:S(2)}, u32[]{:S(2)}) collective-permute-start(f32[48,1536]{1,0:T(8,128)S(1)} %get-tuple-element.309), channel_id=1, source_target_pairs={{0,24},{8,0},{16,8},{24,16},{1,25},{9,1},{17,9},{25,17},{2,26},{10... | collective-permute-start | bytes 884744 | tf_op jit(solution)/shard_map/ppermute | solution.py:56
  661.2 29.3 %collective-permute-start.50 = (f32[48,1536]{1,0:T(8,128)S(1)}, f32[48,1536]{1,0:T(8,128)S(1)}, u32[]{:S(2)}, u32[]{:S(2)}) collective-permute-start(f32[48,1536]{1,0:T(8,128)S(1)} %get-tuple-element.310), channel_id=1, source_target_pairs={{0,16},{8,24},{16,0},{24,8},{1,17},{9,25},{17,1},{25,9},{2,18},{10... | collective-permute-start | bytes 884744 | tf_op jit(solution)/shard_map/ppermute | solution.py:56
  661.2 29.3 %collective-permute-start.49 = (f32[48,1536]{1,0:T(8,128)S(1)}, f32[48,1536]{1,0:T(8,128)S(1)}, u32[]{:S(2)}, u32[]{:S(2)}) collective-permute-start(f32[48,1536]{1,0:T(8,128)S(1)} %get-tuple-element.311), channel_id=1, source_target_pairs={{0,8},{8,16},{16,24},{24,0},{1,9},{9,17},{17,25},{25,1},{2,10},{10... | collective-permute-start | bytes 884744 | tf_op jit(solution)/shard_map/ppermute | solution.py:56
  696.5 14.5 %collective-permute-start.59 = (bf16[2,2,88,384]{3,2,0,1:T(8,128)(2,1)S(1)}, bf16[2,2,88,384]{3,2,0,1:T(8,128)(2,1)S(1)}, u32[]{:S(2)}, u32[]{:S(2)}) collective-permute-start(bf16[2,2,88,384]{3,2,0,1:T(8,128)(2,1)S(1)} %fusion.133), channel_id=1, source_target_pairs={{0,2},{1,3},{2,0},{3,1},{4,6},{5,7},{6,4},{7,5},{8,10},{9,11},{10,... | collective-permute-start | bytes 811016 | tf_op jit(solution)/shard_map/ppermute | solution.py:51
  697.3 22.2 %collective-permute-start.58 = (bf16[2,2,48,1152]{3,2,0,1:T(8,128)(2,1)S(1)}, bf16[2,2,48,1152]{3,2,0,1:T(8,128)(2,1)S(1)}, u32[]{:S(2)}, u32[]{:S(2)}) collective-permute-start(bf16[2,2,48,1152]{3,2,0,1:T(8,128)(2,1)S(1)} %fusion.123), channel_id=1, source_target_pairs={{0,4},{1,5},{2,6},{3,7},{4,0},{5,1},{6,2},{7,3},{8,12},{9,13},{10,... | collective-permute-start | bytes 1327112 | tf_op jit(solution)/shard_map/ppermute | solution.py:51
  699.1 22.0 %collective-permute-start.57 = (bf16[2,2,48,1152]{3,2,0,1:T(8,128)(2,1)S(1)}, bf16[2,2,48,1152]{3,2,0,1:T(8,128)(2,1)S(1)}, u32[]{:S(2)}, u32[]{:S(2)}) collective-permute-start(bf16[2,2,48,1152]{3,2,0,1:T(8,128)(2,1)S(1)} %fusion.122), channel_id=1, source_target_pairs={{0,2},{1,3},{2,0},{3,1},{4,6},{5,7},{6,4},{7,5},{8,10},{9,11},{10,... | collective-permute-start | bytes 1327112 | tf_op jit(solution)/shard_map/ppermute | solution.py:51
  723.6 12.9 %collective-permute-start.61 = (bf16[2,48,1152]{2,1,0:T(8,128)(2,1)S(1)}, bf16[2,48,1152]{2,1,0:T(8,128)(2,1)S(1)}, u32[]{:S(2)}, u32[]{:S(2)}) collective-permute-start(bf16[2,48,1152]{2,1,0:T(8,128)(2,1)S(1)} %fusion.205), channel_id=1, source_target_pairs={{0,4},{1,5},{2,6},{3,7},{4,0},{5,1},{6,2},{7,3},{8,12},{9,13},{10,... | collective-permute-start | bytes 663560 | tf_op jit(solution)/shard_map/ppermute | solution.py:51
  723.8 12.8 %collective-permute-start.62 = (bf16[2,48,1152]{2,1,0:T(8,128)(2,1)S(1)}, bf16[2,48,1152]{2,1,0:T(8,128)(2,1)S(1)}, u32[]{:S(2)}, u32[]{:S(2)}) collective-permute-start(bf16[2,48,1152]{2,1,0:T(8,128)(2,1)S(1)} %fusion.206), channel_id=1, source_target_pairs={{0,2},{1,3},{2,0},{3,1},{4,6},{5,7},{6,4},{7,5},{8,10},{9,11},{10,... | collective-permute-start | bytes 663560 | tf_op jit(solution)/shard_map/ppermute | solution.py:51
  736.9 22.6 %collective-permute-start.69 = (f32[88,384]{1,0:T(8,128)S(1)}, f32[88,384]{1,0:T(8,128)S(1)}, u32[]{:S(2)}, u32[]{:S(2)}) collective-permute-start(f32[88,384]{1,0:T(8,128)S(1)} %get-tuple-element.326), channel_id=1, source_target_pairs={{0,16},{8,24},{16,0},{24,8},{1,17},{9,25},{17,1},{25,9},{2,18},{10... | collective-permute-start | bytes 405512 | tf_op jit(solution)/shard_map/ppermute | solution.py:56
  743.5 15.9 %collective-permute-start.68 = (f32[88,384]{1,0:T(8,128)S(1)}, f32[88,384]{1,0:T(8,128)S(1)}, u32[]{:S(2)}, u32[]{:S(2)}) collective-permute-start(f32[88,384]{1,0:T(8,128)S(1)} %get-tuple-element.327), channel_id=1, source_target_pairs={{0,8},{8,16},{16,24},{24,0},{1,9},{9,17},{17,25},{25,1},{2,10},{10... | collective-permute-start | bytes 405512 | tf_op jit(solution)/shard_map/ppermute | solution.py:56
  745.6 13.8 %collective-permute-start.67 = (f32[48,1152]{1,0:T(8,128)S(1)}, f32[48,1152]{1,0:T(8,128)S(1)}, u32[]{:S(2)}, u32[]{:S(2)}) collective-permute-start(f32[48,1152]{1,0:T(8,128)S(1)} %get-tuple-element.317), channel_id=1, source_target_pairs={{0,24},{8,0},{16,8},{24,16},{1,25},{9,1},{17,9},{25,17},{2,26},{10... | collective-permute-start | bytes 663560 | tf_op jit(solution)/shard_map/ppermute | solution.py:56
  747.5 24.4 %collective-permute-start.66 = (f32[48,1152]{1,0:T(8,128)S(1)}, f32[48,1152]{1,0:T(8,128)S(1)}, u32[]{:S(2)}, u32[]{:S(2)}) collective-permute-start(f32[48,1152]{1,0:T(8,128)S(1)} %get-tuple-element.318), channel_id=1, source_target_pairs={{0,16},{8,24},{16,0},{24,8},{1,17},{9,25},{17,1},{25,9},{2,18},{10... | collective-permute-start | bytes 663560 | tf_op jit(solution)/shard_map/ppermute | solution.py:56
  747.5 25.1 %collective-permute-start.65 = (f32[48,1152]{1,0:T(8,128)S(1)}, f32[48,1152]{1,0:T(8,128)}, u32[]{:S(2)}, u32[]{:S(2)}) collective-permute-start(f32[48,1152]{1,0:T(8,128)S(1)} %get-tuple-element.319), channel_id=1, source_target_pairs={{0,8},{8,16},{16,24},{24,0},{1,9},{9,17},{17,25},{25,1},{2,10},{10... | collective-permute-start | bytes 663560 | tf_op jit(solution)/shard_map/ppermute | solution.py:56
  783.2 41.3 %all-to-all-start.4 = ((f32[32,96,128]{2,1,0:T(8,128)}), f32[32,96,128]{2,1,0:T(8,128)}, u32[]{:S(2)}, u32[]{:S(2)}) async-start(f32[32,96,128]{2,1,0:T(8,128)} %bitcast.437), calls=%async_computation.5 | async-start | bytes 3145728 | tf_op jit(solution)/shard_map/all_to_all | solution.py:899
  (171 other events, 1396.8 us)
Sparse Core Ops, SparseCore 0:
  10.9 163.3 all-gather.4
  177.9 111.1 all-gather.8
  496.8 103.3 reduce-scatter.1
  691.6 55.9 all-gather.6

commit v8 on v7

--- a/solution.py
+++ b/solution.py
@@ -61,6 +61,14 @@
     for bit in (ACROSS, DEEP, CORE):
         value = jnp.concatenate([value, swap(value, bit)])
     return value
+
+
+def gather_split(value):
+    half = value.shape[0] // 2
+    across, deep = swap(value, ACROSS), swap(value, DEEP)
+    diagonal = [swap(across[:half], DEEP), swap(deep[half:], ACROSS)]
+    plane = jnp.concatenate([value, across, deep, *diagonal])
+    return jnp.concatenate([plane, swap(plane, CORE)])
 
 
 def plane_hop(value):
@@ -488,6 +496,7 @@
         grad_context,
         preferred_element_type=jnp.float32,
     )
+    grad_values, grad_probs = flow.advance(grad_values, grad_probs)
     grad_scores = probabilities * (
         grad_probs - jnp.sum(grad_probs * probabilities, axis=-1, keepdims=True)
     )
@@ -503,6 +512,9 @@
         .reshape(rows_here, 3 * D)
         .astype(jnp.bfloat16)
     )
+    if flow.near:
+        grad_proj, head_part = together(grad_proj, head_part)
+    flow.add_product(saved["inputs"], grad_proj)
     grad_bias_all = jnp.sum(grad_proj.astype(jnp.float32), axis=0)
     grad_first = grad_sum_one + trailing_array_multiply(grad_proj, pieces["qkv"])
     grad_embedded, grad_gain_zero, grad_shift_zero = norm_backward(
@@ -527,8 +539,7 @@
             jnp.zeros((tail_rows - 84, TILE), jnp.float32),
         ]
     )
-    grad_embedded, head_part = flow.advance(grad_embedded, head_part)
-    flow.add_product(saved["inputs"], grad_proj)
+    (grad_embedded,) = flow.advance(grad_embedded)
     flow.add_rest(grad_outw, grad_place, tail)
     return grad_embedded, head_part
 
@@ -591,6 +602,8 @@
 
 
 class Flow:
+    near = True
+
     def __init__(self):
         self.lines, self.waiting, self.sums = [], [], []
 
@@ -629,6 +642,8 @@
 
 
 class PlainFlow:
+    near = False
+
     def __init__(self, devices):
         self.devices, self.sums = devices, []
 
@@ -750,7 +765,9 @@
         far = rows_s(plane_facts[4:, :LEN], table_low).reshape(shape)
         looked_t, far = together(plane_end(*looked_t).astype(jnp.float32), far)
         close = rows_s(plane_facts[:4, :LEN], table_low).reshape(shape)
-        looked_s, teacher_tiles = together(close + swap(far, CORE), teacher_tiles)
+        other_facts = gather_near(jnp.stack([shift(facts, 1), shift(facts, 2), shift(facts, 3)]))
+        all_facts = jnp.concatenate([plane_facts[:, None], other_facts], axis=1)
+        looked_s, teacher_tiles, all_facts = together(close + swap(far, CORE), teacher_tiles, all_facts)
         teacher = teacher_pieces(teacher_tiles)
         teacher, looked_s = together(teacher, plane_hop(looked_s))
         middle, _ = attention_forward(teacher, looked_t, lengths)
@@ -758,9 +775,6 @@
         final_t = feed_forward(teacher, middle, {})[0]
         final_t, layer = together(final_t, layer)
         matrices = assemble_layer(layer)
-        matrices, facts = together(matrices, facts)
-        other_facts = gather_near(jnp.stack([shift(facts, 1), shift(facts, 2), shift(facts, 3)]))
-        all_facts = jnp.concatenate([plane_facts[:, None], other_facts], axis=1)
     else:
         table_low = lax.all_gather(columns_low, "dp", axis=0, tiled=True)
         by_plane = lax.all_gather(facts, "dp", axis=0)
@@ -784,15 +798,14 @@
     up, down, qkv, out, place = matrices[:5]
     student = pieces_of((qkv, out, up, down, place), matrices[5].reshape(-1, TILE))
     middle, saved = attention_forward(student, looked_s, lengths)
-    final_s, saved = feed_forward(student, middle, saved)
-
     offsets = jnp.concatenate([mask_pos.reshape(CAP), jnp.zeros((SLOTS - CAP,), jnp.int32)])
     picked_t = final_t[offsets].astype(jnp.bfloat16)
     if near:
-        mentor_picked = gather_near(picked_t).reshape(-1, D)
-        final_s, mentor_picked, all_facts = together(final_s, mentor_picked, all_facts)
+        middle, mentor_picked = together(middle, gather_near(picked_t).reshape(-1, D))
     else:
         mentor_picked = lax.all_gather(picked_t, "vocab", axis=0, tiled=True)
+    final_s, saved = feed_forward(student, middle, saved)
+
     token_total = jnp.sum(all_facts[:, :, LEN]).astype(jnp.float32)
     masked_total = jnp.sum(all_facts[:, :, LEN + 1]).astype(jnp.float32)
     teacher_logit = (
@@ -801,7 +814,7 @@
     peak_t = jnp.max(teacher_logit, axis=1)
     picked_s = final_s[offsets].astype(jnp.bfloat16)
     if near:
-        learner_picked = gather_near(picked_s).reshape(-1, D)
+        learner_picked = gather_split(picked_s).reshape(-1, D)
         learner_picked, teacher_logit, peak_t = together(learner_picked, teacher_logit, peak_t)
     else:
         learner_picked = lax.all_gather(picked_s, "vocab", axis=0, tiled=True)
@@ -889,7 +902,7 @@
     token_grads = lax.all_gather(shares.reshape(-1, width_share), "vocab", axis=0, tiled=True)
     flow.advance()
     flow.advance()
-    (token_grads,) = flow.advance(token_grads)
+    flow.advance()
     sum_down, sum_up, sum_qkv, sum_rest = flow.sums
     if near:
         home_grads = share_lines(sum_up, sum_down, sum_qkv, sum_rest, per, starts)

time: 879 us -> 856 us (0.974)
  starting transfers between devices: 111 us -> 90.5 us
  waiting for transfers between devices: 221 us -> 238 us
  matrix products: 250 us -> 234 us
    ppermute x21, waiting for transfers between devices: 57.8 us -> 88.5 us  [shift(): lax.ppermute(value, 'dp', [(i, (i + steps) % size) for i in range(size)])]
    ppermute x21, starting transfers between devices: 52.9 us -> 29.1 us  [shift(): lax.ppermute(value, 'dp', [(i, (i + steps) % size) for i in range(size)])]
    sub x1 -> x0, matrix products: 18.8 us -> none  [attention_backward(): grad_probs - jnp.sum(grad_probs * probabilities, axis=-1, keepdims=True)]
    ppermute x53 -> x55, waiting for transfers between devices: 124 us -> 113 us  [swap(): return lax.ppermute(value, 'vocab', [(i, i ^ bit) for i in range(8)])]
    unnamed x277 -> x259, local copies, waits for them, and re-layouts: 19.8 us -> 16.9 us
    ppermute x53 -> x55, starting transfers between devices: 47.1 us -> 49.8 us  [swap(): return lax.ppermute(value, 'vocab', [(i, i ^ bit) for i in range(8)])]
  transfers between devices with their start and end apart: 83 -> 85, of which waited for: 42 -> 47; matrix products, arithmetic and copies ran while one was open for 43% -> 38% of each run, Pallas kernels for 4% -> 5%
where the time goes in v8:
time: 856 us; the launch traced here: 846 us
  waiting for transfers between devices  238 us (28%)
  matrix products  234 us (27%)
  other arithmetic  126 us (15%)
  starting transfers between devices  90.5 us (11%)
  local copies, waits for them, and re-layouts  77.7 us (9%)
  Pallas kernels  54.2 us (6%)
  between operations  25.4 us (3%)
    ppermute x55, waiting for transfers between devices, swap(): return lax.ppermute(value, 'vocab', [(i, i ^ bit) for i in range(8)])  113 us
    ppermute x21, waiting for transfers between devices, shift(): lax.ppermute(value, 'dp', [(i, (i + steps) % size) for i in range(size)])  88.5 us
    dot_general x11, matrix products, array_multiply(): return jnp.dot(left_side, right_side, preferred_element_type=jnp.float32)  77.7 us
    dot_general x9, matrix products, matmul_left(): lax.dot_general(left_side, right_side, (((0,), (0,)), ((), ())), preferre...  70.3 us
    ppermute x55, starting transfers between devices, swap(): return lax.ppermute(value, 'vocab', [(i, i ^ bit) for i in range(8)])  49.8 us
    dot_general x9, matrix products, trailing_array_multiply(): lax.dot_general(left_side, right_side, (((1,), (1,)), ((), ())), preferre...  48 us
    ppermute x21, starting transfers between devices, shift(): lax.ppermute(value, 'dp', [(i, (i + steps) % size) for i in range(size)])  29.1 us
    pallas_call x5, Pallas kernels, unpack_matrix(): pl.pallas_call(functools.partial(unpack_kernel, across=across), grid=(hei...  21.2 us
  transfers between devices with their start and end apart: 85, of which 47 were waited for; matrix products, arithmetic and copies ran while one was open for 38% of the time, Pallas kernels for 5%

profile of v8, /device:TPU:0, one launch (start us, length us, event | category | flops | bytes accessed | tf_op | source)
XLA Modules:
  0.0 846.0 jit_solution(4797512000663458043)
XLA Ops:
  17.5 4.7 broadcast_divide_fusion
  28.0 7.2 send_tiles.1
  35.3 8.5 fusion.60
  55.2 4.7 all-to-all-done.3
  63.6 8.5 %fusion.62 = bf16[2048,768]{1,0:T(8,128)(2,1)} fusion(bf16[1920,768]{1,0:T(8,128)(2,1)S(1)} %copy-done, s32[2048]{0:T(1024)S(1)} %bitcast.513), kind=kOutput, calls=%fused_computation.120 | convolution fusion | flops 6045302784 | bytes 6103040 | tf_op jit(solution)/shard_map/dot_general | solution.py:331
  73.9 5.2 add.1074
  79.2 10.5 %collective-permute-done.5 = bf16[192,1920]{1,0:T(8,128)(2,1)} collective-permute-done((bf16[192,1920]{1,0:T(8,128)(2,1)}, bf16[192,1920]{1,0:T(8,128)(2,1)}, u32[]{:S(2)}, u32[]{:S(2)}) %collective-permute-start.5) | collective-permute-done | bytes 737312 | tf_op jit(solution)/shard_map/ppermute | solution.py:56
  89.7 15.8 %all-to-all-done.2 = bf16[32,96,128]{2,1,0:T(8,128)(2,1)} async-done(((bf16[32,96,128]{2,1,0:T(8,128)(2,1)}), bf16[32,96,128]{2,1,0:T(8,128)(2,1)}, u32[]{:S(2)}, u32[]{:S(2)}) %all-to-all-start.2) | async-done | bytes 786464 | tf_op jit(solution)/shard_map/all_to_all | solution.py:733
  115.3 4.7 land_tiles.3
  119.9 25.1 %collective-permute-done.6 = bf16[2,256,768]{2,1,0:T(8,128)(2,1)} collective-permute-done((bf16[2,256,768]{2,1,0:T(8,128)(2,1)}, bf16[2,256,768]{2,1,0:T(8,128)(2,1)}, u32[]{:S(2)}, u32[]{:S(2)}) %collective-permute-start.6) | collective-permute-done | bytes 786464 | tf_op jit(solution)/shard_map/ppermute | solution.py:51
  158.9 7.4 fusion.61
  185.0 7.3 fusion.63
  210.5 5.8 unpack_matrix.9
  216.3 6.2 unpack_matrix.5
  238.1 4.5 copy.105
  247.8 10.8 %fusion.286 = (f32[12,512]{1,0:T(8,128)S(1)}, f32[12,512,512]{1,2,0:T(8,128)}) fusion(pred[512]{0:T(512)(128)(4,1)S(1)} %iota_compare_fusion.27, bf16[1,512,3,12,64]{1,4,3,2,0:T(8,128)(2,1)} %bitcast.468), kind=kOutput, calls=%fused_computation.714 | convolution fusion | flops 415236608 | bytes 14180864 | tf_op jit(solution)/shard_map/sub | solution.py:409
  258.7 6.3 fusion.82
  271.4 23.3 %fusion.288 = (f32[512]{0:T(512)S(1)}, f32[512,768]{1,0:T(8,128)}) fusion(f32[512,768]{1,0:T(8,128)} %multiply_add_fusion.4, f32[768]{0:T(1024)S(1)} %get-tuple-element.246, bf16[3072,768]{1,0:T(8,128)(2,1)} %unpack_matrix.5, bf16[768,3072]{1,0:T(8,128)(2,1)} %unpack_matrix.9, f32[3072]{0:T(1024)S(1)} %slice_bitcast_fusion.42), kind=kOutput, calls=%fused_computation.716 | convolution fusion | flops 4937219584 | bytes 12600320 | tf_op jit(solution)/shard_map/dot_general | solution.py:331
  300.1 12.3 %assemble_layer.1 = (bf16[768,3072]{1,0:T(8,128)(2,1)}, bf16[3072,768]{1,0:T(8,128)(2,1)}, bf16[768,2304]{1,0:T(8,128)(2,1)}, bf16[768,768]{1,0:T(8,128)(2,1)}, ...) custom-call(bf16[32,160,1536]{2,1,0:T(8,128)(2,1)} %bitcast.430), custom_call_target="tpu_custom_call" | custom-call | bytes 60000000 | tf_op jit(solution)/shard_map/assemble_layer/pallas_call | solution.py:285
  320.0 6.0 fusion.59
  344.8 9.0 %collective-permute-done.23 = bf16[2,128,768]{2,1,0:T(8,128)(2,1)S(1)} collective-permute-done((bf16[2,128,768]{2,1,0:T(8,128)(2,1)S(1)}, bf16[2,128,768]{2,1,0:T(8,128)(2,1)S(1)}, u32[]{:S(2)}, u32[]{:S(2)}) %collective-permute-start.23) | collective-permute-done | bytes 393248 | tf_op jit(solution)/shard_map/ppermute | solution.py:51
  357.6 18.0 %fusion.25 = (bf16[512,3072]{1,0:T(8,128)(2,1)S(1)}, f32[512,3072]{1,0:T(8,128)}) fusion(f32[3072]{0:T(1024)S(1)} %slice_bitcast_fusion.41, bf16[768,3072]{1,0:T(8,128)(2,1)S(1)} %bitcast.519, f32[512,768]{1,0:T(8,128)S(1)} %multiply_add_fusion.1), kind=kOutput, calls=%fused_computation.59 | convolution fusion | flops 2520121344 | bytes 15740928 | tf_op jit(solution)/shard_map/dot_general | solution.py:331
  386.6 5.1 collective-permute-done.26
  419.3 7.2 multiply_convert_fusion
  442.2 5.3 fusion.298
  447.5 4.5 collective-permute-done.34
  467.2 7.8 convert_reduce_fusion.1
  478.6 5.9 fusion.117
  487.3 7.5 multiply_reduce_fusion.3
  499.0 6.2 convolution_add_fusion.4
  505.2 6.5 convolution_add_fusion.2
  528.3 6.6 convolution_bitcast_fusion
  542.4 7.2 collective-permute-done.43
  554.4 6.7 fusion.10
  561.1 6.9 fusion.11
  576.4 4.5 collective-permute-done.44
  589.9 6.9 multiply_reduce_fusion.4
  597.7 4.7 fusion.94
  624.8 5.3 convolution_add_fusion.3
  630.1 10.4 %collective-permute-done.49 = f32[192,384]{1,0:T(8,128)S(1)} collective-permute-done((f32[192,384]{1,0:T(8,128)S(1)}, f32[192,384]{1,0:T(8,128)S(1)}, u32[]{:S(2)}, u32[]{:S(2)}) %collective-permute-start.49) | collective-permute-done | bytes 294944 | tf_op jit(solution)/shard_map/ppermute | solution.py:56
  640.5 23.7 %collective-permute-done.52 = f32[48,1536]{1,0:T(8,128)S(1)} collective-permute-done((f32[48,1536]{1,0:T(8,128)S(1)}, f32[48,1536]{1,0:T(8,128)S(1)}, u32[]{:S(2)}, u32[]{:S(2)}) %collective-permute-start.52) | collective-permute-done | bytes 294944 | tf_op jit(solution)/shard_map/ppermute | solution.py:56
  675.5 13.8 %collective-permute-done.59 = bf16[512,192]{0,1:T(8,128)(2,1)S(1)} collective-permute-done((bf16[512,192]{0,1:T(8,128)(2,1)S(1)}, bf16[512,192]{0,1:T(8,128)(2,1)S(1)}, u32[]{:S(2)}, u32[]{:S(2)}) %collective-permute-start.59) | collective-permute-done | bytes 196640 | tf_op jit(solution)/shard_map/ppermute | solution.py:56
  704.4 7.5 collective-permute-done.62
  714.4 5.1 collective-permute-done.64
  729.0 13.9 %collective-permute-done.66 = f32[48,1152]{1,0:T(8,128)S(1)} collective-permute-done((f32[48,1152]{1,0:T(8,128)S(1)}, f32[48,1152]{1,0:T(8,128)S(1)}, u32[]{:S(2)}, u32[]{:S(2)}) %collective-permute-start.66) | collective-permute-done | bytes 221216 | tf_op jit(solution)/shard_map/ppermute | solution.py:56
  748.8 7.4 collective-permute-done.71
  758.2 4.7 pick_tiles.2
  769.2 32.3 %fusion.3 = f32[192,1920]{1,0:T(8,128)} fusion(bf16[16384,192]{0,1:T(8,128)(2,1)} %all-gather.7.cloned.1.call-done, s32[16384]{0:T(1024)S(1)} %bitcast.496), kind=kOutput, calls=%fused_computation.15 | convolution fusion | flops 12111052800 | bytes 7831552 | tf_op jit(solution)/shard_map/dot_general | solution.py:335
  (694 shorter events, 385.4 us)
Async XLA Ops:
  7.2 187.8 %all-gather.5.cloned.1.call-start = ((), (), s32[]{:S(2)}) async-start(), calls=%async_computation.6 | async-start | bytes 15476736 | tf_op jit(solution)/shard_map/all_gather | solution.py:727
  10.7 12.2 %collective-permute-start = (s32[1,640]{1,0:T(1,128)S(1)}, s32[1,640]{1,0:T(1,128)S(1)}, u32[]{:S(2)}, u32[]{:S(2)}) collective-permute-start(s32[1,640]{1,0:T(1,128)S(1)} %broadcast_in_dim.63), channel_id=1, source_target_pairs={{0,2},{1,3},{2,0},{3,1},{4,6},{5,7},{6,4},{7,5},{8,10},{9,11},{10,... | collective-permute-start | bytes 7688 | tf_op jit(solution)/shard_map/ppermute | solution.py:51
  15.9 30.2 %collective-permute-start.3 = (bf16[192,1920]{1,0:T(8,128)(2,1)}, bf16[192,1920]{1,0:T(8,128)(2,1)}, u32[]{:S(2)}, u32[]{:S(2)}) collective-permute-start(bf16[192,1920]{1,0:T(8,128)(2,1)} %convert_bitcast_fusion.1), channel_id=1, source_target_pairs={{0,8},{8,16},{16,24},{24,0},{1,9},{9,17},{17,25},{25,1},{2,10},{10... | collective-permute-start | bytes 2211848 | tf_op jit(solution)/shard_map/ppermute | solution.py:56
  46.1 27.8 %collective-permute-start.4 = (bf16[2,2,512,768]{3,2,1,0:T(8,128)(2,1)}, bf16[2,2,512,768]{3,2,1,0:T(8,128)(2,1)}, u32[]{:S(2)}, u32[]{:S(2)}) collective-permute-start(bf16[2,2,512,768]{3,2,1,0:T(8,128)(2,1)} %bitcast.3), channel_id=1, source_target_pairs={{0,1},{1,0},{2,3},{3,2},{4,5},{5,4},{6,7},{7,6},{8,9},{9,8},{10,11... | collective-permute-start | bytes 9437192 | tf_op jit(solution)/shard_map/ppermute | solution.py:51
  53.5 36.2 %collective-permute-start.5 = (bf16[192,1920]{1,0:T(8,128)(2,1)}, bf16[192,1920]{1,0:T(8,128)(2,1)}, u32[]{:S(2)}, u32[]{:S(2)}) collective-permute-start(bf16[192,1920]{1,0:T(8,128)(2,1)} %collective-permute-done.3), channel_id=1, source_target_pairs={{0,8},{8,16},{16,24},{24,0},{1,9},{9,17},{17,25},{25,1},{2,10},{10... | collective-permute-start | bytes 2211848 | tf_op jit(solution)/shard_map/ppermute | solution.py:56
  60.0 45.5 %all-to-all-start.2 = ((bf16[32,96,128]{2,1,0:T(8,128)(2,1)}), bf16[32,96,128]{2,1,0:T(8,128)(2,1)}, u32[]{:S(2)}, u32[]{:S(2)}) async-start(bf16[32,96,128]{2,1,0:T(8,128)(2,1)} %bitcast.474), calls=%async_computation.2 | async-start | bytes 1572864 | tf_op jit(solution)/shard_map/all_to_all | solution.py:733
  63.3 236.8 %all-gather.9.cloned.1.call-start = ((), (), s32[]{:S(2)}) async-start(), calls=%async_computation.9 | async-start | bytes 16220160 | tf_op jit(solution)/shard_map/all_gather | solution.py:760
  107.8 37.2 %collective-permute-start.6 = (bf16[2,256,768]{2,1,0:T(8,128)(2,1)}, bf16[2,256,768]{2,1,0:T(8,128)(2,1)}, u32[]{:S(2)}, u32[]{:S(2)}) collective-permute-start(bf16[2,256,768]{2,1,0:T(8,128)(2,1)} %slice_bitcast_fusion.12), channel_id=1, source_target_pairs={{0,2},{1,3},{2,0},{3,1},{4,6},{5,7},{6,4},{7,5},{8,10},{9,11},{10,... | collective-permute-start | bytes 2359304 | tf_op jit(solution)/shard_map/ppermute | solution.py:51
  111.3 37.1 %collective-permute-start.7 = (bf16[2,256,768]{2,1,0:T(8,128)(2,1)}, bf16[2,256,768]{2,1,0:T(8,128)(2,1)}, u32[]{:S(2)}, u32[]{:S(2)}) collective-permute-start(bf16[2,256,768]{2,1,0:T(8,128)(2,1)} %slice_bitcast_fusion.11), channel_id=1, source_target_pairs={{0,4},{1,5},{2,6},{3,7},{4,0},{5,1},{6,2},{7,3},{8,12},{9,13},{10,... | collective-permute-start | bytes 2359304 | tf_op jit(solution)/shard_map/ppermute | solution.py:51
  112.8 38.0 %collective-permute-start.8 = (bf16[192,1920]{1,0:T(8,128)(2,1)}, bf16[192,1920]{1,0:T(8,128)(2,1)}, u32[]{:S(2)}, u32[]{:S(2)}) collective-permute-start(bf16[192,1920]{1,0:T(8,128)(2,1)} %collective-permute-done.5), channel_id=1, source_target_pairs={{0,8},{8,16},{16,24},{24,0},{1,9},{9,17},{17,25},{25,1},{2,10},{10... | collective-permute-start | bytes 2211848 | tf_op jit(solution)/shard_map/ppermute | solution.py:56
  151.2 438.7 %reduce-scatter.2.cloned.1.call-start = ((), (), s32[]{:S(2)}) async-start(), calls=%async_computation.7 | async-start | bytes 7372800 | tf_op jit(solution)/shard_map/reduce_scatter | solution.py:871
  167.8 24.5 %collective-permute-start.11 = (bf16[2,2,512,768]{3,2,1,0:T(8,128)(2,1)S(1)}, bf16[2,2,512,768]{3,2,1,0:T(8,128)(2,1)S(1)}, u32[]{:S(2)}, u32[]{:S(2)}) collective-permute-start(bf16[2,2,512,768]{3,2,1,0:T(8,128)(2,1)S(1)} %bitcast.522), channel_id=1, source_target_pairs={{0,1},{1,0},{2,3},{3,2},{4,5},{5,4},{6,7},{7,6},{8,9},{9,8},{10,11... | collective-permute-start | bytes 9437192 | tf_op jit(solution)/shard_map/ppermute | solution.py:51
  197.0 30.5 %collective-permute-start.18 = (bf16[2,256,768]{2,1,0:T(8,128)(2,1)}, bf16[2,256,768]{2,1,0:T(8,128)(2,1)}, u32[]{:S(2)}, u32[]{:S(2)}) collective-permute-start(bf16[2,256,768]{2,1,0:T(8,128)(2,1)} %slice_bitcast_fusion.10), channel_id=1, source_target_pairs={{0,2},{1,3},{2,0},{3,1},{4,6},{5,7},{6,4},{7,5},{8,10},{9,11},{10,... | collective-permute-start | bytes 2359304 | tf_op jit(solution)/shard_map/ppermute | solution.py:51
  200.3 29.6 %collective-permute-start.19 = (bf16[2,256,768]{2,1,0:T(8,128)(2,1)}, bf16[2,256,768]{2,1,0:T(8,128)(2,1)}, u32[]{:S(2)}, u32[]{:S(2)}) collective-permute-start(bf16[2,256,768]{2,1,0:T(8,128)(2,1)} %slice_bitcast_fusion.9), channel_id=1, source_target_pairs={{0,4},{1,5},{2,6},{3,7},{4,0},{5,1},{6,2},{7,3},{8,12},{9,13},{10,... | collective-permute-start | bytes 2359304 | tf_op jit(solution)/shard_map/ppermute | solution.py:51
  244.3 23.7 %collective-permute-start.21 = (bf16[256,768]{1,0:T(8,128)(2,1)}, bf16[256,768]{1,0:T(8,128)(2,1)}, u32[]{:S(2)}, u32[]{:S(2)}) collective-permute-start(bf16[256,768]{1,0:T(8,128)(2,1)} %slice_bitcast_fusion.33), channel_id=1, source_target_pairs={{0,2},{1,3},{2,0},{3,1},{4,6},{5,7},{6,4},{7,5},{8,10},{9,11},{10,... | collective-permute-start | bytes 1179656 | tf_op jit(solution)/shard_map/ppermute | solution.py:51
  247.4 21.6 %collective-permute-start.20 = (bf16[256,768]{1,0:T(8,128)(2,1)S(1)}, bf16[256,768]{1,0:T(8,128)(2,1)}, u32[]{:S(2)}, u32[]{:S(2)}) collective-permute-start(bf16[256,768]{1,0:T(8,128)(2,1)S(1)} %slice_bitcast_fusion.34), channel_id=1, source_target_pairs={{0,4},{1,5},{2,6},{3,7},{4,0},{5,1},{6,2},{7,3},{8,12},{9,13},{10,... | collective-permute-start | bytes 1179656 | tf_op jit(solution)/shard_map/ppermute | solution.py:51
  319.1 23.6 %collective-permute-start.22 = (bf16[1,128,768]{2,1,0:T(8,128)(2,1)S(1)}, bf16[1,128,768]{2,1,0:T(8,128)(2,1)S(1)}, u32[]{:S(2)}, u32[]{:S(2)}) collective-permute-start(bf16[1,128,768]{2,1,0:T(8,128)(2,1)S(1)} %bitcast.462), channel_id=1, source_target_pairs={{0,2},{1,3},{2,0},{3,1},{4,6},{5,7},{6,4},{7,5},{8,10},{9,11},{10,... | collective-permute-start | bytes 589832 | tf_op jit(solution)/shard_map/ppermute | solution.py:51
  440.5 11.6 %collective-permute-start.34 = (f32[2,64,768]{2,1,0:T(8,128)S(1)}, f32[2,64,768]{2,1,0:T(8,128)S(1)}, u32[]{:S(2)}, u32[]{:S(2)}) collective-permute-start(f32[2,64,768]{2,1,0:T(8,128)S(1)} %slice_bitcast_fusion.31), channel_id=1, source_target_pairs={{0,2},{1,3},{2,0},{3,1},{4,6},{5,7},{6,4},{7,5},{8,10},{9,11},{10,... | collective-permute-start | bytes 1179656 | tf_op jit(solution)/shard_map/ppermute | solution.py:51
  441.4 11.2 %collective-permute-start.36 = (f32[2,64,768]{2,1,0:T(8,128)S(1)}, f32[2,64,768]{2,1,0:T(8,128)S(1)}, u32[]{:S(2)}, u32[]{:S(2)}) collective-permute-start(f32[2,64,768]{2,1,0:T(8,128)S(1)} %slice_bitcast_fusion.29), channel_id=1, source_target_pairs={{0,4},{1,5},{2,6},{3,7},{4,0},{5,1},{6,2},{7,3},{8,12},{9,13},{10,... | collective-permute-start | bytes 1179656 | tf_op jit(solution)/shard_map/ppermute | solution.py:51
  478.5 18.5 %collective-permute-start.39 = (f32[768,1536]{1,0:T(8,128)}, f32[768,1536]{1,0:T(8,128)}, u32[]{:S(2)}, u32[]{:S(2)}) collective-permute-start(f32[768,1536]{1,0:T(8,128)} %fusion.70), channel_id=1, source_target_pairs={{0,1},{1,0},{2,3},{3,2},{4,5},{5,4},{6,7},{7,6},{8,9},{9,8},{10,11... | collective-permute-start | bytes 14155784 | tf_op jit(solution)/shard_map/ppermute | solution.py:51
  484.4 20.8 %collective-permute-start.38 = (f32[3072,384]{1,0:T(8,128)}, f32[3072,384]{1,0:T(8,128)}, u32[]{:S(2)}, u32[]{:S(2)}) collective-permute-start(f32[3072,384]{1,0:T(8,128)} %fusion.117), channel_id=1, source_target_pairs={{0,1},{1,0},{2,3},{3,2},{4,5},{5,4},{6,7},{7,6},{8,9},{9,8},{10,11... | collective-permute-start | bytes 14155784 | tf_op jit(solution)/shard_map/ppermute | solution.py:51
  485.6 283.5 %all-gather.7.cloned.1.call-start = ((), (), s32[]{:S(2)}) async-start(), calls=%async_computation.8 | async-start | bytes 7077888 | tf_op jit(solution)/shard_map/all_gather | solution.py:902
  517.4 22.6 %collective-permute-start.41 = (bf16[2,2,192,384]{3,2,0,1:T(8,128)(2,1)}, bf16[2,2,192,384]{3,2,0,1:T(8,128)(2,1)}, u32[]{:S(2)}, u32[]{:S(2)}) collective-permute-start(bf16[2,2,192,384]{3,2,0,1:T(8,128)(2,1)} %fusion.110), channel_id=1, source_target_pairs={{0,4},{1,5},{2,6},{3,7},{4,0},{5,1},{6,2},{7,3},{8,12},{9,13},{10,... | collective-permute-start | bytes 1769480 | tf_op jit(solution)/shard_map/ppermute | solution.py:51
  518.1 23.2 %collective-permute-start.40 = (bf16[2,2,192,384]{3,2,0,1:T(8,128)(2,1)S(1)}, bf16[2,2,192,384]{3,2,0,1:T(8,128)(2,1)}, u32[]{:S(2)}, u32[]{:S(2)}) collective-permute-start(bf16[2,2,192,384]{3,2,0,1:T(8,128)(2,1)S(1)} %fusion.109), channel_id=1, source_target_pairs={{0,2},{1,3},{2,0},{3,1},{4,6},{5,7},{6,4},{7,5},{8,10},{9,11},{10,... | collective-permute-start | bytes 1769480 | tf_op jit(solution)/shard_map/ppermute | solution.py:51
  534.9 14.7 %collective-permute-start.43 = (bf16[2,2,48,1536]{3,2,0,1:T(8,128)(2,1)S(1)}, bf16[2,2,48,1536]{3,2,0,1:T(8,128)(2,1)S(1)}, u32[]{:S(2)}, u32[]{:S(2)}) collective-permute-start(bf16[2,2,48,1536]{3,2,0,1:T(8,128)(2,1)S(1)} %copy-done.66), channel_id=1, source_target_pairs={{0,4},{1,5},{2,6},{3,7},{4,0},{5,1},{6,2},{7,3},{8,12},{9,13},{10,... | collective-permute-start | bytes 1769480 | tf_op jit(solution)/shard_map/ppermute | solution.py:51
  538.5 14.4 %collective-permute-start.42 = (bf16[2,2,48,1536]{3,2,0,1:T(8,128)(2,1)S(1)}, bf16[2,2,48,1536]{3,2,0,1:T(8,128)(2,1)S(1)}, u32[]{:S(2)}, u32[]{:S(2)}) collective-permute-start(bf16[2,2,48,1536]{3,2,0,1:T(8,128)(2,1)S(1)} %fusion.111), channel_id=1, source_target_pairs={{0,2},{1,3},{2,0},{3,1},{4,6},{5,7},{6,4},{7,5},{8,10},{9,11},{10,... | collective-permute-start | bytes 1769480 | tf_op jit(solution)/shard_map/ppermute | solution.py:51
  553.1 17.9 %collective-permute-start.47 = (bf16[2,48,1536]{2,1,0:T(8,128)(2,1)S(1)}, bf16[2,48,1536]{2,1,0:T(8,128)(2,1)S(1)}, u32[]{:S(2)}, u32[]{:S(2)}) collective-permute-start(bf16[2,48,1536]{2,1,0:T(8,128)(2,1)S(1)} %fusion.123), channel_id=1, source_target_pairs={{0,2},{1,3},{2,0},{3,1},{4,6},{5,7},{6,4},{7,5},{8,10},{9,11},{10,... | collective-permute-start | bytes 884744 | tf_op jit(solution)/shard_map/ppermute | solution.py:51
  568.0 13.8 %collective-permute-start.46 = (bf16[2,48,1536]{2,1,0:T(8,128)(2,1)S(1)}, bf16[2,48,1536]{2,1,0:T(8,128)(2,1)S(1)}, u32[]{:S(2)}, u32[]{:S(2)}) collective-permute-start(bf16[2,48,1536]{2,1,0:T(8,128)(2,1)S(1)} %fusion.122), channel_id=1, source_target_pairs={{0,4},{1,5},{2,6},{3,7},{4,0},{5,1},{6,2},{7,3},{8,12},{9,13},{10,... | collective-permute-start | bytes 884744 | tf_op jit(solution)/shard_map/ppermute | solution.py:51
  602.3 20.3 %collective-permute-start.54 = (f32[768,1152]{1,0:T(8,128)}, f32[768,1152]{1,0:T(8,128)}, u32[]{:S(2)}, u32[]{:S(2)}) collective-permute-start(f32[768,1152]{1,0:T(8,128)} %fusion.94), channel_id=1, source_target_pairs={{0,1},{1,0},{2,3},{3,2},{4,5},{5,4},{6,7},{7,6},{8,9},{9,8},{10,11... | collective-permute-start | bytes 10616840 | tf_op jit(solution)/shard_map/ppermute | solution.py:51
  609.8 11.6 %collective-permute-start.50 = (f32[192,384]{1,0:T(8,128)S(1)}, f32[192,384]{1,0:T(8,128)S(1)}, u32[]{:S(2)}, u32[]{:S(2)}) collective-permute-start(f32[192,384]{1,0:T(8,128)S(1)} %get-tuple-element.302), channel_id=1, source_target_pairs={{0,24},{8,0},{16,8},{24,16},{1,25},{9,1},{17,9},{25,17},{2,26},{10... | collective-permute-start | bytes 884744 | tf_op jit(solution)/shard_map/ppermute | solution.py:56
  612.4 28.1 %collective-permute-start.49 = (f32[192,384]{1,0:T(8,128)S(1)}, f32[192,384]{1,0:T(8,128)S(1)}, u32[]{:S(2)}, u32[]{:S(2)}) collective-permute-start(f32[192,384]{1,0:T(8,128)S(1)} %get-tuple-element.303), channel_id=1, source_target_pairs={{0,16},{8,24},{16,0},{24,8},{1,17},{9,25},{17,1},{25,9},{2,18},{10... | collective-permute-start | bytes 884744 | tf_op jit(solution)/shard_map/ppermute | solution.py:56
  613.1 27.5 %collective-permute-start.48 = (f32[192,384]{1,0:T(8,128)S(1)}, f32[192,384]{1,0:T(8,128)S(1)}, u32[]{:S(2)}, u32[]{:S(2)}) collective-permute-start(f32[192,384]{1,0:T(8,128)S(1)} %get-tuple-element.304), channel_id=1, source_target_pairs={{0,8},{8,16},{16,24},{24,0},{1,9},{9,17},{17,25},{25,1},{2,10},{10... | collective-permute-start | bytes 884744 | tf_op jit(solution)/shard_map/ppermute | solution.py:56
  615.8 24.7 %collective-permute-start.53 = (f32[48,1536]{1,0:T(8,128)S(1)}, f32[48,1536]{1,0:T(8,128)S(1)}, u32[]{:S(2)}, u32[]{:S(2)}) collective-permute-start(f32[48,1536]{1,0:T(8,128)S(1)} %get-tuple-element.298), channel_id=1, source_target_pairs={{0,24},{8,0},{16,8},{24,16},{1,25},{9,1},{17,9},{25,17},{2,26},{10... | collective-permute-start | bytes 884744 | tf_op jit(solution)/shard_map/ppermute | solution.py:56
  621.4 42.8 %collective-permute-start.52 = (f32[48,1536]{1,0:T(8,128)S(1)}, f32[48,1536]{1,0:T(8,128)S(1)}, u32[]{:S(2)}, u32[]{:S(2)}) collective-permute-start(f32[48,1536]{1,0:T(8,128)S(1)} %get-tuple-element.299), channel_id=1, source_target_pairs={{0,16},{8,24},{16,0},{24,8},{1,17},{9,25},{17,1},{25,9},{2,18},{10... | collective-permute-start | bytes 884744 | tf_op jit(solution)/shard_map/ppermute | solution.py:56
  622.6 41.6 %collective-permute-start.51 = (f32[48,1536]{1,0:T(8,128)S(1)}, f32[48,1536]{1,0:T(8,128)S(1)}, u32[]{:S(2)}, u32[]{:S(2)}) collective-permute-start(f32[48,1536]{1,0:T(8,128)S(1)} %get-tuple-element.300), channel_id=1, source_target_pairs={{0,8},{8,16},{16,24},{24,0},{1,9},{9,17},{17,25},{25,1},{2,10},{10... | collective-permute-start | bytes 884744 | tf_op jit(solution)/shard_map/ppermute | solution.py:56
  667.7 21.7 %collective-permute-start.56 = (bf16[2,2,48,1152]{3,2,0,1:T(8,128)(2,1)S(1)}, bf16[2,2,48,1152]{3,2,0,1:T(8,128)(2,1)S(1)}, u32[]{:S(2)}, u32[]{:S(2)}) collective-permute-start(bf16[2,2,48,1152]{3,2,0,1:T(8,128)(2,1)S(1)} %fusion.114), channel_id=1, source_target_pairs={{0,4},{1,5},{2,6},{3,7},{4,0},{5,1},{6,2},{7,3},{8,12},{9,13},{10,... | collective-permute-start | bytes 1327112 | tf_op jit(solution)/shard_map/ppermute | solution.py:51
  669.4 19.9 %collective-permute-start.59 = (bf16[512,192]{0,1:T(8,128)(2,1)S(1)}, bf16[512,192]{0,1:T(8,128)(2,1)S(1)}, u32[]{:S(2)}, u32[]{:S(2)}) collective-permute-start(bf16[512,192]{0,1:T(8,128)(2,1)S(1)} %get-tuple-element.312), channel_id=1, source_target_pairs={{0,16},{8,24},{16,0},{24,8},{1,17},{9,25},{17,1},{25,9},{2,18},{10... | collective-permute-start | bytes 589832 | tf_op jit(solution)/shard_map/ppermute | solution.py:56
  671.9 17.4 %collective-permute-start.58 = (bf16[512,192]{0,1:T(8,128)(2,1)S(1)}, bf16[512,192]{0,1:T(8,128)(2,1)S(1)}, u32[]{:S(2)}, u32[]{:S(2)}) collective-permute-start(bf16[512,192]{0,1:T(8,128)(2,1)S(1)} %get-tuple-element.313), channel_id=1, source_target_pairs={{0,8},{8,16},{16,24},{24,0},{1,9},{9,17},{17,25},{25,1},{2,10},{10... | collective-permute-start | bytes 589832 | tf_op jit(solution)/shard_map/ppermute | solution.py:56
  673.9 16.5 %collective-permute-start.55 = (bf16[2,2,48,1152]{3,2,0,1:T(8,128)(2,1)S(1)}, bf16[2,2,48,1152]{3,2,0,1:T(8,128)(2,1)S(1)}, u32[]{:S(2)}, u32[]{:S(2)}) collective-permute-start(bf16[2,2,48,1152]{3,2,0,1:T(8,128)(2,1)S(1)} %fusion.113), channel_id=1, source_target_pairs={{0,2},{1,3},{2,0},{3,1},{4,6},{5,7},{6,4},{7,5},{8,10},{9,11},{10,... | collective-permute-start | bytes 1327112 | tf_op jit(solution)/shard_map/ppermute | solution.py:51
  698.8 13.1 %collective-permute-start.62 = (bf16[2,48,1152]{2,1,0:T(8,128)(2,1)S(1)}, bf16[2,48,1152]{2,1,0:T(8,128)(2,1)S(1)}, u32[]{:S(2)}, u32[]{:S(2)}) collective-permute-start(bf16[2,48,1152]{2,1,0:T(8,128)(2,1)S(1)} %fusion.197), channel_id=1, source_target_pairs={{0,2},{1,3},{2,0},{3,1},{4,6},{5,7},{6,4},{7,5},{8,10},{9,11},{10,... | collective-permute-start | bytes 663560 | tf_op jit(solution)/shard_map/ppermute | solution.py:51
  701.4 12.9 %collective-permute-start.61 = (bf16[2,48,1152]{2,1,0:T(8,128)(2,1)S(1)}, bf16[2,48,1152]{2,1,0:T(8,128)(2,1)S(1)}, u32[]{:S(2)}, u32[]{:S(2)}) collective-permute-start(bf16[2,48,1152]{2,1,0:T(8,128)(2,1)S(1)} %fusion.196), channel_id=1, source_target_pairs={{0,4},{1,5},{2,6},{3,7},{4,0},{5,1},{6,2},{7,3},{8,12},{9,13},{10,... | collective-permute-start | bytes 663560 | tf_op jit(solution)/shard_map/ppermute | solution.py:51
  702.2 17.3 %collective-permute-start.64 = (bf16[2,2,88,384]{3,2,0,1:T(8,128)(2,1)S(1)}, bf16[2,2,88,384]{3,2,0,1:T(8,128)(2,1)S(1)}, u32[]{:S(2)}, u32[]{:S(2)}) collective-permute-start(bf16[2,2,88,384]{3,2,0,1:T(8,128)(2,1)S(1)} %fusion.125), channel_id=1, source_target_pairs={{0,4},{1,5},{2,6},{3,7},{4,0},{5,1},{6,2},{7,3},{8,12},{9,13},{10,... | collective-permute-start | bytes 811016 | tf_op jit(solution)/shard_map/ppermute | solution.py:51
  703.8 15.8 %collective-permute-start.63 = (bf16[2,2,88,384]{3,2,0,1:T(8,128)(2,1)S(1)}, bf16[2,2,88,384]{3,2,0,1:T(8,128)(2,1)S(1)}, u32[]{:S(2)}, u32[]{:S(2)}) collective-permute-start(bf16[2,2,88,384]{3,2,0,1:T(8,128)(2,1)S(1)} %fusion.124), channel_id=1, source_target_pairs={{0,2},{1,3},{2,0},{3,1},{4,6},{5,7},{6,4},{7,5},{8,10},{9,11},{10,... | collective-permute-start | bytes 811016 | tf_op jit(solution)/shard_map/ppermute | solution.py:51
  722.0 20.8 %collective-permute-start.66 = (f32[48,1152]{1,0:T(8,128)S(1)}, f32[48,1152]{1,0:T(8,128)S(1)}, u32[]{:S(2)}, u32[]{:S(2)}) collective-permute-start(f32[48,1152]{1,0:T(8,128)S(1)} %get-tuple-element.307), channel_id=1, source_target_pairs={{0,16},{8,24},{16,0},{24,8},{1,17},{9,25},{17,1},{25,9},{2,18},{10... | collective-permute-start | bytes 663560 | tf_op jit(solution)/shard_map/ppermute | solution.py:56
  724.0 18.9 %collective-permute-start.65 = (f32[48,1152]{1,0:T(8,128)S(1)}, f32[48,1152]{1,0:T(8,128)S(1)}, u32[]{:S(2)}, u32[]{:S(2)}) collective-permute-start(f32[48,1152]{1,0:T(8,128)S(1)} %get-tuple-element.308), channel_id=1, source_target_pairs={{0,8},{8,16},{16,24},{24,0},{1,9},{9,17},{17,25},{25,1},{2,10},{10... | collective-permute-start | bytes 663560 | tf_op jit(solution)/shard_map/ppermute | solution.py:56
  743.0 13.2 %collective-permute-start.71 = (f32[88,384]{1,0:T(8,128)S(1)}, f32[88,384]{1,0:T(8,128)S(1)}, u32[]{:S(2)}, u32[]{:S(2)}) collective-permute-start(f32[88,384]{1,0:T(8,128)S(1)} %get-tuple-element.315), channel_id=1, source_target_pairs={{0,16},{8,24},{16,0},{24,8},{1,17},{9,25},{17,1},{25,9},{2,18},{10... | collective-permute-start | bytes 405512 | tf_op jit(solution)/shard_map/ppermute | solution.py:56
  743.8 12.5 %collective-permute-start.70 = (f32[88,384]{1,0:T(8,128)S(1)}, f32[88,384]{1,0:T(8,128)S(1)}, u32[]{:S(2)}, u32[]{:S(2)}) collective-permute-start(f32[88,384]{1,0:T(8,128)S(1)} %get-tuple-element.316), channel_id=1, source_target_pairs={{0,8},{8,16},{16,24},{24,0},{1,9},{9,17},{17,25},{25,1},{2,10},{10... | collective-permute-start | bytes 405512 | tf_op jit(solution)/shard_map/ppermute | solution.py:56
  762.9 41.3 %all-to-all-start.4 = ((f32[32,96,128]{2,1,0:T(8,128)}), f32[32,96,128]{2,1,0:T(8,128)}, u32[]{:S(2)}, u32[]{:S(2)}) async-start(f32[32,96,128]{2,1,0:T(8,128)} %bitcast.445), calls=%async_computation.5 | async-start | bytes 3145728 | tf_op jit(solution)/shard_map/all_to_all | solution.py:912
  (162 other events, 1290.2 us)
Sparse Core Ops, SparseCore 0:
  10.9 163.4 all-gather.4
  177.9 122.1 all-gather.8
  485.7 104.0 reduce-scatter.1
  692.6 51.9 all-gather.6

commit v9 on v8

--- a/solution.py
+++ b/solution.py
@@ -86,11 +86,13 @@
 
 
 def sum_everywhere(value):
-    for bit in (CORE, ACROSS, DEEP):
-        value = value + swap(value, bit)
-    for step in (1, 2):
-        value = value + lax.ppermute(value, "dp", [(i, i ^ step) for i in range(4)])
-    return value
+    value = value + swap(value, CORE)
+    across, deep, both = (swap(value, bits) for bits in (ACROSS, DEEP, ACROSS | DEEP))
+    value = (value + across) + (deep + both)
+    near, far, farthest = (
+        lax.ppermute(value, "dp", [(i, i ^ step) for i in range(4)]) for step in (1, 2, 3)
+    )
+    return (value + near) + (far + farthest)
 
 
 def upward(table):
@@ -457,10 +459,10 @@
         grad_final, saved["normed_two"], saved["inverse_two"], small_rows[8]
     )
     grad_out = grad_sum_two.astype(jnp.bfloat16)
-    flow.add_product(saved["activated"], grad_out)
+    flow.add_product(saved["activated"], grad_out, offload=True)
     grad_act = trailing_array_multiply(grad_out, pieces["down"])
     grad_hidden = (grad_act * gelu_slope(saved["hidden"])).astype(jnp.bfloat16)
-    flow.add_product(saved["middle_low"], grad_hidden)
+    flow.add_product(saved["middle_low"], grad_hidden, offload=True)
     grad_middle = grad_sum_two + trailing_array_multiply(grad_hidden, pieces["up"])
     grad_sum_one, grad_gain_one, grad_shift_one = norm_backward(
         grad_middle, saved["normed_one"], saved["inverse_one"], small_rows[6]
@@ -500,7 +502,7 @@
     grad_scores = probabilities * (
         grad_probs - jnp.sum(grad_probs * probabilities, axis=-1, keepdims=True)
     )
-    (grad_scores,) = flow.advance(grad_scores.astype(jnp.bfloat16))
+    grad_scores, head_part = flow.advance(grad_scores.astype(jnp.bfloat16), head_part)
     grad_queries = jnp.einsum(
         "shqk,skhd->sqhd", grad_scores, split_heads[:, :, 1], preferred_element_type=jnp.float32
     ) * HEAD_DIM ** (-0.5)
@@ -512,8 +514,6 @@
         .reshape(rows_here, 3 * D)
         .astype(jnp.bfloat16)
     )
-    if flow.near:
-        grad_proj, head_part = together(grad_proj, head_part)
     flow.add_product(saved["inputs"], grad_proj)
     grad_bias_all = jnp.sum(grad_proj.astype(jnp.float32), axis=0)
     grad_first = grad_sum_one + trailing_array_multiply(grad_proj, pieces["qkv"])
@@ -588,11 +588,16 @@
     return at(value, mine, axis) + sent_low(at(value, 1 - mine, axis), bit)
 
 
-def reduce_steps(near, far):
+def reduce_steps(near, far, offload):
     (chip,) = yield [near + swap(far, CORE)]
     chip = chip.reshape(4, 2, 2, chip.shape[0] // CHIPS, chip.shape[1])
     first, second = yield [halved(chip[:2], 2, ACROSS), halved(chip[2:], 1, DEEP)]
     first, second = yield [halved(first, 1, DEEP), halved(second, 1, ACROSS)]
+    if offload:
+        total = lax.psum_scatter(jnp.concatenate([first, second]), "dp", scatter_dimension=0, tiled=False)
+        yield []
+        (total,) = yield [total]
+        return total
     z = lax.axis_index("dp")
     blocks = [
         jnp.where((z + k) % 4 < 2, at(first, (z + k) % 2, 0), at(second, (z + k) % 2, 0)) for k in range(4)
@@ -607,17 +612,17 @@
     def __init__(self):
         self.lines, self.waiting, self.sums = [], [], []
 
-    def add(self, near, far):
-        self.lines.append(reduce_steps(near, far))
+    def add(self, near, far, offload=False):
+        self.lines.append(reduce_steps(near, far, offload))
         self.waiting.append(next(self.lines[-1]))
         self.sums.append(None)
 
-    def add_product(self, left, right):
+    def add_product(self, left, right, offload=False):
         width = right.shape[1] // 2
         core = bit_of(CORE)
         far = matmul_left(left, lax.dynamic_slice_in_dim(right, (1 - core) * width, width, 1))
         near = matmul_left(left, lax.dynamic_slice_in_dim(right, core * width, width, 1))
-        self.add(near, far)
+        self.add(near, far, offload)
 
     def add_rest(self, out, place, tail):
         def half(core):
@@ -647,7 +652,7 @@
     def __init__(self, devices):
         self.devices, self.sums = devices, []
 
-    def add_product(self, left, right):
+    def add_product(self, left, right, offload=False):
         parts = matmul_left(left, right).reshape(self.devices, -1, TILE)
         self.sums.append(lax.psum_scatter(parts, ("dp", "vocab"), scatter_dimension=0, tiled=False))
 
@@ -835,8 +840,12 @@
     )
     if near:
         stats = stats.reshape(5, 2, 2, 2, SLOTS)
-        for axis, bit in ((1, CORE), (2, DEEP), (3, ACROSS)):
-            stats = combine_stats(stats, jnp.flip(swap(stats, bit), axis))
+        stats = combine_stats(stats, jnp.flip(swap(stats, CORE), 1))
+        across, deep, both = (
+            jnp.flip(swap(stats, bits), axes)
+            for bits, axes in ((ACROSS, 3), (DEEP, 2), (ACROSS | DEEP, (2, 3)))
+        )
+        stats = combine_stats(combine_stats(stats, across), combine_stats(deep, both))
         stats = stats.reshape(5, -1)
     else:
         everything = lax.all_gather(stats, "vocab", axis=0)

time: 856 us -> 834 us (0.974)
  waiting for transfers between devices: 238 us -> 211 us
    ppermute x21 -> x15, waiting for transfers between devices: 88.5 us -> 68 us  [shift(): lax.ppermute(value, 'dp', [(i, (i + steps) % size) for i in range(size)])]
    ppermute x21 -> x15, starting transfers between devices: 29.1 us -> 20.4 us  [shift(): lax.ppermute(value, 'dp', [(i, (i + steps) % size) for i in range(size)])]
    ppermute x55 -> x57, waiting for transfers between devices: 113 us -> 111 us  [swap(): return lax.ppermute(value, 'vocab', [(i, i ^ bit) for i in range(8)])]
    ppermute x55 -> x57, starting transfers between devices: 49.8 us -> 51.2 us  [swap(): return lax.ppermute(value, 'vocab', [(i, i ^ bit) for i in range(8)])]
  transfers between devices with their start and end apart: 85 -> 84, of which waited for: 47 -> 46; matrix products, arithmetic and copies ran while one was open for 38% -> 40% of each run, Pallas kernels for 5% -> 5%
where the time goes in v9:
time: 834 us; the launch traced here: 824 us
  matrix products  236 us (28%)
  waiting for transfers between devices  211 us (25%)
  other arithmetic  129 us (15%)
  starting transfers between devices  87.6 us (11%)
  local copies, waits for them, and re-layouts  80.8 us (10%)
  Pallas kernels  54.2 us (6%)
  between operations  25.4 us (3%)
    ppermute x57, waiting for transfers between devices, swap(): return lax.ppermute(value, 'vocab', [(i, i ^ bit) for i in range(8)])  111 us
    dot_general x11, matrix products, array_multiply(): return jnp.dot(left_side, right_side, preferred_element_type=jnp.float32)  77.6 us
    ppermute x15, waiting for transfers between devices, shift(): lax.ppermute(value, 'dp', [(i, (i + steps) % size) for i in range(size)])  68 us
    dot_general x9, matrix products, matmul_left(): lax.dot_general(left_side, right_side, (((0,), (0,)), ((), ())), preferre...  67.3 us
    ppermute x57, starting transfers between devices, swap(): return lax.ppermute(value, 'vocab', [(i, i ^ bit) for i in range(8)])  51.2 us
    dot_general x9, matrix products, trailing_array_multiply(): lax.dot_general(left_side, right_side, (((1,), (1,)), ((), ())), preferre...  46 us
    pallas_call x5, Pallas kernels, unpack_matrix(): pl.pallas_call(functools.partial(unpack_kernel, across=across), grid=(hei...  21.3 us
    ppermute x15, starting transfers between devices, shift(): lax.ppermute(value, 'dp', [(i, (i + steps) % size) for i in range(size)])  20.4 us
  transfers between devices with their start and end apart: 84, of which 46 were waited for; matrix products, arithmetic and copies ran while one was open for 40% of the time, Pallas kernels for 5%

profile of v9, /device:TPU:0, one launch (start us, length us, event | category | flops | bytes accessed | tf_op | source)
XLA Modules:
  0.0 824.2 jit_solution(12031175556831520504)
XLA Ops:
  17.5 4.7 broadcast_divide_fusion
  28.0 7.2 send_tiles.1
  35.3 8.5 %fusion.60 = bf16[2048,768]{1,0:T(8,128)(2,1)} fusion(bf16[1920,768]{1,0:T(8,128)(2,1)S(1)} %copy-done, s32[2048]{0:T(1024)S(1)} %bitcast.500), kind=kOutput, calls=%fused_computation.119 | convolution fusion | flops 6045302784 | bytes 6103040 | tf_op jit(solution)/shard_map/dot_general | solution.py:333
  55.2 4.7 all-to-all-done.3
  63.7 8.5 %fusion.62 = bf16[2048,768]{1,0:T(8,128)(2,1)} fusion(bf16[1920,768]{1,0:T(8,128)(2,1)S(1)} %copy-done, s32[2048]{0:T(1024)S(1)} %bitcast.498), kind=kOutput, calls=%fused_computation.121 | convolution fusion | flops 6045302784 | bytes 6103040 | tf_op jit(solution)/shard_map/dot_general | solution.py:333
  74.0 5.2 add.1011
  79.2 10.4 %collective-permute-done.5 = bf16[192,1920]{1,0:T(8,128)(2,1)} collective-permute-done((bf16[192,1920]{1,0:T(8,128)(2,1)}, bf16[192,1920]{1,0:T(8,128)(2,1)}, u32[]{:S(2)}, u32[]{:S(2)}) %collective-permute-start.5) | collective-permute-done | bytes 737312 | tf_op jit(solution)/shard_map/ppermute | solution.py:56
  89.7 15.8 %all-to-all-done.2 = bf16[32,96,128]{2,1,0:T(8,128)(2,1)} async-done(((bf16[32,96,128]{2,1,0:T(8,128)(2,1)}), bf16[32,96,128]{2,1,0:T(8,128)(2,1)}, u32[]{:S(2)}, u32[]{:S(2)}) %all-to-all-start.2) | async-done | bytes 786464 | tf_op jit(solution)/shard_map/all_to_all | solution.py:738
  115.3 4.7 land_tiles.3
  119.9 25.1 %collective-permute-done.6 = bf16[2,256,768]{2,1,0:T(8,128)(2,1)} collective-permute-done((bf16[2,256,768]{2,1,0:T(8,128)(2,1)}, bf16[2,256,768]{2,1,0:T(8,128)(2,1)}, u32[]{:S(2)}, u32[]{:S(2)}) %collective-permute-start.6) | collective-permute-done | bytes 786464 | tf_op jit(solution)/shard_map/ppermute | solution.py:51
  159.1 7.4 fusion.61
  185.0 7.3 fusion.63
  210.7 5.8 unpack_matrix.9
  216.4 6.2 unpack_matrix.5
  238.0 4.5 copy.105
  248.1 10.8 %fusion.288 = (f32[12,512]{1,0:T(8,128)S(1)}, f32[12,512,512]{1,2,0:T(8,128)}) fusion(pred[512]{0:T(512)(128)(4,1)S(1)} %iota_compare_fusion.27, bf16[1,512,3,12,64]{1,4,3,2,0:T(8,128)(2,1)} %bitcast.449), kind=kOutput, calls=%fused_computation.705 | convolution fusion | flops 415236608 | bytes 14180864 | tf_op jit(solution)/shard_map/sub | solution.py:411
  258.9 6.3 fusion.82
  271.6 23.3 %fusion.290 = (f32[512]{0:T(512)S(1)}, f32[512,768]{1,0:T(8,128)}) fusion(f32[512,768]{1,0:T(8,128)} %multiply_add_fusion.4, f32[768]{0:T(1024)S(1)} %get-tuple-element.232, bf16[3072,768]{1,0:T(8,128)(2,1)} %unpack_matrix.5, bf16[768,3072]{1,0:T(8,128)(2,1)} %unpack_matrix.9, f32[3072]{0:T(1024)S(1)} %slice_bitcast_fusion.42), kind=kOutput, calls=%fused_computation.707 | convolution fusion | flops 4937219584 | bytes 12600320 | tf_op jit(solution)/shard_map/dot_general | solution.py:333
  300.2 12.3 %assemble_layer.1 = (bf16[768,3072]{1,0:T(8,128)(2,1)}, bf16[3072,768]{1,0:T(8,128)(2,1)}, bf16[768,2304]{1,0:T(8,128)(2,1)}, bf16[768,768]{1,0:T(8,128)(2,1)}, ...) custom-call(bf16[32,160,1536]{2,1,0:T(8,128)(2,1)} %bitcast.412), custom_call_target="tpu_custom_call" | custom-call | bytes 60000000 | tf_op jit(solution)/shard_map/assemble_layer/pallas_call | solution.py:287
  320.1 6.0 fusion.59
  345.0 8.9 %collective-permute-done.23 = bf16[2,128,768]{2,1,0:T(8,128)(2,1)S(1)} collective-permute-done((bf16[2,128,768]{2,1,0:T(8,128)(2,1)S(1)}, bf16[2,128,768]{2,1,0:T(8,128)(2,1)S(1)}, u32[]{:S(2)}, u32[]{:S(2)}) %collective-permute-start.23) | collective-permute-done | bytes 393248 | tf_op jit(solution)/shard_map/ppermute | solution.py:51
  357.7 18.0 %fusion.25 = (bf16[512,3072]{1,0:T(8,128)(2,1)S(1)}, f32[512,3072]{1,0:T(8,128)}) fusion(f32[3072]{0:T(1024)S(1)} %slice_bitcast_fusion.41, bf16[768,3072]{1,0:T(8,128)(2,1)S(1)} %bitcast.504, f32[512,768]{1,0:T(8,128)S(1)} %multiply_add_fusion.1), kind=kOutput, calls=%fused_computation.59 | convolution fusion | flops 2520121344 | bytes 15740928 | tf_op jit(solution)/shard_map/dot_general | solution.py:333
  386.7 5.1 collective-permute-done.26
  419.4 7.2 multiply_convert_fusion
  442.4 5.3 fusion.300
  447.8 4.4 collective-permute-done.35
  456.1 4.4 collective-permute-done.38
  467.3 7.8 convert_reduce_fusion.1
  478.7 5.9 fusion.111
  486.1 7.3 multiply_reduce_fusion.3
  498.9 6.1 convolution_add_fusion.4
  505.0 6.6 convolution_add_fusion.2
  528.5 6.6 convolution_bitcast_fusion
  542.2 7.6 collective-permute-done.44
  554.5 6.7 fusion.10
  561.2 9.7 %fusion.11 = bf16[1,12,512,512]{2,3,1,0:T(8,128)(2,1)} fusion(f32[1,12,512,512]{2,3,1,0:T(8,128)} %convolution_bitcast_fusion, f32[12,512,512]{1,2,0:T(8,128)S(1)} %bitcast.406, f32[12,512]{1,0:T(8,128)S(1)} %fusion.10, f32[12,512]{1,0:T(8,128)S(1)} %log_add_fusion), kind=kLoop, calls=%fused_computation.28 | loop fusion | flops 12582912 | bytes 31506432 | tf_op jit(solution)/shard_map/convert_element_type | solution.py:505
  578.6 5.6 collective-permute-done.45
  590.1 5.7 multiply_bitcast_fusion
  595.8 4.9 multiply_bitcast_fusion.1
  604.5 5.1 multiply_reduce_fusion.4
  645.7 5.6 collective-permute-done.55
  651.3 25.1 %collective-permute-done.54 = bf16[512,192]{0,1:T(8,128)(2,1)S(1)} collective-permute-done((bf16[512,192]{0,1:T(8,128)(2,1)S(1)}, bf16[512,192]{0,1:T(8,128)(2,1)S(1)}, u32[]{:S(2)}, u32[]{:S(2)}) %collective-permute-start.54) | collective-permute-done | bytes 196640 | tf_op jit(solution)/shard_map/ppermute | solution.py:56
  691.0 5.1 collective-permute-done.56
  696.2 10.1 %collective-permute-done.59 = bf16[2,2,88,384]{3,2,0,1:T(8,128)(2,1)S(1)} collective-permute-done((bf16[2,2,88,384]{3,2,0,1:T(8,128)(2,1)S(1)}, bf16[2,2,88,384]{3,2,0,1:T(8,128)(2,1)S(1)}, u32[]{:S(2)}, u32[]{:S(2)}) %collective-permute-start.59) | collective-permute-done | bytes 270368 | tf_op jit(solution)/shard_map/ppermute | solution.py:51
  716.0 9.6 %collective-permute-done.61 = f32[48,1152]{1,0:T(8,128)S(1)} collective-permute-done((f32[48,1152]{1,0:T(8,128)S(1)}, f32[48,1152]{1,0:T(8,128)S(1)}, u32[]{:S(2)}, u32[]{:S(2)}) %collective-permute-start.61) | collective-permute-done | bytes 221216 | tf_op jit(solution)/shard_map/ppermute | solution.py:56
  732.4 4.3 collective-permute-done.66
  738.7 4.7 pick_tiles.2
  750.3 32.3 %fusion.3 = f32[192,1920]{1,0:T(8,128)} fusion(bf16[16384,192]{0,1:T(8,128)(2,1)} %all-gather.7.cloned.1.call-done, s32[16384]{0:T(1024)S(1)} %bitcast.481), kind=kOutput, calls=%fused_computation.15 | convolution fusion | flops 12111052800 | bytes 7831552 | tf_op jit(solution)/shard_map/dot_general | solution.py:337
  (672 shorter events, 378.3 us)
Async XLA Ops:
  7.2 187.8 %all-gather.5.cloned.1.call-start = ((), (), s32[]{:S(2)}) async-start(), calls=%async_computation.8 | async-start | bytes 15476736 | tf_op jit(solution)/shard_map/all_gather | solution.py:732
  10.7 12.2 %collective-permute-start = (s32[1,640]{1,0:T(1,128)S(1)}, s32[1,640]{1,0:T(1,128)S(1)}, u32[]{:S(2)}, u32[]{:S(2)}) collective-permute-start(s32[1,640]{1,0:T(1,128)S(1)} %broadcast_in_dim.63), channel_id=1, source_target_pairs={{0,2},{1,3},{2,0},{3,1},{4,6},{5,7},{6,4},{7,5},{8,10},{9,11},{10,... | collective-permute-start | bytes 7688 | tf_op jit(solution)/shard_map/ppermute | solution.py:51
  15.9 30.2 %collective-permute-start.3 = (bf16[192,1920]{1,0:T(8,128)(2,1)}, bf16[192,1920]{1,0:T(8,128)(2,1)}, u32[]{:S(2)}, u32[]{:S(2)}) collective-permute-start(bf16[192,1920]{1,0:T(8,128)(2,1)} %convert_bitcast_fusion), channel_id=1, source_target_pairs={{0,8},{8,16},{16,24},{24,0},{1,9},{9,17},{17,25},{25,1},{2,10},{10... | collective-permute-start | bytes 2211848 | tf_op jit(solution)/shard_map/ppermute | solution.py:56
  46.1 27.9 %collective-permute-start.4 = (bf16[2,2,512,768]{3,2,1,0:T(8,128)(2,1)}, bf16[2,2,512,768]{3,2,1,0:T(8,128)(2,1)}, u32[]{:S(2)}, u32[]{:S(2)}) collective-permute-start(bf16[2,2,512,768]{3,2,1,0:T(8,128)(2,1)} %bitcast.3), channel_id=1, source_target_pairs={{0,1},{1,0},{2,3},{3,2},{4,5},{5,4},{6,7},{7,6},{8,9},{9,8},{10,11... | collective-permute-start | bytes 9437192 | tf_op jit(solution)/shard_map/ppermute | solution.py:51
  49.6 10.3 %all-to-all-start.3 = ((s32[32,1,96]{2,1,0:T(1,128)}), s32[32,1,96]{2,1,0:T(1,128)S(1)}, u32[]{:S(2)}, u32[]{:S(2)}) async-start(s32[32,1,96]{2,1,0:T(1,128)} %reshape.709), calls=%async_computation.3 | async-start | bytes 32768 | tf_op jit(solution)/shard_map/all_to_all | solution.py:739
  53.5 36.2 %collective-permute-start.5 = (bf16[192,1920]{1,0:T(8,128)(2,1)}, bf16[192,1920]{1,0:T(8,128)(2,1)}, u32[]{:S(2)}, u32[]{:S(2)}) collective-permute-start(bf16[192,1920]{1,0:T(8,128)(2,1)} %collective-permute-done.3), channel_id=1, source_target_pairs={{0,8},{8,16},{16,24},{24,0},{1,9},{9,17},{17,25},{25,1},{2,10},{10... | collective-permute-start | bytes 2211848 | tf_op jit(solution)/shard_map/ppermute | solution.py:56
  60.0 45.5 %all-to-all-start.2 = ((bf16[32,96,128]{2,1,0:T(8,128)(2,1)}), bf16[32,96,128]{2,1,0:T(8,128)(2,1)}, u32[]{:S(2)}, u32[]{:S(2)}) async-start(bf16[32,96,128]{2,1,0:T(8,128)(2,1)} %bitcast.455), calls=%async_computation.2 | async-start | bytes 1572864 | tf_op jit(solution)/shard_map/all_to_all | solution.py:738
  63.3 236.8 %all-gather.9.cloned.1.call-start = ((), (), s32[]{:S(2)}) async-start(), calls=%async_computation.13 | async-start | bytes 16220160 | tf_op jit(solution)/shard_map/all_gather | solution.py:765
  107.8 37.2 %collective-permute-start.6 = (bf16[2,256,768]{2,1,0:T(8,128)(2,1)}, bf16[2,256,768]{2,1,0:T(8,128)(2,1)}, u32[]{:S(2)}, u32[]{:S(2)}) collective-permute-start(bf16[2,256,768]{2,1,0:T(8,128)(2,1)} %slice_bitcast_fusion.12), channel_id=1, source_target_pairs={{0,2},{1,3},{2,0},{3,1},{4,6},{5,7},{6,4},{7,5},{8,10},{9,11},{10,... | collective-permute-start | bytes 2359304 | tf_op jit(solution)/shard_map/ppermute | solution.py:51
  111.3 37.1 %collective-permute-start.7 = (bf16[2,256,768]{2,1,0:T(8,128)(2,1)}, bf16[2,256,768]{2,1,0:T(8,128)(2,1)}, u32[]{:S(2)}, u32[]{:S(2)}) collective-permute-start(bf16[2,256,768]{2,1,0:T(8,128)(2,1)} %slice_bitcast_fusion.11), channel_id=1, source_target_pairs={{0,4},{1,5},{2,6},{3,7},{4,0},{5,1},{6,2},{7,3},{8,12},{9,13},{10,... | collective-permute-start | bytes 2359304 | tf_op jit(solution)/shard_map/ppermute | solution.py:51
  112.8 38.0 %collective-permute-start.8 = (bf16[192,1920]{1,0:T(8,128)(2,1)}, bf16[192,1920]{1,0:T(8,128)(2,1)}, u32[]{:S(2)}, u32[]{:S(2)}) collective-permute-start(bf16[192,1920]{1,0:T(8,128)(2,1)} %collective-permute-done.5), channel_id=1, source_target_pairs={{0,8},{8,16},{16,24},{24,0},{1,9},{9,17},{17,25},{25,1},{2,10},{10... | collective-permute-start | bytes 2211848 | tf_op jit(solution)/shard_map/ppermute | solution.py:56
  151.3 438.8 %reduce-scatter.4.cloned.1.call-start = ((), (), s32[]{:S(2)}) async-start(), calls=%async_computation.9 | async-start | bytes 7372800 | tf_op jit(solution)/shard_map/reduce_scatter | solution.py:880
  155.6 10.9 %collective-permute-start.10 = (bf16[256,768]{1,0:T(8,128)(2,1)S(1)}, bf16[256,768]{1,0:T(8,128)(2,1)S(1)}, u32[]{:S(2)}, u32[]{:S(2)}) collective-permute-start(bf16[256,768]{1,0:T(8,128)(2,1)S(1)} %slice_bitcast_fusion.35), channel_id=1, source_target_pairs={{0,2},{1,3},{2,0},{3,1},{4,6},{5,7},{6,4},{7,5},{8,10},{9,11},{10,... | collective-permute-start | bytes 1179656 | tf_op jit(solution)/shard_map/ppermute | solution.py:51
  156.2 10.4 %collective-permute-start.9 = (bf16[256,768]{1,0:T(8,128)(2,1)S(1)}, bf16[256,768]{1,0:T(8,128)(2,1)S(1)}, u32[]{:S(2)}, u32[]{:S(2)}) collective-permute-start(bf16[256,768]{1,0:T(8,128)(2,1)S(1)} %slice_bitcast_fusion.36), channel_id=1, source_target_pairs={{0,4},{1,5},{2,6},{3,7},{4,0},{5,1},{6,2},{7,3},{8,12},{9,13},{10,... | collective-permute-start | bytes 1179656 | tf_op jit(solution)/shard_map/ppermute | solution.py:51
  167.9 24.5 %collective-permute-start.11 = (bf16[2,2,512,768]{3,2,1,0:T(8,128)(2,1)S(1)}, bf16[2,2,512,768]{3,2,1,0:T(8,128)(2,1)S(1)}, u32[]{:S(2)}, u32[]{:S(2)}) collective-permute-start(bf16[2,2,512,768]{3,2,1,0:T(8,128)(2,1)S(1)} %bitcast.507), channel_id=1, source_target_pairs={{0,1},{1,0},{2,3},{3,2},{4,5},{5,4},{6,7},{7,6},{8,9},{9,8},{10,11... | collective-permute-start | bytes 9437192 | tf_op jit(solution)/shard_map/ppermute | solution.py:51
  197.0 30.4 %collective-permute-start.18 = (bf16[2,256,768]{2,1,0:T(8,128)(2,1)}, bf16[2,256,768]{2,1,0:T(8,128)(2,1)}, u32[]{:S(2)}, u32[]{:S(2)}) collective-permute-start(bf16[2,256,768]{2,1,0:T(8,128)(2,1)} %slice_bitcast_fusion.10), channel_id=1, source_target_pairs={{0,2},{1,3},{2,0},{3,1},{4,6},{5,7},{6,4},{7,5},{8,10},{9,11},{10,... | collective-permute-start | bytes 2359304 | tf_op jit(solution)/shard_map/ppermute | solution.py:51
  200.3 29.5 %collective-permute-start.19 = (bf16[2,256,768]{2,1,0:T(8,128)(2,1)}, bf16[2,256,768]{2,1,0:T(8,128)(2,1)}, u32[]{:S(2)}, u32[]{:S(2)}) collective-permute-start(bf16[2,256,768]{2,1,0:T(8,128)(2,1)} %slice_bitcast_fusion.9), channel_id=1, source_target_pairs={{0,4},{1,5},{2,6},{3,7},{4,0},{5,1},{6,2},{7,3},{8,12},{9,13},{10,... | collective-permute-start | bytes 2359304 | tf_op jit(solution)/shard_map/ppermute | solution.py:51
  244.3 23.9 %collective-permute-start.21 = (bf16[256,768]{1,0:T(8,128)(2,1)}, bf16[256,768]{1,0:T(8,128)(2,1)}, u32[]{:S(2)}, u32[]{:S(2)}) collective-permute-start(bf16[256,768]{1,0:T(8,128)(2,1)} %slice_bitcast_fusion.33), channel_id=1, source_target_pairs={{0,2},{1,3},{2,0},{3,1},{4,6},{5,7},{6,4},{7,5},{8,10},{9,11},{10,... | collective-permute-start | bytes 1179656 | tf_op jit(solution)/shard_map/ppermute | solution.py:51
  247.5 21.8 %collective-permute-start.20 = (bf16[256,768]{1,0:T(8,128)(2,1)S(1)}, bf16[256,768]{1,0:T(8,128)(2,1)}, u32[]{:S(2)}, u32[]{:S(2)}) collective-permute-start(bf16[256,768]{1,0:T(8,128)(2,1)S(1)} %slice_bitcast_fusion.34), channel_id=1, source_target_pairs={{0,4},{1,5},{2,6},{3,7},{4,0},{5,1},{6,2},{7,3},{8,12},{9,13},{10,... | collective-permute-start | bytes 1179656 | tf_op jit(solution)/shard_map/ppermute | solution.py:51
  319.2 23.6 %collective-permute-start.22 = (bf16[1,128,768]{2,1,0:T(8,128)(2,1)S(1)}, bf16[1,128,768]{2,1,0:T(8,128)(2,1)S(1)}, u32[]{:S(2)}, u32[]{:S(2)}) collective-permute-start(bf16[1,128,768]{2,1,0:T(8,128)(2,1)S(1)} %bitcast.443), channel_id=1, source_target_pairs={{0,2},{1,3},{2,0},{3,1},{4,6},{5,7},{6,4},{7,5},{8,10},{9,11},{10,... | collective-permute-start | bytes 589832 | tf_op jit(solution)/shard_map/ppermute | solution.py:51
  342.9 11.1 %collective-permute-start.23 = (bf16[2,128,768]{2,1,0:T(8,128)(2,1)S(1)}, bf16[2,128,768]{2,1,0:T(8,128)(2,1)S(1)}, u32[]{:S(2)}, u32[]{:S(2)}) collective-permute-start(bf16[2,128,768]{2,1,0:T(8,128)(2,1)S(1)} %pad_maximum_fusion.5), channel_id=1, source_target_pairs={{0,4},{1,5},{2,6},{3,7},{4,0},{5,1},{6,2},{7,3},{8,12},{9,13},{10,... | collective-permute-start | bytes 1179656 | tf_op jit(solution)/shard_map/ppermute | solution.py:51
  440.6 11.6 %collective-permute-start.35 = (f32[2,64,768]{2,1,0:T(8,128)S(1)}, f32[2,64,768]{2,1,0:T(8,128)S(1)}, u32[]{:S(2)}, u32[]{:S(2)}) collective-permute-start(f32[2,64,768]{2,1,0:T(8,128)S(1)} %slice_bitcast_fusion.31), channel_id=1, source_target_pairs={{0,2},{1,3},{2,0},{3,1},{4,6},{5,7},{6,4},{7,5},{8,10},{9,11},{10,... | collective-permute-start | bytes 1179656 | tf_op jit(solution)/shard_map/ppermute | solution.py:51
  441.8 11.2 %collective-permute-start.37 = (f32[2,64,768]{2,1,0:T(8,128)S(1)}, f32[2,64,768]{2,1,0:T(8,128)S(1)}, u32[]{:S(2)}, u32[]{:S(2)}) collective-permute-start(f32[2,64,768]{2,1,0:T(8,128)S(1)} %slice_bitcast_fusion.29), channel_id=1, source_target_pairs={{0,4},{1,5},{2,6},{3,7},{4,0},{5,1},{6,2},{7,3},{8,12},{9,13},{10,... | collective-permute-start | bytes 1179656 | tf_op jit(solution)/shard_map/ppermute | solution.py:51
  478.7 18.2 %collective-permute-start.40 = (f32[768,1536]{1,0:T(8,128)}, f32[768,1536]{1,0:T(8,128)}, u32[]{:S(2)}, u32[]{:S(2)}) collective-permute-start(f32[768,1536]{1,0:T(8,128)} %fusion.70), channel_id=1, source_target_pairs={{0,1},{1,0},{2,3},{3,2},{4,5},{5,4},{6,7},{7,6},{8,9},{9,8},{10,11... | collective-permute-start | bytes 14155784 | tf_op jit(solution)/shard_map/ppermute | solution.py:51
  484.5 20.4 %collective-permute-start.39 = (f32[3072,384]{1,0:T(8,128)}, f32[3072,384]{1,0:T(8,128)}, u32[]{:S(2)}, u32[]{:S(2)}) collective-permute-start(f32[3072,384]{1,0:T(8,128)} %fusion.111), channel_id=1, source_target_pairs={{0,1},{1,0},{2,3},{3,2},{4,5},{5,4},{6,7},{7,6},{8,9},{9,8},{10,11... | collective-permute-start | bytes 14155784 | tf_op jit(solution)/shard_map/ppermute | solution.py:51
  485.7 193.0 %reduce-scatter.6.cloned.1.call-start = ((), (), s32[]{:S(2)}) async-start(), calls=%async_computation.10 | async-start | bytes 1474560 | tf_op jit(solution)/shard_map/reduce_scatter | solution.py:597
  517.3 22.5 %collective-permute-start.42 = (bf16[2,2,192,384]{3,2,0,1:T(8,128)(2,1)}, bf16[2,2,192,384]{3,2,0,1:T(8,128)(2,1)}, u32[]{:S(2)}, u32[]{:S(2)}) collective-permute-start(bf16[2,2,192,384]{3,2,0,1:T(8,128)(2,1)} %fusion.104), channel_id=1, source_target_pairs={{0,4},{1,5},{2,6},{3,7},{4,0},{5,1},{6,2},{7,3},{8,12},{9,13},{10,... | collective-permute-start | bytes 1769480 | tf_op jit(solution)/shard_map/ppermute | solution.py:51
  518.3 22.8 %collective-permute-start.41 = (bf16[2,2,192,384]{3,2,0,1:T(8,128)(2,1)S(1)}, bf16[2,2,192,384]{3,2,0,1:T(8,128)(2,1)}, u32[]{:S(2)}, u32[]{:S(2)}) collective-permute-start(bf16[2,2,192,384]{3,2,0,1:T(8,128)(2,1)S(1)} %fusion.103), channel_id=1, source_target_pairs={{0,2},{1,3},{2,0},{3,1},{4,6},{5,7},{6,4},{7,5},{8,10},{9,11},{10,... | collective-permute-start | bytes 1769480 | tf_op jit(solution)/shard_map/ppermute | solution.py:51
  535.1 14.7 %collective-permute-start.44 = (bf16[2,2,48,1536]{3,2,0,1:T(8,128)(2,1)S(1)}, bf16[2,2,48,1536]{3,2,0,1:T(8,128)(2,1)S(1)}, u32[]{:S(2)}, u32[]{:S(2)}) collective-permute-start(bf16[2,2,48,1536]{3,2,0,1:T(8,128)(2,1)S(1)} %copy-done.65), channel_id=1, source_target_pairs={{0,4},{1,5},{2,6},{3,7},{4,0},{5,1},{6,2},{7,3},{8,12},{9,13},{10,... | collective-permute-start | bytes 1769480 | tf_op jit(solution)/shard_map/ppermute | solution.py:51
  539.1 14.3 %collective-permute-start.43 = (bf16[2,2,48,1536]{3,2,0,1:T(8,128)(2,1)S(1)}, bf16[2,2,48,1536]{3,2,0,1:T(8,128)(2,1)S(1)}, u32[]{:S(2)}, u32[]{:S(2)}) collective-permute-start(bf16[2,2,48,1536]{3,2,0,1:T(8,128)(2,1)S(1)} %fusion.105), channel_id=1, source_target_pairs={{0,2},{1,3},{2,0},{3,1},{4,6},{5,7},{6,4},{7,5},{8,10},{9,11},{10,... | collective-permute-start | bytes 1769480 | tf_op jit(solution)/shard_map/ppermute | solution.py:51
  553.5 20.7 %collective-permute-start.48 = (bf16[2,48,1536]{2,1,0:T(8,128)(2,1)S(1)}, bf16[2,48,1536]{2,1,0:T(8,128)(2,1)S(1)}, u32[]{:S(2)}, u32[]{:S(2)}) collective-permute-start(bf16[2,48,1536]{2,1,0:T(8,128)(2,1)S(1)} %fusion.117), channel_id=1, source_target_pairs={{0,2},{1,3},{2,0},{3,1},{4,6},{5,7},{6,4},{7,5},{8,10},{9,11},{10,... | collective-permute-start | bytes 884744 | tf_op jit(solution)/shard_map/ppermute | solution.py:51
  570.9 14.2 %collective-permute-start.47 = (bf16[2,48,1536]{2,1,0:T(8,128)(2,1)S(1)}, bf16[2,48,1536]{2,1,0:T(8,128)(2,1)S(1)}, u32[]{:S(2)}, u32[]{:S(2)}) collective-permute-start(bf16[2,48,1536]{2,1,0:T(8,128)(2,1)S(1)} %fusion.116), channel_id=1, source_target_pairs={{0,4},{1,5},{2,6},{3,7},{4,0},{5,1},{6,2},{7,3},{8,12},{9,13},{10,... | collective-permute-start | bytes 884744 | tf_op jit(solution)/shard_map/ppermute | solution.py:51
  572.8 11.5 %collective-permute-start.45 = (bf16[2,192,384]{2,1,0:T(8,128)(2,1)S(1)}, bf16[2,192,384]{2,1,0:T(8,128)(2,1)S(1)}, u32[]{:S(2)}, u32[]{:S(2)}) collective-permute-start(bf16[2,192,384]{2,1,0:T(8,128)(2,1)S(1)} %fusion.114), channel_id=1, source_target_pairs={{0,4},{1,5},{2,6},{3,7},{4,0},{5,1},{6,2},{7,3},{8,12},{9,13},{10,... | collective-permute-start | bytes 884744 | tf_op jit(solution)/shard_map/ppermute | solution.py:51
  601.7 76.9 %reduce-scatter.8.cloned.1.call-start = ((), (), s32[]{:S(2)}) async-start(), calls=%async_computation.11 | async-start | bytes 1474560 | tf_op jit(solution)/shard_map/reduce_scatter | solution.py:597
  612.9 14.2 %collective-permute-start.49 = (f32[768,1152]{1,0:T(8,128)}, f32[768,1152]{1,0:T(8,128)}, u32[]{:S(2)}, u32[]{:S(2)}) collective-permute-start(f32[768,1152]{1,0:T(8,128)} %fusion.88), channel_id=1, source_target_pairs={{0,1},{1,0},{2,3},{3,2},{4,5},{5,4},{6,7},{7,6},{8,9},{9,8},{10,11... | collective-permute-start | bytes 10616840 | tf_op jit(solution)/shard_map/ppermute | solution.py:51
  621.6 128.7 %all-gather.7.cloned.1.call-start = ((), (), s32[]{:S(2)}) async-start(), calls=%async_computation.12 | async-start | bytes 7077888 | tf_op jit(solution)/shard_map/all_gather | solution.py:911
  634.0 42.6 %collective-permute-start.51 = (bf16[2,2,48,1152]{3,2,0,1:T(8,128)(2,1)}, bf16[2,2,48,1152]{3,2,0,1:T(8,128)(2,1)S(1)}, u32[]{:S(2)}, u32[]{:S(2)}) collective-permute-start(bf16[2,2,48,1152]{3,2,0,1:T(8,128)(2,1)} %fusion.108), channel_id=1, source_target_pairs={{0,4},{1,5},{2,6},{3,7},{4,0},{5,1},{6,2},{7,3},{8,12},{9,13},{10,... | collective-permute-start | bytes 1327112 | tf_op jit(solution)/shard_map/ppermute | solution.py:51
  638.0 13.4 %collective-permute-start.55 = (bf16[512,192]{0,1:T(8,128)(2,1)S(1)}, bf16[512,192]{0,1:T(8,128)(2,1)S(1)}, u32[]{:S(2)}, u32[]{:S(2)}) collective-permute-start(bf16[512,192]{0,1:T(8,128)(2,1)S(1)} %get-tuple-element.283), channel_id=1, source_target_pairs={{0,24},{8,0},{16,8},{24,16},{1,25},{9,1},{17,9},{25,17},{2,26},{10... | collective-permute-start | bytes 589832 | tf_op jit(solution)/shard_map/ppermute | solution.py:56
  640.8 35.6 %collective-permute-start.54 = (bf16[512,192]{0,1:T(8,128)(2,1)S(1)}, bf16[512,192]{0,1:T(8,128)(2,1)S(1)}, u32[]{:S(2)}, u32[]{:S(2)}) collective-permute-start(bf16[512,192]{0,1:T(8,128)(2,1)S(1)} %get-tuple-element.284), channel_id=1, source_target_pairs={{0,16},{8,24},{16,0},{24,8},{1,17},{9,25},{17,1},{25,9},{2,18},{10... | collective-permute-start | bytes 589832 | tf_op jit(solution)/shard_map/ppermute | solution.py:56
  641.0 35.5 %collective-permute-start.53 = (bf16[512,192]{0,1:T(8,128)(2,1)S(1)}, bf16[512,192]{0,1:T(8,128)(2,1)S(1)}, u32[]{:S(2)}, u32[]{:S(2)}) collective-permute-start(bf16[512,192]{0,1:T(8,128)(2,1)S(1)} %get-tuple-element.285), channel_id=1, source_target_pairs={{0,8},{8,16},{16,24},{24,0},{1,9},{9,17},{17,25},{25,1},{2,10},{10... | collective-permute-start | bytes 589832 | tf_op jit(solution)/shard_map/ppermute | solution.py:56
  644.2 33.4 %collective-permute-start.50 = (bf16[2,2,48,1152]{3,2,0,1:T(8,128)(2,1)S(1)}, bf16[2,2,48,1152]{3,2,0,1:T(8,128)(2,1)S(1)}, u32[]{:S(2)}, u32[]{:S(2)}) collective-permute-start(bf16[2,2,48,1152]{3,2,0,1:T(8,128)(2,1)S(1)} %fusion.107), channel_id=1, source_target_pairs={{0,2},{1,3},{2,0},{3,1},{4,6},{5,7},{6,4},{7,5},{8,10},{9,11},{10,... | collective-permute-start | bytes 1327112 | tf_op jit(solution)/shard_map/ppermute | solution.py:51
  684.7 11.5 %collective-permute-start.56 = (bf16[2,48,1152]{2,1,0:T(8,128)(2,1)S(1)}, bf16[2,48,1152]{2,1,0:T(8,128)(2,1)S(1)}, u32[]{:S(2)}, u32[]{:S(2)}) collective-permute-start(bf16[2,48,1152]{2,1,0:T(8,128)(2,1)S(1)} %fusion.190), channel_id=1, source_target_pairs={{0,4},{1,5},{2,6},{3,7},{4,0},{5,1},{6,2},{7,3},{8,12},{9,13},{10,... | collective-permute-start | bytes 663560 | tf_op jit(solution)/shard_map/ppermute | solution.py:51
  685.1 21.2 %collective-permute-start.59 = (bf16[2,2,88,384]{3,2,0,1:T(8,128)(2,1)S(1)}, bf16[2,2,88,384]{3,2,0,1:T(8,128)(2,1)S(1)}, u32[]{:S(2)}, u32[]{:S(2)}) collective-permute-start(bf16[2,2,88,384]{3,2,0,1:T(8,128)(2,1)S(1)} %fusion.119), channel_id=1, source_target_pairs={{0,4},{1,5},{2,6},{3,7},{4,0},{5,1},{6,2},{7,3},{8,12},{9,13},{10,... | collective-permute-start | bytes 811016 | tf_op jit(solution)/shard_map/ppermute | solution.py:51
  687.1 19.3 %collective-permute-start.58 = (bf16[2,2,88,384]{3,2,0,1:T(8,128)(2,1)S(1)}, bf16[2,2,88,384]{3,2,0,1:T(8,128)(2,1)S(1)}, u32[]{:S(2)}, u32[]{:S(2)}) collective-permute-start(bf16[2,2,88,384]{3,2,0,1:T(8,128)(2,1)S(1)} %fusion.118), channel_id=1, source_target_pairs={{0,2},{1,3},{2,0},{3,1},{4,6},{5,7},{6,4},{7,5},{8,10},{9,11},{10,... | collective-permute-start | bytes 811016 | tf_op jit(solution)/shard_map/ppermute | solution.py:51
  707.0 18.7 %collective-permute-start.61 = (f32[48,1152]{1,0:T(8,128)S(1)}, f32[48,1152]{1,0:T(8,128)S(1)}, u32[]{:S(2)}, u32[]{:S(2)}) collective-permute-start(f32[48,1152]{1,0:T(8,128)S(1)} %get-tuple-element.279), channel_id=1, source_target_pairs={{0,16},{8,24},{16,0},{24,8},{1,17},{9,25},{17,1},{25,9},{2,18},{10... | collective-permute-start | bytes 663560 | tf_op jit(solution)/shard_map/ppermute | solution.py:56
  709.9 15.7 %collective-permute-start.60 = (f32[48,1152]{1,0:T(8,128)S(1)}, f32[48,1152]{1,0:T(8,128)S(1)}, u32[]{:S(2)}, u32[]{:S(2)}) collective-permute-start(f32[48,1152]{1,0:T(8,128)S(1)} %get-tuple-element.280), channel_id=1, source_target_pairs={{0,8},{8,16},{16,24},{24,0},{1,9},{9,17},{17,25},{25,1},{2,10},{10... | collective-permute-start | bytes 663560 | tf_op jit(solution)/shard_map/ppermute | solution.py:56
  725.8 11.0 %collective-permute-start.66 = (f32[88,384]{1,0:T(8,128)S(1)}, f32[88,384]{1,0:T(8,128)S(1)}, u32[]{:S(2)}, u32[]{:S(2)}) collective-permute-start(f32[88,384]{1,0:T(8,128)S(1)} %get-tuple-element.287), channel_id=1, source_target_pairs={{0,16},{8,24},{16,0},{24,8},{1,17},{9,25},{17,1},{25,9},{2,18},{10... | collective-permute-start | bytes 405512 | tf_op jit(solution)/shard_map/ppermute | solution.py:56
  743.4 41.8 %all-to-all-start.4 = ((f32[32,96,128]{2,1,0:T(8,128)}), f32[32,96,128]{2,1,0:T(8,128)}, u32[]{:S(2)}, u32[]{:S(2)}) async-start(f32[32,96,128]{2,1,0:T(8,128)} %bitcast.423), calls=%async_computation.7 | async-start | bytes 3145728 | tf_op jit(solution)/shard_map/all_to_all | solution.py:921
  (152 other events, 1163.0 us)
Sparse Core Ops, SparseCore 0:
  10.9 163.4 all-gather.4
  178.0 122.1 all-gather.8
  485.8 104.2 reduce-scatter.3
  601.8 29.6 reduce-scatter.5
  634.3 42.4 reduce-scatter.7
  679.7 50.6 all-gather.6

commit v10 on v9

--- a/solution.py
+++ b/solution.py
@@ -462,7 +462,7 @@
     flow.add_product(saved["activated"], grad_out, offload=True)
     grad_act = trailing_array_multiply(grad_out, pieces["down"])
     grad_hidden = (grad_act * gelu_slope(saved["hidden"])).astype(jnp.bfloat16)
-    flow.add_product(saved["middle_low"], grad_hidden, offload=True)
+    flow.add_product(saved["middle_low"], grad_hidden, late=2)
     grad_middle = grad_sum_two + trailing_array_multiply(grad_hidden, pieces["up"])
     grad_sum_one, grad_gain_one, grad_shift_one = norm_backward(
         grad_middle, saved["normed_one"], saved["inverse_one"], small_rows[6]
@@ -588,7 +588,7 @@
     return at(value, mine, axis) + sent_low(at(value, 1 - mine, axis), bit)
 
 
-def reduce_steps(near, far, offload):
+def reduce_steps(near, far, offload, late):
     (chip,) = yield [near + swap(far, CORE)]
     chip = chip.reshape(4, 2, 2, chip.shape[0] // CHIPS, chip.shape[1])
     first, second = yield [halved(chip[:2], 2, ACROSS), halved(chip[2:], 1, DEEP)]
@@ -602,6 +602,8 @@
     blocks = [
         jnp.where((z + k) % 4 < 2, at(first, (z + k) % 2, 0), at(second, (z + k) % 2, 0)) for k in range(4)
     ]
+    for _ in range(late):
+        yield []
     blocks = yield [blocks[0], *(shift(blocks[k], k) for k in (1, 2, 3))]
     return blocks[0] + blocks[1] + blocks[2] + blocks[3]
 
@@ -612,17 +614,17 @@
     def __init__(self):
         self.lines, self.waiting, self.sums = [], [], []
 
-    def add(self, near, far, offload=False):
-        self.lines.append(reduce_steps(near, far, offload))
+    def add(self, near, far, offload=False, late=0):
+        self.lines.append(reduce_steps(near, far, offload, late))
         self.waiting.append(next(self.lines[-1]))
         self.sums.append(None)
 
-    def add_product(self, left, right, offload=False):
+    def add_product(self, left, right, offload=False, late=0):
         width = right.shape[1] // 2
         core = bit_of(CORE)
         far = matmul_left(left, lax.dynamic_slice_in_dim(right, (1 - core) * width, width, 1))
         near = matmul_left(left, lax.dynamic_slice_in_dim(right, core * width, width, 1))
-        self.add(near, far, offload)
+        self.add(near, far, offload, late)
 
     def add_rest(self, out, place, tail):
         def half(core):
@@ -652,7 +654,7 @@
     def __init__(self, devices):
         self.devices, self.sums = devices, []
 
-    def add_product(self, left, right, offload=False):
+    def add_product(self, left, right, offload=False, late=0):
         parts = matmul_left(left, right).reshape(self.devices, -1, TILE)
         self.sums.append(lax.psum_scatter(parts, ("dp", "vocab"), scatter_dimension=0, tiled=False))
 

time: 834 us -> 832 us (level)
    unnamed x241 -> x243, local copies, waits for them, and re-layouts: 16.8 us -> 20 us
    ppermute x15 -> x18, waiting for transfers between devices: 68 us -> 65.6 us  [shift(): lax.ppermute(value, 'dp', [(i, (i + steps) % size) for i in range(size)])]
    ppermute x15 -> x18, starting transfers between devices: 20.4 us -> 21.3 us  [shift(): lax.ppermute(value, 'dp', [(i, (i + steps) % size) for i in range(size)])]
  transfers between devices with their start and end apart: 84 -> 86, of which waited for: 46 -> 48; matrix products, arithmetic and copies ran while one was open for 40% -> 39% of each run, Pallas kernels for 5% -> 5%
where the time goes in v10:
time: 832 us; the launch traced here: 822 us
  matrix products  234 us (28%)
  waiting for transfers between devices  207 us (25%)
  other arithmetic  127 us (15%)
  starting transfers between devices  91.9 us (11%)
  local copies, waits for them, and re-layouts  81.4 us (10%)
  Pallas kernels  54.2 us (7%)
  between operations  25.4 us (3%)
    ppermute x57, waiting for transfers between devices, swap(): return lax.ppermute(value, 'vocab', [(i, i ^ bit) for i in range(8)])  109 us
    dot_general x11, matrix products, array_multiply(): return jnp.dot(left_side, right_side, preferred_element_type=jnp.float32)  77.6 us
    dot_general x9, matrix products, matmul_left(): lax.dot_general(left_side, right_side, (((0,), (0,)), ((), ())), preferre...  68.8 us
    ppermute x18, waiting for transfers between devices, shift(): lax.ppermute(value, 'dp', [(i, (i + steps) % size) for i in range(size)])  65.6 us
    ppermute x57, starting transfers between devices, swap(): return lax.ppermute(value, 'vocab', [(i, i ^ bit) for i in range(8)])  55.4 us
    dot_general x9, matrix products, trailing_array_multiply(): lax.dot_general(left_side, right_side, (((1,), (1,)), ((), ())), preferre...  44.6 us
    ppermute x18, starting transfers between devices, shift(): lax.ppermute(value, 'dp', [(i, (i + steps) % size) for i in range(size)])  21.3 us
    pallas_call x5, Pallas kernels, unpack_matrix(): pl.pallas_call(functools.partial(unpack_kernel, across=across), grid=(hei...  21.2 us
  transfers between devices with their start and end apart: 86, of which 48 were waited for; matrix products, arithmetic and copies ran while one was open for 39% of the time, Pallas kernels for 5%

profile of v10, /device:TPU:0, one launch (start us, length us, event | category | flops | bytes accessed | tf_op | source)
XLA Modules:
  0.0 822.0 jit_solution(13264277959470215881)
XLA Ops:
  17.5 4.7 broadcast_divide_fusion
  28.0 7.2 send_tiles.1
  35.3 8.5 %fusion.60 = bf16[2048,768]{1,0:T(8,128)(2,1)} fusion(bf16[1920,768]{1,0:T(8,128)(2,1)S(1)} %copy-done, s32[2048]{0:T(1024)S(1)} %bitcast.506), kind=kOutput, calls=%fused_computation.119 | convolution fusion | flops 6045302784 | bytes 6103040 | tf_op jit(solution)/shard_map/dot_general | solution.py:333
  55.2 4.7 all-to-all-done.3
  63.6 8.5 %fusion.62 = bf16[2048,768]{1,0:T(8,128)(2,1)} fusion(bf16[1920,768]{1,0:T(8,128)(2,1)S(1)} %copy-done, s32[2048]{0:T(1024)S(1)} %bitcast.504), kind=kOutput, calls=%fused_computation.121 | convolution fusion | flops 6045302784 | bytes 6103040 | tf_op jit(solution)/shard_map/dot_general | solution.py:333
  73.9 5.2 add.1048
  79.2 10.5 %collective-permute-done.5 = bf16[192,1920]{1,0:T(8,128)(2,1)} collective-permute-done((bf16[192,1920]{1,0:T(8,128)(2,1)}, bf16[192,1920]{1,0:T(8,128)(2,1)}, u32[]{:S(2)}, u32[]{:S(2)}) %collective-permute-start.5) | collective-permute-done | bytes 737312 | tf_op jit(solution)/shard_map/ppermute | solution.py:56
  89.7 15.8 %all-to-all-done.2 = bf16[32,96,128]{2,1,0:T(8,128)(2,1)} async-done(((bf16[32,96,128]{2,1,0:T(8,128)(2,1)}), bf16[32,96,128]{2,1,0:T(8,128)(2,1)}, u32[]{:S(2)}, u32[]{:S(2)}) %all-to-all-start.2) | async-done | bytes 786464 | tf_op jit(solution)/shard_map/all_to_all | solution.py:740
  115.3 4.7 land_tiles.3
  119.9 25.1 %collective-permute-done.6 = bf16[2,256,768]{2,1,0:T(8,128)(2,1)} collective-permute-done((bf16[2,256,768]{2,1,0:T(8,128)(2,1)}, bf16[2,256,768]{2,1,0:T(8,128)(2,1)}, u32[]{:S(2)}, u32[]{:S(2)}) %collective-permute-start.6) | collective-permute-done | bytes 786464 | tf_op jit(solution)/shard_map/ppermute | solution.py:51
  158.9 7.4 fusion.61
  184.9 7.3 fusion.63
  210.5 5.8 unpack_matrix.9
  216.2 6.2 unpack_matrix.5
  238.0 4.5 copy.105
  247.7 10.8 %fusion.288 = (f32[12,512]{1,0:T(8,128)S(1)}, f32[12,512,512]{1,2,0:T(8,128)}) fusion(pred[512]{0:T(512)(128)(4,1)S(1)} %iota_compare_fusion.27, bf16[1,512,3,12,64]{1,4,3,2,0:T(8,128)(2,1)} %bitcast.456), kind=kOutput, calls=%fused_computation.709 | convolution fusion | flops 415236608 | bytes 14180864 | tf_op jit(solution)/shard_map/sub | solution.py:411
  258.6 6.3 fusion.82
  271.3 23.3 %fusion.290 = (f32[512]{0:T(512)S(1)}, f32[512,768]{1,0:T(8,128)}) fusion(f32[512,768]{1,0:T(8,128)} %multiply_add_fusion.4, f32[768]{0:T(1024)S(1)} %get-tuple-element.238, bf16[3072,768]{1,0:T(8,128)(2,1)} %unpack_matrix.5, bf16[768,3072]{1,0:T(8,128)(2,1)} %unpack_matrix.9, f32[3072]{0:T(1024)S(1)} %slice_bitcast_fusion.42), kind=kOutput, calls=%fused_computation.711 | convolution fusion | flops 4937219584 | bytes 12600320 | tf_op jit(solution)/shard_map/dot_general | solution.py:333
  300.0 12.3 %assemble_layer.1 = (bf16[768,3072]{1,0:T(8,128)(2,1)}, bf16[3072,768]{1,0:T(8,128)(2,1)}, bf16[768,2304]{1,0:T(8,128)(2,1)}, bf16[768,768]{1,0:T(8,128)(2,1)}, ...) custom-call(bf16[32,160,1536]{2,1,0:T(8,128)(2,1)} %bitcast.419), custom_call_target="tpu_custom_call" | custom-call | bytes 60000000 | tf_op jit(solution)/shard_map/assemble_layer/pallas_call | solution.py:287
  320.0 6.0 fusion.59
  344.8 9.0 %collective-permute-done.23 = bf16[2,128,768]{2,1,0:T(8,128)(2,1)S(1)} collective-permute-done((bf16[2,128,768]{2,1,0:T(8,128)(2,1)S(1)}, bf16[2,128,768]{2,1,0:T(8,128)(2,1)S(1)}, u32[]{:S(2)}, u32[]{:S(2)}) %collective-permute-start.23) | collective-permute-done | bytes 393248 | tf_op jit(solution)/shard_map/ppermute | solution.py:51
  357.5 18.0 %fusion.25 = (bf16[512,3072]{1,0:T(8,128)(2,1)S(1)}, f32[512,3072]{1,0:T(8,128)}) fusion(f32[3072]{0:T(1024)S(1)} %slice_bitcast_fusion.41, bf16[768,3072]{1,0:T(8,128)(2,1)S(1)} %bitcast.510, f32[512,768]{1,0:T(8,128)S(1)} %multiply_add_fusion.1), kind=kOutput, calls=%fused_computation.59 | convolution fusion | flops 2520121344 | bytes 15740928 | tf_op jit(solution)/shard_map/dot_general | solution.py:333
  386.6 5.1 collective-permute-done.26
  419.2 7.2 multiply_convert_fusion
  442.3 5.3 fusion.300
  447.6 4.3 collective-permute-done.35
  455.9 4.4 collective-permute-done.38
  467.0 7.8 convert_reduce_fusion.1
  478.4 5.9 fusion.111
  485.9 7.4 multiply_reduce_fusion.3
  498.7 6.1 convolution_add_fusion.4
  504.8 6.6 convolution_add_fusion.2
  528.4 6.6 convolution_bitcast_fusion
  542.0 7.6 collective-permute-done.44
  554.3 6.7 fusion.10
  561.0 9.7 %fusion.11 = bf16[1,12,512,512]{2,3,1,0:T(8,128)(2,1)} fusion(f32[1,12,512,512]{2,3,1,0:T(8,128)} %convolution_bitcast_fusion, f32[12,512,512]{1,2,0:T(8,128)S(1)} %bitcast.413, f32[12,512]{1,0:T(8,128)S(1)} %fusion.10, f32[12,512]{1,0:T(8,128)S(1)} %log_add_fusion), kind=kLoop, calls=%fused_computation.28 | loop fusion | flops 12582912 | bytes 31506432 | tf_op jit(solution)/shard_map/convert_element_type | solution.py:505
  579.2 4.8 collective-permute-done.45
  584.9 4.9 reduce-scatter.3.cloned.1.call-done
  589.9 4.8 multiply_bitcast_fusion
  605.6 4.6 fusion.88
  640.2 7.1 collective-permute-done.58
  647.3 15.8 %collective-permute-done.57 = bf16[512,192]{0,1:T(8,128)(2,1)S(1)} collective-permute-done((bf16[512,192]{0,1:T(8,128)(2,1)S(1)}, bf16[512,192]{0,1:T(8,128)(2,1)S(1)}, u32[]{:S(2)}, u32[]{:S(2)}) %collective-permute-start.57) | collective-permute-done | bytes 196640 | tf_op jit(solution)/shard_map/ppermute | solution.py:56
  678.0 7.8 collective-permute-done.60
  689.8 6.8 collective-permute-done.62
  707.6 15.0 %collective-permute-done.64 = f32[48,1152]{1,0:T(8,128)S(1)} collective-permute-done((f32[48,1152]{1,0:T(8,128)S(1)}, f32[48,1152]{1,0:T(8,128)S(1)}, u32[]{:S(2)}, u32[]{:S(2)}) %collective-permute-start.64) | collective-permute-done | bytes 221216 | tf_op jit(solution)/shard_map/ppermute | solution.py:56
  729.0 6.5 collective-permute-done.69
  737.4 4.7 pick_tiles.2
  748.3 32.3 %fusion.3 = f32[192,1920]{1,0:T(8,128)} fusion(bf16[16384,192]{0,1:T(8,128)(2,1)} %all-gather.7.cloned.1.call-done, s32[16384]{0:T(1024)S(1)} %bitcast.487), kind=kOutput, calls=%fused_computation.15 | convolution fusion | flops 12111052800 | bytes 7831552 | tf_op jit(solution)/shard_map/dot_general | solution.py:337
  (678 shorter events, 379.2 us)
Async XLA Ops:
  7.2 187.7 %all-gather.5.cloned.1.call-start = ((), (), s32[]{:S(2)}) async-start(), calls=%async_computation.7 | async-start | bytes 15476736 | tf_op jit(solution)/shard_map/all_gather | solution.py:734
  10.7 12.2 %collective-permute-start = (s32[1,640]{1,0:T(1,128)S(1)}, s32[1,640]{1,0:T(1,128)S(1)}, u32[]{:S(2)}, u32[]{:S(2)}) collective-permute-start(s32[1,640]{1,0:T(1,128)S(1)} %broadcast_in_dim.63), channel_id=1, source_target_pairs={{0,2},{1,3},{2,0},{3,1},{4,6},{5,7},{6,4},{7,5},{8,10},{9,11},{10,... | collective-permute-start | bytes 7688 | tf_op jit(solution)/shard_map/ppermute | solution.py:51
  15.9 30.2 %collective-permute-start.3 = (bf16[192,1920]{1,0:T(8,128)(2,1)}, bf16[192,1920]{1,0:T(8,128)(2,1)}, u32[]{:S(2)}, u32[]{:S(2)}) collective-permute-start(bf16[192,1920]{1,0:T(8,128)(2,1)} %convert_bitcast_fusion), channel_id=1, source_target_pairs={{0,8},{8,16},{16,24},{24,0},{1,9},{9,17},{17,25},{25,1},{2,10},{10... | collective-permute-start | bytes 2211848 | tf_op jit(solution)/shard_map/ppermute | solution.py:56
  46.1 27.8 %collective-permute-start.4 = (bf16[2,2,512,768]{3,2,1,0:T(8,128)(2,1)}, bf16[2,2,512,768]{3,2,1,0:T(8,128)(2,1)}, u32[]{:S(2)}, u32[]{:S(2)}) collective-permute-start(bf16[2,2,512,768]{3,2,1,0:T(8,128)(2,1)} %bitcast.3), channel_id=1, source_target_pairs={{0,1},{1,0},{2,3},{3,2},{4,5},{5,4},{6,7},{7,6},{8,9},{9,8},{10,11... | collective-permute-start | bytes 9437192 | tf_op jit(solution)/shard_map/ppermute | solution.py:51
  53.4 36.2 %collective-permute-start.5 = (bf16[192,1920]{1,0:T(8,128)(2,1)}, bf16[192,1920]{1,0:T(8,128)(2,1)}, u32[]{:S(2)}, u32[]{:S(2)}) collective-permute-start(bf16[192,1920]{1,0:T(8,128)(2,1)} %collective-permute-done.3), channel_id=1, source_target_pairs={{0,8},{8,16},{16,24},{24,0},{1,9},{9,17},{17,25},{25,1},{2,10},{10... | collective-permute-start | bytes 2211848 | tf_op jit(solution)/shard_map/ppermute | solution.py:56
  60.0 45.5 %all-to-all-start.2 = ((bf16[32,96,128]{2,1,0:T(8,128)(2,1)}), bf16[32,96,128]{2,1,0:T(8,128)(2,1)}, u32[]{:S(2)}, u32[]{:S(2)}) async-start(bf16[32,96,128]{2,1,0:T(8,128)(2,1)} %bitcast.462), calls=%async_computation.2 | async-start | bytes 1572864 | tf_op jit(solution)/shard_map/all_to_all | solution.py:740
  63.3 236.7 %all-gather.9.cloned.1.call-start = ((), (), s32[]{:S(2)}) async-start(), calls=%async_computation.11 | async-start | bytes 16220160 | tf_op jit(solution)/shard_map/all_gather | solution.py:767
  107.8 37.2 %collective-permute-start.6 = (bf16[2,256,768]{2,1,0:T(8,128)(2,1)}, bf16[2,256,768]{2,1,0:T(8,128)(2,1)}, u32[]{:S(2)}, u32[]{:S(2)}) collective-permute-start(bf16[2,256,768]{2,1,0:T(8,128)(2,1)} %slice_bitcast_fusion.12), channel_id=1, source_target_pairs={{0,2},{1,3},{2,0},{3,1},{4,6},{5,7},{6,4},{7,5},{8,10},{9,11},{10,... | collective-permute-start | bytes 2359304 | tf_op jit(solution)/shard_map/ppermute | solution.py:51
  111.3 37.1 %collective-permute-start.7 = (bf16[2,256,768]{2,1,0:T(8,128)(2,1)}, bf16[2,256,768]{2,1,0:T(8,128)(2,1)}, u32[]{:S(2)}, u32[]{:S(2)}) collective-permute-start(bf16[2,256,768]{2,1,0:T(8,128)(2,1)} %slice_bitcast_fusion.11), channel_id=1, source_target_pairs={{0,4},{1,5},{2,6},{3,7},{4,0},{5,1},{6,2},{7,3},{8,12},{9,13},{10,... | collective-permute-start | bytes 2359304 | tf_op jit(solution)/shard_map/ppermute | solution.py:51
  112.8 38.0 %collective-permute-start.8 = (bf16[192,1920]{1,0:T(8,128)(2,1)}, bf16[192,1920]{1,0:T(8,128)(2,1)}, u32[]{:S(2)}, u32[]{:S(2)}) collective-permute-start(bf16[192,1920]{1,0:T(8,128)(2,1)} %collective-permute-done.5), channel_id=1, source_target_pairs={{0,8},{8,16},{16,24},{24,0},{1,9},{9,17},{17,25},{25,1},{2,10},{10... | collective-permute-start | bytes 2211848 | tf_op jit(solution)/shard_map/ppermute | solution.py:56
  151.2 438.7 %reduce-scatter.3.cloned.1.call-start = ((), (), s32[]{:S(2)}) async-start(), calls=%async_computation.8 | async-start | bytes 7372800 | tf_op jit(solution)/shard_map/reduce_scatter | solution.py:882
  155.5 10.9 %collective-permute-start.10 = (bf16[256,768]{1,0:T(8,128)(2,1)S(1)}, bf16[256,768]{1,0:T(8,128)(2,1)S(1)}, u32[]{:S(2)}, u32[]{:S(2)}) collective-permute-start(bf16[256,768]{1,0:T(8,128)(2,1)S(1)} %slice_bitcast_fusion.35), channel_id=1, source_target_pairs={{0,2},{1,3},{2,0},{3,1},{4,6},{5,7},{6,4},{7,5},{8,10},{9,11},{10,... | collective-permute-start | bytes 1179656 | tf_op jit(solution)/shard_map/ppermute | solution.py:51
  167.8 24.5 %collective-permute-start.11 = (bf16[2,2,512,768]{3,2,1,0:T(8,128)(2,1)S(1)}, bf16[2,2,512,768]{3,2,1,0:T(8,128)(2,1)S(1)}, u32[]{:S(2)}, u32[]{:S(2)}) collective-permute-start(bf16[2,2,512,768]{3,2,1,0:T(8,128)(2,1)S(1)} %bitcast.513), channel_id=1, source_target_pairs={{0,1},{1,0},{2,3},{3,2},{4,5},{5,4},{6,7},{7,6},{8,9},{9,8},{10,11... | collective-permute-start | bytes 9437192 | tf_op jit(solution)/shard_map/ppermute | solution.py:51
  197.0 30.4 %collective-permute-start.18 = (bf16[2,256,768]{2,1,0:T(8,128)(2,1)}, bf16[2,256,768]{2,1,0:T(8,128)(2,1)}, u32[]{:S(2)}, u32[]{:S(2)}) collective-permute-start(bf16[2,256,768]{2,1,0:T(8,128)(2,1)} %slice_bitcast_fusion.10), channel_id=1, source_target_pairs={{0,2},{1,3},{2,0},{3,1},{4,6},{5,7},{6,4},{7,5},{8,10},{9,11},{10,... | collective-permute-start | bytes 2359304 | tf_op jit(solution)/shard_map/ppermute | solution.py:51
  200.2 29.6 %collective-permute-start.19 = (bf16[2,256,768]{2,1,0:T(8,128)(2,1)}, bf16[2,256,768]{2,1,0:T(8,128)(2,1)}, u32[]{:S(2)}, u32[]{:S(2)}) collective-permute-start(bf16[2,256,768]{2,1,0:T(8,128)(2,1)} %slice_bitcast_fusion.9), channel_id=1, source_target_pairs={{0,4},{1,5},{2,6},{3,7},{4,0},{5,1},{6,2},{7,3},{8,12},{9,13},{10,... | collective-permute-start | bytes 2359304 | tf_op jit(solution)/shard_map/ppermute | solution.py:51
  244.2 23.7 %collective-permute-start.21 = (bf16[256,768]{1,0:T(8,128)(2,1)}, bf16[256,768]{1,0:T(8,128)(2,1)}, u32[]{:S(2)}, u32[]{:S(2)}) collective-permute-start(bf16[256,768]{1,0:T(8,128)(2,1)} %slice_bitcast_fusion.33), channel_id=1, source_target_pairs={{0,2},{1,3},{2,0},{3,1},{4,6},{5,7},{6,4},{7,5},{8,10},{9,11},{10,... | collective-permute-start | bytes 1179656 | tf_op jit(solution)/shard_map/ppermute | solution.py:51
  247.3 21.6 %collective-permute-start.20 = (bf16[256,768]{1,0:T(8,128)(2,1)S(1)}, bf16[256,768]{1,0:T(8,128)(2,1)}, u32[]{:S(2)}, u32[]{:S(2)}) collective-permute-start(bf16[256,768]{1,0:T(8,128)(2,1)S(1)} %slice_bitcast_fusion.34), channel_id=1, source_target_pairs={{0,4},{1,5},{2,6},{3,7},{4,0},{5,1},{6,2},{7,3},{8,12},{9,13},{10,... | collective-permute-start | bytes 1179656 | tf_op jit(solution)/shard_map/ppermute | solution.py:51
  319.0 23.6 %collective-permute-start.22 = (bf16[1,128,768]{2,1,0:T(8,128)(2,1)S(1)}, bf16[1,128,768]{2,1,0:T(8,128)(2,1)S(1)}, u32[]{:S(2)}, u32[]{:S(2)}) collective-permute-start(bf16[1,128,768]{2,1,0:T(8,128)(2,1)S(1)} %bitcast.450), channel_id=1, source_target_pairs={{0,2},{1,3},{2,0},{3,1},{4,6},{5,7},{6,4},{7,5},{8,10},{9,11},{10,... | collective-permute-start | bytes 589832 | tf_op jit(solution)/shard_map/ppermute | solution.py:51
  342.7 11.1 %collective-permute-start.23 = (bf16[2,128,768]{2,1,0:T(8,128)(2,1)S(1)}, bf16[2,128,768]{2,1,0:T(8,128)(2,1)S(1)}, u32[]{:S(2)}, u32[]{:S(2)}) collective-permute-start(bf16[2,128,768]{2,1,0:T(8,128)(2,1)S(1)} %pad_maximum_fusion.4), channel_id=1, source_target_pairs={{0,4},{1,5},{2,6},{3,7},{4,0},{5,1},{6,2},{7,3},{8,12},{9,13},{10,... | collective-permute-start | bytes 1179656 | tf_op jit(solution)/shard_map/ppermute | solution.py:51
  440.4 11.6 %collective-permute-start.35 = (f32[2,64,768]{2,1,0:T(8,128)S(1)}, f32[2,64,768]{2,1,0:T(8,128)S(1)}, u32[]{:S(2)}, u32[]{:S(2)}) collective-permute-start(f32[2,64,768]{2,1,0:T(8,128)S(1)} %slice_bitcast_fusion.31), channel_id=1, source_target_pairs={{0,2},{1,3},{2,0},{3,1},{4,6},{5,7},{6,4},{7,5},{8,10},{9,11},{10,... | collective-permute-start | bytes 1179656 | tf_op jit(solution)/shard_map/ppermute | solution.py:51
  441.5 11.2 %collective-permute-start.37 = (f32[2,64,768]{2,1,0:T(8,128)S(1)}, f32[2,64,768]{2,1,0:T(8,128)S(1)}, u32[]{:S(2)}, u32[]{:S(2)}) collective-permute-start(f32[2,64,768]{2,1,0:T(8,128)S(1)} %slice_bitcast_fusion.29), channel_id=1, source_target_pairs={{0,4},{1,5},{2,6},{3,7},{4,0},{5,1},{6,2},{7,3},{8,12},{9,13},{10,... | collective-permute-start | bytes 1179656 | tf_op jit(solution)/shard_map/ppermute | solution.py:51
  478.4 18.3 %collective-permute-start.40 = (f32[768,1536]{1,0:T(8,128)}, f32[768,1536]{1,0:T(8,128)}, u32[]{:S(2)}, u32[]{:S(2)}) collective-permute-start(f32[768,1536]{1,0:T(8,128)} %fusion.70), channel_id=1, source_target_pairs={{0,1},{1,0},{2,3},{3,2},{4,5},{5,4},{6,7},{7,6},{8,9},{9,8},{10,11... | collective-permute-start | bytes 14155784 | tf_op jit(solution)/shard_map/ppermute | solution.py:51
  484.3 20.5 %collective-permute-start.39 = (f32[3072,384]{1,0:T(8,128)}, f32[3072,384]{1,0:T(8,128)}, u32[]{:S(2)}, u32[]{:S(2)}) collective-permute-start(f32[3072,384]{1,0:T(8,128)} %fusion.111), channel_id=1, source_target_pairs={{0,1},{1,0},{2,3},{3,2},{4,5},{5,4},{6,7},{7,6},{8,9},{9,8},{10,11... | collective-permute-start | bytes 14155784 | tf_op jit(solution)/shard_map/ppermute | solution.py:51
  485.5 181.6 %reduce-scatter.5.cloned.1.call-start = ((), (), s32[]{:S(2)}) async-start(), calls=%async_computation.9 | async-start | bytes 1474560 | tf_op jit(solution)/shard_map/reduce_scatter | solution.py:597
  517.1 22.5 %collective-permute-start.42 = (bf16[2,2,192,384]{3,2,0,1:T(8,128)(2,1)}, bf16[2,2,192,384]{3,2,0,1:T(8,128)(2,1)}, u32[]{:S(2)}, u32[]{:S(2)}) collective-permute-start(bf16[2,2,192,384]{3,2,0,1:T(8,128)(2,1)} %fusion.104), channel_id=1, source_target_pairs={{0,4},{1,5},{2,6},{3,7},{4,0},{5,1},{6,2},{7,3},{8,12},{9,13},{10,... | collective-permute-start | bytes 1769480 | tf_op jit(solution)/shard_map/ppermute | solution.py:51
  518.1 22.8 %collective-permute-start.41 = (bf16[2,2,192,384]{3,2,0,1:T(8,128)(2,1)S(1)}, bf16[2,2,192,384]{3,2,0,1:T(8,128)(2,1)}, u32[]{:S(2)}, u32[]{:S(2)}) collective-permute-start(bf16[2,2,192,384]{3,2,0,1:T(8,128)(2,1)S(1)} %fusion.103), channel_id=1, source_target_pairs={{0,2},{1,3},{2,0},{3,1},{4,6},{5,7},{6,4},{7,5},{8,10},{9,11},{10,... | collective-permute-start | bytes 1769480 | tf_op jit(solution)/shard_map/ppermute | solution.py:51
  535.0 14.7 %collective-permute-start.44 = (bf16[2,2,48,1536]{3,2,0,1:T(8,128)(2,1)S(1)}, bf16[2,2,48,1536]{3,2,0,1:T(8,128)(2,1)S(1)}, u32[]{:S(2)}, u32[]{:S(2)}) collective-permute-start(bf16[2,2,48,1536]{3,2,0,1:T(8,128)(2,1)S(1)} %copy-done.65), channel_id=1, source_target_pairs={{0,4},{1,5},{2,6},{3,7},{4,0},{5,1},{6,2},{7,3},{8,12},{9,13},{10,... | collective-permute-start | bytes 1769480 | tf_op jit(solution)/shard_map/ppermute | solution.py:51
  538.7 14.3 %collective-permute-start.43 = (bf16[2,2,48,1536]{3,2,0,1:T(8,128)(2,1)S(1)}, bf16[2,2,48,1536]{3,2,0,1:T(8,128)(2,1)S(1)}, u32[]{:S(2)}, u32[]{:S(2)}) collective-permute-start(bf16[2,2,48,1536]{3,2,0,1:T(8,128)(2,1)S(1)} %fusion.105), channel_id=1, source_target_pairs={{0,2},{1,3},{2,0},{3,1},{4,6},{5,7},{6,4},{7,5},{8,10},{9,11},{10,... | collective-permute-start | bytes 1769480 | tf_op jit(solution)/shard_map/ppermute | solution.py:51
  553.2 20.7 %collective-permute-start.48 = (bf16[2,48,1536]{2,1,0:T(8,128)(2,1)S(1)}, bf16[2,48,1536]{2,1,0:T(8,128)(2,1)S(1)}, u32[]{:S(2)}, u32[]{:S(2)}) collective-permute-start(bf16[2,48,1536]{2,1,0:T(8,128)(2,1)S(1)} %fusion.117), channel_id=1, source_target_pairs={{0,2},{1,3},{2,0},{3,1},{4,6},{5,7},{6,4},{7,5},{8,10},{9,11},{10,... | collective-permute-start | bytes 884744 | tf_op jit(solution)/shard_map/ppermute | solution.py:51
  570.7 14.1 %collective-permute-start.47 = (bf16[2,48,1536]{2,1,0:T(8,128)(2,1)S(1)}, bf16[2,48,1536]{2,1,0:T(8,128)(2,1)S(1)}, u32[]{:S(2)}, u32[]{:S(2)}) collective-permute-start(bf16[2,48,1536]{2,1,0:T(8,128)(2,1)S(1)} %fusion.116), channel_id=1, source_target_pairs={{0,4},{1,5},{2,6},{3,7},{4,0},{5,1},{6,2},{7,3},{8,12},{9,13},{10,... | collective-permute-start | bytes 884744 | tf_op jit(solution)/shard_map/ppermute | solution.py:51
  572.6 11.4 %collective-permute-start.45 = (bf16[2,192,384]{2,1,0:T(8,128)(2,1)S(1)}, bf16[2,192,384]{2,1,0:T(8,128)(2,1)S(1)}, u32[]{:S(2)}, u32[]{:S(2)}) collective-permute-start(bf16[2,192,384]{2,1,0:T(8,128)(2,1)S(1)} %fusion.114), channel_id=1, source_target_pairs={{0,4},{1,5},{2,6},{3,7},{4,0},{5,1},{6,2},{7,3},{8,12},{9,13},{10,... | collective-permute-start | bytes 884744 | tf_op jit(solution)/shard_map/ppermute | solution.py:51
  610.2 13.1 %collective-permute-start.52 = (f32[768,1152]{1,0:T(8,128)}, f32[768,1152]{1,0:T(8,128)}, u32[]{:S(2)}, u32[]{:S(2)}) collective-permute-start(f32[768,1152]{1,0:T(8,128)} %fusion.88), channel_id=1, source_target_pairs={{0,1},{1,0},{2,3},{3,2},{4,5},{5,4},{6,7},{7,6},{8,9},{9,8},{10,11... | collective-permute-start | bytes 10616840 | tf_op jit(solution)/shard_map/ppermute | solution.py:51
  617.7 130.7 %all-gather.7.cloned.1.call-start = ((), (), s32[]{:S(2)}) async-start(), calls=%async_computation.10 | async-start | bytes 7077888 | tf_op jit(solution)/shard_map/all_gather | solution.py:913
  630.5 33.6 %collective-permute-start.54 = (bf16[2,2,48,1152]{3,2,0,1:T(8,128)(2,1)}, bf16[2,2,48,1152]{3,2,0,1:T(8,128)(2,1)}, u32[]{:S(2)}, u32[]{:S(2)}) collective-permute-start(bf16[2,2,48,1152]{3,2,0,1:T(8,128)(2,1)} %fusion.108), channel_id=1, source_target_pairs={{0,4},{1,5},{2,6},{3,7},{4,0},{5,1},{6,2},{7,3},{8,12},{9,13},{10,... | collective-permute-start | bytes 1327112 | tf_op jit(solution)/shard_map/ppermute | solution.py:51
  632.4 14.9 %collective-permute-start.58 = (bf16[512,192]{0,1:T(8,128)(2,1)S(1)}, bf16[512,192]{0,1:T(8,128)(2,1)S(1)}, u32[]{:S(2)}, u32[]{:S(2)}) collective-permute-start(bf16[512,192]{0,1:T(8,128)(2,1)S(1)} %get-tuple-element.293), channel_id=1, source_target_pairs={{0,24},{8,0},{16,8},{24,16},{1,25},{9,1},{17,9},{25,17},{2,26},{10... | collective-permute-start | bytes 589832 | tf_op jit(solution)/shard_map/ppermute | solution.py:56
  635.1 27.9 %collective-permute-start.57 = (bf16[512,192]{0,1:T(8,128)(2,1)S(1)}, bf16[512,192]{0,1:T(8,128)(2,1)S(1)}, u32[]{:S(2)}, u32[]{:S(2)}) collective-permute-start(bf16[512,192]{0,1:T(8,128)(2,1)S(1)} %get-tuple-element.294), channel_id=1, source_target_pairs={{0,16},{8,24},{16,0},{24,8},{1,17},{9,25},{17,1},{25,9},{2,18},{10... | collective-permute-start | bytes 589832 | tf_op jit(solution)/shard_map/ppermute | solution.py:56
  635.4 27.6 %collective-permute-start.56 = (bf16[512,192]{0,1:T(8,128)(2,1)S(1)}, bf16[512,192]{0,1:T(8,128)(2,1)S(1)}, u32[]{:S(2)}, u32[]{:S(2)}) collective-permute-start(bf16[512,192]{0,1:T(8,128)(2,1)S(1)} %get-tuple-element.295), channel_id=1, source_target_pairs={{0,8},{8,16},{16,24},{24,0},{1,9},{9,17},{17,25},{25,1},{2,10},{10... | collective-permute-start | bytes 589832 | tf_op jit(solution)/shard_map/ppermute | solution.py:56
  638.6 27.4 %collective-permute-start.53 = (bf16[2,2,48,1152]{3,2,0,1:T(8,128)(2,1)S(1)}, bf16[2,2,48,1152]{3,2,0,1:T(8,128)(2,1)S(1)}, u32[]{:S(2)}, u32[]{:S(2)}) collective-permute-start(bf16[2,2,48,1152]{3,2,0,1:T(8,128)(2,1)S(1)} %fusion.107), channel_id=1, source_target_pairs={{0,2},{1,3},{2,0},{3,1},{4,6},{5,7},{6,4},{7,5},{8,10},{9,11},{10,... | collective-permute-start | bytes 1327112 | tf_op jit(solution)/shard_map/ppermute | solution.py:51
  670.9 25.8 %collective-permute-start.51 = (f32[48,1536]{1,0:T(8,128)S(1)}, f32[48,1536]{1,0:T(8,128)S(1)}, u32[]{:S(2)}, u32[]{:S(2)}) collective-permute-start(f32[48,1536]{1,0:T(8,128)S(1)} %get-tuple-element.284), channel_id=1, source_target_pairs={{0,24},{8,0},{16,8},{24,16},{1,25},{9,1},{17,9},{25,17},{2,26},{10... | collective-permute-start | bytes 884744 | tf_op jit(solution)/shard_map/ppermute | solution.py:56
  671.0 26.6 %collective-permute-start.50 = (f32[48,1536]{1,0:T(8,128)S(1)}, f32[48,1536]{1,0:T(8,128)S(1)}, u32[]{:S(2)}, u32[]{:S(2)}) collective-permute-start(f32[48,1536]{1,0:T(8,128)S(1)} %get-tuple-element.285), channel_id=1, source_target_pairs={{0,16},{8,24},{16,0},{24,8},{1,17},{9,25},{17,1},{25,9},{2,18},{10... | collective-permute-start | bytes 884744 | tf_op jit(solution)/shard_map/ppermute | solution.py:56
  671.6 26.0 %collective-permute-start.49 = (f32[48,1536]{1,0:T(8,128)S(1)}, f32[48,1536]{1,0:T(8,128)S(1)}, u32[]{:S(2)}, u32[]{:S(2)}) collective-permute-start(f32[48,1536]{1,0:T(8,128)S(1)} %get-tuple-element.286), channel_id=1, source_target_pairs={{0,8},{8,16},{16,24},{24,0},{1,9},{9,17},{17,25},{25,1},{2,10},{10... | collective-permute-start | bytes 884744 | tf_op jit(solution)/shard_map/ppermute | solution.py:56
  674.6 11.2 %collective-permute-start.60 = (bf16[2,48,1152]{2,1,0:T(8,128)(2,1)S(1)}, bf16[2,48,1152]{2,1,0:T(8,128)(2,1)S(1)}, u32[]{:S(2)}, u32[]{:S(2)}) collective-permute-start(bf16[2,48,1152]{2,1,0:T(8,128)(2,1)S(1)} %fusion.191), channel_id=1, source_target_pairs={{0,2},{1,3},{2,0},{3,1},{4,6},{5,7},{6,4},{7,5},{8,10},{9,11},{10,... | collective-permute-start | bytes 663560 | tf_op jit(solution)/shard_map/ppermute | solution.py:51
  676.2 12.5 %collective-permute-start.59 = (bf16[2,48,1152]{2,1,0:T(8,128)(2,1)S(1)}, bf16[2,48,1152]{2,1,0:T(8,128)(2,1)S(1)}, u32[]{:S(2)}, u32[]{:S(2)}) collective-permute-start(bf16[2,48,1152]{2,1,0:T(8,128)(2,1)S(1)} %fusion.190), channel_id=1, source_target_pairs={{0,4},{1,5},{2,6},{3,7},{4,0},{5,1},{6,2},{7,3},{8,12},{9,13},{10,... | collective-permute-start | bytes 663560 | tf_op jit(solution)/shard_map/ppermute | solution.py:51
  701.4 21.2 %collective-permute-start.64 = (f32[48,1152]{1,0:T(8,128)S(1)}, f32[48,1152]{1,0:T(8,128)S(1)}, u32[]{:S(2)}, u32[]{:S(2)}) collective-permute-start(f32[48,1152]{1,0:T(8,128)S(1)} %get-tuple-element.289), channel_id=1, source_target_pairs={{0,16},{8,24},{16,0},{24,8},{1,17},{9,25},{17,1},{25,9},{2,18},{10... | collective-permute-start | bytes 663560 | tf_op jit(solution)/shard_map/ppermute | solution.py:56
  703.4 19.2 %collective-permute-start.63 = (f32[48,1152]{1,0:T(8,128)S(1)}, f32[48,1152]{1,0:T(8,128)S(1)}, u32[]{:S(2)}, u32[]{:S(2)}) collective-permute-start(f32[48,1152]{1,0:T(8,128)S(1)} %get-tuple-element.290), channel_id=1, source_target_pairs={{0,8},{8,16},{16,24},{24,0},{1,9},{9,17},{17,25},{25,1},{2,10},{10... | collective-permute-start | bytes 663560 | tf_op jit(solution)/shard_map/ppermute | solution.py:56
  722.7 12.7 %collective-permute-start.69 = (f32[88,384]{1,0:T(8,128)S(1)}, f32[88,384]{1,0:T(8,128)S(1)}, u32[]{:S(2)}, u32[]{:S(2)}) collective-permute-start(f32[88,384]{1,0:T(8,128)S(1)} %get-tuple-element.297), channel_id=1, source_target_pairs={{0,16},{8,24},{16,0},{24,8},{1,17},{9,25},{17,1},{25,9},{2,18},{10... | collective-permute-start | bytes 405512 | tf_op jit(solution)/shard_map/ppermute | solution.py:56
  723.0 12.5 %collective-permute-start.68 = (f32[88,384]{1,0:T(8,128)S(1)}, f32[88,384]{1,0:T(8,128)S(1)}, u32[]{:S(2)}, u32[]{:S(2)}) collective-permute-start(f32[88,384]{1,0:T(8,128)S(1)} %get-tuple-element.298), channel_id=1, source_target_pairs={{0,8},{8,16},{16,24},{24,0},{1,9},{9,17},{17,25},{25,1},{2,10},{10... | collective-permute-start | bytes 405512 | tf_op jit(solution)/shard_map/ppermute | solution.py:56
  742.1 41.2 %all-to-all-start.4 = ((f32[32,96,128]{2,1,0:T(8,128)}), f32[32,96,128]{2,1,0:T(8,128)}, u32[]{:S(2)}, u32[]{:S(2)}) async-start(f32[32,96,128]{2,1,0:T(8,128)} %bitcast.430), calls=%async_computation.6 | async-start | bytes 3145728 | tf_op jit(solution)/shard_map/all_to_all | solution.py:923
  (155 other events, 1201.1 us)
Sparse Core Ops, SparseCore 0:
  10.9 163.3 all-gather.4
  177.8 122.0 all-gather.8
  485.6 104.2 reduce-scatter.2
  617.8 38.5 reduce-scatter.4
  669.3 53.2 all-gather.6

commit v11 on v10

--- a/solution.py
+++ b/solution.py
@@ -254,12 +254,18 @@
     )(index, source)
 
 
-def assemble_kernel(arrived, up, down, qkv, out, place, tail, landed, sem):
-    copy = pltpu.make_async_copy(arrived, landed, sem)
-    copy.start()
-    copy.wait()
+def assemble_kernel(arrived, up, down, qkv, out, place, tail, landed, sems):
+    def arrival(block):
+        return pltpu.make_async_copy(arrived.at[block], landed.at[block], sems.at[block])
+
+    def begin(block, carry):
+        arrival(block).start()
+        return carry
+
+    lax.fori_loop(0, landed.shape[0], begin, 0)
 
     def one_device(block, carry):
+        arrival(block).wait()
         chip, core = block // 2, block % 2
 
         def put(target, row, lines, width, source_row, source_column):
@@ -292,7 +298,7 @@
         + [jax.ShapeDtypeStruct((devices, 8, TILE), jnp.float32)],
         scratch_shapes=[
             pltpu.VMEM((devices, *SHARE), jnp.bfloat16),
-            pltpu.SemaphoreType.DMA,
+            pltpu.SemaphoreType.DMA((devices,)),
         ],
         compiler_params=pltpu.CompilerParams(vmem_limit_bytes=VMEM_LIMIT),
         cost_estimate=pl.CostEstimate(flops=0, bytes_accessed=60_000_000, transcendentals=0),

time: 832 us -> 831 us (level)
  no operation moved by 1% of the time
where the time goes in v11:
time: 831 us; the launch traced here: 821 us
  matrix products  234 us (28%)
  waiting for transfers between devices  207 us (25%)
  other arithmetic  127 us (15%)
  starting transfers between devices  91.9 us (11%)
  local copies, waits for them, and re-layouts  81.5 us (10%)
  Pallas kernels  53 us (6%)
  between operations  25.4 us (3%)
    ppermute x57, waiting for transfers between devices, swap(): return lax.ppermute(value, 'vocab', [(i, i ^ bit) for i in range(8)])  109 us
    dot_general x11, matrix products, array_multiply(): return jnp.dot(left_side, right_side, preferred_element_type=jnp.float32)  77.6 us
    dot_general x9, matrix products, matmul_left(): lax.dot_general(left_side, right_side, (((0,), (0,)), ((), ())), preferre...  68.8 us
    ppermute x18, waiting for transfers between devices, shift(): lax.ppermute(value, 'dp', [(i, (i + steps) % size) for i in range(size)])  65.6 us
    ppermute x57, starting transfers between devices, swap(): return lax.ppermute(value, 'vocab', [(i, i ^ bit) for i in range(8)])  55.3 us
    dot_general x9, matrix products, trailing_array_multiply(): lax.dot_general(left_side, right_side, (((1,), (1,)), ((), ())), preferre...  44.6 us
    ppermute x18, starting transfers between devices, shift(): lax.ppermute(value, 'dp', [(i, (i + steps) % size) for i in range(size)])  21.3 us
    pallas_call x5, Pallas kernels, unpack_matrix(): pl.pallas_call(functools.partial(unpack_kernel, across=across), grid=(hei...  21.2 us
  transfers between devices with their start and end apart: 86, of which 48 were waited for; matrix products, arithmetic and copies ran while one was open for 39% of the time, Pallas kernels for 5%

profile of v11, /device:TPU:0, one launch (start us, length us, event | category | flops | bytes accessed | tf_op | source)
XLA Modules:
  0.0 820.9 jit_solution(6781285798073038854)
XLA Ops:
  17.5 4.7 broadcast_divide_fusion
  28.0 7.2 send_tiles.1
  35.3 8.5 %fusion.60 = bf16[2048,768]{1,0:T(8,128)(2,1)} fusion(bf16[1920,768]{1,0:T(8,128)(2,1)S(1)} %copy-done, s32[2048]{0:T(1024)S(1)} %bitcast.506), kind=kOutput, calls=%fused_computation.119 | convolution fusion | flops 6045302784 | bytes 6103040 | tf_op jit(solution)/shard_map/dot_general | solution.py:339
  55.2 4.7 all-to-all-done.3
  63.6 8.5 %fusion.62 = bf16[2048,768]{1,0:T(8,128)(2,1)} fusion(bf16[1920,768]{1,0:T(8,128)(2,1)S(1)} %copy-done, s32[2048]{0:T(1024)S(1)} %bitcast.504), kind=kOutput, calls=%fused_computation.121 | convolution fusion | flops 6045302784 | bytes 6103040 | tf_op jit(solution)/shard_map/dot_general | solution.py:339
  73.9 5.2 add.1048
  79.2 10.5 %collective-permute-done.5 = bf16[192,1920]{1,0:T(8,128)(2,1)} collective-permute-done((bf16[192,1920]{1,0:T(8,128)(2,1)}, bf16[192,1920]{1,0:T(8,128)(2,1)}, u32[]{:S(2)}, u32[]{:S(2)}) %collective-permute-start.5) | collective-permute-done | bytes 737312 | tf_op jit(solution)/shard_map/ppermute | solution.py:56
  89.7 15.8 %all-to-all-done.2 = bf16[32,96,128]{2,1,0:T(8,128)(2,1)} async-done(((bf16[32,96,128]{2,1,0:T(8,128)(2,1)}), bf16[32,96,128]{2,1,0:T(8,128)(2,1)}, u32[]{:S(2)}, u32[]{:S(2)}) %all-to-all-start.2) | async-done | bytes 786464 | tf_op jit(solution)/shard_map/all_to_all | solution.py:746
  115.3 4.7 land_tiles.3
  119.9 25.1 %collective-permute-done.6 = bf16[2,256,768]{2,1,0:T(8,128)(2,1)} collective-permute-done((bf16[2,256,768]{2,1,0:T(8,128)(2,1)}, bf16[2,256,768]{2,1,0:T(8,128)(2,1)}, u32[]{:S(2)}, u32[]{:S(2)}) %collective-permute-start.6) | collective-permute-done | bytes 786464 | tf_op jit(solution)/shard_map/ppermute | solution.py:51
  158.9 7.4 fusion.61
  184.9 7.3 fusion.63
  210.5 5.8 unpack_matrix.9
  216.2 6.2 unpack_matrix.5
  238.0 4.5 copy.105
  247.7 10.8 %fusion.288 = (f32[12,512]{1,0:T(8,128)S(1)}, f32[12,512,512]{1,2,0:T(8,128)}) fusion(pred[512]{0:T(512)(128)(4,1)S(1)} %iota_compare_fusion.27, bf16[1,512,3,12,64]{1,4,3,2,0:T(8,128)(2,1)} %bitcast.456), kind=kOutput, calls=%fused_computation.709 | convolution fusion | flops 415236608 | bytes 14180864 | tf_op jit(solution)/shard_map/sub | solution.py:417
  258.6 6.3 fusion.82
  271.3 23.3 %fusion.290 = (f32[512]{0:T(512)S(1)}, f32[512,768]{1,0:T(8,128)}) fusion(f32[512,768]{1,0:T(8,128)} %multiply_add_fusion.4, f32[768]{0:T(1024)S(1)} %get-tuple-element.238, bf16[3072,768]{1,0:T(8,128)(2,1)} %unpack_matrix.5, bf16[768,3072]{1,0:T(8,128)(2,1)} %unpack_matrix.9, f32[3072]{0:T(1024)S(1)} %slice_bitcast_fusion.42), kind=kOutput, calls=%fused_computation.711 | convolution fusion | flops 4937219584 | bytes 12600320 | tf_op jit(solution)/shard_map/dot_general | solution.py:339
  300.0 11.1 %assemble_layer.1 = (bf16[768,3072]{1,0:T(8,128)(2,1)}, bf16[3072,768]{1,0:T(8,128)(2,1)}, bf16[768,2304]{1,0:T(8,128)(2,1)}, bf16[768,768]{1,0:T(8,128)(2,1)}, ...) custom-call(bf16[32,160,1536]{2,1,0:T(8,128)(2,1)} %bitcast.419), custom_call_target="tpu_custom_call" | custom-call | bytes 60000000 | tf_op jit(solution)/shard_map/assemble_layer/pallas_call | solution.py:293
  318.8 6.0 fusion.59
  343.6 9.0 %collective-permute-done.23 = bf16[2,128,768]{2,1,0:T(8,128)(2,1)S(1)} collective-permute-done((bf16[2,128,768]{2,1,0:T(8,128)(2,1)S(1)}, bf16[2,128,768]{2,1,0:T(8,128)(2,1)S(1)}, u32[]{:S(2)}, u32[]{:S(2)}) %collective-permute-start.23) | collective-permute-done | bytes 393248 | tf_op jit(solution)/shard_map/ppermute | solution.py:51
  356.3 18.0 %fusion.25 = (bf16[512,3072]{1,0:T(8,128)(2,1)S(1)}, f32[512,3072]{1,0:T(8,128)}) fusion(f32[3072]{0:T(1024)S(1)} %slice_bitcast_fusion.41, bf16[768,3072]{1,0:T(8,128)(2,1)S(1)} %bitcast.510, f32[512,768]{1,0:T(8,128)S(1)} %multiply_add_fusion.1), kind=kOutput, calls=%fused_computation.59 | convolution fusion | flops 2520121344 | bytes 15740928 | tf_op jit(solution)/shard_map/dot_general | solution.py:339
  385.4 5.1 collective-permute-done.26
  418.0 7.2 multiply_convert_fusion
  441.1 5.3 fusion.300
  446.4 4.3 collective-permute-done.35
  454.7 4.4 collective-permute-done.38
  465.9 7.8 convert_reduce_fusion.1
  477.2 5.9 fusion.111
  484.7 7.4 multiply_reduce_fusion.3
  497.5 6.1 convolution_add_fusion.4
  503.6 6.6 convolution_add_fusion.2
  527.2 6.6 convolution_bitcast_fusion
  540.8 7.7 collective-permute-done.44
  553.1 6.7 fusion.10
  559.8 9.7 %fusion.11 = bf16[1,12,512,512]{2,3,1,0:T(8,128)(2,1)} fusion(f32[1,12,512,512]{2,3,1,0:T(8,128)} %convolution_bitcast_fusion, f32[12,512,512]{1,2,0:T(8,128)S(1)} %bitcast.413, f32[12,512]{1,0:T(8,128)S(1)} %fusion.10, f32[12,512]{1,0:T(8,128)S(1)} %log_add_fusion), kind=kLoop, calls=%fused_computation.28 | loop fusion | flops 12582912 | bytes 31506432 | tf_op jit(solution)/shard_map/convert_element_type | solution.py:511
  578.0 4.8 collective-permute-done.45
  583.8 4.9 reduce-scatter.3.cloned.1.call-done
  588.7 4.8 multiply_bitcast_fusion
  604.4 4.6 fusion.88
  639.0 7.1 collective-permute-done.58
  646.1 15.8 %collective-permute-done.57 = bf16[512,192]{0,1:T(8,128)(2,1)S(1)} collective-permute-done((bf16[512,192]{0,1:T(8,128)(2,1)S(1)}, bf16[512,192]{0,1:T(8,128)(2,1)S(1)}, u32[]{:S(2)}, u32[]{:S(2)}) %collective-permute-start.57) | collective-permute-done | bytes 196640 | tf_op jit(solution)/shard_map/ppermute | solution.py:56
  676.8 7.9 collective-permute-done.60
  688.6 6.8 collective-permute-done.62
  706.4 15.0 %collective-permute-done.64 = f32[48,1152]{1,0:T(8,128)S(1)} collective-permute-done((f32[48,1152]{1,0:T(8,128)S(1)}, f32[48,1152]{1,0:T(8,128)S(1)}, u32[]{:S(2)}, u32[]{:S(2)}) %collective-permute-start.64) | collective-permute-done | bytes 221216 | tf_op jit(solution)/shard_map/ppermute | solution.py:56
  727.8 6.4 collective-permute-done.69
  736.2 4.7 pick_tiles.2
  747.2 32.3 %fusion.3 = f32[192,1920]{1,0:T(8,128)} fusion(bf16[16384,192]{0,1:T(8,128)(2,1)} %all-gather.7.cloned.1.call-done, s32[16384]{0:T(1024)S(1)} %bitcast.487), kind=kOutput, calls=%fused_computation.15 | convolution fusion | flops 12111052800 | bytes 7831552 | tf_op jit(solution)/shard_map/dot_general | solution.py:343
  (678 shorter events, 379.2 us)
Async XLA Ops:
  7.2 187.7 %all-gather.5.cloned.1.call-start = ((), (), s32[]{:S(2)}) async-start(), calls=%async_computation.7 | async-start | bytes 15476736 | tf_op jit(solution)/shard_map/all_gather | solution.py:740
  10.7 12.2 %collective-permute-start = (s32[1,640]{1,0:T(1,128)S(1)}, s32[1,640]{1,0:T(1,128)S(1)}, u32[]{:S(2)}, u32[]{:S(2)}) collective-permute-start(s32[1,640]{1,0:T(1,128)S(1)} %broadcast_in_dim.63), channel_id=1, source_target_pairs={{0,2},{1,3},{2,0},{3,1},{4,6},{5,7},{6,4},{7,5},{8,10},{9,11},{10,... | collective-permute-start | bytes 7688 | tf_op jit(solution)/shard_map/ppermute | solution.py:51
  15.9 30.2 %collective-permute-start.3 = (bf16[192,1920]{1,0:T(8,128)(2,1)}, bf16[192,1920]{1,0:T(8,128)(2,1)}, u32[]{:S(2)}, u32[]{:S(2)}) collective-permute-start(bf16[192,1920]{1,0:T(8,128)(2,1)} %convert_bitcast_fusion), channel_id=1, source_target_pairs={{0,8},{8,16},{16,24},{24,0},{1,9},{9,17},{17,25},{25,1},{2,10},{10... | collective-permute-start | bytes 2211848 | tf_op jit(solution)/shard_map/ppermute | solution.py:56
  46.1 27.8 %collective-permute-start.4 = (bf16[2,2,512,768]{3,2,1,0:T(8,128)(2,1)}, bf16[2,2,512,768]{3,2,1,0:T(8,128)(2,1)}, u32[]{:S(2)}, u32[]{:S(2)}) collective-permute-start(bf16[2,2,512,768]{3,2,1,0:T(8,128)(2,1)} %bitcast.3), channel_id=1, source_target_pairs={{0,1},{1,0},{2,3},{3,2},{4,5},{5,4},{6,7},{7,6},{8,9},{9,8},{10,11... | collective-permute-start | bytes 9437192 | tf_op jit(solution)/shard_map/ppermute | solution.py:51
  53.4 36.2 %collective-permute-start.5 = (bf16[192,1920]{1,0:T(8,128)(2,1)}, bf16[192,1920]{1,0:T(8,128)(2,1)}, u32[]{:S(2)}, u32[]{:S(2)}) collective-permute-start(bf16[192,1920]{1,0:T(8,128)(2,1)} %collective-permute-done.3), channel_id=1, source_target_pairs={{0,8},{8,16},{16,24},{24,0},{1,9},{9,17},{17,25},{25,1},{2,10},{10... | collective-permute-start | bytes 2211848 | tf_op jit(solution)/shard_map/ppermute | solution.py:56
  60.0 45.5 %all-to-all-start.2 = ((bf16[32,96,128]{2,1,0:T(8,128)(2,1)}), bf16[32,96,128]{2,1,0:T(8,128)(2,1)}, u32[]{:S(2)}, u32[]{:S(2)}) async-start(bf16[32,96,128]{2,1,0:T(8,128)(2,1)} %bitcast.462), calls=%async_computation.2 | async-start | bytes 1572864 | tf_op jit(solution)/shard_map/all_to_all | solution.py:746
  63.3 236.7 %all-gather.9.cloned.1.call-start = ((), (), s32[]{:S(2)}) async-start(), calls=%async_computation.11 | async-start | bytes 16220160 | tf_op jit(solution)/shard_map/all_gather | solution.py:773
  107.8 37.2 %collective-permute-start.6 = (bf16[2,256,768]{2,1,0:T(8,128)(2,1)}, bf16[2,256,768]{2,1,0:T(8,128)(2,1)}, u32[]{:S(2)}, u32[]{:S(2)}) collective-permute-start(bf16[2,256,768]{2,1,0:T(8,128)(2,1)} %slice_bitcast_fusion.12), channel_id=1, source_target_pairs={{0,2},{1,3},{2,0},{3,1},{4,6},{5,7},{6,4},{7,5},{8,10},{9,11},{10,... | collective-permute-start | bytes 2359304 | tf_op jit(solution)/shard_map/ppermute | solution.py:51
  111.3 37.1 %collective-permute-start.7 = (bf16[2,256,768]{2,1,0:T(8,128)(2,1)}, bf16[2,256,768]{2,1,0:T(8,128)(2,1)}, u32[]{:S(2)}, u32[]{:S(2)}) collective-permute-start(bf16[2,256,768]{2,1,0:T(8,128)(2,1)} %slice_bitcast_fusion.11), channel_id=1, source_target_pairs={{0,4},{1,5},{2,6},{3,7},{4,0},{5,1},{6,2},{7,3},{8,12},{9,13},{10,... | collective-permute-start | bytes 2359304 | tf_op jit(solution)/shard_map/ppermute | solution.py:51
  112.8 38.0 %collective-permute-start.8 = (bf16[192,1920]{1,0:T(8,128)(2,1)}, bf16[192,1920]{1,0:T(8,128)(2,1)}, u32[]{:S(2)}, u32[]{:S(2)}) collective-permute-start(bf16[192,1920]{1,0:T(8,128)(2,1)} %collective-permute-done.5), channel_id=1, source_target_pairs={{0,8},{8,16},{16,24},{24,0},{1,9},{9,17},{17,25},{25,1},{2,10},{10... | collective-permute-start | bytes 2211848 | tf_op jit(solution)/shard_map/ppermute | solution.py:56
  151.2 437.5 %reduce-scatter.3.cloned.1.call-start = ((), (), s32[]{:S(2)}) async-start(), calls=%async_computation.8 | async-start | bytes 7372800 | tf_op jit(solution)/shard_map/reduce_scatter | solution.py:888
  155.5 10.9 %collective-permute-start.10 = (bf16[256,768]{1,0:T(8,128)(2,1)S(1)}, bf16[256,768]{1,0:T(8,128)(2,1)S(1)}, u32[]{:S(2)}, u32[]{:S(2)}) collective-permute-start(bf16[256,768]{1,0:T(8,128)(2,1)S(1)} %slice_bitcast_fusion.35), channel_id=1, source_target_pairs={{0,2},{1,3},{2,0},{3,1},{4,6},{5,7},{6,4},{7,5},{8,10},{9,11},{10,... | collective-permute-start | bytes 1179656 | tf_op jit(solution)/shard_map/ppermute | solution.py:51
  167.8 24.5 %collective-permute-start.11 = (bf16[2,2,512,768]{3,2,1,0:T(8,128)(2,1)S(1)}, bf16[2,2,512,768]{3,2,1,0:T(8,128)(2,1)S(1)}, u32[]{:S(2)}, u32[]{:S(2)}) collective-permute-start(bf16[2,2,512,768]{3,2,1,0:T(8,128)(2,1)S(1)} %bitcast.513), channel_id=1, source_target_pairs={{0,1},{1,0},{2,3},{3,2},{4,5},{5,4},{6,7},{7,6},{8,9},{9,8},{10,11... | collective-permute-start | bytes 9437192 | tf_op jit(solution)/shard_map/ppermute | solution.py:51
  197.0 30.4 %collective-permute-start.18 = (bf16[2,256,768]{2,1,0:T(8,128)(2,1)}, bf16[2,256,768]{2,1,0:T(8,128)(2,1)}, u32[]{:S(2)}, u32[]{:S(2)}) collective-permute-start(bf16[2,256,768]{2,1,0:T(8,128)(2,1)} %slice_bitcast_fusion.10), channel_id=1, source_target_pairs={{0,2},{1,3},{2,0},{3,1},{4,6},{5,7},{6,4},{7,5},{8,10},{9,11},{10,... | collective-permute-start | bytes 2359304 | tf_op jit(solution)/shard_map/ppermute | solution.py:51
  200.2 29.6 %collective-permute-start.19 = (bf16[2,256,768]{2,1,0:T(8,128)(2,1)}, bf16[2,256,768]{2,1,0:T(8,128)(2,1)}, u32[]{:S(2)}, u32[]{:S(2)}) collective-permute-start(bf16[2,256,768]{2,1,0:T(8,128)(2,1)} %slice_bitcast_fusion.9), channel_id=1, source_target_pairs={{0,4},{1,5},{2,6},{3,7},{4,0},{5,1},{6,2},{7,3},{8,12},{9,13},{10,... | collective-permute-start | bytes 2359304 | tf_op jit(solution)/shard_map/ppermute | solution.py:51
  244.2 23.7 %collective-permute-start.21 = (bf16[256,768]{1,0:T(8,128)(2,1)}, bf16[256,768]{1,0:T(8,128)(2,1)}, u32[]{:S(2)}, u32[]{:S(2)}) collective-permute-start(bf16[256,768]{1,0:T(8,128)(2,1)} %slice_bitcast_fusion.33), channel_id=1, source_target_pairs={{0,2},{1,3},{2,0},{3,1},{4,6},{5,7},{6,4},{7,5},{8,10},{9,11},{10,... | collective-permute-start | bytes 1179656 | tf_op jit(solution)/shard_map/ppermute | solution.py:51
  247.3 21.6 %collective-permute-start.20 = (bf16[256,768]{1,0:T(8,128)(2,1)S(1)}, bf16[256,768]{1,0:T(8,128)(2,1)}, u32[]{:S(2)}, u32[]{:S(2)}) collective-permute-start(bf16[256,768]{1,0:T(8,128)(2,1)S(1)} %slice_bitcast_fusion.34), channel_id=1, source_target_pairs={{0,4},{1,5},{2,6},{3,7},{4,0},{5,1},{6,2},{7,3},{8,12},{9,13},{10,... | collective-permute-start | bytes 1179656 | tf_op jit(solution)/shard_map/ppermute | solution.py:51
  317.8 23.6 %collective-permute-start.22 = (bf16[1,128,768]{2,1,0:T(8,128)(2,1)S(1)}, bf16[1,128,768]{2,1,0:T(8,128)(2,1)S(1)}, u32[]{:S(2)}, u32[]{:S(2)}) collective-permute-start(bf16[1,128,768]{2,1,0:T(8,128)(2,1)S(1)} %bitcast.450), channel_id=1, source_target_pairs={{0,2},{1,3},{2,0},{3,1},{4,6},{5,7},{6,4},{7,5},{8,10},{9,11},{10,... | collective-permute-start | bytes 589832 | tf_op jit(solution)/shard_map/ppermute | solution.py:51
  341.5 11.1 %collective-permute-start.23 = (bf16[2,128,768]{2,1,0:T(8,128)(2,1)S(1)}, bf16[2,128,768]{2,1,0:T(8,128)(2,1)S(1)}, u32[]{:S(2)}, u32[]{:S(2)}) collective-permute-start(bf16[2,128,768]{2,1,0:T(8,128)(2,1)S(1)} %pad_maximum_fusion.4), channel_id=1, source_target_pairs={{0,4},{1,5},{2,6},{3,7},{4,0},{5,1},{6,2},{7,3},{8,12},{9,13},{10,... | collective-permute-start | bytes 1179656 | tf_op jit(solution)/shard_map/ppermute | solution.py:51
  439.2 11.6 %collective-permute-start.35 = (f32[2,64,768]{2,1,0:T(8,128)S(1)}, f32[2,64,768]{2,1,0:T(8,128)S(1)}, u32[]{:S(2)}, u32[]{:S(2)}) collective-permute-start(f32[2,64,768]{2,1,0:T(8,128)S(1)} %slice_bitcast_fusion.31), channel_id=1, source_target_pairs={{0,2},{1,3},{2,0},{3,1},{4,6},{5,7},{6,4},{7,5},{8,10},{9,11},{10,... | collective-permute-start | bytes 1179656 | tf_op jit(solution)/shard_map/ppermute | solution.py:51
  440.4 11.2 %collective-permute-start.37 = (f32[2,64,768]{2,1,0:T(8,128)S(1)}, f32[2,64,768]{2,1,0:T(8,128)S(1)}, u32[]{:S(2)}, u32[]{:S(2)}) collective-permute-start(f32[2,64,768]{2,1,0:T(8,128)S(1)} %slice_bitcast_fusion.29), channel_id=1, source_target_pairs={{0,4},{1,5},{2,6},{3,7},{4,0},{5,1},{6,2},{7,3},{8,12},{9,13},{10,... | collective-permute-start | bytes 1179656 | tf_op jit(solution)/shard_map/ppermute | solution.py:51
  477.2 18.3 %collective-permute-start.40 = (f32[768,1536]{1,0:T(8,128)}, f32[768,1536]{1,0:T(8,128)}, u32[]{:S(2)}, u32[]{:S(2)}) collective-permute-start(f32[768,1536]{1,0:T(8,128)} %fusion.70), channel_id=1, source_target_pairs={{0,1},{1,0},{2,3},{3,2},{4,5},{5,4},{6,7},{7,6},{8,9},{9,8},{10,11... | collective-permute-start | bytes 14155784 | tf_op jit(solution)/shard_map/ppermute | solution.py:51
  483.1 20.5 %collective-permute-start.39 = (f32[3072,384]{1,0:T(8,128)}, f32[3072,384]{1,0:T(8,128)}, u32[]{:S(2)}, u32[]{:S(2)}) collective-permute-start(f32[3072,384]{1,0:T(8,128)} %fusion.111), channel_id=1, source_target_pairs={{0,1},{1,0},{2,3},{3,2},{4,5},{5,4},{6,7},{7,6},{8,9},{9,8},{10,11... | collective-permute-start | bytes 14155784 | tf_op jit(solution)/shard_map/ppermute | solution.py:51
  484.3 181.6 %reduce-scatter.5.cloned.1.call-start = ((), (), s32[]{:S(2)}) async-start(), calls=%async_computation.9 | async-start | bytes 1474560 | tf_op jit(solution)/shard_map/reduce_scatter | solution.py:603
  516.0 22.5 %collective-permute-start.42 = (bf16[2,2,192,384]{3,2,0,1:T(8,128)(2,1)}, bf16[2,2,192,384]{3,2,0,1:T(8,128)(2,1)}, u32[]{:S(2)}, u32[]{:S(2)}) collective-permute-start(bf16[2,2,192,384]{3,2,0,1:T(8,128)(2,1)} %fusion.104), channel_id=1, source_target_pairs={{0,4},{1,5},{2,6},{3,7},{4,0},{5,1},{6,2},{7,3},{8,12},{9,13},{10,... | collective-permute-start | bytes 1769480 | tf_op jit(solution)/shard_map/ppermute | solution.py:51
  516.9 22.8 %collective-permute-start.41 = (bf16[2,2,192,384]{3,2,0,1:T(8,128)(2,1)S(1)}, bf16[2,2,192,384]{3,2,0,1:T(8,128)(2,1)}, u32[]{:S(2)}, u32[]{:S(2)}) collective-permute-start(bf16[2,2,192,384]{3,2,0,1:T(8,128)(2,1)S(1)} %fusion.103), channel_id=1, source_target_pairs={{0,2},{1,3},{2,0},{3,1},{4,6},{5,7},{6,4},{7,5},{8,10},{9,11},{10,... | collective-permute-start | bytes 1769480 | tf_op jit(solution)/shard_map/ppermute | solution.py:51
  533.8 14.7 %collective-permute-start.44 = (bf16[2,2,48,1536]{3,2,0,1:T(8,128)(2,1)S(1)}, bf16[2,2,48,1536]{3,2,0,1:T(8,128)(2,1)S(1)}, u32[]{:S(2)}, u32[]{:S(2)}) collective-permute-start(bf16[2,2,48,1536]{3,2,0,1:T(8,128)(2,1)S(1)} %copy-done.65), channel_id=1, source_target_pairs={{0,4},{1,5},{2,6},{3,7},{4,0},{5,1},{6,2},{7,3},{8,12},{9,13},{10,... | collective-permute-start | bytes 1769480 | tf_op jit(solution)/shard_map/ppermute | solution.py:51
  537.5 14.3 %collective-permute-start.43 = (bf16[2,2,48,1536]{3,2,0,1:T(8,128)(2,1)S(1)}, bf16[2,2,48,1536]{3,2,0,1:T(8,128)(2,1)S(1)}, u32[]{:S(2)}, u32[]{:S(2)}) collective-permute-start(bf16[2,2,48,1536]{3,2,0,1:T(8,128)(2,1)S(1)} %fusion.105), channel_id=1, source_target_pairs={{0,2},{1,3},{2,0},{3,1},{4,6},{5,7},{6,4},{7,5},{8,10},{9,11},{10,... | collective-permute-start | bytes 1769480 | tf_op jit(solution)/shard_map/ppermute | solution.py:51
  552.1 20.7 %collective-permute-start.48 = (bf16[2,48,1536]{2,1,0:T(8,128)(2,1)S(1)}, bf16[2,48,1536]{2,1,0:T(8,128)(2,1)S(1)}, u32[]{:S(2)}, u32[]{:S(2)}) collective-permute-start(bf16[2,48,1536]{2,1,0:T(8,128)(2,1)S(1)} %fusion.117), channel_id=1, source_target_pairs={{0,2},{1,3},{2,0},{3,1},{4,6},{5,7},{6,4},{7,5},{8,10},{9,11},{10,... | collective-permute-start | bytes 884744 | tf_op jit(solution)/shard_map/ppermute | solution.py:51
  569.6 14.2 %collective-permute-start.47 = (bf16[2,48,1536]{2,1,0:T(8,128)(2,1)S(1)}, bf16[2,48,1536]{2,1,0:T(8,128)(2,1)S(1)}, u32[]{:S(2)}, u32[]{:S(2)}) collective-permute-start(bf16[2,48,1536]{2,1,0:T(8,128)(2,1)S(1)} %fusion.116), channel_id=1, source_target_pairs={{0,4},{1,5},{2,6},{3,7},{4,0},{5,1},{6,2},{7,3},{8,12},{9,13},{10,... | collective-permute-start | bytes 884744 | tf_op jit(solution)/shard_map/ppermute | solution.py:51
  571.5 11.4 %collective-permute-start.45 = (bf16[2,192,384]{2,1,0:T(8,128)(2,1)S(1)}, bf16[2,192,384]{2,1,0:T(8,128)(2,1)S(1)}, u32[]{:S(2)}, u32[]{:S(2)}) collective-permute-start(bf16[2,192,384]{2,1,0:T(8,128)(2,1)S(1)} %fusion.114), channel_id=1, source_target_pairs={{0,4},{1,5},{2,6},{3,7},{4,0},{5,1},{6,2},{7,3},{8,12},{9,13},{10,... | collective-permute-start | bytes 884744 | tf_op jit(solution)/shard_map/ppermute | solution.py:51
  609.0 13.1 %collective-permute-start.52 = (f32[768,1152]{1,0:T(8,128)}, f32[768,1152]{1,0:T(8,128)}, u32[]{:S(2)}, u32[]{:S(2)}) collective-permute-start(f32[768,1152]{1,0:T(8,128)} %fusion.88), channel_id=1, source_target_pairs={{0,1},{1,0},{2,3},{3,2},{4,5},{5,4},{6,7},{7,6},{8,9},{9,8},{10,11... | collective-permute-start | bytes 10616840 | tf_op jit(solution)/shard_map/ppermute | solution.py:51
  616.5 130.7 %all-gather.7.cloned.1.call-start = ((), (), s32[]{:S(2)}) async-start(), calls=%async_computation.10 | async-start | bytes 7077888 | tf_op jit(solution)/shard_map/all_gather | solution.py:919
  629.3 33.6 %collective-permute-start.54 = (bf16[2,2,48,1152]{3,2,0,1:T(8,128)(2,1)}, bf16[2,2,48,1152]{3,2,0,1:T(8,128)(2,1)}, u32[]{:S(2)}, u32[]{:S(2)}) collective-permute-start(bf16[2,2,48,1152]{3,2,0,1:T(8,128)(2,1)} %fusion.108), channel_id=1, source_target_pairs={{0,4},{1,5},{2,6},{3,7},{4,0},{5,1},{6,2},{7,3},{8,12},{9,13},{10,... | collective-permute-start | bytes 1327112 | tf_op jit(solution)/shard_map/ppermute | solution.py:51
  631.2 14.9 %collective-permute-start.58 = (bf16[512,192]{0,1:T(8,128)(2,1)S(1)}, bf16[512,192]{0,1:T(8,128)(2,1)S(1)}, u32[]{:S(2)}, u32[]{:S(2)}) collective-permute-start(bf16[512,192]{0,1:T(8,128)(2,1)S(1)} %get-tuple-element.293), channel_id=1, source_target_pairs={{0,24},{8,0},{16,8},{24,16},{1,25},{9,1},{17,9},{25,17},{2,26},{10... | collective-permute-start | bytes 589832 | tf_op jit(solution)/shard_map/ppermute | solution.py:56
  634.0 27.9 %collective-permute-start.57 = (bf16[512,192]{0,1:T(8,128)(2,1)S(1)}, bf16[512,192]{0,1:T(8,128)(2,1)S(1)}, u32[]{:S(2)}, u32[]{:S(2)}) collective-permute-start(bf16[512,192]{0,1:T(8,128)(2,1)S(1)} %get-tuple-element.294), channel_id=1, source_target_pairs={{0,16},{8,24},{16,0},{24,8},{1,17},{9,25},{17,1},{25,9},{2,18},{10... | collective-permute-start | bytes 589832 | tf_op jit(solution)/shard_map/ppermute | solution.py:56
  634.3 27.6 %collective-permute-start.56 = (bf16[512,192]{0,1:T(8,128)(2,1)S(1)}, bf16[512,192]{0,1:T(8,128)(2,1)S(1)}, u32[]{:S(2)}, u32[]{:S(2)}) collective-permute-start(bf16[512,192]{0,1:T(8,128)(2,1)S(1)} %get-tuple-element.295), channel_id=1, source_target_pairs={{0,8},{8,16},{16,24},{24,0},{1,9},{9,17},{17,25},{25,1},{2,10},{10... | collective-permute-start | bytes 589832 | tf_op jit(solution)/shard_map/ppermute | solution.py:56
  637.4 27.4 %collective-permute-start.53 = (bf16[2,2,48,1152]{3,2,0,1:T(8,128)(2,1)S(1)}, bf16[2,2,48,1152]{3,2,0,1:T(8,128)(2,1)S(1)}, u32[]{:S(2)}, u32[]{:S(2)}) collective-permute-start(bf16[2,2,48,1152]{3,2,0,1:T(8,128)(2,1)S(1)} %fusion.107), channel_id=1, source_target_pairs={{0,2},{1,3},{2,0},{3,1},{4,6},{5,7},{6,4},{7,5},{8,10},{9,11},{10,... | collective-permute-start | bytes 1327112 | tf_op jit(solution)/shard_map/ppermute | solution.py:51
  669.7 25.8 %collective-permute-start.51 = (f32[48,1536]{1,0:T(8,128)S(1)}, f32[48,1536]{1,0:T(8,128)S(1)}, u32[]{:S(2)}, u32[]{:S(2)}) collective-permute-start(f32[48,1536]{1,0:T(8,128)S(1)} %get-tuple-element.284), channel_id=1, source_target_pairs={{0,24},{8,0},{16,8},{24,16},{1,25},{9,1},{17,9},{25,17},{2,26},{10... | collective-permute-start | bytes 884744 | tf_op jit(solution)/shard_map/ppermute | solution.py:56
  669.8 26.6 %collective-permute-start.50 = (f32[48,1536]{1,0:T(8,128)S(1)}, f32[48,1536]{1,0:T(8,128)S(1)}, u32[]{:S(2)}, u32[]{:S(2)}) collective-permute-start(f32[48,1536]{1,0:T(8,128)S(1)} %get-tuple-element.285), channel_id=1, source_target_pairs={{0,16},{8,24},{16,0},{24,8},{1,17},{9,25},{17,1},{25,9},{2,18},{10... | collective-permute-start | bytes 884744 | tf_op jit(solution)/shard_map/ppermute | solution.py:56
  670.4 26.0 %collective-permute-start.49 = (f32[48,1536]{1,0:T(8,128)S(1)}, f32[48,1536]{1,0:T(8,128)S(1)}, u32[]{:S(2)}, u32[]{:S(2)}) collective-permute-start(f32[48,1536]{1,0:T(8,128)S(1)} %get-tuple-element.286), channel_id=1, source_target_pairs={{0,8},{8,16},{16,24},{24,0},{1,9},{9,17},{17,25},{25,1},{2,10},{10... | collective-permute-start | bytes 884744 | tf_op jit(solution)/shard_map/ppermute | solution.py:56
  673.4 11.2 %collective-permute-start.60 = (bf16[2,48,1152]{2,1,0:T(8,128)(2,1)S(1)}, bf16[2,48,1152]{2,1,0:T(8,128)(2,1)S(1)}, u32[]{:S(2)}, u32[]{:S(2)}) collective-permute-start(bf16[2,48,1152]{2,1,0:T(8,128)(2,1)S(1)} %fusion.191), channel_id=1, source_target_pairs={{0,2},{1,3},{2,0},{3,1},{4,6},{5,7},{6,4},{7,5},{8,10},{9,11},{10,... | collective-permute-start | bytes 663560 | tf_op jit(solution)/shard_map/ppermute | solution.py:51
  675.0 12.5 %collective-permute-start.59 = (bf16[2,48,1152]{2,1,0:T(8,128)(2,1)S(1)}, bf16[2,48,1152]{2,1,0:T(8,128)(2,1)S(1)}, u32[]{:S(2)}, u32[]{:S(2)}) collective-permute-start(bf16[2,48,1152]{2,1,0:T(8,128)(2,1)S(1)} %fusion.190), channel_id=1, source_target_pairs={{0,4},{1,5},{2,6},{3,7},{4,0},{5,1},{6,2},{7,3},{8,12},{9,13},{10,... | collective-permute-start | bytes 663560 | tf_op jit(solution)/shard_map/ppermute | solution.py:51
  700.3 21.2 %collective-permute-start.64 = (f32[48,1152]{1,0:T(8,128)S(1)}, f32[48,1152]{1,0:T(8,128)S(1)}, u32[]{:S(2)}, u32[]{:S(2)}) collective-permute-start(f32[48,1152]{1,0:T(8,128)S(1)} %get-tuple-element.289), channel_id=1, source_target_pairs={{0,16},{8,24},{16,0},{24,8},{1,17},{9,25},{17,1},{25,9},{2,18},{10... | collective-permute-start | bytes 663560 | tf_op jit(solution)/shard_map/ppermute | solution.py:56
  702.2 19.2 %collective-permute-start.63 = (f32[48,1152]{1,0:T(8,128)S(1)}, f32[48,1152]{1,0:T(8,128)S(1)}, u32[]{:S(2)}, u32[]{:S(2)}) collective-permute-start(f32[48,1152]{1,0:T(8,128)S(1)} %get-tuple-element.290), channel_id=1, source_target_pairs={{0,8},{8,16},{16,24},{24,0},{1,9},{9,17},{17,25},{25,1},{2,10},{10... | collective-permute-start | bytes 663560 | tf_op jit(solution)/shard_map/ppermute | solution.py:56
  721.6 12.7 %collective-permute-start.69 = (f32[88,384]{1,0:T(8,128)S(1)}, f32[88,384]{1,0:T(8,128)S(1)}, u32[]{:S(2)}, u32[]{:S(2)}) collective-permute-start(f32[88,384]{1,0:T(8,128)S(1)} %get-tuple-element.297), channel_id=1, source_target_pairs={{0,16},{8,24},{16,0},{24,8},{1,17},{9,25},{17,1},{25,9},{2,18},{10... | collective-permute-start | bytes 405512 | tf_op jit(solution)/shard_map/ppermute | solution.py:56
  721.8 12.5 %collective-permute-start.68 = (f32[88,384]{1,0:T(8,128)S(1)}, f32[88,384]{1,0:T(8,128)S(1)}, u32[]{:S(2)}, u32[]{:S(2)}) collective-permute-start(f32[88,384]{1,0:T(8,128)S(1)} %get-tuple-element.298), channel_id=1, source_target_pairs={{0,8},{8,16},{16,24},{24,0},{1,9},{9,17},{17,25},{25,1},{2,10},{10... | collective-permute-start | bytes 405512 | tf_op jit(solution)/shard_map/ppermute | solution.py:56
  740.9 41.2 %all-to-all-start.4 = ((f32[32,96,128]{2,1,0:T(8,128)}), f32[32,96,128]{2,1,0:T(8,128)}, u32[]{:S(2)}, u32[]{:S(2)}) async-start(f32[32,96,128]{2,1,0:T(8,128)} %bitcast.430), calls=%async_computation.6 | async-start | bytes 3145728 | tf_op jit(solution)/shard_map/all_to_all | solution.py:929
  (155 other events, 1201.2 us)
Sparse Core Ops, SparseCore 0:
  10.9 163.3 all-gather.4
  177.8 122.0 all-gather.8
  484.4 104.2 reduce-scatter.2
  616.6 38.5 reduce-scatter.4
  668.1 53.2 all-gather.6
